TPU v7x, 32 devices: a whole 2x2x4 slice. The times are simulated.
32 devices in a mesh: tm: 16 (over z, x, core), rows: 2 (over y).
Axes of the slice: x: 2, y: 2, z: 4, core: 2. Of those that a mesh axis runs over, the one named last changes fastest.
Arguments:
- video: bfloat16 [32, 16, 480, 128], P('tm', 'rows'), may hold values from -1000 to 1000, as said below
- spatial_weight: bfloat16 [3, 3, 128, 128], replicated, may hold values from -0.1875 to 0.1875
- norm_gain: float32 [128], replicated, may hold values from 0.5 to 1.5
- norm_shift: float32 [128], replicated, may hold values from -3 to 3
- temporal_weight: bfloat16 [3, 3, 128, 128], replicated, may hold values from -0.3125 to 0.3125
Outputs:
- encoded: bfloat16 [32, 16, 480, 128], P('tm', 'rows')
Inputs may be any that keep to these rules, and one draw needn't show every extreme that they name: `video`: feature values are finite and of moderate size.
All inputs are finite; a program needn't handle non-finite values.
Results may differ from a plain program's by a relative error of at most 0.0065.
Values may be sent and summed in bfloat16 or wider, within the bound.
No kernel may reach another device: no remote copies, remote signals or barrier semaphores. Data moves between devices by JAX's collectives and lax.ppermute only.
A program may use at most 64 MiB of HBM per device.

v0:
```python
import jax
import jax.numpy as jnp
from jax import lax
from jax.sharding import PartitionSpec as P

GROUPS = 32


def padded_2(array, sides, width):
    for axis, dim in sides:
        size, length = (lax.axis_size(axis), array.shape[dim])
        up = [(i, (i + 1) % size) for i in range(size - 1)]
        down = [(j, i) for i, j in up]
        last = lax.slice_in_dim(array, length - width, length, axis=dim)
        leading = lax.slice_in_dim(array, 0, width, axis=dim)
        before = lax.ppermute(last, axis, up)
        after = lax.ppermute(leading, axis, down)
        array = jnp.concatenate([before, array, after], axis=dim)
    return array


def temporal_layer(extended, lead, dilation, kernels):
    own = extended.shape[0] - lead
    total = extended[lead:].astype(jnp.float32)
    for tap_index in range(3):
        start = lead - tap_index * dilation
        total = total + jnp.einsum(
            "trwc,cd->trwd",
            extended[start : start + own],
            kernels[tap_index],
            preferred_element_type=jnp.float32,
        )
    return total.astype(jnp.bfloat16)


def body(video, spatial_weight, norm_gain, norm_shift, temporal_weight):
    fr_local, band, width, chans = video.shape
    padded = padded_2(video, (("rows", 1),), 1)
    padded = jnp.pad(padded, ((0, 0), (0, 0), (1, 1), (0, 0)))
    pieces = [
        padded[:, row_tap : row_tap + band, col_tap : col_tap + width, :]
        for row_tap in range(3)
        for col_tap in range(3)
    ]
    patches = jnp.concatenate(pieces, axis=-1).reshape(fr_local * band * width, 9 * chans)
    conv = jnp.dot(
        patches, spatial_weight.reshape(9 * chans, chans), preferred_element_type=jnp.float32
    )
    per_group = chans // GROUPS
    grouped = conv.reshape(fr_local, band, width, GROUPS, per_group)
    part_sum = jnp.sum(grouped, axis=(1, 2, 4))
    part_square = jnp.sum(grouped * grouped, axis=(1, 2, 4))
    total_sum, total_square = lax.psum((part_sum, part_square), "rows")
    count = jnp.float32(band * lax.axis_size("rows") * width * per_group)
    mean = total_sum / count
    var = total_square / count - mean * mean
    normed = (grouped - mean[:, None, None, :, None]) * lax.rsqrt(var + 1e-05)[
        :, None, None, :, None
    ]
    normed = normed.reshape(fr_local, band, width, chans) * norm_gain + norm_shift
    hidden = jax.nn.silu(normed).astype(jnp.bfloat16)
    current = lax.all_to_all(hidden, "tm", split_axis=2, concat_axis=0, tiled=True)
    for layer, dilation in enumerate((1, 2, 4)):
        lead = 2 * dilation
        extended = jnp.pad(current, ((lead, 0), (0, 0), (0, 0), (0, 0)))
        current = temporal_layer(extended, lead, dilation, temporal_weight[layer])
    return lax.all_to_all(current, "tm", split_axis=0, concat_axis=2, tiled=True)


def solution(mesh):
    return jax.shard_map(
        body,
        mesh=mesh,
        in_specs=(P("tm", "rows", None, None), P(), P(), P(), P()),
        out_specs=P("tm", "rows", None, None),
        check_vma=False,
    )
```

profile of v0, /device:TPU:0, one launch (start us, length us, event | category | flops | bytes accessed | tf_op | source)
XLA Modules:
  0.0 154.3 jit_solution(4578269416225532073)
XLA Ops:
  0.0 1.1 fusion.36
  1.1 4.9 %collective-permute-start = (bf16[2,1,480,128]{3,2,1,0:T(8,128)(2,1)S(1)}, bf16[2,1,480,128]{3,2,1,0:T(8,128)(2,1)S(1)}, u32[]{:S(2)}, u32[]{:S(2)}) collective-permute-start(bf16[2,1,480,128]{3,2,1,0:T(8,128)(2,1)S(1)} %get-tuple-element.9), channel_id=1, source_target_pairs={{0,1},{2,3},{4,5},{6,7},{8,9},{10,11},{12,13},{14,15},{16,17},{18,... | collective-permute-start | bytes 737288 | tf_op jit(solution)/shard_map/ppermute | solution.py:16
  6.0 1.3 collective-permute-start.1
  7.3 1.2 copy.14
  8.5 0.1 dot_general.35
  8.5 0.0 copy-start
  8.6 2.6 %collective-permute-done = bf16[2,1,480,128]{3,2,1,0:T(8,128)(2,1)S(1)} collective-permute-done((bf16[2,1,480,128]{3,2,1,0:T(8,128)(2,1)S(1)}, bf16[2,1,480,128]{3,2,1,0:T(8,128)(2,1)S(1)}, u32[]{:S(2)}, u32[]{:S(2)}) %collective-permute-start) | collective-permute-done | bytes 245792 | tf_op jit(solution)/shard_map/ppermute | solution.py:16
  11.2 4.1 %collective-permute-done.1 = bf16[2,1,480,128]{3,2,1,0:T(8,128)(2,1)S(1)} collective-permute-done((bf16[2,1,480,128]{3,2,1,0:T(8,128)(2,1)S(1)}, bf16[2,1,480,128]{3,2,1,0:T(8,128)(2,1)S(1)}, u32[]{:S(2)}, u32[]{:S(2)}) %collective-permute-start.1) | collective-permute-done | bytes 245792 | tf_op jit(solution)/shard_map/ppermute | solution.py:17
  15.3 2.1 %fusion.7 = bf16[2,10,482,128]{3,2,1,0:T(8,128)(2,1)S(1)} fusion(bf16[2,1,480,128]{3,2,1,0:T(8,128)(2,1)S(1)} %collective-permute-done.1, bf16[2,8,480,128]{3,2,1,0:T(8,128)(2,1)} %param.5, bf16[2,1,480,128]{3,2,1,0:T(8,128)(2,1)S(1)} %collective-permute-done), kind=kLoop, calls=%fused_computation.15 | loop fusion | flops 14807040 | bytes 4925440 | tf_op jit(solution)/shard_map/concatenate | solution.py:18
  17.4 0.3 slice_dynamic-update-slice_fusion.5
  17.7 0.0 copy-done
  17.7 0.5 fusion.9
  18.2 0.8 slice_dynamic-update-slice_fusion.4
  19.0 0.5 slice_dynamic-update-slice_fusion.3
  19.5 0.5 constant_dynamic-update-slice_fusion
  20.0 0.8 slice_dynamic-update-slice_fusion.2
  20.8 0.5 slice_dynamic-update-slice_fusion.1
  21.3 0.5 fusion.8
  21.8 0.8 slice_dynamic-update-slice_fusion
  22.6 7.1 %fusion.35 = (f32[2,32]{1,0:T(2,128)S(1)}, f32[2,32]{1,0:T(2,128)S(1)}, f32[2,8,480,32,4]{2,3,4,1,0:T(8,128)}) fusion(bf16[32,4,1152,1,1]{2,1,0,4,3:T(4,128)(2,1)S(1)} %bitcast.100, bf16[2,8,480,1152]{3,2,1,0:T(8,128)(2,1)S(1)} %slice_dynamic-update-slice_fusion), kind=kOutput, calls=%fused_computation.54 | convolution fusion | flops 2267873280 | bytes 21922304 | tf_op jit(solution)/shard_map/dot_general | solution.py:46
  29.7 5.1 %all-reduce.4 = (f32[2,32]{1,0:T(2,128)S(1)}, f32[2,32]{1,0:T(2,128)S(1)}) all-reduce(f32[2,32]{1,0:T(2,128)S(1)} %get-tuple-element.6, f32[2,32]{1,0:T(2,128)S(1)} %get-tuple-element.5), channel_id=1, replica_groups=mesh['tm'=16,'rows'=2] {'rows'}, use_global_device_ids=true, to_apply=%region_3.4 | all-reduce | flops 128 | bytes 1024 | tf_op jit(solution)/shard_map/psum | solution.py:53
  34.8 2.9 %subtract_multiply_fusion = f32[2,8,480,32,4]{2,3,4,1,0:T(8,128)S(1)} fusion(f32[2,8,480,32,4]{2,3,4,1,0:T(8,128)} %get-tuple-element.13, f32[2,32]{1,0:T(2,128)S(1)} %get-tuple-element.12, f32[2,32]{1,0:T(2,128)S(1)} %get-tuple-element.11), kind=kLoop, calls=%fused_computation.7 | loop fusion | flops 1966080 | bytes 7864832 | tf_op jit(solution)/shard_map/mul | solution.py:57
  37.7 0.0 copy-start.2
  37.7 0.0 copy-start.3
  37.7 2.4 %copy.16 = f32[2,8,480,32,4]{2,1,4,3,0:T(8,128)S(1)} copy(f32[2,8,480,32,4]{2,3,4,1,0:T(8,128)S(1)} %subtract_multiply_fusion) | data formatting | bytes 7864320 | tf_op jit(solution)/shard_map/mul | solution.py:57
  40.1 0.0 copy-done.2
  40.1 0.0 copy-done.3
  40.2 1.4 multiply_convert_fusion
  41.6 3.4 %copy.17 = bf16[2,8,480,128]{3,1,0,2:T(8,128)(2,1)} copy(bf16[2,8,480,128]{2,1,3,0:T(8,128)(2,1)S(1)} %multiply_convert_fusion) | data formatting | bytes 3932160 | tf_op jit(solution)/shard_map/convert_element_type | solution.py:61
  45.0 0.0 copy-start.1
  45.0 51.1 %all_to_all.36 = bf16[2,8,480,128]{3,1,0,2:T(8,128)(2,1)S(1)} all-to-all(bf16[2,8,480,128]{3,1,0,2:T(8,128)(2,1)} %copy.17), channel_id=1, replica_groups=mesh['tm'=16,'rows'=2] {'tm'}, dimensions={2} | all-to-all | bytes 3932160 | tf_op jit(solution)/shard_map/all_to_all | solution.py:62
  96.1 0.3 copy.19
  96.4 0.0 copy-done.1
  96.4 0.7 fusion.22
  97.1 0.7 fusion.24
  97.7 0.9 add_convert_fusion.2
  98.7 0.7 fusion.17
  99.3 0.7 fusion.19
  100.0 1.0 add_convert_fusion.1
  101.0 0.7 fusion.12
  101.7 0.7 fusion.14
  102.3 1.0 add_convert_fusion
  103.3 49.4 %all_to_all.37 = bf16[32,8,30,128]{3,1,2,0:T(8,128)(2,1)S(1)} all-to-all(bf16[32,8,30,128]{3,1,2,0:T(8,128)(2,1)S(1)} %add_convert_fusion), channel_id=1, replica_groups=mesh['tm'=16,'rows'=2] {'tm'}, dimensions={0} | all-to-all | bytes 3932160 | tf_op jit(solution)/shard_map/all_to_all | solution.py:67
  152.6 0.1 copy.20
  152.8 1.5 copy.21
  (1 shorter events, 0.0 us)
Async XLA Ops:
  1.1 10.1 %collective-permute-start = (bf16[2,1,480,128]{3,2,1,0:T(8,128)(2,1)S(1)}, bf16[2,1,480,128]{3,2,1,0:T(8,128)(2,1)S(1)}, u32[]{:S(2)}, u32[]{:S(2)}) collective-permute-start(bf16[2,1,480,128]{3,2,1,0:T(8,128)(2,1)S(1)} %get-tuple-element.9), channel_id=1, source_target_pairs={{0,1},{2,3},{4,5},{6,7},{8,9},{10,11},{12,13},{14,15},{16,17},{18,... | collective-permute-start | bytes 737288 | tf_op jit(solution)/shard_map/ppermute | solution.py:16
  6.0 9.3 %collective-permute-start.1 = (bf16[2,1,480,128]{3,2,1,0:T(8,128)(2,1)S(1)}, bf16[2,1,480,128]{3,2,1,0:T(8,128)(2,1)S(1)}, u32[]{:S(2)}, u32[]{:S(2)}) collective-permute-start(bf16[2,1,480,128]{3,2,1,0:T(8,128)(2,1)S(1)} %get-tuple-element.10), channel_id=1, source_target_pairs={{1,0},{3,2},{5,4},{7,6},{9,8},{11,10},{13,12},{15,14},{17,16},{19,... | collective-permute-start | bytes 737288 | tf_op jit(solution)/shard_map/ppermute | solution.py:17
  8.5 9.2 %copy-start = (bf16[2,8,480,128]{3,2,1,0:T(8,128)(2,1)S(1)}, bf16[2,8,480,128]{3,2,1,0:T(8,128)(2,1)}, u32[]{:S(2)}) copy-start(bf16[2,8,480,128]{3,2,1,0:T(8,128)(2,1)} %param.5) | copy-start | bytes 5898244
  37.7 2.5 %copy-start.2 = (f32[128]{0:T(128)S(1)}, f32[128]{0:T(128)}, u32[]{:S(2)}) copy-start(f32[128]{0:T(128)} %param.8) | copy-start | bytes 1540
  37.7 2.5 %copy-start.3 = (f32[128]{0:T(128)S(1)}, f32[128]{0:T(128)}, u32[]{:S(2)}) copy-start(f32[128]{0:T(128)} %param.7) | copy-start | bytes 1540
  45.0 51.4 %copy-start.1 = (bf16[3,3,128,128]{3,2,1,0:T(8,128)(2,1)S(1)}, bf16[3,3,128,128]{3,2,1,0:T(8,128)(2,1)}, u32[]{:S(2)}) copy-start(bf16[3,3,128,128]{3,2,1,0:T(8,128)(2,1)} %param.9) | copy-start | bytes 884740
where the time goes:
time: 155 us; the launch traced here: 154 us
  blocking collectives  106 us (68%)
  local copies, waits for them, and re-layouts  14.3 us (9%)
  matrix products  13.9 us (9%)
  other arithmetic  7.38 us (5%)
  waiting for transfers between devices  6.75 us (4%)
  starting transfers between devices  6.18 us (4%)
    all_to_all x1, blocking collectives, body(): lax.all_to_all(hidden, 'tm', split_axis=2, concat_axis=0, tiled=True)  51.1 us
    all_to_all x1, blocking collectives, body(): lax.all_to_all(current, 'tm', split_axis=0, concat_axis=2, tiled=True)  49.4 us
    dot_general x1, matrix products, body(): jnp.dot(patches, spatial_weight.reshape(9 * chans, chans), preferred_elem...  7.05 us
    dot_general x9, matrix products, temporal_layer(): jnp.einsum('trwc,cd->trwd', extended[start:start + own], kernels[tap_inde...  6.83 us
    psum x1, blocking collectives, body(): total_sum, total_square = lax.psum((part_sum, part_square), 'rows')  5.1 us
    ppermute x1, starting transfers between devices, padded_2(): before = lax.ppermute(last, axis, up)  4.89 us
    ppermute x1, waiting for transfers between devices, padded_2(): after = lax.ppermute(leading, axis, down)  4.13 us
    unnamed x14, local copies, waits for them, and re-layouts  3.41 us
  transfers between devices with their start and end apart: 2, of which 2 were waited for; matrix products, arithmetic and copies ran while one was open for 1% of the time, Pallas kernels for 0%

commit v1 on v0

v1 whole, which is shorter than its diff:
```python
import functools

import jax
import jax.numpy as jnp
from jax import lax
from jax.experimental import pallas as pl
from jax.experimental.pallas import tpu as pltpu
from jax.sharding import PartitionSpec as P

GROUPS = 32
SPAN = 8
CHUNKS = 4
VMEM = pltpu.VMEM
ANY = pl.ANY
F32 = jnp.float32
BF16 = jnp.bfloat16


def vspec():
    return pl.BlockSpec(memory_space=VMEM)


def sspec():
    return pl.BlockSpec(memory_space=pltpu.SMEM)


def params(mib):
    return pltpu.CompilerParams(vmem_limit_bytes=mib << 20)


def cost(flops, nbytes):
    return pl.CostEstimate(flops=int(flops), bytes_accessed=int(nbytes), transcendentals=0)


def shifted_sum(taps):
    width, ch = taps.shape[0], taps.shape[1] // 3
    column = lax.broadcasted_iota(jnp.int32, (width, ch), 0)
    left = jnp.where(column == 0, 0.0, pltpu.roll(taps[:, :ch], 1, 0))
    right = jnp.where(column == width - 1, 0.0, pltpu.roll(taps[:, 2 * ch :], width - 1, 0))
    return left + taps[:, ch : 2 * ch] + right


def fold(value):
    return jnp.sum(value.reshape(value.shape[0] // 8, 8, value.shape[1]), axis=0)


def conv_kernel(band, video_ref, weight_ref, inner_ref, edge_ref, sums_ref, wide_ref):
    ch = video_ref.shape[-1]

    @pl.when(pl.program_id(0) == 0)
    def _():
        wide_ref[...] = jnp.zeros_like(wide_ref)
        for out in range(2):
            for col in range(3):
                for row in range(3):
                    wide_ref[
                        (out + row) * ch : (out + row + 1) * ch,
                        (out * 3 + col) * ch : (out * 3 + col + 1) * ch,
                    ] = weight_ref[row, col]

    total = jnp.zeros((8, ch), F32)
    square = jnp.zeros((8, ch), F32)
    for first in range(0, band, 2):
        rows = [r for r in range(first - 1, first + 3) if 0 <= r < band]
        lhs = jnp.concatenate([video_ref[0, r] for r in rows], axis=-1)
        skip = (rows[0] - (first - 1)) * ch
        wide = jnp.dot(
            lhs, wide_ref[skip : skip + len(rows) * ch, :], preferred_element_type=F32
        )
        for out in range(2):
            value = shifted_sum(wide[:, out * 3 * ch : (out + 1) * 3 * ch])
            row = first + out
            if row == 0:
                edge_ref[0, 0] = value
            elif row == band - 1:
                edge_ref[0, 1] = value
            else:
                inner_ref[0, row - 1] = value
                total = total + fold(value)
                square = square + fold(value * value)
    sums_ref[0, 0] = total
    sums_ref[0, 1] = square


def conv_call(video, weight):
    frames, band, width, ch = video.shape
    return pl.pallas_call(
        functools.partial(conv_kernel, band),
        grid=(frames,),
        in_specs=[
            pl.BlockSpec((1, band, width, ch), lambda f: (f, 0, 0, 0)),
            pl.BlockSpec(weight.shape, lambda f: (0, 0, 0, 0)),
        ],
        out_specs=[
            pl.BlockSpec((1, band - 2, width, ch), lambda f: (f, 0, 0, 0)),
            pl.BlockSpec((1, 2, width, ch), lambda f: (f, 0, 0, 0)),
            pl.BlockSpec((1, 2, 8, ch), lambda f: (f, 0, 0, 0)),
        ],
        out_shape=[
            jax.ShapeDtypeStruct((frames, band - 2, width, ch), F32),
            jax.ShapeDtypeStruct((frames, 2, width, ch), F32),
            jax.ShapeDtypeStruct((frames, 2, 8, ch), F32),
        ],
        scratch_shapes=[VMEM((4 * ch, 6 * ch), BF16)],
        compiler_params=params(32),
        cost_estimate=cost(frames * band * width * 18 * ch * ch, frames * band * width * ch * 6),
        name="conv",
    )(video, weight)


def edge_kernel(flag_ref, part_ref, above_ref, below_ref, weight_ref, sums_ref, edge_ref, out_sums_ref):
    frames = part_ref.shape[0]
    for frame in range(frames):
        total, square = sums_ref[frame, 0], sums_ref[frame, 1]
        for side, (halo_ref, tap) in enumerate(((above_ref, 0), (below_ref, 2))):
            halo = halo_ref[frame]
            halo = jnp.where(flag_ref[side] > 0, halo, jnp.zeros_like(halo))
            taps = jnp.concatenate([weight_ref[tap, col] for col in range(3)], axis=-1)
            wide = jnp.dot(halo, taps, preferred_element_type=F32)
            value = part_ref[frame, side] + shifted_sum(wide)
            edge_ref[frame, side] = value
            total = total + fold(value)
            square = square + fold(value * value)
        out_sums_ref[frame, 0] = total
        out_sums_ref[frame, 1] = square


def edge_call(flags, part, above, below, weight, sums):
    return pl.pallas_call(
        edge_kernel,
        in_specs=[sspec()] + [vspec()] * 5,
        out_specs=[vspec()] * 2,
        out_shape=[
            jax.ShapeDtypeStruct(part.shape, F32),
            jax.ShapeDtypeStruct(sums.shape, F32),
        ],
        compiler_params=params(32),
        cost_estimate=cost(part.size * 6 * part.shape[-1], part.size * 10),
        name="edge",
    )(flags, part, above, below, weight, sums)


def over_groups(value, per_group):
    lane = lax.broadcasted_iota(jnp.int32, value.shape, 1)
    lanes = value.shape[1]
    step = 1
    while step < per_group:
        value = value + pltpu.roll(value, lanes - step, 1)
        step *= 2
    value = jnp.where(lane % per_group == 0, value, 0.0)
    step = 1
    while step < per_group:
        value = value + pltpu.roll(value, step, 1)
        step *= 2
    return value


def norm_kernel(count, per_group, members, chunks, me_ref, inner_ref, edge_ref, own_ref, peer_ref, gain_ref, shift_ref, *refs):
    outs, hidden_ref = refs[:-1], refs[-1]
    frames, inner, width, ch = inner_ref.shape
    band = inner + 2
    for frame in range(frames):
        sums = [
            jnp.broadcast_to(
                jnp.sum(own_ref[frame, i] + peer_ref[frame, i], axis=0, keepdims=True), (8, ch)
            )
            for i in range(2)
        ]
        mean = over_groups(sums[0], per_group) / count
        var = over_groups(sums[1], per_group) / count - mean * mean
        scale = (lax.rsqrt(var + 1e-05) * gain_ref[...])[:1]
        mean = mean[:1]
        shift = shift_ref[...]

        def put(row, value):
            v = (value - mean) * scale + shift
            v = 0.5 * v * (1.0 + jnp.tanh(0.5 * v))
            hidden_ref[frame, row] = v.astype(BF16)

        put(0, edge_ref[frame, 0])
        put(band - 1, edge_ref[frame, 1])

        @pl.loop(0, inner)
        def _(row):
            put(row + 1, inner_ref[frame, row])

    flat = hidden_ref.reshape(frames, band * width, ch)
    size = band * width // (members * chunks)
    me = me_ref[0]
    for chunk in range(chunks):
        for k in range(members):
            start = pl.multiple_of(((me ^ k) * chunks + chunk) * size, 16)
            outs[chunk * members + k][...] = flat[:, pl.ds(start, size), :]


def norm_call(me, inner, edge, own, peer, gain, shift, count, members, chunks):
    frames, rows, width, ch = inner.shape
    band = rows + 2
    size = band * width // (members * chunks)
    return pl.pallas_call(
        functools.partial(norm_kernel, count, ch // GROUPS, members, chunks),
        in_specs=[sspec()] + [vspec()] * 6,
        out_specs=[vspec()] * (members * chunks),
        out_shape=[jax.ShapeDtypeStruct((frames, size, ch), BF16)] * (members * chunks),
        scratch_shapes=[VMEM((frames, band, width, ch), BF16)],
        compiler_params=params(40),
        cost_estimate=cost(frames * band * width * ch * 10, frames * band * width * ch * 6),
        name="norm",
    )(me, inner, edge, own, peer, gain.reshape(1, ch), shift.reshape(1, ch))


def pair_weights(weight_ref, layer, wide_ref):
    ch = weight_ref.shape[-1]
    wide_ref[...] = jnp.zeros_like(wide_ref)
    for out in range(2):
        for tap in range(3):
            row = out + 2 - tap
            wide_ref[row * ch : (row + 1) * ch, out * ch : (out + 1) * ch] = weight_ref[layer, tap]


def pair(read, write, time, dilation, wide_ref):
    ch = wide_ref.shape[1] // 2
    frames = [read(time + (a - 2) * dilation) for a in range(4)]
    both = jnp.dot(jnp.concatenate(frames, axis=-1), wide_ref[...], preferred_element_type=F32)
    write(time, (both[:, :ch] + frames[2].astype(F32)).astype(BF16))
    write(time + dilation, (both[:, ch:] + frames[3].astype(F32)).astype(BF16))


def early_kernel(members, me_ref, *refs):
    pieces, (halo_ref, weight_ref, out_ref, u0_ref, u1_ref, wide_ref) = refs[:members], refs[members:]
    step = pieces[0].shape[0]
    u0_ref[: SPAN - 2] = halo_ref[...]
    for k in range(members):
        u0_ref[pl.ds(SPAN - 2 + (me_ref[0] ^ k) * step, step)] = pieces[k][...]
    pair_weights(weight_ref, 0, wide_ref)

    def write1(t, value):
        u1_ref[t + 4] = value

    def write2(t, value):
        out_ref[t] = value

    for time in range(-4, SPAN, 2):
        pair(lambda t: u0_ref[t + SPAN - 2], write1, time, 1, wide_ref)
    pair_weights(weight_ref, 1, wide_ref)
    for time in range(0, SPAN, 4):
        for odd in range(2):
            pair(lambda t: u1_ref[t + 4], write2, time + odd, 2, wide_ref)


def early_call(me, pieces, halo, weight):
    members = len(pieces)
    _, size, ch = pieces[0].shape
    return pl.pallas_call(
        functools.partial(early_kernel, members),
        in_specs=[sspec()] + [vspec()] * (members + 2),
        out_specs=vspec(),
        out_shape=jax.ShapeDtypeStruct((SPAN, size, ch), BF16),
        scratch_shapes=[
            VMEM((2 * SPAN - 2, size, ch), BF16),
            VMEM((SPAN + 4, size, ch), BF16),
            VMEM((4 * ch, 2 * ch), BF16),
        ],
        compiler_params=params(32),
        cost_estimate=cost(20 * size * 6 * ch * ch, 22 * size * ch * 2),
        name="early",
    )(me, *pieces, halo, weight)


def late_kernel(members, me_ref, own_ref, halo_ref, weight_ref, *refs):
    outs, (u3_ref, wide_ref) = refs[:members], refs[members:]
    step = outs[0].shape[0]
    pair_weights(weight_ref, 2, wide_ref)

    def write3(t, value):
        u3_ref[t] = value

    for time in range(4):
        pair(
            lambda t: own_ref[t] if t >= 0 else halo_ref[t + SPAN], write3, time, 4, wide_ref
        )
    for k in range(members):
        outs[k][...] = u3_ref[pl.ds((me_ref[0] ^ k) * step, step)]


def late_call(me, own, halo, weight, members):
    frames, size, ch = own.shape
    return pl.pallas_call(
        functools.partial(late_kernel, members),
        in_specs=[sspec()] + [vspec()] * 3,
        out_specs=[vspec()] * members,
        out_shape=[jax.ShapeDtypeStruct((frames // members, size, ch), BF16)] * members,
        scratch_shapes=[VMEM(own.shape, BF16), VMEM((4 * ch, 2 * ch), BF16)],
        compiler_params=params(32),
        cost_estimate=cost(8 * size * 6 * ch * ch, 24 * size * ch * 2),
        name="late",
    )(me, own, halo, weight)


def place_kernel(members, chunks, me_ref, *refs):
    pieces, (out_ref, sem) = refs[: members * chunks], refs[members * chunks :]
    copies = [
        pltpu.make_async_copy(
            pieces[chunk * members + k],
            out_ref.at[:, me_ref[0] ^ k, chunk],
            sem.at[chunk * members + k],
        )
        for chunk in range(chunks)
        for k in range(members)
    ]
    for copy in copies:
        copy.start()
    for copy in copies:
        copy.wait()


def place_call(me, pieces, members, chunks):
    frames, size, ch = pieces[0].shape
    return pl.pallas_call(
        functools.partial(place_kernel, members, chunks),
        in_specs=[sspec()] + [pl.BlockSpec(memory_space=ANY)] * len(pieces),
        out_specs=pl.BlockSpec(memory_space=ANY),
        out_shape=jax.ShapeDtypeStruct((frames, members, chunks, size, ch), BF16),
        scratch_shapes=[pltpu.SemaphoreType.DMA((len(pieces),))],
        cost_estimate=cost(0, 2 * len(pieces) * frames * size * ch * 2),
        name="place",
    )(me, *pieces)


def halo_rows(video):
    size, row = lax.axis_size("rows"), lax.axis_index("rows")
    band = video.shape[1]
    if size == 2:
        mine = lax.dynamic_slice_in_dim(video, jnp.where(row == 0, band - 1, 0), 1, axis=1)[:, 0]
        other = lax.ppermute(mine, "rows", [(0, 1), (1, 0)])
        return other, other
    up = [(i, i + 1) for i in range(size - 1)]
    down = [(j, i) for i, j in up]
    return lax.ppermute(video[:, -1], "rows", up), lax.ppermute(video[:, 0], "rows", down)


def other_sums(sums):
    if lax.axis_size("rows") == 2:
        return lax.ppermute(sums, "rows", [(0, 1), (1, 0)])
    return lax.psum(sums, "rows") - sums


def body(video, spatial_weight, norm_gain, norm_shift, temporal_weight):
    frames, band, width, ch = video.shape
    total, here = lax.axis_size("tm"), lax.axis_index("tm")
    members = SPAN // frames
    me = jnp.reshape(here % members, (1,)).astype(jnp.int32)
    row, rows = lax.axis_index("rows"), lax.axis_size("rows")
    flags = jnp.stack([row > 0, row < rows - 1]).astype(jnp.int32)
    swaps = [[(i, i ^ k) for i in range(total)] for k in range(members)]
    onward = [(i, i + members) for i in range(total - members)]

    above, below = halo_rows(video)
    inner, part, sums = conv_call(video, spatial_weight)
    edge, sums = edge_call(flags, part, above, below, spatial_weight, sums)
    count = band * rows * width * (ch // GROUPS)
    pieces = norm_call(
        me, inner, edge, sums, other_sums(sums), norm_gain, norm_shift, count, members, CHUNKS
    )

    def swap(four):
        return [four[0]] + [lax.ppermute(four[k], "tm", swaps[k]) for k in range(1, members)]

    mine = [swap(pieces[c * members : (c + 1) * members]) for c in range(CHUNKS)]
    results = []
    for four in mine:
        slots = [
            functools.reduce(
                lambda acc, k: jnp.where(me[0] == (slot ^ k), four[k], acc),
                range(1, members),
                four[0],
            )
            for slot in range(1, members)
        ]
        tail = jnp.concatenate(slots, axis=0)[-(SPAN - 2) :]
        halo = lax.ppermute(tail, "tm", onward)
        u2 = early_call(me, four, halo, temporal_weight)
        before = lax.ppermute(u2, "tm", onward)
        results += swap(late_call(me, u2, before, temporal_weight, members))
    out = place_call(me, results, members, CHUNKS)
    return out.reshape(frames, band, width, ch)


def solution(mesh):
    return jax.shard_map(
        body,
        mesh=mesh,
        in_specs=(P("tm", "rows", None, None), P(), P(), P(), P()),
        out_specs=P("tm", "rows", None, None),
        check_vma=False,
    )
```

time: 155 us -> 199 us (1.28)
  blocking collectives: 106 us -> 0 us
  Pallas kernels: 0 us -> 73.5 us
  waiting for transfers between devices: 6.75 us -> 61 us
  starting transfers between devices: 6.18 us -> 50 us
  matrix products: 13.9 us -> 0 us
  other arithmetic: 7.38 us -> 0.45 us
    all_to_all x2 -> x0, blocking collectives: 100 us -> none  [the longest x1 51.1 us: body(): lax.all_to_all(hidden, 'tm', split_axis=2, concat_axis=0, tiled=True)]
    pallas_call x0 -> x12, Pallas kernels: none -> 73.5 us  [the longest x1 60.8 us: place_call(): pl.pallas_call(functools.partial(place_kernel, members, chunks), in_specs...]
    ppermute x2 -> x34, waiting for transfers between devices: 6.75 us -> 61 us  [the longest x4 32 us: body(): before = lax.ppermute(u2, 'tm', onward)]
    ppermute x2 -> x34, starting transfers between devices: 6.18 us -> 50 us  [the longest x4 17.5 us: body(): before = lax.ppermute(u2, 'tm', onward)]
    dot_general x10 -> x0, matrix products: 13.9 us -> none  [the longest x1 7.05 us: body(): jnp.dot(patches, spatial_weight.reshape(9 * chans, chans), preferred_elem...]
    unnamed x14 -> x68, local copies, waits for them, and re-layouts: 3.41 us -> 11.7 us
    psum x1 -> x0, blocking collectives: 5.1 us -> none  [body(): total_sum, total_square = lax.psum((part_sum, part_square), 'rows')]
    convert_element_type x1 -> x0, local copies, waits for them, and re-layouts: 3.36 us -> none  [body(): hidden = jax.nn.silu(normed).astype(jnp.bfloat16)]
  transfers between devices with their start and end apart: 2 -> 34, of which waited for: 2 -> 19; matrix products, arithmetic and copies ran while one was open for 1% -> 0% of each run, Pallas kernels for 0% -> 5%
where the time goes in v1:
time: 199 us; the launch traced here: 198 us
  Pallas kernels  73.5 us (37%)
  waiting for transfers between devices  61 us (31%)
  starting transfers between devices  50 us (25%)
  local copies, waits for them, and re-layouts  12.7 us (6%)
    pallas_call x1, Pallas kernels, place_call(): pl.pallas_call(functools.partial(place_kernel, members, chunks), in_specs...  60.8 us
    ppermute x4, waiting for transfers between devices, body(): before = lax.ppermute(u2, 'tm', onward)  32 us
    ppermute x24, waiting for transfers between devices, swap(): lax.ppermute(four[k], 'tm', swaps[k])  19.1 us
    ppermute x4, starting transfers between devices, body(): before = lax.ppermute(u2, 'tm', onward)  17.5 us
    ppermute x24, starting transfers between devices, swap(): lax.ppermute(four[k], 'tm', swaps[k])  15.6 us
    ppermute x4, starting transfers between devices, body(): halo = lax.ppermute(tail, 'tm', onward)  12.4 us
    unnamed x68, local copies, waits for them, and re-layouts  11.7 us
    ppermute x4, waiting for transfers between devices, body(): halo = lax.ppermute(tail, 'tm', onward)  7.77 us
  transfers between devices with their start and end apart: 34, of which 19 were waited for; matrix products, arithmetic and copies ran while one was open for 0% of the time, Pallas kernels for 5%

profile of v1, /device:TPU:0, one launch (start us, length us, event | category | flops | bytes accessed | tf_op | source)
XLA Modules:
  0.0 198.2 jit_solution(3342464184599392810)
XLA Ops:
  0.0 1.0 dynamic-slice_bitcast_fusion
  1.0 3.0 %collective-permute-start = (bf16[2,480,128]{2,1,0:T(8,128)(2,1)S(1)}, bf16[2,480,128]{2,1,0:T(8,128)(2,1)S(1)}, u32[]{:S(2)}, u32[]{:S(2)}) collective-permute-start(bf16[2,480,128]{2,1,0:T(8,128)(2,1)S(1)} %dynamic-slice_bitcast_fusion), channel_id=1, source_target_pairs={{0,1},{1,0},{2,3},{3,2},{4,5},{5,4},{6,7},{7,6},{8,9},{9,8},{10,11... | collective-permute-start | bytes 737288 | tf_op jit(solution)/shard_map/ppermute | solution.py:335
  4.1 1.0 copy-done.3
  5.0 1.5 copy-done.9
  6.6 3.6 %conv.1 = (f32[2,6,480,128]{3,2,1,0:T(8,128)S(1)}, f32[2,2,480,128]{3,2,1,0:T(8,128)S(1)}, f32[2,2,8,128]{3,2,1,0:T(8,128)S(1)}) custom-call(bf16[2,8,480,128]{3,2,1,0:T(8,128)(2,1)S(1)} %copy-done.9, bf16[3,3,128,128]{3,2,1,0:T(8,128)(2,1)S(1)} %copy-done.3), custom_call_target="tpu_custom_call" | custom-call | flops 2264924160 | bytes 5898240 | tf_op jit(solution)/shard_map/conv/pallas_call | solution.py:87
  10.2 1.2 edge.1
  11.4 0.9 copy-done.1
  12.3 1.5 collective-permute-start.1
  13.8 2.2 %collective-permute-done.1.peer_ref = f32[2,2,8,128]{3,2,1,0:T(8,128)S(1)} collective-permute-done((f32[2,2,8,128]{3,2,1,0:T(8,128)S(1)}, f32[2,2,8,128]{3,2,1,0:T(8,128)S(1)}, u32[]{:S(2)}, u32[]{:S(2)}) %collective-permute-start.1) | collective-permute-done | bytes 16416 | tf_op jit(solution)/shard_map/ppermute | solution.py:344
  16.0 1.2 copy-done.2
  17.3 2.5 %norm.1 = (bf16[2,240,128]{2,1,0:T(8,128)(2,1)S(1)}, bf16[2,240,128]{2,1,0:T(8,128)(2,1)S(1)}, bf16[2,240,128]{2,1,0:T(8,128)(2,1)S(1)}, bf16[2,240,128]{2,1,0:T...) custom-call(s32[1]{0:T(128)} %bitcast.me_ref, ...), custom_call_target="tpu_custom_call" | custom-call | flops 9830400 | bytes 5898240 | tf_op jit(solution)/shard_map/norm/pallas_call | solution.py:200
  25.6 1.5 collective-permute-start.27
  27.8 1.5 collective-permute-start.19
  29.3 2.6 %collective-permute-done.27.refs_2_ = bf16[2,240,128]{2,1,0:T(8,128)(2,1)S(1)} collective-permute-done((bf16[2,240,128]{2,1,0:T(8,128)(2,1)}, bf16[2,240,128]{2,1,0:T(8,128)(2,1)S(1)}, u32[]{:S(2)}, u32[]{:S(2)}) %collective-permute-start.27) | collective-permute-done | bytes 122912 | tf_op jit(solution)/shard_map/ppermute | solution.py:367
  32.0 1.9 collective-permute-done.28.refs_3_
  33.8 1.5 collective-permute-start.11
  35.9 1.3 collective-permute-done.19.refs_2_
  37.2 1.9 collective-permute-done.20.refs_3_
  39.1 1.5 collective-permute-start.3
  41.3 1.2 collective-permute-done.11.refs_2_
  42.5 3.5 %collective-permute-start.29 = (bf16[6,240,128]{2,1,0:T(8,128)(2,1)S(1)}, bf16[6,240,128]{2,1,0:T(8,128)(2,1)S(1)}, u32[]{:S(2)}, u32[]{:S(2)}) collective-permute-start(bf16[6,240,128]{2,1,0:T(8,128)(2,1)S(1)} %pad_maximum_fusion.3), channel_id=1, source_target_pairs={{0,8},{2,10},{4,12},{6,14},{8,16},{10,18},{12,20},{14,22},{16,24},... | collective-permute-start | bytes 1105928 | tf_op jit(solution)/shard_map/ppermute | solution.py:381
  46.0 3.5 %collective-permute-start.21 = (bf16[6,240,128]{2,1,0:T(8,128)(2,1)S(1)}, bf16[6,240,128]{2,1,0:T(8,128)(2,1)S(1)}, u32[]{:S(2)}, u32[]{:S(2)}) collective-permute-start(bf16[6,240,128]{2,1,0:T(8,128)(2,1)S(1)} %pad_maximum_fusion.2), channel_id=1, source_target_pairs={{0,8},{2,10},{4,12},{6,14},{8,16},{10,18},{12,20},{14,22},{16,24},... | collective-permute-start | bytes 1105928 | tf_op jit(solution)/shard_map/ppermute | solution.py:381
  49.6 3.5 %collective-permute-start.13 = (bf16[6,240,128]{2,1,0:T(8,128)(2,1)S(1)}, bf16[6,240,128]{2,1,0:T(8,128)(2,1)S(1)}, u32[]{:S(2)}, u32[]{:S(2)}) collective-permute-start(bf16[6,240,128]{2,1,0:T(8,128)(2,1)S(1)} %pad_maximum_fusion.1), channel_id=1, source_target_pairs={{0,8},{2,10},{4,12},{6,14},{8,16},{10,18},{12,20},{14,22},{16,24},... | collective-permute-start | bytes 1105928 | tf_op jit(solution)/shard_map/ppermute | solution.py:381
  53.2 1.9 collective-permute-start.5
  55.2 0.9 early.7.own_ref
  56.1 4.2 %collective-permute-start.30 = (bf16[8,240,128]{2,1,0:T(8,128)(2,1)S(1)}, bf16[8,240,128]{2,1,0:T(8,128)(2,1)S(1)}, u32[]{:S(2)}, u32[]{:S(2)}) collective-permute-start(bf16[8,240,128]{2,1,0:T(8,128)(2,1)S(1)} %early.7.own_ref), channel_id=1, source_target_pairs={{0,8},{2,10},{4,12},{6,14},{8,16},{10,18},{12,20},{14,22},{16,24},... | collective-permute-start | bytes 1474568 | tf_op jit(solution)/shard_map/ppermute | solution.py:383
  60.3 2.6 %collective-permute-done.21.refs_4_ = bf16[6,240,128]{2,1,0:T(8,128)(2,1)S(1)} collective-permute-done((bf16[6,240,128]{2,1,0:T(8,128)(2,1)S(1)}, bf16[6,240,128]{2,1,0:T(8,128)(2,1)S(1)}, u32[]{:S(2)}, u32[]{:S(2)}) %collective-permute-start.21) | collective-permute-done | bytes 368672 | tf_op jit(solution)/shard_map/ppermute | solution.py:381
  62.9 0.9 early.6.own_ref
  63.8 4.4 %collective-permute-start.22 = (bf16[8,240,128]{2,1,0:T(8,128)(2,1)S(1)}, bf16[8,240,128]{2,1,0:T(8,128)(2,1)S(1)}, u32[]{:S(2)}, u32[]{:S(2)}) collective-permute-start(bf16[8,240,128]{2,1,0:T(8,128)(2,1)S(1)} %early.6.own_ref), channel_id=1, source_target_pairs={{0,8},{2,10},{4,12},{6,14},{8,16},{10,18},{12,20},{14,22},{16,24},... | collective-permute-start | bytes 1474568 | tf_op jit(solution)/shard_map/ppermute | solution.py:383
  68.2 2.6 %collective-permute-done.13.refs_4_ = bf16[6,240,128]{2,1,0:T(8,128)(2,1)S(1)} collective-permute-done((bf16[6,240,128]{2,1,0:T(8,128)(2,1)S(1)}, bf16[6,240,128]{2,1,0:T(8,128)(2,1)S(1)}, u32[]{:S(2)}, u32[]{:S(2)}) %collective-permute-start.13) | collective-permute-done | bytes 368672 | tf_op jit(solution)/shard_map/ppermute | solution.py:381
  70.8 0.9 early.5.own_ref
  71.7 4.4 %collective-permute-start.14 = (bf16[8,240,128]{2,1,0:T(8,128)(2,1)S(1)}, bf16[8,240,128]{2,1,0:T(8,128)(2,1)S(1)}, u32[]{:S(2)}, u32[]{:S(2)}) collective-permute-start(bf16[8,240,128]{2,1,0:T(8,128)(2,1)S(1)} %early.5.own_ref), channel_id=1, source_target_pairs={{0,8},{2,10},{4,12},{6,14},{8,16},{10,18},{12,20},{14,22},{16,24},... | collective-permute-start | bytes 1474568 | tf_op jit(solution)/shard_map/ppermute | solution.py:383
  76.1 2.6 %collective-permute-done.5.refs_4_ = bf16[6,240,128]{2,1,0:T(8,128)(2,1)S(1)} collective-permute-done((bf16[6,240,128]{2,1,0:T(8,128)(2,1)S(1)}, bf16[6,240,128]{2,1,0:T(8,128)(2,1)S(1)}, u32[]{:S(2)}, u32[]{:S(2)}) %collective-permute-start.5) | collective-permute-done | bytes 368672 | tf_op jit(solution)/shard_map/ppermute | solution.py:381
  78.7 0.9 early.4.own_ref
  79.6 4.4 %collective-permute-start.6 = (bf16[8,240,128]{2,1,0:T(8,128)(2,1)S(1)}, bf16[8,240,128]{2,1,0:T(8,128)(2,1)S(1)}, u32[]{:S(2)}, u32[]{:S(2)}) collective-permute-start(bf16[8,240,128]{2,1,0:T(8,128)(2,1)S(1)} %early.4.own_ref), channel_id=1, source_target_pairs={{0,8},{2,10},{4,12},{6,14},{8,16},{10,18},{12,20},{14,22},{16,24},... | collective-permute-start | bytes 1474568 | tf_op jit(solution)/shard_map/ppermute | solution.py:383
  84.0 5.2 %collective-permute-done.30.halo_ref = bf16[8,240,128]{2,1,0:T(8,128)(2,1)S(1)} collective-permute-done((bf16[8,240,128]{2,1,0:T(8,128)(2,1)S(1)}, bf16[8,240,128]{2,1,0:T(8,128)(2,1)S(1)}, u32[]{:S(2)}, u32[]{:S(2)}) %collective-permute-start.30) | collective-permute-done | bytes 491552 | tf_op jit(solution)/shard_map/ppermute | solution.py:383
  89.8 1.6 collective-permute-start.32
  91.4 8.4 %collective-permute-done.22.halo_ref = bf16[8,240,128]{2,1,0:T(8,128)(2,1)S(1)} collective-permute-done((bf16[8,240,128]{2,1,0:T(8,128)(2,1)S(1)}, bf16[8,240,128]{2,1,0:T(8,128)(2,1)S(1)}, u32[]{:S(2)}, u32[]{:S(2)}) %collective-permute-start.22) | collective-permute-done | bytes 491552 | tf_op jit(solution)/shard_map/ppermute | solution.py:383
  100.3 10.0 %collective-permute-done.14.halo_ref = bf16[8,240,128]{2,1,0:T(8,128)(2,1)S(1)} collective-permute-done((bf16[8,240,128]{2,1,0:T(8,128)(2,1)S(1)}, bf16[8,240,128]{2,1,0:T(8,128)(2,1)S(1)}, u32[]{:S(2)}, u32[]{:S(2)}) %collective-permute-start.14) | collective-permute-done | bytes 491552 | tf_op jit(solution)/shard_map/ppermute | solution.py:383
  110.8 8.3 %collective-permute-done.6.halo_ref = bf16[8,240,128]{2,1,0:T(8,128)(2,1)S(1)} collective-permute-done((bf16[8,240,128]{2,1,0:T(8,128)(2,1)S(1)}, bf16[8,240,128]{2,1,0:T(8,128)(2,1)S(1)}, u32[]{:S(2)}, u32[]{:S(2)}) %collective-permute-start.6) | collective-permute-done | bytes 491552 | tf_op jit(solution)/shard_map/ppermute | solution.py:383
  119.1 1.5 collective-permute-start.24
  122.4 1.6 collective-permute-start.16
  124.7 2.3 %collective-permute-done.25.refs_11_ = bf16[2,240,128]{2,1,0:T(8,128)(2,1)S(1)} collective-permute-done((bf16[2,240,128]{2,1,0:T(8,128)(2,1)S(1)}, bf16[2,240,128]{2,1,0:T(8,128)(2,1)S(1)}, u32[]{:S(2)}, u32[]{:S(2)}) %collective-permute-start.25) | collective-permute-done | bytes 122912 | tf_op jit(solution)/shard_map/ppermute | solution.py:367
  127.0 2.3 %collective-permute-start.9 = (bf16[2,240,128]{2,1,0:T(8,128)(2,1)S(1)}, bf16[2,240,128]{2,1,0:T(8,128)(2,1)S(1)}, u32[]{:S(2)}, u32[]{:S(2)}) collective-permute-start(bf16[2,240,128]{2,1,0:T(8,128)(2,1)S(1)} %get-tuple-element.54), channel_id=1, source_target_pairs={{0,6},{2,4},{4,2},{6,0},{8,14},{10,12},{12,10},{14,8},{16,22},{18,... | collective-permute-start | bytes 368648 | tf_op jit(solution)/shard_map/ppermute | solution.py:367
  129.7 2.3 %collective-permute-done.17.refs_7_ = bf16[2,240,128]{2,1,0:T(8,128)(2,1)S(1)} collective-permute-done((bf16[2,240,128]{2,1,0:T(8,128)(2,1)S(1)}, bf16[2,240,128]{2,1,0:T(8,128)(2,1)S(1)}, u32[]{:S(2)}, u32[]{:S(2)}) %collective-permute-start.17) | collective-permute-done | bytes 122912 | tf_op jit(solution)/shard_map/ppermute | solution.py:367
  132.0 2.9 %collective-permute-done.8.refs_2_ = bf16[2,240,128]{2,1,0:T(8,128)(2,1)S(1)} collective-permute-done((bf16[2,240,128]{2,1,0:T(8,128)(2,1)S(1)}, bf16[2,240,128]{2,1,0:T(8,128)(2,1)S(1)}, u32[]{:S(2)}, u32[]{:S(2)}) %collective-permute-start.8) | collective-permute-done | bytes 122912 | tf_op jit(solution)/shard_map/ppermute | solution.py:367
  134.9 1.8 collective-permute-done.9.refs_3_
  137.4 60.8 %place.1 = bf16[2,4,4,240,128]{4,3,2,1,0:T(8,128)(2,1)} custom-call(s32[1]{0:T(128)} %bitcast.me_ref, bf16[2,240,128]{2,1,0:T(8,128)(2,1)} %copy-done.8, bf16[2,240,128]{2,1,0:T(8,128)(2,1)} %copy-done.31, bf16[2,240,128]{2,1,0:T(8,128)(2,1)} %copy-done.32, bf16[2,240,128]{2,1,0:T(8,128)(2,1)} %copy-done.33, bf16[2,240,128]{2,1,0:T(8,128)(2,1)} %copy-done.7, ...), custom_call_target="tpu_custom_call" | custom-call | bytes 3932160 | tf_op jit(solution)/shard_map/place/pallas_call | solution.py:319
  (110 shorter events, 13.0 us)
Async XLA Ops:
  1.0 9.2 %collective-permute-start = (bf16[2,480,128]{2,1,0:T(8,128)(2,1)S(1)}, bf16[2,480,128]{2,1,0:T(8,128)(2,1)S(1)}, u32[]{:S(2)}, u32[]{:S(2)}) collective-permute-start(bf16[2,480,128]{2,1,0:T(8,128)(2,1)S(1)} %dynamic-slice_bitcast_fusion), channel_id=1, source_target_pairs={{0,1},{1,0},{2,3},{3,2},{4,5},{5,4},{6,7},{7,6},{8,9},{9,8},{10,11... | collective-permute-start | bytes 737288 | tf_op jit(solution)/shard_map/ppermute | solution.py:335
  6.6 9.5 %copy-start.10 = (f32[128]{0:T(128)S(1)}, f32[128]{0:T(128)}, u32[]{:S(2)}) copy-start(f32[128]{0:T(128)} %param.7) | copy-start | bytes 1540
  6.6 9.5 %copy-start.11 = (f32[128]{0:T(128)S(1)}, f32[128]{0:T(128)}, u32[]{:S(2)}) copy-start(f32[128]{0:T(128)} %param.8) | copy-start | bytes 1540
  12.3 3.7 %collective-permute-start.1 = (f32[2,2,8,128]{3,2,1,0:T(8,128)S(1)}, f32[2,2,8,128]{3,2,1,0:T(8,128)S(1)}, u32[]{:S(2)}, u32[]{:S(2)}) collective-permute-start(f32[2,2,8,128]{3,2,1,0:T(8,128)S(1)} %get-tuple-element.46.own_ref), channel_id=1, source_target_pairs={{0,1},{1,0},{2,3},{3,2},{4,5},{5,4},{6,7},{7,6},{8,9},{9,8},{10,11... | collective-permute-start | bytes 49160 | tf_op jit(solution)/shard_map/ppermute | solution.py:344
  25.6 15.1 %copy-start.13 = (bf16[2,240,128]{2,1,0:T(8,128)(2,1)S(1)}, bf16[2,240,128]{2,1,0:T(8,128)(2,1)}, u32[]{:S(2)}) copy-start(bf16[2,240,128]{2,1,0:T(8,128)(2,1)} %copy-done.12) | copy-start | bytes 368644
  25.6 3.6 %collective-permute-start.26 = (bf16[2,240,128]{2,1,0:T(8,128)(2,1)}, bf16[2,240,128]{2,1,0:T(8,128)(2,1)S(1)}, u32[]{:S(2)}, u32[]{:S(2)}) collective-permute-start(bf16[2,240,128]{2,1,0:T(8,128)(2,1)} %get-tuple-element.72), channel_id=1, source_target_pairs={{0,2},{2,0},{4,6},{6,4},{8,10},{10,8},{12,14},{14,12},{16,18},{18,... | collective-permute-start | bytes 368648 | tf_op jit(solution)/shard_map/ppermute | solution.py:367
  25.6 6.3 %collective-permute-start.27 = (bf16[2,240,128]{2,1,0:T(8,128)(2,1)}, bf16[2,240,128]{2,1,0:T(8,128)(2,1)S(1)}, u32[]{:S(2)}, u32[]{:S(2)}) collective-permute-start(bf16[2,240,128]{2,1,0:T(8,128)(2,1)} %get-tuple-element.73), channel_id=1, source_target_pairs={{0,4},{2,6},{4,0},{6,2},{8,12},{10,14},{12,8},{14,10},{16,20},{18,... | collective-permute-start | bytes 368648 | tf_op jit(solution)/shard_map/ppermute | solution.py:367
  27.1 6.7 %collective-permute-start.28 = (bf16[2,240,128]{2,1,0:T(8,128)(2,1)}, bf16[2,240,128]{2,1,0:T(8,128)(2,1)S(1)}, u32[]{:S(2)}, u32[]{:S(2)}) collective-permute-start(bf16[2,240,128]{2,1,0:T(8,128)(2,1)} %get-tuple-element.74), channel_id=1, source_target_pairs={{0,6},{2,4},{4,2},{6,0},{8,14},{10,12},{12,10},{14,8},{16,22},{18,... | collective-permute-start | bytes 368648 | tf_op jit(solution)/shard_map/ppermute | solution.py:367
  27.5 7.9 %collective-permute-start.18 = (bf16[2,240,128]{2,1,0:T(8,128)(2,1)}, bf16[2,240,128]{2,1,0:T(8,128)(2,1)S(1)}, u32[]{:S(2)}, u32[]{:S(2)}) collective-permute-start(bf16[2,240,128]{2,1,0:T(8,128)(2,1)} %copy-done.21), channel_id=1, source_target_pairs={{0,2},{2,0},{4,6},{6,4},{8,10},{10,8},{12,14},{14,12},{16,18},{18,... | collective-permute-start | bytes 368648 | tf_op jit(solution)/shard_map/ppermute | solution.py:367
  27.8 9.5 %collective-permute-start.19 = (bf16[2,240,128]{2,1,0:T(8,128)(2,1)}, bf16[2,240,128]{2,1,0:T(8,128)(2,1)S(1)}, u32[]{:S(2)}, u32[]{:S(2)}) collective-permute-start(bf16[2,240,128]{2,1,0:T(8,128)(2,1)} %copy-done.20), channel_id=1, source_target_pairs={{0,4},{2,6},{4,0},{6,2},{8,12},{10,14},{12,8},{14,10},{16,20},{18,... | collective-permute-start | bytes 368648 | tf_op jit(solution)/shard_map/ppermute | solution.py:367
  29.3 9.8 %collective-permute-start.20 = (bf16[2,240,128]{2,1,0:T(8,128)(2,1)}, bf16[2,240,128]{2,1,0:T(8,128)(2,1)S(1)}, u32[]{:S(2)}, u32[]{:S(2)}) collective-permute-start(bf16[2,240,128]{2,1,0:T(8,128)(2,1)} %copy-done.19), channel_id=1, source_target_pairs={{0,6},{2,4},{4,2},{6,0},{8,14},{10,12},{12,10},{14,8},{16,22},{18,... | collective-permute-start | bytes 368648 | tf_op jit(solution)/shard_map/ppermute | solution.py:367
  31.9 8.8 %collective-permute-start.10 = (bf16[2,240,128]{2,1,0:T(8,128)(2,1)}, bf16[2,240,128]{2,1,0:T(8,128)(2,1)S(1)}, u32[]{:S(2)}, u32[]{:S(2)}) collective-permute-start(bf16[2,240,128]{2,1,0:T(8,128)(2,1)} %copy-done.18), channel_id=1, source_target_pairs={{0,2},{2,0},{4,6},{6,4},{8,10},{10,8},{12,14},{14,12},{16,18},{18,... | collective-permute-start | bytes 368648 | tf_op jit(solution)/shard_map/ppermute | solution.py:367
  33.8 8.7 %collective-permute-start.11 = (bf16[2,240,128]{2,1,0:T(8,128)(2,1)}, bf16[2,240,128]{2,1,0:T(8,128)(2,1)S(1)}, u32[]{:S(2)}, u32[]{:S(2)}) collective-permute-start(bf16[2,240,128]{2,1,0:T(8,128)(2,1)} %copy-done.17), channel_id=1, source_target_pairs={{0,4},{2,6},{4,0},{6,2},{8,12},{10,14},{12,8},{14,10},{16,20},{18,... | collective-permute-start | bytes 368648 | tf_op jit(solution)/shard_map/ppermute | solution.py:367
  35.4 10.6 %collective-permute-start.12 = (bf16[2,240,128]{2,1,0:T(8,128)(2,1)}, bf16[2,240,128]{2,1,0:T(8,128)(2,1)S(1)}, u32[]{:S(2)}, u32[]{:S(2)}) collective-permute-start(bf16[2,240,128]{2,1,0:T(8,128)(2,1)} %copy-done.16), channel_id=1, source_target_pairs={{0,6},{2,4},{4,2},{6,0},{8,14},{10,12},{12,10},{14,8},{16,22},{18,... | collective-permute-start | bytes 368648 | tf_op jit(solution)/shard_map/ppermute | solution.py:367
  37.2 12.4 %collective-permute-start.2 = (bf16[2,240,128]{2,1,0:T(8,128)(2,1)}, bf16[2,240,128]{2,1,0:T(8,128)(2,1)S(1)}, u32[]{:S(2)}, u32[]{:S(2)}) collective-permute-start(bf16[2,240,128]{2,1,0:T(8,128)(2,1)} %copy-done.15), channel_id=1, source_target_pairs={{0,2},{2,0},{4,6},{6,4},{8,10},{10,8},{12,14},{14,12},{16,18},{18,... | collective-permute-start | bytes 368648 | tf_op jit(solution)/shard_map/ppermute | solution.py:367
  39.1 14.0 %collective-permute-start.3 = (bf16[2,240,128]{2,1,0:T(8,128)(2,1)}, bf16[2,240,128]{2,1,0:T(8,128)(2,1)S(1)}, u32[]{:S(2)}, u32[]{:S(2)}) collective-permute-start(bf16[2,240,128]{2,1,0:T(8,128)(2,1)} %copy-done.14), channel_id=1, source_target_pairs={{0,4},{2,6},{4,0},{6,2},{8,12},{10,14},{12,8},{14,10},{16,20},{18,... | collective-permute-start | bytes 368648 | tf_op jit(solution)/shard_map/ppermute | solution.py:367
  40.7 14.5 %copy-start = (bf16[3,3,128,128]{3,2,1,0:T(8,128)(2,1)S(1)}, bf16[3,3,128,128]{3,2,1,0:T(8,128)(2,1)}, u32[]{:S(2)}) copy-start(bf16[3,3,128,128]{3,2,1,0:T(8,128)(2,1)} %weight_ref.11) | copy-start | bytes 884740
  40.8 12.4 %collective-permute-start.4 = (bf16[2,240,128]{2,1,0:T(8,128)(2,1)S(1)}, bf16[2,240,128]{2,1,0:T(8,128)(2,1)S(1)}, u32[]{:S(2)}, u32[]{:S(2)}) collective-permute-start(bf16[2,240,128]{2,1,0:T(8,128)(2,1)S(1)} %copy-done.13), channel_id=1, source_target_pairs={{0,6},{2,4},{4,2},{6,0},{8,14},{10,12},{12,10},{14,8},{16,22},{18,... | collective-permute-start | bytes 368648 | tf_op jit(solution)/shard_map/ppermute | solution.py:367
  42.5 12.7 %collective-permute-start.29 = (bf16[6,240,128]{2,1,0:T(8,128)(2,1)S(1)}, bf16[6,240,128]{2,1,0:T(8,128)(2,1)S(1)}, u32[]{:S(2)}, u32[]{:S(2)}) collective-permute-start(bf16[6,240,128]{2,1,0:T(8,128)(2,1)S(1)} %pad_maximum_fusion.3), channel_id=1, source_target_pairs={{0,8},{2,10},{4,12},{6,14},{8,16},{10,18},{12,20},{14,22},{16,24},... | collective-permute-start | bytes 1105928 | tf_op jit(solution)/shard_map/ppermute | solution.py:381
  46.0 16.9 %collective-permute-start.21 = (bf16[6,240,128]{2,1,0:T(8,128)(2,1)S(1)}, bf16[6,240,128]{2,1,0:T(8,128)(2,1)S(1)}, u32[]{:S(2)}, u32[]{:S(2)}) collective-permute-start(bf16[6,240,128]{2,1,0:T(8,128)(2,1)S(1)} %pad_maximum_fusion.2), channel_id=1, source_target_pairs={{0,8},{2,10},{4,12},{6,14},{8,16},{10,18},{12,20},{14,22},{16,24},... | collective-permute-start | bytes 1105928 | tf_op jit(solution)/shard_map/ppermute | solution.py:381
  49.6 21.2 %collective-permute-start.13 = (bf16[6,240,128]{2,1,0:T(8,128)(2,1)S(1)}, bf16[6,240,128]{2,1,0:T(8,128)(2,1)S(1)}, u32[]{:S(2)}, u32[]{:S(2)}) collective-permute-start(bf16[6,240,128]{2,1,0:T(8,128)(2,1)S(1)} %pad_maximum_fusion.1), channel_id=1, source_target_pairs={{0,8},{2,10},{4,12},{6,14},{8,16},{10,18},{12,20},{14,22},{16,24},... | collective-permute-start | bytes 1105928 | tf_op jit(solution)/shard_map/ppermute | solution.py:381
  53.2 25.5 %collective-permute-start.5 = (bf16[6,240,128]{2,1,0:T(8,128)(2,1)S(1)}, bf16[6,240,128]{2,1,0:T(8,128)(2,1)S(1)}, u32[]{:S(2)}, u32[]{:S(2)}) collective-permute-start(bf16[6,240,128]{2,1,0:T(8,128)(2,1)S(1)} %pad_maximum_fusion), channel_id=1, source_target_pairs={{0,8},{2,10},{4,12},{6,14},{8,16},{10,18},{12,20},{14,22},{16,24},... | collective-permute-start | bytes 1105928 | tf_op jit(solution)/shard_map/ppermute | solution.py:381
  56.1 33.2 %collective-permute-start.30 = (bf16[8,240,128]{2,1,0:T(8,128)(2,1)S(1)}, bf16[8,240,128]{2,1,0:T(8,128)(2,1)S(1)}, u32[]{:S(2)}, u32[]{:S(2)}) collective-permute-start(bf16[8,240,128]{2,1,0:T(8,128)(2,1)S(1)} %early.7.own_ref), channel_id=1, source_target_pairs={{0,8},{2,10},{4,12},{6,14},{8,16},{10,18},{12,20},{14,22},{16,24},... | collective-permute-start | bytes 1474568 | tf_op jit(solution)/shard_map/ppermute | solution.py:383
  63.8 36.0 %collective-permute-start.22 = (bf16[8,240,128]{2,1,0:T(8,128)(2,1)S(1)}, bf16[8,240,128]{2,1,0:T(8,128)(2,1)S(1)}, u32[]{:S(2)}, u32[]{:S(2)}) collective-permute-start(bf16[8,240,128]{2,1,0:T(8,128)(2,1)S(1)} %early.6.own_ref), channel_id=1, source_target_pairs={{0,8},{2,10},{4,12},{6,14},{8,16},{10,18},{12,20},{14,22},{16,24},... | collective-permute-start | bytes 1474568 | tf_op jit(solution)/shard_map/ppermute | solution.py:383
  71.7 38.6 %collective-permute-start.14 = (bf16[8,240,128]{2,1,0:T(8,128)(2,1)S(1)}, bf16[8,240,128]{2,1,0:T(8,128)(2,1)S(1)}, u32[]{:S(2)}, u32[]{:S(2)}) collective-permute-start(bf16[8,240,128]{2,1,0:T(8,128)(2,1)S(1)} %early.5.own_ref), channel_id=1, source_target_pairs={{0,8},{2,10},{4,12},{6,14},{8,16},{10,18},{12,20},{14,22},{16,24},... | collective-permute-start | bytes 1474568 | tf_op jit(solution)/shard_map/ppermute | solution.py:383
  79.6 39.6 %collective-permute-start.6 = (bf16[8,240,128]{2,1,0:T(8,128)(2,1)S(1)}, bf16[8,240,128]{2,1,0:T(8,128)(2,1)S(1)}, u32[]{:S(2)}, u32[]{:S(2)}) collective-permute-start(bf16[8,240,128]{2,1,0:T(8,128)(2,1)S(1)} %early.4.own_ref), channel_id=1, source_target_pairs={{0,8},{2,10},{4,12},{6,14},{8,16},{10,18},{12,20},{14,22},{16,24},... | collective-permute-start | bytes 1474568 | tf_op jit(solution)/shard_map/ppermute | solution.py:383
  89.7 32.1 %copy-start.5 = (bf16[2,240,128]{2,1,0:T(8,128)(2,1)}, bf16[2,240,128]{2,1,0:T(8,128)(2,1)S(1)}, u32[]{:S(2)}) copy-start(bf16[2,240,128]{2,1,0:T(8,128)(2,1)S(1)} %get-tuple-element.75.refs_12_) | copy-start | bytes 368644
  89.7 30.9 %collective-permute-start.31 = (bf16[2,240,128]{2,1,0:T(8,128)(2,1)S(1)}, bf16[2,240,128]{2,1,0:T(8,128)(2,1)S(1)}, u32[]{:S(2)}, u32[]{:S(2)}) collective-permute-start(bf16[2,240,128]{2,1,0:T(8,128)(2,1)S(1)} %get-tuple-element.76), channel_id=1, source_target_pairs={{0,2},{2,0},{4,6},{6,4},{8,10},{10,8},{12,14},{14,12},{16,18},{18,... | collective-permute-start | bytes 368648 | tf_op jit(solution)/shard_map/ppermute | solution.py:367
  89.8 30.8 %collective-permute-start.32 = (bf16[2,240,128]{2,1,0:T(8,128)(2,1)S(1)}, bf16[2,240,128]{2,1,0:T(8,128)(2,1)S(1)}, u32[]{:S(2)}, u32[]{:S(2)}) collective-permute-start(bf16[2,240,128]{2,1,0:T(8,128)(2,1)S(1)} %get-tuple-element.77), channel_id=1, source_target_pairs={{0,4},{2,6},{4,0},{6,2},{8,12},{10,14},{12,8},{14,10},{16,20},{18,... | collective-permute-start | bytes 368648 | tf_op jit(solution)/shard_map/ppermute | solution.py:367
  99.8 22.7 %collective-permute-start.33 = (bf16[2,240,128]{2,1,0:T(8,128)(2,1)S(1)}, bf16[2,240,128]{2,1,0:T(8,128)(2,1)S(1)}, u32[]{:S(2)}, u32[]{:S(2)}) collective-permute-start(bf16[2,240,128]{2,1,0:T(8,128)(2,1)S(1)} %get-tuple-element.78), channel_id=1, source_target_pairs={{0,6},{2,4},{4,2},{6,0},{8,14},{10,12},{12,10},{14,8},{16,22},{18,... | collective-permute-start | bytes 368648 | tf_op jit(solution)/shard_map/ppermute | solution.py:367
  100.2 22.2 %copy-start.6 = (bf16[2,240,128]{2,1,0:T(8,128)(2,1)}, bf16[2,240,128]{2,1,0:T(8,128)(2,1)S(1)}, u32[]{:S(2)}) copy-start(bf16[2,240,128]{2,1,0:T(8,128)(2,1)S(1)} %get-tuple-element.67.refs_8_) | copy-start | bytes 368644
  110.3 13.7 %collective-permute-start.23 = (bf16[2,240,128]{2,1,0:T(8,128)(2,1)S(1)}, bf16[2,240,128]{2,1,0:T(8,128)(2,1)S(1)}, u32[]{:S(2)}, u32[]{:S(2)}) collective-permute-start(bf16[2,240,128]{2,1,0:T(8,128)(2,1)S(1)} %get-tuple-element.68), channel_id=1, source_target_pairs={{0,2},{2,0},{4,6},{6,4},{8,10},{10,8},{12,14},{14,12},{16,18},{18,... | collective-permute-start | bytes 368648 | tf_op jit(solution)/shard_map/ppermute | solution.py:367
  110.8 11.7 %copy-start.7 = (bf16[2,240,128]{2,1,0:T(8,128)(2,1)}, bf16[2,240,128]{2,1,0:T(8,128)(2,1)S(1)}, u32[]{:S(2)}) copy-start(bf16[2,240,128]{2,1,0:T(8,128)(2,1)S(1)} %get-tuple-element.59.refs_4_) | copy-start | bytes 368644
  119.1 5.3 %collective-permute-start.24 = (bf16[2,240,128]{2,1,0:T(8,128)(2,1)S(1)}, bf16[2,240,128]{2,1,0:T(8,128)(2,1)S(1)}, u32[]{:S(2)}, u32[]{:S(2)}) collective-permute-start(bf16[2,240,128]{2,1,0:T(8,128)(2,1)S(1)} %get-tuple-element.69), channel_id=1, source_target_pairs={{0,4},{2,6},{4,0},{6,2},{8,12},{10,14},{12,8},{14,10},{16,20},{18,... | collective-permute-start | bytes 368648 | tf_op jit(solution)/shard_map/ppermute | solution.py:367
  120.6 16.1 %copy-start.22 = (bf16[2,240,128]{2,1,0:T(8,128)(2,1)}, bf16[2,240,128]{2,1,0:T(8,128)(2,1)S(1)}, u32[]{:S(2)}) copy-start(bf16[2,240,128]{2,1,0:T(8,128)(2,1)S(1)} %collective-permute-done.31.refs_13_) | copy-start | bytes 368644
  120.6 6.3 %collective-permute-start.25 = (bf16[2,240,128]{2,1,0:T(8,128)(2,1)S(1)}, bf16[2,240,128]{2,1,0:T(8,128)(2,1)S(1)}, u32[]{:S(2)}, u32[]{:S(2)}) collective-permute-start(bf16[2,240,128]{2,1,0:T(8,128)(2,1)S(1)} %get-tuple-element.70), channel_id=1, source_target_pairs={{0,6},{2,4},{4,2},{6,0},{8,14},{10,12},{12,10},{14,8},{16,22},{18,... | collective-permute-start | bytes 368648 | tf_op jit(solution)/shard_map/ppermute | solution.py:367
  120.7 16.1 %copy-start.23 = (bf16[2,240,128]{2,1,0:T(8,128)(2,1)}, bf16[2,240,128]{2,1,0:T(8,128)(2,1)S(1)}, u32[]{:S(2)}) copy-start(bf16[2,240,128]{2,1,0:T(8,128)(2,1)S(1)} %collective-permute-done.32.refs_14_) | copy-start | bytes 368644
  120.7 6.3 %collective-permute-start.15 = (bf16[2,240,128]{2,1,0:T(8,128)(2,1)S(1)}, bf16[2,240,128]{2,1,0:T(8,128)(2,1)S(1)}, u32[]{:S(2)}, u32[]{:S(2)}) collective-permute-start(bf16[2,240,128]{2,1,0:T(8,128)(2,1)S(1)} %get-tuple-element.60), channel_id=1, source_target_pairs={{0,2},{2,0},{4,6},{6,4},{8,10},{10,8},{12,14},{14,12},{16,18},{18,... | collective-permute-start | bytes 368648 | tf_op jit(solution)/shard_map/ppermute | solution.py:367
  122.4 14.3 %copy-start.24 = (bf16[2,240,128]{2,1,0:T(8,128)(2,1)}, bf16[2,240,128]{2,1,0:T(8,128)(2,1)S(1)}, u32[]{:S(2)}) copy-start(bf16[2,240,128]{2,1,0:T(8,128)(2,1)S(1)} %collective-permute-done.33.refs_15_) | copy-start | bytes 368644
  122.4 7.2 %collective-permute-start.16 = (bf16[2,240,128]{2,1,0:T(8,128)(2,1)S(1)}, bf16[2,240,128]{2,1,0:T(8,128)(2,1)S(1)}, u32[]{:S(2)}, u32[]{:S(2)}) collective-permute-start(bf16[2,240,128]{2,1,0:T(8,128)(2,1)S(1)} %get-tuple-element.61), channel_id=1, source_target_pairs={{0,4},{2,6},{4,0},{6,2},{8,12},{10,14},{12,8},{14,10},{16,20},{18,... | collective-permute-start | bytes 368648 | tf_op jit(solution)/shard_map/ppermute | solution.py:367
  124.0 12.8 %copy-start.25 = (bf16[2,240,128]{2,1,0:T(8,128)(2,1)}, bf16[2,240,128]{2,1,0:T(8,128)(2,1)S(1)}, u32[]{:S(2)}) copy-start(bf16[2,240,128]{2,1,0:T(8,128)(2,1)S(1)} %collective-permute-done.23.refs_9_) | copy-start | bytes 368644
  124.0 8.0 %collective-permute-start.17 = (bf16[2,240,128]{2,1,0:T(8,128)(2,1)S(1)}, bf16[2,240,128]{2,1,0:T(8,128)(2,1)S(1)}, u32[]{:S(2)}, u32[]{:S(2)}) collective-permute-start(bf16[2,240,128]{2,1,0:T(8,128)(2,1)S(1)} %get-tuple-element.62), channel_id=1, source_target_pairs={{0,6},{2,4},{4,2},{6,0},{8,14},{10,12},{12,10},{14,8},{16,22},{18,... | collective-permute-start | bytes 368648 | tf_op jit(solution)/shard_map/ppermute | solution.py:367
  124.4 12.4 %copy-start.26 = (bf16[2,240,128]{2,1,0:T(8,128)(2,1)}, bf16[2,240,128]{2,1,0:T(8,128)(2,1)S(1)}, u32[]{:S(2)}) copy-start(bf16[2,240,128]{2,1,0:T(8,128)(2,1)S(1)} %collective-permute-done.24.refs_10_) | copy-start | bytes 368644
  124.4 7.6 %collective-permute-start.7 = (bf16[2,240,128]{2,1,0:T(8,128)(2,1)S(1)}, bf16[2,240,128]{2,1,0:T(8,128)(2,1)S(1)}, u32[]{:S(2)}, u32[]{:S(2)}) collective-permute-start(bf16[2,240,128]{2,1,0:T(8,128)(2,1)S(1)} %get-tuple-element.52), channel_id=1, source_target_pairs={{0,2},{2,0},{4,6},{6,4},{8,10},{10,8},{12,14},{14,12},{16,18},{18,... | collective-permute-start | bytes 368648 | tf_op jit(solution)/shard_map/ppermute | solution.py:367
  127.0 9.8 %copy-start.27 = (bf16[2,240,128]{2,1,0:T(8,128)(2,1)}, bf16[2,240,128]{2,1,0:T(8,128)(2,1)S(1)}, u32[]{:S(2)}) copy-start(bf16[2,240,128]{2,1,0:T(8,128)(2,1)S(1)} %collective-permute-done.25.refs_11_) | copy-start | bytes 368644
  127.0 8.0 %collective-permute-start.8 = (bf16[2,240,128]{2,1,0:T(8,128)(2,1)S(1)}, bf16[2,240,128]{2,1,0:T(8,128)(2,1)S(1)}, u32[]{:S(2)}, u32[]{:S(2)}) collective-permute-start(bf16[2,240,128]{2,1,0:T(8,128)(2,1)S(1)} %get-tuple-element.53), channel_id=1, source_target_pairs={{0,4},{2,6},{4,0},{6,2},{8,12},{10,14},{12,8},{14,10},{16,20},{18,... | collective-permute-start | bytes 368648 | tf_op jit(solution)/shard_map/ppermute | solution.py:367
  127.0 9.8 %copy-start.28 = (bf16[2,240,128]{2,1,0:T(8,128)(2,1)}, bf16[2,240,128]{2,1,0:T(8,128)(2,1)S(1)}, u32[]{:S(2)}) copy-start(bf16[2,240,128]{2,1,0:T(8,128)(2,1)S(1)} %collective-permute-done.15.refs_5_) | copy-start | bytes 368644
  127.0 9.8 %collective-permute-start.9 = (bf16[2,240,128]{2,1,0:T(8,128)(2,1)S(1)}, bf16[2,240,128]{2,1,0:T(8,128)(2,1)S(1)}, u32[]{:S(2)}, u32[]{:S(2)}) collective-permute-start(bf16[2,240,128]{2,1,0:T(8,128)(2,1)S(1)} %get-tuple-element.54), channel_id=1, source_target_pairs={{0,6},{2,4},{4,2},{6,0},{8,14},{10,12},{12,10},{14,8},{16,22},{18,... | collective-permute-start | bytes 368648 | tf_op jit(solution)/shard_map/ppermute | solution.py:367
  (20 other events, 34.1 us)

commit v2 on v1

--- a/solution.py
+++ b/solution.py
@@ -9,7 +9,8 @@
 
 GROUPS = 32
 SPAN = 8
-CHUNKS = 4
+IN_SIZES = (240, 720)
+OUT_SIZES = ((240,), (240, 240, 240))
 VMEM = pltpu.VMEM
 ANY = pl.ANY
 F32 = jnp.float32
@@ -44,8 +45,17 @@
     return jnp.sum(value.reshape(value.shape[0] // 8, 8, value.shape[1]), axis=0)
 
 
-def conv_kernel(band, video_ref, weight_ref, inner_ref, edge_ref, sums_ref, wide_ref):
-    ch = video_ref.shape[-1]
+def conv_kernel(band, sources, *refs):
+    video_refs = refs[:sources]
+    if sources == 2:
+        pick_ref, refs = refs[2], refs[:2] + refs[3:]
+    weight_ref, inner_ref, edge_ref, sums_ref, wide_ref = refs[sources:]
+    ch = weight_ref.shape[-1]
+
+    def read(row):
+        if sources == 1:
+            return video_refs[0][0, row]
+        return jnp.where(pick_ref[0] > 0, video_refs[1][0, row], video_refs[0][0, row])
 
     @pl.when(pl.program_id(0) == 0)
     def _():
@@ -62,7 +72,7 @@
     square = jnp.zeros((8, ch), F32)
     for first in range(0, band, 2):
         rows = [r for r in range(first - 1, first + 3) if 0 <= r < band]
-        lhs = jnp.concatenate([video_ref[0, r] for r in rows], axis=-1)
+        lhs = jnp.concatenate([read(r) for r in rows], axis=-1)
         skip = (rows[0] - (first - 1)) * ch
         wide = jnp.dot(
             lhs, wide_ref[skip : skip + len(rows) * ch, :], preferred_element_type=F32
@@ -82,15 +92,14 @@
     sums_ref[0, 1] = square
 
 
-def conv_call(video, weight):
-    frames, band, width, ch = video.shape
-    return pl.pallas_call(
-        functools.partial(conv_kernel, band),
+def conv_call(videos, weight, *pick):
+    frames, band, width, ch = videos[0].shape
+    return pl.pallas_call(
+        functools.partial(conv_kernel, band, len(videos)),
         grid=(frames,),
-        in_specs=[
-            pl.BlockSpec((1, band, width, ch), lambda f: (f, 0, 0, 0)),
-            pl.BlockSpec(weight.shape, lambda f: (0, 0, 0, 0)),
-        ],
+        in_specs=[pl.BlockSpec((1, band, width, ch), lambda f: (f, 0, 0, 0)) for _ in videos]
+        + [sspec() for _ in pick]
+        + [pl.BlockSpec(weight.shape, lambda f: (0, 0, 0, 0))],
         out_specs=[
             pl.BlockSpec((1, band - 2, width, ch), lambda f: (f, 0, 0, 0)),
             pl.BlockSpec((1, 2, width, ch), lambda f: (f, 0, 0, 0)),
@@ -102,10 +111,10 @@
             jax.ShapeDtypeStruct((frames, 2, 8, ch), F32),
         ],
         scratch_shapes=[VMEM((4 * ch, 6 * ch), BF16)],
-        compiler_params=params(32),
+        compiler_params=params(12),
         cost_estimate=cost(frames * band * width * 18 * ch * ch, frames * band * width * ch * 6),
         name="conv",
-    )(video, weight)
+    )(*videos, *pick, weight)
 
 
 def edge_kernel(flag_ref, part_ref, above_ref, below_ref, weight_ref, sums_ref, edge_ref, out_sums_ref):
@@ -134,7 +143,7 @@
             jax.ShapeDtypeStruct(part.shape, F32),
             jax.ShapeDtypeStruct(sums.shape, F32),
         ],
-        compiler_params=params(32),
+        compiler_params=params(12),
         cost_estimate=cost(part.size * 6 * part.shape[-1], part.size * 10),
         name="edge",
     )(flags, part, above, below, weight, sums)
@@ -155,15 +164,14 @@
     return value
 
 
-def norm_kernel(count, per_group, members, chunks, me_ref, inner_ref, edge_ref, own_ref, peer_ref, gain_ref, shift_ref, *refs):
+def norm_kernel(count, per_group, members, sizes, flag_ref, inner_ref, edge_ref, sums_ref, gain_ref, shift_ref, *refs):
     outs, hidden_ref = refs[:-1], refs[-1]
     frames, inner, width, ch = inner_ref.shape
     band = inner + 2
+    alive = flag_ref[1] > 0
     for frame in range(frames):
         sums = [
-            jnp.broadcast_to(
-                jnp.sum(own_ref[frame, i] + peer_ref[frame, i], axis=0, keepdims=True), (8, ch)
-            )
+            jnp.broadcast_to(jnp.sum(sums_ref[frame, i], axis=0, keepdims=True), (8, ch))
             for i in range(2)
         ]
         mean = over_groups(sums[0], per_group) / count
@@ -175,7 +183,7 @@
         def put(row, value):
             v = (value - mean) * scale + shift
             v = 0.5 * v * (1.0 + jnp.tanh(0.5 * v))
-            hidden_ref[frame, row] = v.astype(BF16)
+            hidden_ref[frame, row] = jnp.where(alive, v, 0.0).astype(BF16)
 
         put(0, edge_ref[frame, 0])
         put(band - 1, edge_ref[frame, 1])
@@ -185,28 +193,30 @@
             put(row + 1, inner_ref[frame, row])
 
     flat = hidden_ref.reshape(frames, band * width, ch)
-    size = band * width // (members * chunks)
-    me = me_ref[0]
-    for chunk in range(chunks):
+    me = flag_ref[0]
+    offset = 0
+    for i, size in enumerate(sizes):
         for k in range(members):
-            start = pl.multiple_of(((me ^ k) * chunks + chunk) * size, 16)
-            outs[chunk * members + k][...] = flat[:, pl.ds(start, size), :]
-
-
-def norm_call(me, inner, edge, own, peer, gain, shift, count, members, chunks):
+            start = pl.multiple_of((me ^ k) * sum(sizes) + offset, 16)
+            outs[i * members + k][...] = flat[:, pl.ds(start, size), :]
+        offset += size
+
+
+def norm_call(flags, inner, edge, sums, gain, shift, count, members, sizes):
     frames, rows, width, ch = inner.shape
     band = rows + 2
-    size = band * width // (members * chunks)
-    return pl.pallas_call(
-        functools.partial(norm_kernel, count, ch // GROUPS, members, chunks),
-        in_specs=[sspec()] + [vspec()] * 6,
-        out_specs=[vspec()] * (members * chunks),
-        out_shape=[jax.ShapeDtypeStruct((frames, size, ch), BF16)] * (members * chunks),
+    return pl.pallas_call(
+        functools.partial(norm_kernel, count, ch // GROUPS, members, sizes),
+        in_specs=[sspec()] + [vspec()] * 5,
+        out_specs=[vspec()] * (members * len(sizes)),
+        out_shape=[
+            jax.ShapeDtypeStruct((frames, size, ch), BF16) for size in sizes for _ in range(members)
+        ],
         scratch_shapes=[VMEM((frames, band, width, ch), BF16)],
-        compiler_params=params(40),
+        compiler_params=params(16),
         cost_estimate=cost(frames * band * width * ch * 10, frames * band * width * ch * 6),
         name="norm",
-    )(me, inner, edge, own, peer, gain.reshape(1, ch), shift.reshape(1, ch))
+    )(flags, inner, edge, sums, gain.reshape(1, ch), shift.reshape(1, ch))
 
 
 def pair_weights(weight_ref, layer, wide_ref):
@@ -226,12 +236,17 @@
     write(time + dilation, (both[:, ch:] + frames[3].astype(F32)).astype(BF16))
 
 
-def early_kernel(members, me_ref, *refs):
-    pieces, (halo_ref, weight_ref, out_ref, u0_ref, u1_ref, wide_ref) = refs[:members], refs[members:]
+def early_kernel(members, offset, size, me_ref, *refs):
+    pieces, guests = refs[:members], refs[members : 2 * members]
+    halo_ref, weight_ref, out_ref, u0_ref, u1_ref, wide_ref = refs[2 * members :]
     step = pieces[0].shape[0]
-    u0_ref[: SPAN - 2] = halo_ref[...]
+    lead = SPAN - 2
+    rows = pl.ds(offset, size)
     for k in range(members):
-        u0_ref[pl.ds(SPAN - 2 + (me_ref[0] ^ k) * step, step)] = pieces[k][...]
+        other = me_ref[0] ^ k
+        u0_ref[pl.ds(lead + other * step, step)] = pieces[k][:, rows]
+        u0_ref[other + (other & 2)] = guests[k][0, rows]
+    u0_ref[2:4] = halo_ref[:, rows]
     pair_weights(weight_ref, 0, wide_ref)
 
     def write1(t, value):
@@ -241,19 +256,18 @@
         out_ref[t] = value
 
     for time in range(-4, SPAN, 2):
-        pair(lambda t: u0_ref[t + SPAN - 2], write1, time, 1, wide_ref)
+        pair(lambda t: u0_ref[t + lead], write1, time, 1, wide_ref)
     pair_weights(weight_ref, 1, wide_ref)
     for time in range(0, SPAN, 4):
         for odd in range(2):
             pair(lambda t: u1_ref[t + 4], write2, time + odd, 2, wide_ref)
 
 
-def early_call(me, pieces, halo, weight):
-    members = len(pieces)
-    _, size, ch = pieces[0].shape
-    return pl.pallas_call(
-        functools.partial(early_kernel, members),
-        in_specs=[sspec()] + [vspec()] * (members + 2),
+def early_call(me, pieces, guests, halo, weight, offset, size):
+    members, ch = len(pieces), pieces[0].shape[-1]
+    return pl.pallas_call(
+        functools.partial(early_kernel, members, offset, size),
+        in_specs=[sspec()] + [vspec()] * (2 * members + 2),
         out_specs=vspec(),
         out_shape=jax.ShapeDtypeStruct((SPAN, size, ch), BF16),
         scratch_shapes=[
@@ -261,10 +275,10 @@
             VMEM((SPAN + 4, size, ch), BF16),
             VMEM((4 * ch, 2 * ch), BF16),
         ],
-        compiler_params=params(32),
+        compiler_params=params(12),
         cost_estimate=cost(20 * size * 6 * ch * ch, 22 * size * ch * 2),
         name="early",
-    )(me, *pieces, halo, weight)
+    )(me, *pieces, *guests, halo, weight)
 
 
 def late_kernel(members, me_ref, own_ref, halo_ref, weight_ref, *refs):
@@ -291,38 +305,38 @@
         out_specs=[vspec()] * members,
         out_shape=[jax.ShapeDtypeStruct((frames // members, size, ch), BF16)] * members,
         scratch_shapes=[VMEM(own.shape, BF16), VMEM((4 * ch, 2 * ch), BF16)],
-        compiler_params=params(32),
+        compiler_params=params(12),
         cost_estimate=cost(8 * size * 6 * ch * ch, 24 * size * ch * 2),
         name="late",
     )(me, own, halo, weight)
 
 
-def place_kernel(members, chunks, me_ref, *refs):
-    pieces, (out_ref, sem) = refs[: members * chunks], refs[members * chunks :]
-    copies = [
-        pltpu.make_async_copy(
-            pieces[chunk * members + k],
-            out_ref.at[:, me_ref[0] ^ k, chunk],
-            sem.at[chunk * members + k],
-        )
-        for chunk in range(chunks)
-        for k in range(members)
-    ]
+def place_kernel(members, sizes, me_ref, *refs):
+    pieces, (out_ref, sem) = refs[: members * len(sizes)], refs[members * len(sizes) :]
+    copies = []
+    offset = 0
+    for i, size in enumerate(sizes):
+        for k in range(members):
+            n = i * members + k
+            place = out_ref.at[:, me_ref[0] ^ k, pl.ds(offset, size)]
+            copies.append(pltpu.make_async_copy(pieces[n], place, sem.at[n]))
+        offset += size
     for copy in copies:
         copy.start()
     for copy in copies:
         copy.wait()
 
 
-def place_call(me, pieces, members, chunks):
-    frames, size, ch = pieces[0].shape
-    return pl.pallas_call(
-        functools.partial(place_kernel, members, chunks),
-        in_specs=[sspec()] + [pl.BlockSpec(memory_space=ANY)] * len(pieces),
+def place_call(me, pieces, members, sizes):
+    frames, _, ch = pieces[0].shape
+    return pl.pallas_call(
+        functools.partial(place_kernel, members, sizes),
+        in_specs=[sspec()] + [vspec()] * len(pieces),
         out_specs=pl.BlockSpec(memory_space=ANY),
-        out_shape=jax.ShapeDtypeStruct((frames, members, chunks, size, ch), BF16),
+        out_shape=jax.ShapeDtypeStruct((frames, members, sum(sizes), ch), BF16),
         scratch_shapes=[pltpu.SemaphoreType.DMA((len(pieces),))],
-        cost_estimate=cost(0, 2 * len(pieces) * frames * size * ch * 2),
+        compiler_params=params(8),
+        cost_estimate=cost(0, 2 * members * frames * sum(sizes) * ch * 2),
         name="place",
     )(me, *pieces)
 
@@ -345,6 +359,10 @@
     return lax.psum(sums, "rows") - sums
 
 
+def after(value, *others):
+    return lax.optimization_barrier((value, *others))[0]
+
+
 def body(video, spatial_weight, norm_gain, norm_shift, temporal_weight):
     frames, band, width, ch = video.shape
     total, here = lax.axis_size("tm"), lax.axis_index("tm")
@@ -354,35 +372,57 @@
     flags = jnp.stack([row > 0, row < rows - 1]).astype(jnp.int32)
     swaps = [[(i, i ^ k) for i in range(total)] for k in range(members)]
     onward = [(i, i + members) for i in range(total - members)]
-
+    guest_pairs = [
+        [(i, i + members - 1 + odd) for i in range(1, total - members, 2)] for odd in range(2)
+    ]
+    odd = me % 2
+
+    guests = [lax.ppermute(video[f : f + 1], "tm", guest_pairs[f]) for f in range(2)]
     above, below = halo_rows(video)
-    inner, part, sums = conv_call(video, spatial_weight)
+    inner, part, sums = conv_call([video], spatial_weight)
     edge, sums = edge_call(flags, part, above, below, spatial_weight, sums)
+    sums = sums + other_sums(sums)
     count = band * rows * width * (ch // GROUPS)
+    exists = jnp.concatenate([me, jnp.ones_like(me)])
     pieces = norm_call(
-        me, inner, edge, sums, other_sums(sums), norm_gain, norm_shift, count, members, CHUNKS
+        exists, inner, edge, sums, norm_gain, norm_shift, count, members, IN_SIZES
+    )
+
+    guest_sums = [lax.ppermute(sums[f : f + 1], "tm", guest_pairs[f]) for f in range(2)]
+    guest_sums = guest_sums[0] + guest_sums[1]
+    guest_rows = halo_rows(jnp.where(odd[0] > 0, guests[1], guests[0]))
+    guest_inner, guest_part, guest_own = conv_call(guests, spatial_weight, odd)
+    guest_edge, _ = edge_call(flags, guest_part, *guest_rows, spatial_weight, guest_own)
+    exists = jnp.concatenate([me, (here >= members).astype(jnp.int32).reshape(1)])
+    guest_pieces = norm_call(
+        exists, guest_inner, guest_edge, guest_sums, norm_gain, norm_shift, count, members, IN_SIZES
     )
 
     def swap(four):
         return [four[0]] + [lax.ppermute(four[k], "tm", swaps[k]) for k in range(1, members)]
 
-    mine = [swap(pieces[c * members : (c + 1) * members]) for c in range(CHUNKS)]
-    results = []
-    for four in mine:
-        slots = [
-            functools.reduce(
-                lambda acc, k: jnp.where(me[0] == (slot ^ k), four[k], acc),
-                range(1, members),
-                four[0],
+    results, u2s = [], []
+    for i, size in enumerate(IN_SIZES):
+        four = swap(pieces[i * members : (i + 1) * members])
+        guest_four = swap(guest_pieces[i * members : (i + 1) * members])
+        middle = functools.reduce(
+            lambda acc, k: jnp.where(me[0] == (2 ^ k), four[k], acc), range(1, members), four[0]
+        )
+        halo = lax.ppermute(middle, "tm", onward)
+        offset = 0
+        for part_size in OUT_SIZES[i]:
+            u2s.append(
+                early_call(me, four, guest_four, halo, temporal_weight, offset, part_size)
             )
-            for slot in range(1, members)
-        ]
-        tail = jnp.concatenate(slots, axis=0)[-(SPAN - 2) :]
-        halo = lax.ppermute(tail, "tm", onward)
-        u2 = early_call(me, four, halo, temporal_weight)
+            offset += part_size
+    befores = []
+    for i, u2 in enumerate(u2s):
+        if i >= 2:
+            u2 = after(u2, befores[i - 2])
         before = lax.ppermute(u2, "tm", onward)
-        results += swap(late_call(me, u2, before, temporal_weight, members))
-    out = place_call(me, results, members, CHUNKS)
+        befores.append(before)
+        results += swap(late_call(me, u2s[i], before, temporal_weight, members))
+    out = place_call(me, results, members, [n for sizes in OUT_SIZES for n in sizes])
     return out.reshape(frames, band, width, ch)
 
 

time: 199 us -> 154 us (0.77)
  Pallas kernels: 73.5 us -> 21.4 us
  starting transfers between devices: 50 us -> 62.3 us
  local copies, waits for them, and re-layouts: 12.7 us -> 9.71 us
  waiting for transfers between devices: 61 us -> 58.7 us
    pallas_call x6 -> x7, Pallas kernels: 67.9 us -> 11.8 us  [the longest x2 6.91 us: conv_call(): pl.pallas_call(functools.partial(conv_kernel, band, len(videos)), grid=(f...]
    ppermute x24, waiting for transfers between devices: 19.1 us -> 35.9 us  [swap(): lax.ppermute(four[k], 'tm', swaps[k])]
    ppermute x24, starting transfers between devices: 15.6 us -> 27.4 us  [swap(): lax.ppermute(four[k], 'tm', swaps[k])]
    ppermute x4, waiting for transfers between devices: 32 us -> 22.8 us  [body(): before = lax.ppermute(u2, 'tm', onward)]
    ppermute x4 -> x6, waiting for transfers between devices: 7.77 us -> 0.02 us  [the longest x2 0.01 us: body(): lax.ppermute(sums[f:f + 1], 'tm', guest_pairs[f])]
    unnamed x68 -> x24, local copies, waits for them, and re-layouts: 11.7 us -> 6.64 us
    ppermute x4, starting transfers between devices: 17.5 us -> 13.2 us  [body(): before = lax.ppermute(u2, 'tm', onward)]
    ppermute x4 -> x6, starting transfers between devices: 12.4 us -> 16.4 us  [the longest x2 11.8 us: body(): halo = lax.ppermute(middle, 'tm', onward)]
  transfers between devices with their start and end apart: 34 -> 37, of which waited for: 19 -> 11; matrix products, arithmetic and copies ran while one was open for 0% -> 2% of each run, Pallas kernels for 5% -> 12%
where the time goes in v2:
time: 154 us
  starting transfers between devices  62.3 us (40%)
  waiting for transfers between devices  58.7 us (38%)
  Pallas kernels  21.4 us (14%)
  local copies, waits for them, and re-layouts  9.71 us (6%)
    ppermute x24, waiting for transfers between devices, swap(): lax.ppermute(four[k], 'tm', swaps[k])  35.9 us
    ppermute x24, starting transfers between devices, swap(): lax.ppermute(four[k], 'tm', swaps[k])  27.4 us
    ppermute x4, waiting for transfers between devices, body(): before = lax.ppermute(u2, 'tm', onward)  22.8 us
    ppermute x4, starting transfers between devices, body(): before = lax.ppermute(u2, 'tm', onward)  13.2 us
    ppermute x2, starting transfers between devices, body(): halo = lax.ppermute(middle, 'tm', onward)  11.8 us
    pallas_call x2, Pallas kernels, conv_call(): pl.pallas_call(functools.partial(conv_kernel, band, len(videos)), grid=(f...  6.91 us
    unnamed x24, local copies, waits for them, and re-layouts  6.64 us
    pallas_call x2, Pallas kernels, norm_call(): pl.pallas_call(functools.partial(norm_kernel, count, ch // GROUPS, member...  4.96 us
  transfers between devices with their start and end apart: 37, of which 11 were waited for; matrix products, arithmetic and copies ran while one was open for 2% of the time, Pallas kernels for 12%

profile of v2, /device:TPU:0, one launch (start us, length us, event | category | flops | bytes accessed | tf_op | source)
XLA Modules:
  0.0 153.7 jit_solution(17194811745273152275)
XLA Ops:
  0.0 1.7 %dynamic-slice_bitcast_fusion = bf16[2,480,128]{2,1,0:T(8,128)(2,1)} fusion(bf16[2,8,480,128]{3,2,1,0:T(8,128)(2,1)} %refs_0_.1, s32[]{:T(128)S(6)} %select_n.69), kind=kLoop, calls=%fused_computation.1 | loop fusion | bytes 491524 | tf_op jit(solution)/shard_map/squeeze | solution.py:348
  1.7 3.0 %collective-permute-start = (bf16[2,480,128]{2,1,0:T(8,128)(2,1)}, bf16[2,480,128]{2,1,0:T(8,128)(2,1)S(1)}, u32[]{:S(2)}, u32[]{:S(2)}) collective-permute-start(bf16[2,480,128]{2,1,0:T(8,128)(2,1)} %dynamic-slice_bitcast_fusion), channel_id=1, source_target_pairs={{0,1},{1,0},{2,3},{3,2},{4,5},{5,4},{6,7},{7,6},{8,9},{9,8},{10,11... | collective-permute-start | bytes 737288 | tf_op jit(solution)/shard_map/ppermute | solution.py:349
  4.7 1.5 %copy-done.1 = bf16[2,8,480,128]{3,2,1,0:T(8,128)(2,1)S(1)} copy-done((bf16[2,8,480,128]{3,2,1,0:T(8,128)(2,1)S(1)}, bf16[2,8,480,128]{3,2,1,0:T(8,128)(2,1)}, u32[]{:S(2)}) %copy-start.1) | copy-done | bytes 1966104
  6.2 1.0 copy-done.3
  7.2 3.6 %conv.2 = (f32[2,6,480,128]{3,2,1,0:T(8,128)S(1)}, f32[2,2,480,128]{3,2,1,0:T(8,128)S(1)}, f32[2,2,8,128]{3,2,1,0:T(8,128)S(1)}) custom-call(bf16[2,8,480,128]{3,2,1,0:T(8,128)(2,1)S(1)} %copy-done.1, bf16[3,3,128,128]{3,2,1,0:T(8,128)(2,1)S(1)} %copy-done.3), custom_call_target="tpu_custom_call" | custom-call | flops 2264924160 | bytes 5898240 | tf_op jit(solution)/shard_map/conv/pallas_call | solution.py:97
  10.8 1.2 edge.2
  12.0 0.9 copy-done.5
  12.9 1.7 %collective-permute-start.1 = (f32[2,2,8,128]{3,2,1,0:T(8,128)S(1)}, f32[2,2,8,128]{3,2,1,0:T(8,128)S(1)}, u32[]{:S(2)}, u32[]{:S(2)}) collective-permute-start(f32[2,2,8,128]{3,2,1,0:T(8,128)S(1)} %get-tuple-element.52), channel_id=1, source_target_pairs={{0,1},{1,0},{2,3},{3,2},{4,5},{5,4},{6,7},{7,6},{8,9},{9,8},{10,11... | collective-permute-start | bytes 49160 | tf_op jit(solution)/shard_map/ppermute | solution.py:358
  14.7 1.4 fusion.1
  16.1 1.6 %collective-permute-start.5 = (bf16[1,8,480,128]{3,2,1,0:T(8,128)(2,1)}, bf16[1,8,480,128]{3,2,1,0:T(8,128)(2,1)}, u32[]{:S(2)}, u32[]{:S(2)}) collective-permute-start(bf16[1,8,480,128]{3,2,1,0:T(8,128)(2,1)} %get-tuple-element.92), channel_id=1, source_target_pairs={{2,8},{6,12},{10,16},{14,20},{18,24},{22,28},{3,9},{7,13},{11,17},... | collective-permute-start | bytes 2949128 | tf_op jit(solution)/shard_map/ppermute | solution.py:380
  17.7 1.6 %collective-permute-start.6 = (bf16[1,8,480,128]{3,2,1,0:T(8,128)(2,1)}, bf16[1,8,480,128]{3,2,1,0:T(8,128)(2,1)}, u32[]{:S(2)}, u32[]{:S(2)}) collective-permute-start(bf16[1,8,480,128]{3,2,1,0:T(8,128)(2,1)} %get-tuple-element.91), channel_id=1, source_target_pairs={{2,10},{6,14},{10,18},{14,22},{18,26},{22,30},{3,11},{7,15},{11,19... | collective-permute-start | bytes 2949128 | tf_op jit(solution)/shard_map/ppermute | solution.py:380
  20.8 1.2 copy-done.6
  22.0 3.4 %norm.2 = (bf16[2,240,128]{2,1,0:T(8,128)(2,1)S(1)}, bf16[2,240,128]{2,1,0:T(8,128)(2,1)S(1)}, bf16[2,240,128]{2,1,0:T(8,128)(2,1)S(1)}, bf16[2,240,128]{2,1,0:T...) custom-call(s32[2]{0:T(128)S(1)} %pad_add_fusion.flag_ref, ...), custom_call_target="tpu_custom_call" | custom-call | flops 9830400 | bytes 5898240 | tf_op jit(solution)/shard_map/norm/pallas_call | solution.py:208
  27.4 7.7 %collective-permute-start.18 = (bf16[2,720,128]{2,1,0:T(8,128)(2,1)}, bf16[2,720,128]{2,1,0:T(8,128)(2,1)S(1)}, u32[]{:S(2)}, u32[]{:S(2)}) collective-permute-start(bf16[2,720,128]{2,1,0:T(8,128)(2,1)} %get-tuple-element.70), channel_id=1, source_target_pairs={{0,2},{2,0},{4,6},{6,4},{8,10},{10,8},{12,14},{14,12},{16,18},{18,... | collective-permute-start | bytes 1105928 | tf_op jit(solution)/shard_map/ppermute | solution.py:402
  35.1 1.5 collective-permute-start.19
  36.6 6.3 %collective-permute-start.20 = (bf16[2,720,128]{2,1,0:T(8,128)(2,1)}, bf16[2,720,128]{2,1,0:T(8,128)(2,1)S(1)}, u32[]{:S(2)}, u32[]{:S(2)}) collective-permute-start(bf16[2,720,128]{2,1,0:T(8,128)(2,1)} %get-tuple-element.72), channel_id=1, source_target_pairs={{0,6},{2,4},{4,2},{6,0},{8,14},{10,12},{12,10},{14,8},{16,22},{18,... | collective-permute-start | bytes 1105928 | tf_op jit(solution)/shard_map/ppermute | solution.py:402
  43.0 1.6 %collective-permute-start.3 = (bf16[2,240,128]{2,1,0:T(8,128)(2,1)}, bf16[2,240,128]{2,1,0:T(8,128)(2,1)S(1)}, u32[]{:S(2)}, u32[]{:S(2)}) collective-permute-start(bf16[2,240,128]{2,1,0:T(8,128)(2,1)} %copy-done.10), channel_id=1, source_target_pairs={{0,4},{2,6},{4,0},{6,2},{8,12},{10,14},{12,8},{14,10},{16,20},{18,... | collective-permute-start | bytes 368648 | tf_op jit(solution)/shard_map/ppermute | solution.py:402
  44.6 12.9 %collective-permute-done.20.refs_3_ = bf16[2,720,128]{2,1,0:T(8,128)(2,1)S(1)} collective-permute-done((bf16[2,720,128]{2,1,0:T(8,128)(2,1)}, bf16[2,720,128]{2,1,0:T(8,128)(2,1)S(1)}, u32[]{:S(2)}, u32[]{:S(2)}) %collective-permute-start.20) | collective-permute-done | bytes 368672 | tf_op jit(solution)/shard_map/ppermute | solution.py:402
  57.6 8.4 %collective-permute-start.24 = (bf16[2,720,128]{2,1,0:T(8,128)(2,1)S(1)}, bf16[2,720,128]{2,1,0:T(8,128)(2,1)S(1)}, u32[]{:S(2)}, u32[]{:S(2)}) collective-permute-start(bf16[2,720,128]{2,1,0:T(8,128)(2,1)S(1)} %select_select_fusion), channel_id=1, source_target_pairs={{0,8},{2,10},{4,12},{6,14},{8,16},{10,18},{12,20},{14,22},{16,24},... | collective-permute-start | bytes 1105928 | tf_op jit(solution)/shard_map/ppermute | solution.py:411
  66.0 1.0 fusion
  67.6 3.5 %collective-permute-start.13 = (bf16[2,240,128]{2,1,0:T(8,128)(2,1)S(1)}, bf16[2,240,128]{2,1,0:T(8,128)(2,1)S(1)}, u32[]{:S(2)}, u32[]{:S(2)}) collective-permute-start(bf16[2,240,128]{2,1,0:T(8,128)(2,1)S(1)} %select_select_fusion.1), channel_id=1, source_target_pairs={{0,8},{2,10},{4,12},{6,14},{8,16},{10,18},{12,20},{14,22},{16,24},... | collective-permute-start | bytes 368648 | tf_op jit(solution)/shard_map/ppermute | solution.py:411
  71.1 3.3 %conv.3 = (f32[1,6,480,128]{3,2,1,0:T(8,128)S(1)}, f32[1,2,480,128]{3,2,1,0:T(8,128)S(1)}, f32[1,2,8,128]{3,2,1,0:T(8,128)S(1)}) custom-call(bf16[1,8,480,128]{3,2,1,0:T(8,128)(2,1)} %collective-permute-done.5.refs_0_, bf16[1,8,480,128]{3,2,1,0:T(8,128)(2,1)} %collective-permute-done.6.refs_1_, s32[1]{0:T(128)S(6)} %select_n.70.refs_2_, ...), custom_call_target="tpu_custom_call" | custom-call | flops 1132462080 | bytes 2949120 | tf_op jit(solution)/shard_map/conv/pallas_call | solution.py:97
  74.4 1.5 %edge.3 = (f32[1,2,480,128]{3,2,1,0:T(8,128)S(1)}, f32[1,2,8,128]{3,2,1,0:T(8,128)}) custom-call(s32[2]{0:T(128)S(1)} %add_convert_fusion.flag_ref, f32[1,2,480,128]{3,2,1,0:T(8,128)S(1)} %get-tuple-element.58.part_ref, bf16[1,480,128]{2,1,0:T(8,128)(2,1)S(1)} %collective-permute-done.7.above_ref.below_ref, ...), custom_call_target="tpu_custom_call" | custom-call | flops 94371840 | bytes 1228800 | tf_op jit(solution)/shard_map/edge/pallas_call | solution.py:138
  76.0 1.5 norm.3
  78.6 0.9 collective-permute-start.23
  80.2 9.8 %collective-permute-done.11.refs_6_ = bf16[1,240,128]{2,1,0:T(8,128)(2,1)S(1)} collective-permute-done((bf16[1,240,128]{2,1,0:T(8,128)(2,1)S(1)}, bf16[1,240,128]{2,1,0:T(8,128)(2,1)S(1)}, u32[]{:S(2)}, u32[]{:S(2)}) %collective-permute-start.11) | collective-permute-done | bytes 61472 | tf_op jit(solution)/shard_map/ppermute | solution.py:402
  90.0 3.6 %collective-permute-done.12.refs_7_ = bf16[1,240,128]{2,1,0:T(8,128)(2,1)S(1)} collective-permute-done((bf16[1,240,128]{2,1,0:T(8,128)(2,1)S(1)}, bf16[1,240,128]{2,1,0:T(8,128)(2,1)S(1)}, u32[]{:S(2)}, u32[]{:S(2)}) %collective-permute-start.12) | collective-permute-done | bytes 61472 | tf_op jit(solution)/shard_map/ppermute | solution.py:402
  93.6 0.9 early.4.own_ref
  94.5 2.1 %collective-permute-start.14 = (bf16[8,240,128]{2,1,0:T(8,128)(2,1)S(1)}, bf16[8,240,128]{2,1,0:T(8,128)(2,1)S(1)}, u32[]{:S(2)}, u32[]{:S(2)}) collective-permute-start(bf16[8,240,128]{2,1,0:T(8,128)(2,1)S(1)} %early.4.own_ref), channel_id=1, source_target_pairs={{0,8},{2,10},{4,12},{6,14},{8,16},{10,18},{12,20},{14,22},{16,24},... | collective-permute-start | bytes 1474568 | tf_op jit(solution)/shard_map/ppermute | solution.py:422
  96.7 0.9 early.5.own_ref
  97.6 2.3 %collective-permute-start.25 = (bf16[8,240,128]{2,1,0:T(8,128)(2,1)S(1)}, bf16[8,240,128]{2,1,0:T(8,128)(2,1)S(1)}, u32[]{:S(2)}, u32[]{:S(2)}) collective-permute-start(bf16[8,240,128]{2,1,0:T(8,128)(2,1)S(1)} %early.5.own_ref), channel_id=1, source_target_pairs={{0,8},{2,10},{4,12},{6,14},{8,16},{10,18},{12,20},{14,22},{16,24},... | collective-permute-start | bytes 1474568 | tf_op jit(solution)/shard_map/ppermute | solution.py:422
  99.8 0.9 early.6.own_ref
  100.7 7.5 %collective-permute-done.14.halo_ref = bf16[8,240,128]{2,1,0:T(8,128)(2,1)S(1)} collective-permute-done((bf16[8,240,128]{2,1,0:T(8,128)(2,1)S(1)}, bf16[8,240,128]{2,1,0:T(8,128)(2,1)S(1)}, u32[]{:S(2)}, u32[]{:S(2)}) %collective-permute-start.14) | collective-permute-done | bytes 491552 | tf_op jit(solution)/shard_map/ppermute | solution.py:422
  108.2 4.4 %collective-permute-start.29 = (bf16[8,240,128]{2,1,0:T(8,128)(2,1)S(1)}, bf16[8,240,128]{2,1,0:T(8,128)(2,1)S(1)}, u32[]{:S(2)}, u32[]{:S(2)}) collective-permute-start(bf16[8,240,128]{2,1,0:T(8,128)(2,1)S(1)} %early.6.own_ref), channel_id=1, source_target_pairs={{0,8},{2,10},{4,12},{6,14},{8,16},{10,18},{12,20},{14,22},{16,24},... | collective-permute-start | bytes 1474568 | tf_op jit(solution)/shard_map/ppermute | solution.py:422
  112.6 0.9 early.7.own_ref
  113.5 5.2 %collective-permute-done.25.halo_ref = bf16[8,240,128]{2,1,0:T(8,128)(2,1)S(1)} collective-permute-done((bf16[8,240,128]{2,1,0:T(8,128)(2,1)S(1)}, bf16[8,240,128]{2,1,0:T(8,128)(2,1)S(1)}, u32[]{:S(2)}, u32[]{:S(2)}) %collective-permute-start.25) | collective-permute-done | bytes 491552 | tf_op jit(solution)/shard_map/ppermute | solution.py:422
  118.8 4.4 %collective-permute-start.33 = (bf16[8,240,128]{2,1,0:T(8,128)(2,1)S(1)}, bf16[8,240,128]{2,1,0:T(8,128)(2,1)S(1)}, u32[]{:S(2)}, u32[]{:S(2)}) collective-permute-start(bf16[8,240,128]{2,1,0:T(8,128)(2,1)S(1)} %early.7.own_ref), channel_id=1, source_target_pairs={{0,8},{2,10},{4,12},{6,14},{8,16},{10,18},{12,20},{14,22},{16,24},... | collective-permute-start | bytes 1474568 | tf_op jit(solution)/shard_map/ppermute | solution.py:422
  123.7 1.3 collective-permute-start.16
  126.1 3.2 %collective-permute-done.29.halo_ref = bf16[8,240,128]{2,1,0:T(8,128)(2,1)S(1)} collective-permute-done((bf16[8,240,128]{2,1,0:T(8,128)(2,1)S(1)}, bf16[8,240,128]{2,1,0:T(8,128)(2,1)S(1)}, u32[]{:S(2)}, u32[]{:S(2)}) %collective-permute-start.29) | collective-permute-done | bytes 491552 | tf_op jit(solution)/shard_map/ppermute | solution.py:422
  129.8 1.3 collective-permute-start.27
  131.7 6.8 %collective-permute-done.33.halo_ref = bf16[8,240,128]{2,1,0:T(8,128)(2,1)S(1)} collective-permute-done((bf16[8,240,128]{2,1,0:T(8,128)(2,1)S(1)}, bf16[8,240,128]{2,1,0:T(8,128)(2,1)S(1)}, u32[]{:S(2)}, u32[]{:S(2)}) %collective-permute-start.33) | collective-permute-done | bytes 491552 | tf_op jit(solution)/shard_map/ppermute | solution.py:422
  139.0 1.6 %collective-permute-start.31 = (bf16[2,240,128]{2,1,0:T(8,128)(2,1)S(1)}, bf16[2,240,128]{2,1,0:T(8,128)(2,1)S(1)}, u32[]{:S(2)}, u32[]{:S(2)}) collective-permute-start(bf16[2,240,128]{2,1,0:T(8,128)(2,1)S(1)} %get-tuple-element.84), channel_id=1, source_target_pairs={{0,4},{2,6},{4,0},{6,2},{8,12},{10,14},{12,8},{14,10},{16,20},{18,... | collective-permute-start | bytes 368648 | tf_op jit(solution)/shard_map/ppermute | solution.py:402
  141.3 1.5 collective-permute-start.35
  142.8 2.4 %collective-permute-done.31.refs_10_ = bf16[2,240,128]{2,1,0:T(8,128)(2,1)S(1)} collective-permute-done((bf16[2,240,128]{2,1,0:T(8,128)(2,1)S(1)}, bf16[2,240,128]{2,1,0:T(8,128)(2,1)S(1)}, u32[]{:S(2)}, u32[]{:S(2)}) %collective-permute-start.31) | collective-permute-done | bytes 122912 | tf_op jit(solution)/shard_map/ppermute | solution.py:402
  145.2 1.9 %collective-permute-done.32.refs_11_ = bf16[2,240,128]{2,1,0:T(8,128)(2,1)S(1)} collective-permute-done((bf16[2,240,128]{2,1,0:T(8,128)(2,1)S(1)}, bf16[2,240,128]{2,1,0:T(8,128)(2,1)S(1)}, u32[]{:S(2)}, u32[]{:S(2)}) %collective-permute-start.32) | collective-permute-done | bytes 122912 | tf_op jit(solution)/shard_map/ppermute | solution.py:402
  147.1 3.4 %collective-permute-done.35.refs_14_ = bf16[2,240,128]{2,1,0:T(8,128)(2,1)S(1)} collective-permute-done((bf16[2,240,128]{2,1,0:T(8,128)(2,1)S(1)}, bf16[2,240,128]{2,1,0:T(8,128)(2,1)S(1)}, u32[]{:S(2)}, u32[]{:S(2)}) %collective-permute-start.35) | collective-permute-done | bytes 122912 | tf_op jit(solution)/shard_map/ppermute | solution.py:402
  150.5 1.9 %collective-permute-done.36.refs_15_ = bf16[2,240,128]{2,1,0:T(8,128)(2,1)S(1)} collective-permute-done((bf16[2,240,128]{2,1,0:T(8,128)(2,1)S(1)}, bf16[2,240,128]{2,1,0:T(8,128)(2,1)S(1)}, u32[]{:S(2)}, u32[]{:S(2)}) %collective-permute-start.36) | collective-permute-done | bytes 122912 | tf_op jit(solution)/shard_map/ppermute | solution.py:402
  152.4 1.4 place.1
  (76 shorter events, 9.9 us)
Async XLA Ops:
  1.7 9.2 %collective-permute-start = (bf16[2,480,128]{2,1,0:T(8,128)(2,1)}, bf16[2,480,128]{2,1,0:T(8,128)(2,1)S(1)}, u32[]{:S(2)}, u32[]{:S(2)}) collective-permute-start(bf16[2,480,128]{2,1,0:T(8,128)(2,1)} %dynamic-slice_bitcast_fusion), channel_id=1, source_target_pairs={{0,1},{1,0},{2,3},{3,2},{4,5},{5,4},{6,7},{7,6},{8,9},{9,8},{10,11... | collective-permute-start | bytes 737288 | tf_op jit(solution)/shard_map/ppermute | solution.py:349
  4.7 1.5 %copy-start.1 = (bf16[2,8,480,128]{3,2,1,0:T(8,128)(2,1)S(1)}, bf16[2,8,480,128]{3,2,1,0:T(8,128)(2,1)}, u32[]{:S(2)}) copy-start(bf16[2,8,480,128]{3,2,1,0:T(8,128)(2,1)} %refs_0_.1) | copy-start | bytes 5898244
  6.2 1.0 copy-start.3
  7.2 7.4 %copy-start.2 = (bf16[2,8,480,128]{3,2,1,0:T(8,128)(2,1)S(1)}, bf16[2,8,480,128]{3,2,1,0:T(8,128)(2,1)}, u32[]{:S(2)}) copy-start(bf16[2,8,480,128]{3,2,1,0:T(8,128)(2,1)} %refs_0_.1) | copy-start | bytes 5898244
  12.0 0.9 copy-start.5
  12.9 7.8 %copy-start.7 = (f32[128]{0:T(128)S(1)}, f32[128]{0:T(128)}, u32[]{:S(2)}) copy-start(f32[128]{0:T(128)} %param.7) | copy-start | bytes 1540
  12.9 7.8 %copy-start.8 = (f32[128]{0:T(128)S(1)}, f32[128]{0:T(128)}, u32[]{:S(2)}) copy-start(f32[128]{0:T(128)} %param.8) | copy-start | bytes 1540
  12.9 6.4 %collective-permute-start.1 = (f32[2,2,8,128]{3,2,1,0:T(8,128)S(1)}, f32[2,2,8,128]{3,2,1,0:T(8,128)S(1)}, u32[]{:S(2)}, u32[]{:S(2)}) collective-permute-start(f32[2,2,8,128]{3,2,1,0:T(8,128)S(1)} %get-tuple-element.52), channel_id=1, source_target_pairs={{0,1},{1,0},{2,3},{3,2},{4,5},{5,4},{6,7},{7,6},{8,9},{9,8},{10,11... | collective-permute-start | bytes 49160 | tf_op jit(solution)/shard_map/ppermute | solution.py:358
  16.1 41.5 %collective-permute-start.5 = (bf16[1,8,480,128]{3,2,1,0:T(8,128)(2,1)}, bf16[1,8,480,128]{3,2,1,0:T(8,128)(2,1)}, u32[]{:S(2)}, u32[]{:S(2)}) collective-permute-start(bf16[1,8,480,128]{3,2,1,0:T(8,128)(2,1)} %get-tuple-element.92), channel_id=1, source_target_pairs={{2,8},{6,12},{10,16},{14,20},{18,24},{22,28},{3,9},{7,13},{11,17},... | collective-permute-start | bytes 2949128 | tf_op jit(solution)/shard_map/ppermute | solution.py:380
  17.7 48.3 %collective-permute-start.6 = (bf16[1,8,480,128]{3,2,1,0:T(8,128)(2,1)}, bf16[1,8,480,128]{3,2,1,0:T(8,128)(2,1)}, u32[]{:S(2)}, u32[]{:S(2)}) collective-permute-start(bf16[1,8,480,128]{3,2,1,0:T(8,128)(2,1)} %get-tuple-element.91), channel_id=1, source_target_pairs={{2,10},{6,14},{10,18},{14,22},{18,26},{22,30},{3,11},{7,15},{11,19... | collective-permute-start | bytes 2949128 | tf_op jit(solution)/shard_map/ppermute | solution.py:380
  19.3 15.8 %collective-permute-start.8 = (f32[1,2,8,128]{3,2,1,0:T(8,128)S(1)}, f32[1,2,8,128]{3,2,1,0:T(8,128)S(1)}, u32[]{:S(2)}, u32[]{:S(2)}) collective-permute-start(f32[1,2,8,128]{3,2,1,0:T(8,128)S(1)} %get-tuple-element.94), channel_id=1, source_target_pairs={{2,8},{6,12},{10,16},{14,20},{18,24},{22,28},{3,9},{7,13},{11,17},... | collective-permute-start | bytes 24584 | tf_op jit(solution)/shard_map/ppermute | solution.py:391
  20.0 16.6 %collective-permute-start.9 = (f32[1,2,8,128]{3,2,1,0:T(8,128)S(1)}, f32[1,2,8,128]{3,2,1,0:T(8,128)S(1)}, u32[]{:S(2)}, u32[]{:S(2)}) collective-permute-start(f32[1,2,8,128]{3,2,1,0:T(8,128)S(1)} %get-tuple-element.93), channel_id=1, source_target_pairs={{2,10},{6,14},{10,18},{14,22},{18,26},{22,30},{3,11},{7,15},{11,19... | collective-permute-start | bytes 24584 | tf_op jit(solution)/shard_map/ppermute | solution.py:391
  20.8 1.2 copy-start.6
  25.4 0.7 copy-start.9
  26.0 0.7 copy-start.10
  27.4 43.7 %copy-start.4 = (bf16[3,3,128,128]{3,2,1,0:T(8,128)(2,1)S(1)}, bf16[3,3,128,128]{3,2,1,0:T(8,128)(2,1)}, u32[]{:S(2)}) copy-start(bf16[3,3,128,128]{3,2,1,0:T(8,128)(2,1)} %weight_ref.7) | copy-start | bytes 884740
  27.4 15.6 %collective-permute-start.18 = (bf16[2,720,128]{2,1,0:T(8,128)(2,1)}, bf16[2,720,128]{2,1,0:T(8,128)(2,1)S(1)}, u32[]{:S(2)}, u32[]{:S(2)}) collective-permute-start(bf16[2,720,128]{2,1,0:T(8,128)(2,1)} %get-tuple-element.70), channel_id=1, source_target_pairs={{0,2},{2,0},{4,6},{6,4},{8,10},{10,8},{12,14},{14,12},{16,18},{18,... | collective-permute-start | bytes 1105928 | tf_op jit(solution)/shard_map/ppermute | solution.py:402
  35.1 7.9 %collective-permute-start.19 = (bf16[2,720,128]{2,1,0:T(8,128)(2,1)}, bf16[2,720,128]{2,1,0:T(8,128)(2,1)S(1)}, u32[]{:S(2)}, u32[]{:S(2)}) collective-permute-start(bf16[2,720,128]{2,1,0:T(8,128)(2,1)} %get-tuple-element.71), channel_id=1, source_target_pairs={{0,4},{2,6},{4,0},{6,2},{8,12},{10,14},{12,8},{14,10},{16,20},{18,... | collective-permute-start | bytes 1105928 | tf_op jit(solution)/shard_map/ppermute | solution.py:402
  36.6 20.9 %collective-permute-start.20 = (bf16[2,720,128]{2,1,0:T(8,128)(2,1)}, bf16[2,720,128]{2,1,0:T(8,128)(2,1)S(1)}, u32[]{:S(2)}, u32[]{:S(2)}) collective-permute-start(bf16[2,720,128]{2,1,0:T(8,128)(2,1)} %get-tuple-element.72), channel_id=1, source_target_pairs={{0,6},{2,4},{4,2},{6,0},{8,14},{10,12},{12,10},{14,8},{16,22},{18,... | collective-permute-start | bytes 1105928 | tf_op jit(solution)/shard_map/ppermute | solution.py:402
  43.0 24.6 %collective-permute-start.2 = (bf16[2,240,128]{2,1,0:T(8,128)(2,1)}, bf16[2,240,128]{2,1,0:T(8,128)(2,1)S(1)}, u32[]{:S(2)}, u32[]{:S(2)}) collective-permute-start(bf16[2,240,128]{2,1,0:T(8,128)(2,1)} %copy-done.11), channel_id=1, source_target_pairs={{0,2},{2,0},{4,6},{6,4},{8,10},{10,8},{12,14},{14,12},{16,18},{18,... | collective-permute-start | bytes 368648 | tf_op jit(solution)/shard_map/ppermute | solution.py:402
  43.0 24.5 %collective-permute-start.3 = (bf16[2,240,128]{2,1,0:T(8,128)(2,1)}, bf16[2,240,128]{2,1,0:T(8,128)(2,1)S(1)}, u32[]{:S(2)}, u32[]{:S(2)}) collective-permute-start(bf16[2,240,128]{2,1,0:T(8,128)(2,1)} %copy-done.10), channel_id=1, source_target_pairs={{0,4},{2,6},{4,0},{6,2},{8,12},{10,14},{12,8},{14,10},{16,20},{18,... | collective-permute-start | bytes 368648 | tf_op jit(solution)/shard_map/ppermute | solution.py:402
  57.5 10.1 %collective-permute-start.4 = (bf16[2,240,128]{2,1,0:T(8,128)(2,1)}, bf16[2,240,128]{2,1,0:T(8,128)(2,1)S(1)}, u32[]{:S(2)}, u32[]{:S(2)}) collective-permute-start(bf16[2,240,128]{2,1,0:T(8,128)(2,1)} %copy-done.9), channel_id=1, source_target_pairs={{0,6},{2,4},{4,2},{6,0},{8,14},{10,12},{12,10},{14,8},{16,22},{18,... | collective-permute-start | bytes 368648 | tf_op jit(solution)/shard_map/ppermute | solution.py:402
  57.6 39.0 %collective-permute-start.24 = (bf16[2,720,128]{2,1,0:T(8,128)(2,1)S(1)}, bf16[2,720,128]{2,1,0:T(8,128)(2,1)S(1)}, u32[]{:S(2)}, u32[]{:S(2)}) collective-permute-start(bf16[2,720,128]{2,1,0:T(8,128)(2,1)S(1)} %select_select_fusion), channel_id=1, source_target_pairs={{0,8},{2,10},{4,12},{6,14},{8,16},{10,18},{12,20},{14,22},{16,24},... | collective-permute-start | bytes 1105928 | tf_op jit(solution)/shard_map/ppermute | solution.py:411
  67.0 7.5 %collective-permute-start.7 = (bf16[1,480,128]{2,1,0:T(8,128)(2,1)S(1)}, bf16[1,480,128]{2,1,0:T(8,128)(2,1)S(1)}, u32[]{:S(2)}, u32[]{:S(2)}) collective-permute-start(bf16[1,480,128]{2,1,0:T(8,128)(2,1)S(1)} %fusion), channel_id=1, source_target_pairs={{0,1},{1,0},{2,3},{3,2},{4,5},{5,4},{6,7},{7,6},{8,9},{9,8},{10,11... | collective-permute-start | bytes 368648 | tf_op jit(solution)/shard_map/ppermute | solution.py:349
  67.6 11.0 %collective-permute-start.13 = (bf16[2,240,128]{2,1,0:T(8,128)(2,1)S(1)}, bf16[2,240,128]{2,1,0:T(8,128)(2,1)S(1)}, u32[]{:S(2)}, u32[]{:S(2)}) collective-permute-start(bf16[2,240,128]{2,1,0:T(8,128)(2,1)S(1)} %select_select_fusion.1), channel_id=1, source_target_pairs={{0,8},{2,10},{4,12},{6,14},{8,16},{10,18},{12,20},{14,22},{16,24},... | collective-permute-start | bytes 368648 | tf_op jit(solution)/shard_map/ppermute | solution.py:411
  74.4 19.2 %copy-start = (bf16[3,3,128,128]{3,2,1,0:T(8,128)(2,1)S(1)}, bf16[3,3,128,128]{3,2,1,0:T(8,128)(2,1)}, u32[]{:S(2)}) copy-start(bf16[3,3,128,128]{3,2,1,0:T(8,128)(2,1)} %weight_ref.11) | copy-start | bytes 884740
  77.5 2.0 %collective-permute-start.10 = (bf16[1,240,128]{2,1,0:T(8,128)(2,1)S(1)}, bf16[1,240,128]{2,1,0:T(8,128)(2,1)S(1)}, u32[]{:S(2)}, u32[]{:S(2)}) collective-permute-start(bf16[1,240,128]{2,1,0:T(8,128)(2,1)S(1)} %get-tuple-element.62), channel_id=1, source_target_pairs={{0,2},{2,0},{4,6},{6,4},{8,10},{10,8},{12,14},{14,12},{16,18},{18,... | collective-permute-start | bytes 184328 | tf_op jit(solution)/shard_map/ppermute | solution.py:402
  77.6 19.0 %collective-permute-start.21 = (bf16[1,720,128]{2,1,0:T(8,128)(2,1)S(1)}, bf16[1,720,128]{2,1,0:T(8,128)(2,1)S(1)}, u32[]{:S(2)}, u32[]{:S(2)}) collective-permute-start(bf16[1,720,128]{2,1,0:T(8,128)(2,1)S(1)} %get-tuple-element.74), channel_id=1, source_target_pairs={{0,2},{2,0},{4,6},{6,4},{8,10},{10,8},{12,14},{14,12},{16,18},{18,... | collective-permute-start | bytes 552968 | tf_op jit(solution)/shard_map/ppermute | solution.py:402
  78.1 18.6 %collective-permute-start.22 = (bf16[1,720,128]{2,1,0:T(8,128)(2,1)S(1)}, bf16[1,720,128]{2,1,0:T(8,128)(2,1)S(1)}, u32[]{:S(2)}, u32[]{:S(2)}) collective-permute-start(bf16[1,720,128]{2,1,0:T(8,128)(2,1)S(1)} %get-tuple-element.75), channel_id=1, source_target_pairs={{0,4},{2,6},{4,0},{6,2},{8,12},{10,14},{12,8},{14,10},{16,20},{18,... | collective-permute-start | bytes 552968 | tf_op jit(solution)/shard_map/ppermute | solution.py:402
  78.6 18.0 %collective-permute-start.23 = (bf16[1,720,128]{2,1,0:T(8,128)(2,1)S(1)}, bf16[1,720,128]{2,1,0:T(8,128)(2,1)S(1)}, u32[]{:S(2)}, u32[]{:S(2)}) collective-permute-start(bf16[1,720,128]{2,1,0:T(8,128)(2,1)S(1)} %get-tuple-element.76), channel_id=1, source_target_pairs={{0,6},{2,4},{4,2},{6,0},{8,14},{10,12},{12,10},{14,8},{16,22},{18,... | collective-permute-start | bytes 552968 | tf_op jit(solution)/shard_map/ppermute | solution.py:402
  79.5 10.5 %collective-permute-start.11 = (bf16[1,240,128]{2,1,0:T(8,128)(2,1)S(1)}, bf16[1,240,128]{2,1,0:T(8,128)(2,1)S(1)}, u32[]{:S(2)}, u32[]{:S(2)}) collective-permute-start(bf16[1,240,128]{2,1,0:T(8,128)(2,1)S(1)} %get-tuple-element.63), channel_id=1, source_target_pairs={{0,4},{2,6},{4,0},{6,2},{8,12},{10,14},{12,8},{14,10},{16,20},{18,... | collective-permute-start | bytes 184328 | tf_op jit(solution)/shard_map/ppermute | solution.py:402
  90.0 3.6 %collective-permute-start.12 = (bf16[1,240,128]{2,1,0:T(8,128)(2,1)S(1)}, bf16[1,240,128]{2,1,0:T(8,128)(2,1)S(1)}, u32[]{:S(2)}, u32[]{:S(2)}) collective-permute-start(bf16[1,240,128]{2,1,0:T(8,128)(2,1)S(1)} %get-tuple-element.64), channel_id=1, source_target_pairs={{0,6},{2,4},{4,2},{6,0},{8,14},{10,12},{12,10},{14,8},{16,22},{18,... | collective-permute-start | bytes 184328 | tf_op jit(solution)/shard_map/ppermute | solution.py:402
  94.5 13.7 %collective-permute-start.14 = (bf16[8,240,128]{2,1,0:T(8,128)(2,1)S(1)}, bf16[8,240,128]{2,1,0:T(8,128)(2,1)S(1)}, u32[]{:S(2)}, u32[]{:S(2)}) collective-permute-start(bf16[8,240,128]{2,1,0:T(8,128)(2,1)S(1)} %early.4.own_ref), channel_id=1, source_target_pairs={{0,8},{2,10},{4,12},{6,14},{8,16},{10,18},{12,20},{14,22},{16,24},... | collective-permute-start | bytes 1474568 | tf_op jit(solution)/shard_map/ppermute | solution.py:422
  97.6 21.2 %collective-permute-start.25 = (bf16[8,240,128]{2,1,0:T(8,128)(2,1)S(1)}, bf16[8,240,128]{2,1,0:T(8,128)(2,1)S(1)}, u32[]{:S(2)}, u32[]{:S(2)}) collective-permute-start(bf16[8,240,128]{2,1,0:T(8,128)(2,1)S(1)} %early.5.own_ref), channel_id=1, source_target_pairs={{0,8},{2,10},{4,12},{6,14},{8,16},{10,18},{12,20},{14,22},{16,24},... | collective-permute-start | bytes 1474568 | tf_op jit(solution)/shard_map/ppermute | solution.py:422
  108.2 21.1 %collective-permute-start.29 = (bf16[8,240,128]{2,1,0:T(8,128)(2,1)S(1)}, bf16[8,240,128]{2,1,0:T(8,128)(2,1)S(1)}, u32[]{:S(2)}, u32[]{:S(2)}) collective-permute-start(bf16[8,240,128]{2,1,0:T(8,128)(2,1)S(1)} %early.6.own_ref), channel_id=1, source_target_pairs={{0,8},{2,10},{4,12},{6,14},{8,16},{10,18},{12,20},{14,22},{16,24},... | collective-permute-start | bytes 1474568 | tf_op jit(solution)/shard_map/ppermute | solution.py:422
  118.8 19.8 %collective-permute-start.33 = (bf16[8,240,128]{2,1,0:T(8,128)(2,1)S(1)}, bf16[8,240,128]{2,1,0:T(8,128)(2,1)S(1)}, u32[]{:S(2)}, u32[]{:S(2)}) collective-permute-start(bf16[8,240,128]{2,1,0:T(8,128)(2,1)S(1)} %early.7.own_ref), channel_id=1, source_target_pairs={{0,8},{2,10},{4,12},{6,14},{8,16},{10,18},{12,20},{14,22},{16,24},... | collective-permute-start | bytes 1474568 | tf_op jit(solution)/shard_map/ppermute | solution.py:422
  123.7 6.1 %collective-permute-start.15 = (bf16[2,240,128]{2,1,0:T(8,128)(2,1)S(1)}, bf16[2,240,128]{2,1,0:T(8,128)(2,1)S(1)}, u32[]{:S(2)}, u32[]{:S(2)}) collective-permute-start(bf16[2,240,128]{2,1,0:T(8,128)(2,1)S(1)} %get-tuple-element.66), channel_id=1, source_target_pairs={{0,2},{2,0},{4,6},{6,4},{8,10},{10,8},{12,14},{14,12},{16,18},{18,... | collective-permute-start | bytes 368648 | tf_op jit(solution)/shard_map/ppermute | solution.py:402
  123.7 7.4 %collective-permute-start.16 = (bf16[2,240,128]{2,1,0:T(8,128)(2,1)S(1)}, bf16[2,240,128]{2,1,0:T(8,128)(2,1)S(1)}, u32[]{:S(2)}, u32[]{:S(2)}) collective-permute-start(bf16[2,240,128]{2,1,0:T(8,128)(2,1)S(1)} %get-tuple-element.67), channel_id=1, source_target_pairs={{0,4},{2,6},{4,0},{6,2},{8,12},{10,14},{12,8},{14,10},{16,20},{18,... | collective-permute-start | bytes 368648 | tf_op jit(solution)/shard_map/ppermute | solution.py:402
  125.1 14.0 %collective-permute-start.17 = (bf16[2,240,128]{2,1,0:T(8,128)(2,1)S(1)}, bf16[2,240,128]{2,1,0:T(8,128)(2,1)S(1)}, u32[]{:S(2)}, u32[]{:S(2)}) collective-permute-start(bf16[2,240,128]{2,1,0:T(8,128)(2,1)S(1)} %get-tuple-element.68), channel_id=1, source_target_pairs={{0,6},{2,4},{4,2},{6,0},{8,14},{10,12},{12,10},{14,8},{16,22},{18,... | collective-permute-start | bytes 368648 | tf_op jit(solution)/shard_map/ppermute | solution.py:402
  129.3 11.3 %collective-permute-start.26 = (bf16[2,240,128]{2,1,0:T(8,128)(2,1)S(1)}, bf16[2,240,128]{2,1,0:T(8,128)(2,1)S(1)}, u32[]{:S(2)}, u32[]{:S(2)}) collective-permute-start(bf16[2,240,128]{2,1,0:T(8,128)(2,1)S(1)} %get-tuple-element.78), channel_id=1, source_target_pairs={{0,2},{2,0},{4,6},{6,4},{8,10},{10,8},{12,14},{14,12},{16,18},{18,... | collective-permute-start | bytes 368648 | tf_op jit(solution)/shard_map/ppermute | solution.py:402
  129.8 11.2 %collective-permute-start.27 = (bf16[2,240,128]{2,1,0:T(8,128)(2,1)S(1)}, bf16[2,240,128]{2,1,0:T(8,128)(2,1)S(1)}, u32[]{:S(2)}, u32[]{:S(2)}) collective-permute-start(bf16[2,240,128]{2,1,0:T(8,128)(2,1)S(1)} %get-tuple-element.79), channel_id=1, source_target_pairs={{0,4},{2,6},{4,0},{6,2},{8,12},{10,14},{12,8},{14,10},{16,20},{18,... | collective-permute-start | bytes 368648 | tf_op jit(solution)/shard_map/ppermute | solution.py:402
  131.1 10.1 %collective-permute-start.28 = (bf16[2,240,128]{2,1,0:T(8,128)(2,1)S(1)}, bf16[2,240,128]{2,1,0:T(8,128)(2,1)S(1)}, u32[]{:S(2)}, u32[]{:S(2)}) collective-permute-start(bf16[2,240,128]{2,1,0:T(8,128)(2,1)S(1)} %get-tuple-element.80), channel_id=1, source_target_pairs={{0,6},{2,4},{4,2},{6,0},{8,14},{10,12},{12,10},{14,8},{16,22},{18,... | collective-permute-start | bytes 368648 | tf_op jit(solution)/shard_map/ppermute | solution.py:402
  138.5 4.3 %collective-permute-start.30 = (bf16[2,240,128]{2,1,0:T(8,128)(2,1)S(1)}, bf16[2,240,128]{2,1,0:T(8,128)(2,1)S(1)}, u32[]{:S(2)}, u32[]{:S(2)}) collective-permute-start(bf16[2,240,128]{2,1,0:T(8,128)(2,1)S(1)} %get-tuple-element.83), channel_id=1, source_target_pairs={{0,2},{2,0},{4,6},{6,4},{8,10},{10,8},{12,14},{14,12},{16,18},{18,... | collective-permute-start | bytes 368648 | tf_op jit(solution)/shard_map/ppermute | solution.py:402
  139.0 6.2 %collective-permute-start.31 = (bf16[2,240,128]{2,1,0:T(8,128)(2,1)S(1)}, bf16[2,240,128]{2,1,0:T(8,128)(2,1)S(1)}, u32[]{:S(2)}, u32[]{:S(2)}) collective-permute-start(bf16[2,240,128]{2,1,0:T(8,128)(2,1)S(1)} %get-tuple-element.84), channel_id=1, source_target_pairs={{0,4},{2,6},{4,0},{6,2},{8,12},{10,14},{12,8},{14,10},{16,20},{18,... | collective-permute-start | bytes 368648 | tf_op jit(solution)/shard_map/ppermute | solution.py:402
  140.6 6.4 %collective-permute-start.32 = (bf16[2,240,128]{2,1,0:T(8,128)(2,1)S(1)}, bf16[2,240,128]{2,1,0:T(8,128)(2,1)S(1)}, u32[]{:S(2)}, u32[]{:S(2)}) collective-permute-start(bf16[2,240,128]{2,1,0:T(8,128)(2,1)S(1)} %get-tuple-element.85), channel_id=1, source_target_pairs={{0,6},{2,4},{4,2},{6,0},{8,14},{10,12},{12,10},{14,8},{16,22},{18,... | collective-permute-start | bytes 368648 | tf_op jit(solution)/shard_map/ppermute | solution.py:402
  141.0 6.1 %collective-permute-start.34 = (bf16[2,240,128]{2,1,0:T(8,128)(2,1)S(1)}, bf16[2,240,128]{2,1,0:T(8,128)(2,1)S(1)}, u32[]{:S(2)}, u32[]{:S(2)}) collective-permute-start(bf16[2,240,128]{2,1,0:T(8,128)(2,1)S(1)} %get-tuple-element.88), channel_id=1, source_target_pairs={{0,2},{2,0},{4,6},{6,4},{8,10},{10,8},{12,14},{14,12},{16,18},{18,... | collective-permute-start | bytes 368648 | tf_op jit(solution)/shard_map/ppermute | solution.py:402
  141.3 9.2 %collective-permute-start.35 = (bf16[2,240,128]{2,1,0:T(8,128)(2,1)S(1)}, bf16[2,240,128]{2,1,0:T(8,128)(2,1)S(1)}, u32[]{:S(2)}, u32[]{:S(2)}) collective-permute-start(bf16[2,240,128]{2,1,0:T(8,128)(2,1)S(1)} %get-tuple-element.89), channel_id=1, source_target_pairs={{0,4},{2,6},{4,0},{6,2},{8,12},{10,14},{12,8},{14,10},{16,20},{18,... | collective-permute-start | bytes 368648 | tf_op jit(solution)/shard_map/ppermute | solution.py:402
  142.8 9.6 %collective-permute-start.36 = (bf16[2,240,128]{2,1,0:T(8,128)(2,1)S(1)}, bf16[2,240,128]{2,1,0:T(8,128)(2,1)S(1)}, u32[]{:S(2)}, u32[]{:S(2)}) collective-permute-start(bf16[2,240,128]{2,1,0:T(8,128)(2,1)S(1)} %get-tuple-element.90), channel_id=1, source_target_pairs={{0,6},{2,4},{4,2},{6,0},{8,14},{10,12},{12,10},{14,8},{16,22},{18,... | collective-permute-start | bytes 368648 | tf_op jit(solution)/shard_map/ppermute | solution.py:402
  (1 other events, 0.6 us)

commit v3 on v2

v3 whole, which is shorter than its diff:
```python
import functools

import jax
import jax.numpy as jnp
from jax import lax
from jax.experimental import pallas as pl
from jax.experimental.pallas import tpu as pltpu
from jax.sharding import PartitionSpec as P

GROUPS = 32
SPAN = 8
OWN_SIZES = (480, 480)
GUEST_SIZES = (320, 640)
OUT_SIZES = (320, 320, 192, 128)
VMEM = pltpu.VMEM
ANY = pl.ANY
F32 = jnp.float32
BF16 = jnp.bfloat16


def vspec():
    return pl.BlockSpec(memory_space=VMEM)


def params(mib):
    return pltpu.CompilerParams(vmem_limit_bytes=mib << 20)


COST = pl.CostEstimate(flops=0, bytes_accessed=0, transcendentals=0)
LONG = pl.CostEstimate(flops=20_000_000_000, bytes_accessed=0, transcendentals=0)


def hspec():
    return pl.BlockSpec(memory_space=ANY)


def hbm(value):
    return pltpu.with_memory_space_constraint(value, pltpu.HBM)


def shifted_sum(taps):
    width, ch = taps.shape[0], taps.shape[1] // 3
    column = lax.broadcasted_iota(jnp.int32, (width, ch), 0)
    left = jnp.where(column == 0, 0.0, pltpu.roll(taps[:, :ch], 1, 0))
    right = jnp.where(column == width - 1, 0.0, pltpu.roll(taps[:, 2 * ch :], width - 1, 0))
    return left + taps[:, ch : 2 * ch] + right


def fold(value):
    return jnp.sum(value.reshape(value.shape[0] // 8, 8, value.shape[1]), axis=0)


def widen(weight_ref, wide_ref):
    ch = weight_ref.shape[-1]
    wide_ref[...] = jnp.zeros_like(wide_ref)
    for out in range(2):
        for col in range(3):
            for row in range(3):
                wide_ref[
                    (out + row) * ch : (out + row + 1) * ch,
                    (out * 3 + col) * ch : (out * 3 + col + 1) * ch,
                ] = weight_ref[row, col]


def conv_rows(band, read, wide_ref, write):
    ch = wide_ref.shape[0] // 4
    for first in range(0, band, 2):
        lhs = jnp.concatenate([read(r) for r in range(first - 1, first + 3)], axis=-1)
        wide = jnp.dot(lhs, wide_ref[...], preferred_element_type=F32)
        for out in range(2):
            write(first + out, shifted_sum(wide[:, out * 3 * ch : (out + 1) * 3 * ch]))


def padded_read(band, row_of, above, below):
    row, rows = lax.axis_index("rows"), lax.axis_size("rows")

    def read(r):
        if r < 0:
            return jnp.where(row > 0, above(), jnp.zeros_like(above()))
        if r == band:
            return jnp.where(row < rows - 1, below(), jnp.zeros_like(below()))
        return row_of(r)

    return read


def conv_kernel(band, video_ref, weight_ref, out_ref, sums_ref, wide_ref):
    @pl.when(pl.program_id(0) == 0)
    def _():
        widen(weight_ref, wide_ref)

    ch = weight_ref.shape[-1]
    sums = [jnp.zeros((8, ch), F32), jnp.zeros((8, ch), F32)]

    def read(row):
        if 0 <= row < band:
            return video_ref[0, row]
        return jnp.zeros_like(video_ref[0, 0])

    def write(row, value):
        out_ref[0, row] = value
        if 0 < row < band - 1:
            sums[0] = sums[0] + fold(value)
            sums[1] = sums[1] + fold(value * value)

    conv_rows(band, read, wide_ref, write)
    sums_ref[0, 0] = sums[0]
    sums_ref[0, 1] = sums[1]


def frame_spec(*shape):
    return pl.BlockSpec((1,) + shape, lambda f, *_: (f,) + (0,) * len(shape))


def conv_call(video, weight):
    frames, band, width, ch = video.shape
    return pl.pallas_call(
        functools.partial(conv_kernel, band),
        grid=(frames,),
        in_specs=[
            frame_spec(band, width, ch),
            pl.BlockSpec(weight.shape, lambda f: (0, 0, 0, 0)),
        ],
        out_specs=[frame_spec(band, width, ch), frame_spec(2, 8, ch)],
        out_shape=[
            jax.ShapeDtypeStruct(video.shape, F32),
            jax.ShapeDtypeStruct((frames, 2, 8, ch), F32),
        ],
        scratch_shapes=[VMEM((4 * ch, 6 * ch), BF16)],
        compiler_params=params(16),
        cost_estimate=LONG,
        name="conv",
    )(hbm(video), hbm(weight))


def edge_kernel(conv_ref, above_ref, below_ref, weight_ref, sums_ref, out_ref, out_sums_ref):
    side = pl.program_id(1)
    row, rows = lax.axis_index("rows"), lax.axis_size("rows")

    @pl.when(side == 0)
    def _():
        out_sums_ref[...] = sums_ref[...]

    def add(halo_ref, tap, there):
        halo = jnp.where(there, halo_ref[0], jnp.zeros_like(halo_ref[0]))
        taps = jnp.concatenate([weight_ref[tap, col] for col in range(3)], axis=-1)
        wide = jnp.dot(halo, taps, preferred_element_type=F32)
        value = conv_ref[0, 0] + shifted_sum(wide)
        out_ref[0, 0] = value
        out_sums_ref[0, 0] += fold(value)
        out_sums_ref[0, 1] += fold(value * value)

    @pl.when(side == 0)
    def _():
        add(above_ref, 0, row > 0)

    @pl.when(side == 1)
    def _():
        add(below_ref, 2, row < rows - 1)


def edge_call(conv, above, below, weight, sums):
    frames, band, width, ch = conv.shape
    edge = pl.BlockSpec((1, 1, width, ch), lambda f, side: (f, side * (band - 1), 0, 0))
    return pl.pallas_call(
        edge_kernel,
        grid=(frames, 2),
        in_specs=[
            edge,
            frame_spec(width, ch),
            frame_spec(width, ch),
            pl.BlockSpec(weight.shape, lambda f, side: (0, 0, 0, 0)),
            frame_spec(2, 8, ch),
        ],
        out_specs=[edge, frame_spec(2, 8, ch)],
        out_shape=[
            jax.ShapeDtypeStruct(conv.shape, F32),
            jax.ShapeDtypeStruct(sums.shape, F32),
        ],
        input_output_aliases={0: 0},
        compiler_params=params(12),
        cost_estimate=COST,
        name="edge",
    )(conv, above, below, hbm(weight), sums)


def over_groups(value, per_group):
    lane = lax.broadcasted_iota(jnp.int32, value.shape, 1)
    lanes = value.shape[1]
    step = 1
    while step < per_group:
        value = value + pltpu.roll(value, lanes - step, 1)
        step *= 2
    value = jnp.where(lane % per_group == 0, value, 0.0)
    step = 1
    while step < per_group:
        value = value + pltpu.roll(value, step, 1)
        step *= 2
    return value


def norm_frame(conv_ref, frame, sums, count, gain_ref, shift_ref, hidden_ref, alive=None):
    band, _, ch = conv_ref.shape[1:]
    total = [
        over_groups(jnp.broadcast_to(jnp.sum(x, axis=0, keepdims=True), (8, ch)), ch // GROUPS)
        for x in sums
    ]
    mean = total[0] / count
    var = total[1] / count - mean * mean
    scale = (lax.rsqrt(var + 1e-05) * gain_ref[...])[:1]
    mean = mean[:1]
    shift = shift_ref[...]

    @pl.loop(0, band)
    def _(row):
        v = (conv_ref[frame, row] - mean) * scale + shift
        v = 0.5 * v * (1.0 + jnp.tanh(0.5 * v))
        if alive is not None:
            v = jnp.where(alive, v, 0.0)
        hidden_ref[frame, row] = v.astype(BF16)


def piece_copies(hidden_ref, frame, outs, sizes, members, sem):
    frames, band, width, ch = hidden_ref.shape
    flat = hidden_ref.reshape(frames, band * width, ch)
    me = lax.axis_index("tm") % members
    copies, offset = [], 0
    for i, size in enumerate(sizes):
        for k in range(members):
            n = i * members + k
            start = pl.multiple_of((me ^ k) * sum(sizes) + offset, 16)
            copies.append(
                pltpu.make_async_copy(
                    flat.at[frame, pl.ds(start, size)], outs[n].at[frame], sem.at[n, frame]
                )
            )
        offset += size
    return copies


def norm_kernel(count, members, sizes, conv_ref, own_ref, other_ref, above_ref, below_ref, gain_ref, shift_ref, packet_ref, *refs):
    outs, (hidden_ref, sem) = refs[:-2], refs[-2:]
    frames, band, width, ch = conv_ref.shape
    for frame in range(frames):
        sums = [own_ref[frame, i] + other_ref[frame, i] for i in range(2)]
        packet_ref[frame, :width] = above_ref[frame]
        packet_ref[frame, width : 2 * width] = below_ref[frame]
        for i in range(2):
            rest = sums[i]
            for part in range(3):
                short = rest.astype(BF16).astype(F32)
                rest = rest - short
                at = 2 * width + (i * 3 + part) * 16
                packet_ref[frame, at : at + 16] = jnp.concatenate(
                    [short, jnp.zeros_like(short)], axis=0
                ).astype(BF16)
        norm_frame(conv_ref, frame, sums, count, gain_ref, shift_ref, hidden_ref)
        for copy in piece_copies(hidden_ref, frame, outs, sizes, members, sem):
            copy.start()
    for frame in range(frames):
        for copy in piece_copies(hidden_ref, frame, outs, sizes, members, sem):
            copy.wait()


def piece_shapes(frames, members, sizes, ch):
    return [pltpu.HBM((frames, size, ch), BF16) for size in sizes for _ in range(members)]


def norm_call(conv, own, other, above, below, gain, shift, count, members, sizes):
    frames, band, width, ch = conv.shape
    pieces = members * len(sizes)
    return pl.pallas_call(
        functools.partial(norm_kernel, count, members, sizes),
        in_specs=[vspec()] * 7,
        out_specs=[vspec()] + [hspec()] * pieces,
        out_shape=[jax.ShapeDtypeStruct((frames, 2 * width + 96, ch), BF16)]
        + piece_shapes(frames, members, sizes, ch),
        scratch_shapes=[
            VMEM((frames, band, width, ch), BF16),
            pltpu.SemaphoreType.DMA((pieces, frames)),
        ],
        compiler_params=params(16),
        cost_estimate=COST,
        name="norm",
    )(conv, own, other, above, below, gain.reshape(1, ch), shift.reshape(1, ch))


def guest_kernel(count, members, sizes, video_hbm, packet_ref, weight_ref, gain_ref, shift_ref, *refs):
    outs, (video_ref, conv_ref, hidden_ref, wide_ref, in_sem, sem) = refs[:-6], refs[-6:]
    frames, band, width, ch = video_hbm.shape
    here = lax.axis_index("tm")

    @pl.when(jnp.logical_and(here >= members, here % 2 == 0))
    def _():
        loads = [
            pltpu.make_async_copy(video_hbm.at[f], video_ref.at[f], in_sem.at[f])
            for f in range(frames)
        ]
        for copy in loads:
            copy.start()
        widen(weight_ref, wide_ref)
        for frame in range(frames):
            loads[frame].wait()

            def write(row, value):
                conv_ref[frame, row] = value

            read = padded_read(
                band,
                lambda r: video_ref[frame, r],
                lambda: packet_ref[frame, :width],
                lambda: packet_ref[frame, width : 2 * width],
            )
            conv_rows(band, read, wide_ref, write)
            sums = []
            for i in range(2):
                at = 2 * width + i * 48
                parts = packet_ref[frame, at : at + 48].astype(F32)
                sums.append(parts[:16] + parts[16:32] + parts[32:])
            norm_frame(conv_ref, frame, sums, count, gain_ref, shift_ref, hidden_ref)
            for copy in piece_copies(hidden_ref, frame, outs, sizes, members, sem):
                copy.start()
        for frame in range(frames):
            for copy in piece_copies(hidden_ref, frame, outs, sizes, members, sem):
                copy.wait()

    @pl.when(here < members)
    def _():
        hidden_ref[...] = jnp.zeros_like(hidden_ref)
        for frame in range(frames):
            for copy in piece_copies(hidden_ref, frame, outs, sizes, members, sem):
                copy.start()
        for frame in range(frames):
            for copy in piece_copies(hidden_ref, frame, outs, sizes, members, sem):
                copy.wait()


def guest_call(video, packet, weight, gain, shift, count, members, sizes):
    frames, band, width, ch = video.shape
    pieces = members * len(sizes)
    return pl.pallas_call(
        functools.partial(guest_kernel, count, members, sizes),
        in_specs=[hspec()] + [vspec()] * 4,
        out_specs=[hspec()] * pieces,
        out_shape=piece_shapes(frames, members, sizes, ch),
        scratch_shapes=[
            VMEM(video.shape, BF16),
            VMEM(video.shape, F32),
            VMEM(video.shape, BF16),
            VMEM((4 * ch, 6 * ch), BF16),
            pltpu.SemaphoreType.DMA((frames,)),
            pltpu.SemaphoreType.DMA((pieces, frames)),
        ],
        compiler_params=params(24),
        cost_estimate=LONG,
        name="guest",
    )(video, packet, weight, gain.reshape(1, ch), shift.reshape(1, ch))


def pair_weights(weight_ref, layer, wide_ref):
    ch = weight_ref.shape[-1]
    wide_ref[...] = jnp.zeros_like(wide_ref)
    for out in range(2):
        for tap in range(3):
            row = out + 2 - tap
            wide_ref[row * ch : (row + 1) * ch, out * ch : (out + 1) * ch] = weight_ref[layer, tap]


def pair(read, write, time, dilation, wide_ref):
    ch = wide_ref.shape[1] // 2
    frames = [read(time + (a - 2) * dilation) for a in range(4)]
    both = jnp.dot(jnp.concatenate(frames, axis=-1), wide_ref[...], preferred_element_type=F32)
    write(time, (both[:, :ch] + frames[2].astype(F32)).astype(BF16))
    write(time + dilation, (both[:, ch:] + frames[3].astype(F32)).astype(BF16))


def early_kernel(members, spans, size, *refs):
    own, guest = spans
    count = [len({i for i, *_ in kind}) for kind in spans]
    pieces, refs = refs[: count[0] * members], refs[count[0] * members :]
    halos, refs = refs[: count[0]], refs[count[0] :]
    guests, refs = refs[: count[1] * members], refs[count[1] * members :]
    weight_ref, out_ref, u0_ref, u1_ref, wide_ref = refs
    step = pieces[0].shape[0]
    lead = SPAN - 2
    me = lax.axis_index("tm") % members
    for i, source, target, rows in own:
        for k in range(members):
            u0_ref[pl.ds(lead + (me ^ k) * step, step), target : target + rows] = pieces[
                i * members + k
            ][:, source : source + rows]
        u0_ref[2:4, target : target + rows] = halos[i][:, source : source + rows]
    for i, source, target, rows in guest:
        for k in range(members):

            @pl.when((me ^ k) % 2 == 0)
            def _():
                u0_ref[pl.ds(2 * (me ^ k), step), target : target + rows] = guests[
                    i * members + k
                ][:, source : source + rows]

    pair_weights(weight_ref, 0, wide_ref)

    def write1(t, value):
        u1_ref[t + 4] = value

    def write2(t, value):
        out_ref[t] = value

    for time in range(-4, SPAN, 2):
        pair(lambda t: u0_ref[t + lead], write1, time, 1, wide_ref)
    pair_weights(weight_ref, 1, wide_ref)
    for time in range(0, SPAN, 4):
        for odd in range(2):
            pair(lambda t: u1_ref[t + 4], write2, time + odd, 2, wide_ref)


def overlaps(sizes, first, last):
    found, at = [], 0
    for i, size in enumerate(sizes):
        low, high = max(first, at), min(last, at + size)
        if low < high:
            found.append((i, low - at, low - first, high - low))
        at += size
    return found


def early_call(own, halos, guest, weight, first, size):
    members, ch = len(own[0]), weight.shape[-1]
    spans, arrays = [], []
    for kind, (blocks, sizes) in enumerate(((own, OWN_SIZES), (guest, GUEST_SIZES))):
        parts = overlaps(sizes, first, first + size)
        base = parts[0][0]
        spans.append([(i - base, *rest) for i, *rest in parts])
        arrays += sum([blocks[i] for i, *_ in parts], [])
        if kind == 0:
            arrays += [halos[i] for i, *_ in parts]
    return pl.pallas_call(
        functools.partial(early_kernel, members, spans, size),
        in_specs=[vspec()] * (len(arrays) + 1),
        out_specs=vspec(),
        out_shape=jax.ShapeDtypeStruct((SPAN, size, ch), BF16),
        scratch_shapes=[
            VMEM((2 * SPAN - 2, size, ch), BF16),
            VMEM((SPAN + 4, size, ch), BF16),
            VMEM((4 * ch, 2 * ch), BF16),
        ],
        compiler_params=params(16),
        cost_estimate=COST,
        name="early",
    )(*arrays, weight)


def late_kernel(members, own_ref, halo_ref, weight_ref, *refs):
    outs, (u3_ref, wide_ref) = refs[:members], refs[members:]
    step = outs[0].shape[0]
    pair_weights(weight_ref, 2, wide_ref)

    def write3(t, value):
        u3_ref[t] = value

    for time in range(4):
        pair(
            lambda t: own_ref[t] if t >= 0 else halo_ref[t + SPAN], write3, time, 4, wide_ref
        )
    me = lax.axis_index("tm") % members
    for k in range(members):
        outs[k][...] = u3_ref[pl.ds((me ^ k) * step, step)]


def late_call(own, halo, weight, members):
    frames, size, ch = own.shape
    return pl.pallas_call(
        functools.partial(late_kernel, members),
        in_specs=[vspec()] * 3,
        out_specs=[vspec()] * members,
        out_shape=[jax.ShapeDtypeStruct((frames // members, size, ch), BF16)] * members,
        scratch_shapes=[VMEM(own.shape, BF16), VMEM((4 * ch, 2 * ch), BF16)],
        compiler_params=params(12),
        cost_estimate=COST,
        name="late",
    )(own, halo, weight)


def place_kernel(members, sizes, *refs):
    pieces, (out_ref, sem) = refs[: members * len(sizes)], refs[members * len(sizes) :]
    me = lax.axis_index("tm") % members
    copies = []
    offset = 0
    for i, size in enumerate(sizes):
        for k in range(members):
            n = i * members + k
            place = out_ref.at[:, me ^ k, pl.ds(offset, size)]
            copies.append(pltpu.make_async_copy(pieces[n], place, sem.at[n]))
        offset += size
    for copy in copies:
        copy.start()
    for copy in copies:
        copy.wait()


def place_call(pieces, members, sizes):
    frames, _, ch = pieces[0].shape
    return pl.pallas_call(
        functools.partial(place_kernel, members, sizes),
        in_specs=[vspec()] * len(pieces),
        out_specs=pl.BlockSpec(memory_space=ANY),
        out_shape=jax.ShapeDtypeStruct((frames, members, sum(sizes), ch), BF16),
        scratch_shapes=[pltpu.SemaphoreType.DMA((len(pieces),))],
        compiler_params=params(8),
        cost_estimate=COST,
        name="place",
    )(*pieces)


def halo_rows(video):
    size, row = lax.axis_size("rows"), lax.axis_index("rows")
    band = video.shape[1]
    if size == 2:
        mine = lax.dynamic_slice_in_dim(video, jnp.where(row == 0, band - 1, 0), 1, axis=1)[:, 0]
        other = lax.ppermute(mine, "rows", [(0, 1), (1, 0)])
        return other, other
    up = [(i, i + 1) for i in range(size - 1)]
    down = [(j, i) for i, j in up]
    return lax.ppermute(video[:, -1], "rows", up), lax.ppermute(video[:, 0], "rows", down)


def other_sums(sums):
    if lax.axis_size("rows") == 2:
        return lax.ppermute(sums, "rows", [(0, 1), (1, 0)])
    return lax.psum(sums, "rows") - sums


def after(value, *others):
    return lax.optimization_barrier((value, *others))[0]


def body(video, spatial_weight, norm_gain, norm_shift, temporal_weight):
    frames, band, width, ch = video.shape
    total = lax.axis_size("tm")
    me = lax.axis_index("tm") % (SPAN // frames)
    rows = lax.axis_size("rows")
    members = SPAN // frames
    swaps = [[(i, i ^ k) for i in range(total)] for k in range(members)]
    onward = [(i, i + members) for i in range(total - members)]
    guest_pairs = [(i, i + members - 1) for i in range(1, total - members, 2)]
    guest_swaps = [[(i, i ^ k) for i in range(0, total, 2)] for k in range(members)]

    guest_video = lax.ppermute(video, "tm", guest_pairs)
    above, below = halo_rows(video)
    conv, sums = conv_call(video, spatial_weight)
    conv, sums = edge_call(conv, above, below, spatial_weight, sums)
    count = band * rows * width * (ch // GROUPS)
    packet, *pieces = norm_call(
        conv, sums, other_sums(sums), above, below, norm_gain, norm_shift, count, members, OWN_SIZES
    )
    guest_packet = lax.ppermute(packet, "tm", guest_pairs)

    def swap(four, pairs, waits=None):
        got = [four[0]]
        for k in range(1, members):
            value = four[k] if waits is None else after(four[k], waits[k])
            got.append(lax.ppermute(value, "tm", pairs[k]))
        return got

    def blocks(arrays):
        return [arrays[i : i + members] for i in range(0, len(arrays), members)]

    def forward(value):
        value = after(value, passed[-2]) if len(passed) > 1 else value
        passed.append(lax.ppermute(value, "tm", onward))
        return passed[-1]

    guest_pieces = guest_call(
        guest_video, guest_packet, spatial_weight, norm_gain, norm_shift, count, members, GUEST_SIZES
    )
    passed, own, halos, guest = [], [], [], []
    for four, guest_four in zip(blocks(pieces), blocks(guest_pieces), strict=True):
        own.append(swap(four, swaps, guest[-1] if own else None))
        four = after(own[-1], guest_pieces[0])
        middle = functools.reduce(
            lambda acc, k: jnp.where(me == (2 ^ k), four[k], acc), range(1, members), four[0]
        )
        halos.append(forward(middle))
        guest.append(swap(guest_four, guest_swaps, own[-1] if guest else None))
    results, first = [], 0
    for size in OUT_SIZES:
        u2 = early_call(own, halos, guest, temporal_weight, first, size)
        late = late_call(u2, forward(u2), temporal_weight, members)
        results.append(swap(late, swaps, results[-1] if results else None))
        first += size
    out = place_call(sum(results, []), members, OUT_SIZES)
    return out.reshape(frames, band, width, ch)


def solution(mesh):
    return jax.shard_map(
        body,
        mesh=mesh,
        in_specs=(P("tm", "rows", None, None), P(), P(), P(), P()),
        out_specs=P("tm", "rows", None, None),
        check_vma=False,
    )
```

time: 154 us -> 130 us (0.84)
  waiting for transfers between devices: 58.7 us -> 33.6 us
  starting transfers between devices: 62.3 us -> 76 us
  local copies, waits for them, and re-layouts: 9.71 us -> 1.01 us
  Pallas kernels: 21.4 us -> 18.6 us
    ppermute x34 -> x32, waiting for transfers between devices: 58.7 us -> 31.8 us  [the longest x6 17.2 us: forward(): passed.append(lax.ppermute(value, 'tm', onward))]
    ppermute x34 -> x32, starting transfers between devices: 57 us -> 71 us  [the longest x24 36.1 us: swap(): got.append(lax.ppermute(value, 'tm', pairs[k]))]
    unnamed x24 -> x16, local copies, waits for them, and re-layouts: 6.64 us -> 0.04 us
    pallas_call x14 -> x12, Pallas kernels: 20 us -> 17.2 us  [the longest x1 4.86 us: conv_call(): pl.pallas_call(functools.partial(conv_kernel, band), grid=(frames,), in_s...]
    ppermute x1, waiting for transfers between devices: 0.01 us -> 1.84 us  [other_sums(): return lax.ppermute(sums, 'rows', [(0, 1), (1, 0)])]
    ppermute x2 -> x1, starting transfers between devices: 3.54 us -> 3.03 us  [halo_rows(): other = lax.ppermute(mine, 'rows', [(0, 1), (1, 0)])]
  transfers between devices with their start and end apart: 37 -> 34, of which waited for: 11 -> 13; matrix products, arithmetic and copies ran while one was open for 2% -> 1% of each run, Pallas kernels for 12% -> 13%
where the time goes in v3:
time: 130 us
  starting transfers between devices  76 us (58%)
  waiting for transfers between devices  33.6 us (26%)
  Pallas kernels  18.6 us (14%)
    ppermute x24, starting transfers between devices, swap(): got.append(lax.ppermute(value, 'tm', pairs[k]))  36.1 us
    ppermute x6, starting transfers between devices, forward(): passed.append(lax.ppermute(value, 'tm', onward))  33.3 us
    ppermute x6, waiting for transfers between devices, forward(): passed.append(lax.ppermute(value, 'tm', onward))  17.2 us
    ppermute x24, waiting for transfers between devices, swap(): got.append(lax.ppermute(value, 'tm', pairs[k]))  14.6 us
    pallas_call x1, Pallas kernels, conv_call(): pl.pallas_call(functools.partial(conv_kernel, band), grid=(frames,), in_s...  4.86 us
    pallas_call x4, Pallas kernels, early_call(): pl.pallas_call(functools.partial(early_kernel, members, spans, size), in_...  3.76 us
    ppermute x1, starting transfers between devices, halo_rows(): other = lax.ppermute(mine, 'rows', [(0, 1), (1, 0)])  3.03 us
    pallas_call x1, Pallas kernels, norm_call(): pl.pallas_call(functools.partial(norm_kernel, count, members, sizes), in_...  2.8 us
  transfers between devices with their start and end apart: 34, of which 13 were waited for; matrix products, arithmetic and copies ran while one was open for 1% of the time, Pallas kernels for 13%

profile of v3, /device:TPU:0, one launch (start us, length us, event | category | flops | bytes accessed | tf_op | source)
XLA Modules:
  0.0 129.7 jit_solution(189091715992991366)
XLA Ops:
  0.0 0.8 collective-permute-start.5
  0.8 1.0 dynamic-slice_bitcast_fusion
  1.8 3.0 %collective-permute-start = (bf16[2,480,128]{2,1,0:T(8,128)(2,1)S(1)}, bf16[2,480,128]{2,1,0:T(8,128)(2,1)S(1)}, u32[]{:S(2)}, u32[]{:S(2)}) collective-permute-start(bf16[2,480,128]{2,1,0:T(8,128)(2,1)S(1)} %dynamic-slice_bitcast_fusion), channel_id=1, source_target_pairs={{0,1},{1,0},{2,3},{3,2},{4,5},{5,4},{6,7},{7,6},{8,9},{9,8},{10,11... | collective-permute-start | bytes 737288 | tf_op jit(solution)/shard_map/ppermute | solution.py:521
  4.8 4.9 %conv.1 = (f32[2,8,480,128]{3,2,1,0:T(8,128)S(1)}, f32[2,2,8,128]{3,2,1,0:T(8,128)S(1)}) custom-call(bf16[2,8,480,128]{3,2,1,0:T(8,128)(2,1)} %video_ref.1, bf16[3,3,128,128]{3,2,1,0:T(8,128)(2,1)} %weight_ref.9), custom_call_target="tpu_custom_call" | custom-call | flops 20000000000 | tf_op jit(solution)/shard_map/conv/pallas_call | solution.py:117
  9.7 2.1 %edge.1 = (f32[2,8,480,128]{3,2,1,0:T(8,128)S(1)}, f32[2,2,8,128]{3,2,1,0:T(8,128)S(1)}) custom-call(f32[2,8,480,128]{3,2,1,0:T(8,128)S(1)} %get-tuple-element.69.conv_ref, bf16[2,480,128]{2,1,0:T(8,128)(2,1)S(1)} %collective-permute-done.above_ref.below_ref, ...), custom_call_target="tpu_custom_call", output_to_operand_aliasing={{0}: (0, {})} | custom-call | tf_op jit(solution)/shard_map/edge/pallas_call | solution.py:165
  11.8 2.0 %collective-permute-start.1 = (f32[2,2,8,128]{3,2,1,0:T(8,128)S(1)}, f32[2,2,8,128]{3,2,1,0:T(8,128)S(1)}, u32[]{:S(2)}, u32[]{:S(2)}) collective-permute-start(f32[2,2,8,128]{3,2,1,0:T(8,128)S(1)} %get-tuple-element.72.own_ref), channel_id=1, source_target_pairs={{0,1},{1,0},{2,3},{3,2},{4,5},{5,4},{6,7},{7,6},{8,9},{9,8},{10,11... | collective-permute-start | bytes 49160 | tf_op jit(solution)/shard_map/ppermute | solution.py:530
  13.8 1.8 %collective-permute-done.1.other_ref = f32[2,2,8,128]{3,2,1,0:T(8,128)S(1)} collective-permute-done((f32[2,2,8,128]{3,2,1,0:T(8,128)S(1)}, f32[2,2,8,128]{3,2,1,0:T(8,128)S(1)}, u32[]{:S(2)}, u32[]{:S(2)}) %collective-permute-start.1) | collective-permute-done | bytes 16416 | tf_op jit(solution)/shard_map/ppermute | solution.py:530
  15.6 2.8 %norm.1 = (bf16[2,1056,128]{2,1,0:T(8,128)(2,1)S(1)}, bf16[2,480,128]{2,1,0:T(8,128)(2,1)}, bf16[2,480,128]{2,1,0:T(8,128)(2,1)}, bf16[2,480,128]{2,1,0:T(8,128)...) custom-call(f32[2,8,480,128]{3,2,1,0:T(8,128)S(1)} %get-tuple-elemen, ...), custom_call_target="tpu_custom_call" | custom-call | tf_op jit(solution)/shard_map/norm/pallas_call | solution.py:272
  18.4 0.7 collective-permute-start.6
  19.1 4.4 %collective-permute-start.2 = (bf16[2,480,128]{2,1,0:T(8,128)(2,1)}, bf16[2,480,128]{2,1,0:T(8,128)(2,1)S(1)}, u32[]{:S(2)}, u32[]{:S(2)}) collective-permute-start(bf16[2,480,128]{2,1,0:T(8,128)(2,1)} %get-tuple-element.74), channel_id=1, source_target_pairs={{0,2},{2,0},{4,6},{6,4},{8,10},{10,8},{12,14},{14,12},{16,18},{18,... | collective-permute-start | bytes 737288 | tf_op jit(solution)/shard_map/ppermute | solution.py:563
  23.5 1.5 %collective-permute-start.3 = (bf16[2,480,128]{2,1,0:T(8,128)(2,1)}, bf16[2,480,128]{2,1,0:T(8,128)(2,1)S(1)}, u32[]{:S(2)}, u32[]{:S(2)}) collective-permute-start(bf16[2,480,128]{2,1,0:T(8,128)(2,1)} %get-tuple-element.75), channel_id=1, source_target_pairs={{0,4},{2,6},{4,0},{6,2},{8,12},{10,14},{12,8},{14,10},{16,20},{18,... | collective-permute-start | bytes 737288 | tf_op jit(solution)/shard_map/ppermute | solution.py:563
  25.1 1.7 %guest.1 = (bf16[2,320,128]{2,1,0:T(8,128)(2,1)}, bf16[2,320,128]{2,1,0:T(8,128)(2,1)}, bf16[2,320,128]{2,1,0:T(8,128)(2,1)}, bf16[2,320,128]{2,1,0:T(8,128)(2,1...) custom-call(bf16[2,8,480,128]{3,2,1,0:T(8,128)(2,1)S(1)} %collective, ...), custom_call_target="tpu_custom_call" | custom-call | flops 20000000000 | tf_op jit(solution)/shard_map/guest/pallas_call | solution.py:341
  26.8 10.7 %collective-permute-start.10 = (bf16[2,320,128]{2,1,0:T(8,128)(2,1)}, bf16[2,320,128]{2,1,0:T(8,128)(2,1)S(1)}, u32[]{:S(2)}, u32[]{:S(2)}) collective-permute-start(bf16[2,320,128]{2,1,0:T(8,128)(2,1)} %get-tuple-element.85), channel_id=1, source_target_pairs={{0,6},{4,2},{8,14},{12,10},{16,22},{20,18},{24,30},{28,26},{1,7},{... | collective-permute-start | bytes 491528 | tf_op jit(solution)/shard_map/ppermute | solution.py:563
  37.5 2.4 %collective-permute-start.9 = (bf16[2,320,128]{2,1,0:T(8,128)(2,1)}, bf16[2,320,128]{2,1,0:T(8,128)(2,1)S(1)}, u32[]{:S(2)}, u32[]{:S(2)}) collective-permute-start(bf16[2,320,128]{2,1,0:T(8,128)(2,1)} %get-tuple-element.84), channel_id=1, source_target_pairs={{0,4},{4,0},{8,12},{12,8},{16,20},{20,16},{24,28},{28,24},{1,5},{5... | collective-permute-start | bytes 491528 | tf_op jit(solution)/shard_map/ppermute | solution.py:563
  39.9 1.3 %collective-permute-start.8 = (bf16[2,320,128]{2,1,0:T(8,128)(2,1)}, bf16[2,320,128]{2,1,0:T(8,128)(2,1)S(1)}, u32[]{:S(2)}, u32[]{:S(2)}) collective-permute-start(bf16[2,320,128]{2,1,0:T(8,128)(2,1)} %get-tuple-element.83), channel_id=1, source_target_pairs={{0,2},{4,6},{8,10},{12,14},{16,18},{20,22},{24,26},{28,30},{1,3},{... | collective-permute-start | bytes 491528 | tf_op jit(solution)/shard_map/ppermute | solution.py:563
  41.3 1.1 collective-permute-start.17
  42.4 2.8 %collective-permute-done.9.refs_7_ = bf16[2,320,128]{2,1,0:T(8,128)(2,1)S(1)} collective-permute-done((bf16[2,320,128]{2,1,0:T(8,128)(2,1)}, bf16[2,320,128]{2,1,0:T(8,128)(2,1)S(1)}, u32[]{:S(2)}, u32[]{:S(2)}) %collective-permute-start.9) | collective-permute-done | bytes 163872 | tf_op jit(solution)/shard_map/ppermute | solution.py:563
  45.5 8.5 %collective-permute-start.7 = (bf16[2,480,128]{2,1,0:T(8,128)(2,1)S(1)}, bf16[2,480,128]{2,1,0:T(8,128)(2,1)S(1)}, u32[]{:S(2)}, u32[]{:S(2)}) collective-permute-start(bf16[2,480,128]{2,1,0:T(8,128)(2,1)S(1)} %select_select_fusion.1), channel_id=1, source_target_pairs={{0,8},{2,10},{4,12},{6,14},{8,16},{10,18},{12,20},{14,22},{16,24},... | collective-permute-start | bytes 737288 | tf_op jit(solution)/shard_map/ppermute | solution.py:571
  54.0 1.4 %collective-permute-done.16.refs_6_.refs_2_ = bf16[2,480,128]{2,1,0:T(8,128)(2,1)S(1)} collective-permute-done((bf16[2,480,128]{2,1,0:T(8,128)(2,1)}, bf16[2,480,128]{2,1,0:T(8,128)(2,1)S(1)}, u32[]{:S(2)}, u32[]{:S(2)}) %collective-permute-start.16) | collective-permute-done | bytes 245792 | tf_op jit(solution)/shard_map/ppermute | solution.py:563
  55.4 2.7 %collective-permute-start.21 = (bf16[2,640,128]{2,1,0:T(8,128)(2,1)}, bf16[2,640,128]{2,1,0:T(8,128)(2,1)S(1)}, u32[]{:S(2)}, u32[]{:S(2)}) collective-permute-start(bf16[2,640,128]{2,1,0:T(8,128)(2,1)} %get-tuple-element.108), channel_id=1, source_target_pairs={{0,6},{4,2},{8,14},{12,10},{16,22},{20,18},{24,30},{28,26},{1,7},{... | collective-permute-start | bytes 983048 | tf_op jit(solution)/shard_map/ppermute | solution.py:563
  58.1 2.6 %collective-permute-start.20 = (bf16[2,640,128]{2,1,0:T(8,128)(2,1)}, bf16[2,640,128]{2,1,0:T(8,128)(2,1)S(1)}, u32[]{:S(2)}, u32[]{:S(2)}) collective-permute-start(bf16[2,640,128]{2,1,0:T(8,128)(2,1)} %get-tuple-element.106), channel_id=1, source_target_pairs={{0,4},{4,0},{8,12},{12,8},{16,20},{20,16},{24,28},{28,24},{1,5},{5... | collective-permute-start | bytes 983048 | tf_op jit(solution)/shard_map/ppermute | solution.py:563
  60.7 1.4 %collective-permute-start.19 = (bf16[2,640,128]{2,1,0:T(8,128)(2,1)}, bf16[2,640,128]{2,1,0:T(8,128)(2,1)S(1)}, u32[]{:S(2)}, u32[]{:S(2)}) collective-permute-start(bf16[2,640,128]{2,1,0:T(8,128)(2,1)} %get-tuple-element.104), channel_id=1, source_target_pairs={{0,2},{4,6},{8,10},{12,14},{16,18},{20,22},{24,26},{28,30},{1,3},{... | collective-permute-start | bytes 983048 | tf_op jit(solution)/shard_map/ppermute | solution.py:563
  62.2 8.1 %collective-permute-start.18 = (bf16[2,480,128]{2,1,0:T(8,128)(2,1)S(1)}, bf16[2,480,128]{2,1,0:T(8,128)(2,1)S(1)}, u32[]{:S(2)}, u32[]{:S(2)}) collective-permute-start(bf16[2,480,128]{2,1,0:T(8,128)(2,1)S(1)} %select_select_fusion), channel_id=1, source_target_pairs={{0,8},{2,10},{4,12},{6,14},{8,16},{10,18},{12,20},{14,22},{16,24},... | collective-permute-start | bytes 737288 | tf_op jit(solution)/shard_map/ppermute | solution.py:571
  70.4 1.2 early.4.own_ref
  71.5 3.5 %collective-permute-start.11 = (bf16[8,320,128]{2,1,0:T(8,128)(2,1)S(1)}, bf16[8,320,128]{2,1,0:T(8,128)(2,1)S(1)}, u32[]{:S(2)}, u32[]{:S(2)}) collective-permute-start(bf16[8,320,128]{2,1,0:T(8,128)(2,1)S(1)} %early.4.own_ref), channel_id=1, source_target_pairs={{0,8},{2,10},{4,12},{6,14},{8,16},{10,18},{12,20},{14,22},{16,24},... | collective-permute-start | bytes 1966088 | tf_op jit(solution)/shard_map/ppermute | solution.py:571
  75.0 1.6 %collective-permute-done.18.refs_9_.refs_4_ = bf16[2,480,128]{2,1,0:T(8,128)(2,1)S(1)} collective-permute-done((bf16[2,480,128]{2,1,0:T(8,128)(2,1)S(1)}, bf16[2,480,128]{2,1,0:T(8,128)(2,1)S(1)}, u32[]{:S(2)}, u32[]{:S(2)}) %collective-permute-start.18) | collective-permute-done | bytes 245792 | tf_op jit(solution)/shard_map/ppermute | solution.py:571
  76.7 1.2 early.5.own_ref
  77.8 4.4 %collective-permute-start.22 = (bf16[8,320,128]{2,1,0:T(8,128)(2,1)S(1)}, bf16[8,320,128]{2,1,0:T(8,128)(2,1)S(1)}, u32[]{:S(2)}, u32[]{:S(2)}) collective-permute-start(bf16[8,320,128]{2,1,0:T(8,128)(2,1)S(1)} %early.5.own_ref), channel_id=1, source_target_pairs={{0,8},{2,10},{4,12},{6,14},{8,16},{10,18},{12,20},{14,22},{16,24},... | collective-permute-start | bytes 1966088 | tf_op jit(solution)/shard_map/ppermute | solution.py:571
  82.3 0.8 early.6.own_ref
  83.1 7.6 %collective-permute-done.11.halo_ref = bf16[8,320,128]{2,1,0:T(8,128)(2,1)S(1)} collective-permute-done((bf16[8,320,128]{2,1,0:T(8,128)(2,1)S(1)}, bf16[8,320,128]{2,1,0:T(8,128)(2,1)S(1)}, u32[]{:S(2)}, u32[]{:S(2)}) %collective-permute-start.11) | collective-permute-done | bytes 655392 | tf_op jit(solution)/shard_map/ppermute | solution.py:571
  90.7 4.4 %collective-permute-start.26 = (bf16[8,192,128]{2,1,0:T(8,128)(2,1)S(1)}, bf16[8,192,128]{2,1,0:T(8,128)(2,1)S(1)}, u32[]{:S(2)}, u32[]{:S(2)}) collective-permute-start(bf16[8,192,128]{2,1,0:T(8,128)(2,1)S(1)} %early.6.own_ref), channel_id=1, source_target_pairs={{0,8},{2,10},{4,12},{6,14},{8,16},{10,18},{12,20},{14,22},{16,24},... | collective-permute-start | bytes 1179656 | tf_op jit(solution)/shard_map/ppermute | solution.py:571
  95.8 0.8 collective-permute-start.13
  96.5 1.1 collective-permute-start.12
  97.6 0.6 early.7.own_ref
  98.2 6.5 %collective-permute-done.22.halo_ref = bf16[8,320,128]{2,1,0:T(8,128)(2,1)S(1)} collective-permute-done((bf16[8,320,128]{2,1,0:T(8,128)(2,1)S(1)}, bf16[8,320,128]{2,1,0:T(8,128)(2,1)S(1)}, u32[]{:S(2)}, u32[]{:S(2)}) %collective-permute-start.22) | collective-permute-done | bytes 655392 | tf_op jit(solution)/shard_map/ppermute | solution.py:571
  104.7 4.4 %collective-permute-start.30 = (bf16[8,128,128]{2,1,0:T(8,128)(2,1)S(1)}, bf16[8,128,128]{2,1,0:T(8,128)(2,1)S(1)}, u32[]{:S(2)}, u32[]{:S(2)}) collective-permute-start(bf16[8,128,128]{2,1,0:T(8,128)(2,1)S(1)} %early.7.own_ref), channel_id=1, source_target_pairs={{0,8},{2,10},{4,12},{6,14},{8,16},{10,18},{12,20},{14,22},{16,24},... | collective-permute-start | bytes 786440 | tf_op jit(solution)/shard_map/ppermute | solution.py:571
  109.1 0.6 late.5
  109.8 0.8 collective-permute-start.24
  110.6 1.1 collective-permute-start.23
  111.7 1.5 %collective-permute-done.26.halo_ref = bf16[8,192,128]{2,1,0:T(8,128)(2,1)S(1)} collective-permute-done((bf16[8,192,128]{2,1,0:T(8,128)(2,1)S(1)}, bf16[8,192,128]{2,1,0:T(8,128)(2,1)S(1)}, u32[]{:S(2)}, u32[]{:S(2)}) %collective-permute-start.26) | collective-permute-done | bytes 393248 | tf_op jit(solution)/shard_map/ppermute | solution.py:571
  113.6 2.7 %collective-permute-done.25.refs_7_ = bf16[2,320,128]{2,1,0:T(8,128)(2,1)S(1)} collective-permute-done((bf16[2,320,128]{2,1,0:T(8,128)(2,1)S(1)}, bf16[2,320,128]{2,1,0:T(8,128)(2,1)S(1)}, u32[]{:S(2)}, u32[]{:S(2)}) %collective-permute-start.25) | collective-permute-done | bytes 163872 | tf_op jit(solution)/shard_map/ppermute | solution.py:563
  116.4 1.9 %collective-permute-done.24.refs_6_ = bf16[2,320,128]{2,1,0:T(8,128)(2,1)S(1)} collective-permute-done((bf16[2,320,128]{2,1,0:T(8,128)(2,1)S(1)}, bf16[2,320,128]{2,1,0:T(8,128)(2,1)S(1)}, u32[]{:S(2)}, u32[]{:S(2)}) %collective-permute-start.24) | collective-permute-done | bytes 163872 | tf_op jit(solution)/shard_map/ppermute | solution.py:563
  118.4 1.9 %collective-permute-start.28 = (bf16[2,192,128]{2,1,0:T(8,128)(2,1)S(1)}, bf16[2,192,128]{2,1,0:T(8,128)(2,1)S(1)}, u32[]{:S(2)}, u32[]{:S(2)}) collective-permute-start(bf16[2,192,128]{2,1,0:T(8,128)(2,1)S(1)} %get-tuple-element.122), channel_id=1, source_target_pairs={{0,4},{2,6},{4,0},{6,2},{8,12},{10,14},{12,8},{14,10},{16,20},{18,... | collective-permute-start | bytes 294920 | tf_op jit(solution)/shard_map/ppermute | solution.py:563
  121.2 0.9 collective-permute-start.33
  122.1 2.0 %collective-permute-done.28.refs_10_ = bf16[2,192,128]{2,1,0:T(8,128)(2,1)S(1)} collective-permute-done((bf16[2,192,128]{2,1,0:T(8,128)(2,1)S(1)}, bf16[2,192,128]{2,1,0:T(8,128)(2,1)S(1)}, u32[]{:S(2)}, u32[]{:S(2)}) %collective-permute-start.28) | collective-permute-done | bytes 98336 | tf_op jit(solution)/shard_map/ppermute | solution.py:563
  124.0 1.0 collective-permute-start.32
  125.4 2.9 %collective-permute-done.32.refs_14_ = bf16[2,128,128]{2,1,0:T(8,128)(2,1)S(1)} collective-permute-done((bf16[2,128,128]{2,1,0:T(8,128)(2,1)S(1)}, bf16[2,128,128]{2,1,0:T(8,128)(2,1)S(1)}, u32[]{:S(2)}, u32[]{:S(2)}) %collective-permute-start.32) | collective-permute-done | bytes 65568 | tf_op jit(solution)/shard_map/ppermute | solution.py:563
  128.3 1.4 %place.1 = bf16[2,4,960,128]{3,2,1,0:T(8,128)(2,1)} custom-call(bf16[2,320,128]{2,1,0:T(8,128)(2,1)S(1)} %get-tuple-element.87.refs_0_, bf16[2,320,128]{2,1,0:T(8,128)(2,1)S(1)} %collective-permute-done.12.refs_1_, bf16[2,320,128]{2,1,0:T(8,128)(2,1)S(1)} %collective-permute-done.13.refs_2_, bf16[2,320,128]{2,1,0:T(8,128)(2,1)S(1)} %collective-permute-done.14.refs_3_, ...), custom_call_target="tpu_custom_call" | custom-call | tf_op jit(solution)/shard_map/place/pallas_call | solution.py:504
  (52 shorter events, 3.0 us)
Async XLA Ops:
  0.0 25.0 %collective-permute-start.5 = (bf16[2,8,480,128]{3,2,1,0:T(8,128)(2,1)}, bf16[2,8,480,128]{3,2,1,0:T(8,128)(2,1)S(1)}, u32[]{:S(2)}, u32[]{:S(2)}) collective-permute-start(bf16[2,8,480,128]{3,2,1,0:T(8,128)(2,1)} %video_ref.1), channel_id=1, source_target_pairs={{2,8},{6,12},{10,16},{14,20},{18,24},{22,28},{3,9},{7,13},{11,17},... | collective-permute-start | bytes 5898248 | tf_op jit(solution)/shard_map/ppermute | solution.py:549
  1.8 7.9 %collective-permute-start = (bf16[2,480,128]{2,1,0:T(8,128)(2,1)S(1)}, bf16[2,480,128]{2,1,0:T(8,128)(2,1)S(1)}, u32[]{:S(2)}, u32[]{:S(2)}) collective-permute-start(bf16[2,480,128]{2,1,0:T(8,128)(2,1)S(1)} %dynamic-slice_bitcast_fusion), channel_id=1, source_target_pairs={{0,1},{1,0},{2,3},{3,2},{4,5},{5,4},{6,7},{7,6},{8,9},{9,8},{10,11... | collective-permute-start | bytes 737288 | tf_op jit(solution)/shard_map/ppermute | solution.py:521
  9.7 6.0 %copy-start.6 = (f32[128]{0:T(128)S(1)}, f32[128]{0:T(128)}, u32[]{:S(2)}) copy-start(f32[128]{0:T(128)} %param.7) | copy-start | bytes 1540
  9.7 5.9 %copy-start.7 = (f32[128]{0:T(128)S(1)}, f32[128]{0:T(128)}, u32[]{:S(2)}) copy-start(f32[128]{0:T(128)} %param.8) | copy-start | bytes 1540
  11.8 3.8 %collective-permute-start.1 = (f32[2,2,8,128]{3,2,1,0:T(8,128)S(1)}, f32[2,2,8,128]{3,2,1,0:T(8,128)S(1)}, u32[]{:S(2)}, u32[]{:S(2)}) collective-permute-start(f32[2,2,8,128]{3,2,1,0:T(8,128)S(1)} %get-tuple-element.72.own_ref), channel_id=1, source_target_pairs={{0,1},{1,0},{2,3},{3,2},{4,5},{5,4},{6,7},{7,6},{8,9},{9,8},{10,11... | collective-permute-start | bytes 49160 | tf_op jit(solution)/shard_map/ppermute | solution.py:530
  15.6 9.4 %copy-start.4 = (bf16[3,3,128,128]{3,2,1,0:T(8,128)(2,1)S(1)}, bf16[3,3,128,128]{3,2,1,0:T(8,128)(2,1)}, u32[]{:S(2)}) copy-start(bf16[3,3,128,128]{3,2,1,0:T(8,128)(2,1)} %weight_ref.9) | copy-start | bytes 884740
  18.4 6.6 %collective-permute-start.6 = (bf16[2,1056,128]{2,1,0:T(8,128)(2,1)S(1)}, bf16[2,1056,128]{2,1,0:T(8,128)(2,1)S(1)}, u32[]{:S(2)}, u32[]{:S(2)}) collective-permute-start(bf16[2,1056,128]{2,1,0:T(8,128)(2,1)S(1)} %get-tuple-element.77), channel_id=1, source_target_pairs={{2,8},{6,12},{10,16},{14,20},{18,24},{22,28},{3,9},{7,13},{11,17},... | collective-permute-start | bytes 1622024 | tf_op jit(solution)/shard_map/ppermute | solution.py:557
  19.1 20.8 %collective-permute-start.2 = (bf16[2,480,128]{2,1,0:T(8,128)(2,1)}, bf16[2,480,128]{2,1,0:T(8,128)(2,1)S(1)}, u32[]{:S(2)}, u32[]{:S(2)}) collective-permute-start(bf16[2,480,128]{2,1,0:T(8,128)(2,1)} %get-tuple-element.74), channel_id=1, source_target_pairs={{0,2},{2,0},{4,6},{6,4},{8,10},{10,8},{12,14},{14,12},{16,18},{18,... | collective-permute-start | bytes 737288 | tf_op jit(solution)/shard_map/ppermute | solution.py:563
  23.5 17.7 %collective-permute-start.3 = (bf16[2,480,128]{2,1,0:T(8,128)(2,1)}, bf16[2,480,128]{2,1,0:T(8,128)(2,1)S(1)}, u32[]{:S(2)}, u32[]{:S(2)}) collective-permute-start(bf16[2,480,128]{2,1,0:T(8,128)(2,1)} %get-tuple-element.75), channel_id=1, source_target_pairs={{0,4},{2,6},{4,0},{6,2},{8,12},{10,14},{12,8},{14,10},{16,20},{18,... | collective-permute-start | bytes 737288 | tf_op jit(solution)/shard_map/ppermute | solution.py:563
  25.0 20.4 %copy-start.3 = (bf16[2,480,128]{2,1,0:T(8,128)(2,1)S(1)}, bf16[2,480,128]{2,1,0:T(8,128)(2,1)}, u32[]{:S(2)}) copy-start(bf16[2,480,128]{2,1,0:T(8,128)(2,1)} %get-tuple-element.82.refs_0_) | copy-start | bytes 737284
  25.0 37.1 %copy-start.1 = (bf16[2,480,128]{2,1,0:T(8,128)(2,1)S(1)}, bf16[2,480,128]{2,1,0:T(8,128)(2,1)}, u32[]{:S(2)}) copy-start(bf16[2,480,128]{2,1,0:T(8,128)(2,1)} %get-tuple-element.101.refs_4_.refs_0_) | copy-start | bytes 737284
  25.0 16.2 %collective-permute-start.4 = (bf16[2,480,128]{2,1,0:T(8,128)(2,1)}, bf16[2,480,128]{2,1,0:T(8,128)(2,1)S(1)}, u32[]{:S(2)}, u32[]{:S(2)}) collective-permute-start(bf16[2,480,128]{2,1,0:T(8,128)(2,1)} %get-tuple-element.76), channel_id=1, source_target_pairs={{0,6},{2,4},{4,2},{6,0},{8,14},{10,12},{12,10},{14,8},{16,22},{18,... | collective-permute-start | bytes 737288 | tf_op jit(solution)/shard_map/ppermute | solution.py:563
  26.8 43.6 %copy-start = (bf16[3,3,128,128]{3,2,1,0:T(8,128)(2,1)S(1)}, bf16[3,3,128,128]{3,2,1,0:T(8,128)(2,1)}, u32[]{:S(2)}) copy-start(bf16[3,3,128,128]{3,2,1,0:T(8,128)(2,1)} %weight_ref.13) | copy-start | bytes 884740
  26.8 43.6 %copy-start.5 = (bf16[2,320,128]{2,1,0:T(8,128)(2,1)S(1)}, bf16[2,320,128]{2,1,0:T(8,128)(2,1)}, u32[]{:S(2)}) copy-start(bf16[2,320,128]{2,1,0:T(8,128)(2,1)} %get-tuple-element.78.refs_5_) | copy-start | bytes 491524
  26.8 14.5 %collective-permute-start.10 = (bf16[2,320,128]{2,1,0:T(8,128)(2,1)}, bf16[2,320,128]{2,1,0:T(8,128)(2,1)S(1)}, u32[]{:S(2)}, u32[]{:S(2)}) collective-permute-start(bf16[2,320,128]{2,1,0:T(8,128)(2,1)} %get-tuple-element.85), channel_id=1, source_target_pairs={{0,6},{4,2},{8,14},{12,10},{16,22},{20,18},{24,30},{28,26},{1,7},{... | collective-permute-start | bytes 491528 | tf_op jit(solution)/shard_map/ppermute | solution.py:563
  37.5 7.7 %collective-permute-start.9 = (bf16[2,320,128]{2,1,0:T(8,128)(2,1)}, bf16[2,320,128]{2,1,0:T(8,128)(2,1)S(1)}, u32[]{:S(2)}, u32[]{:S(2)}) collective-permute-start(bf16[2,320,128]{2,1,0:T(8,128)(2,1)} %get-tuple-element.84), channel_id=1, source_target_pairs={{0,4},{4,0},{8,12},{12,8},{16,20},{20,16},{24,28},{28,24},{1,5},{5... | collective-permute-start | bytes 491528 | tf_op jit(solution)/shard_map/ppermute | solution.py:563
  39.9 5.5 %collective-permute-start.8 = (bf16[2,320,128]{2,1,0:T(8,128)(2,1)}, bf16[2,320,128]{2,1,0:T(8,128)(2,1)S(1)}, u32[]{:S(2)}, u32[]{:S(2)}) collective-permute-start(bf16[2,320,128]{2,1,0:T(8,128)(2,1)} %get-tuple-element.83), channel_id=1, source_target_pairs={{0,2},{4,6},{8,10},{12,14},{16,18},{20,22},{24,26},{28,30},{1,3},{... | collective-permute-start | bytes 491528 | tf_op jit(solution)/shard_map/ppermute | solution.py:563
  41.3 12.8 %collective-permute-start.17 = (bf16[2,480,128]{2,1,0:T(8,128)(2,1)}, bf16[2,480,128]{2,1,0:T(8,128)(2,1)S(1)}, u32[]{:S(2)}, u32[]{:S(2)}) collective-permute-start(bf16[2,480,128]{2,1,0:T(8,128)(2,1)} %get-tuple-element.97), channel_id=1, source_target_pairs={{0,6},{2,4},{4,2},{6,0},{8,14},{10,12},{12,10},{14,8},{16,22},{18,... | collective-permute-start | bytes 737288 | tf_op jit(solution)/shard_map/ppermute | solution.py:563
  45.2 10.2 %collective-permute-start.16 = (bf16[2,480,128]{2,1,0:T(8,128)(2,1)}, bf16[2,480,128]{2,1,0:T(8,128)(2,1)S(1)}, u32[]{:S(2)}, u32[]{:S(2)}) collective-permute-start(bf16[2,480,128]{2,1,0:T(8,128)(2,1)} %get-tuple-element.95), channel_id=1, source_target_pairs={{0,4},{2,6},{4,0},{6,2},{8,12},{10,14},{12,8},{14,10},{16,20},{18,... | collective-permute-start | bytes 737288 | tf_op jit(solution)/shard_map/ppermute | solution.py:563
  45.4 10.0 %collective-permute-start.15 = (bf16[2,480,128]{2,1,0:T(8,128)(2,1)}, bf16[2,480,128]{2,1,0:T(8,128)(2,1)S(1)}, u32[]{:S(2)}, u32[]{:S(2)}) collective-permute-start(bf16[2,480,128]{2,1,0:T(8,128)(2,1)} %get-tuple-element.93), channel_id=1, source_target_pairs={{0,2},{2,0},{4,6},{6,4},{8,10},{10,8},{12,14},{14,12},{16,18},{18,... | collective-permute-start | bytes 737288 | tf_op jit(solution)/shard_map/ppermute | solution.py:563
  45.5 24.8 %collective-permute-start.7 = (bf16[2,480,128]{2,1,0:T(8,128)(2,1)S(1)}, bf16[2,480,128]{2,1,0:T(8,128)(2,1)S(1)}, u32[]{:S(2)}, u32[]{:S(2)}) collective-permute-start(bf16[2,480,128]{2,1,0:T(8,128)(2,1)S(1)} %select_select_fusion.1), channel_id=1, source_target_pairs={{0,8},{2,10},{4,12},{6,14},{8,16},{10,18},{12,20},{14,22},{16,24},... | collective-permute-start | bytes 737288 | tf_op jit(solution)/shard_map/ppermute | solution.py:571
  55.4 21.2 %collective-permute-start.21 = (bf16[2,640,128]{2,1,0:T(8,128)(2,1)}, bf16[2,640,128]{2,1,0:T(8,128)(2,1)S(1)}, u32[]{:S(2)}, u32[]{:S(2)}) collective-permute-start(bf16[2,640,128]{2,1,0:T(8,128)(2,1)} %get-tuple-element.108), channel_id=1, source_target_pairs={{0,6},{4,2},{8,14},{12,10},{16,22},{20,18},{24,30},{28,26},{1,7},{... | collective-permute-start | bytes 983048 | tf_op jit(solution)/shard_map/ppermute | solution.py:563
  58.1 18.6 %collective-permute-start.20 = (bf16[2,640,128]{2,1,0:T(8,128)(2,1)}, bf16[2,640,128]{2,1,0:T(8,128)(2,1)S(1)}, u32[]{:S(2)}, u32[]{:S(2)}) collective-permute-start(bf16[2,640,128]{2,1,0:T(8,128)(2,1)} %get-tuple-element.106), channel_id=1, source_target_pairs={{0,4},{4,0},{8,12},{12,8},{16,20},{20,16},{24,28},{28,24},{1,5},{5... | collective-permute-start | bytes 983048 | tf_op jit(solution)/shard_map/ppermute | solution.py:563
  60.7 15.9 %copy-start.2 = (bf16[2,640,128]{2,1,0:T(8,128)(2,1)S(1)}, bf16[2,640,128]{2,1,0:T(8,128)(2,1)}, u32[]{:S(2)}) copy-start(bf16[2,640,128]{2,1,0:T(8,128)(2,1)} %get-tuple-element.102.refs_10_.refs_5_) | copy-start | bytes 983044
  60.7 15.9 %collective-permute-start.19 = (bf16[2,640,128]{2,1,0:T(8,128)(2,1)}, bf16[2,640,128]{2,1,0:T(8,128)(2,1)S(1)}, u32[]{:S(2)}, u32[]{:S(2)}) collective-permute-start(bf16[2,640,128]{2,1,0:T(8,128)(2,1)} %get-tuple-element.104), channel_id=1, source_target_pairs={{0,2},{4,6},{8,10},{12,14},{16,18},{20,22},{24,26},{28,30},{1,3},{... | collective-permute-start | bytes 983048 | tf_op jit(solution)/shard_map/ppermute | solution.py:563
  62.2 14.4 %collective-permute-start.18 = (bf16[2,480,128]{2,1,0:T(8,128)(2,1)S(1)}, bf16[2,480,128]{2,1,0:T(8,128)(2,1)S(1)}, u32[]{:S(2)}, u32[]{:S(2)}) collective-permute-start(bf16[2,480,128]{2,1,0:T(8,128)(2,1)S(1)} %select_select_fusion), channel_id=1, source_target_pairs={{0,8},{2,10},{4,12},{6,14},{8,16},{10,18},{12,20},{14,22},{16,24},... | collective-permute-start | bytes 737288 | tf_op jit(solution)/shard_map/ppermute | solution.py:571
  71.5 19.2 %collective-permute-start.11 = (bf16[8,320,128]{2,1,0:T(8,128)(2,1)S(1)}, bf16[8,320,128]{2,1,0:T(8,128)(2,1)S(1)}, u32[]{:S(2)}, u32[]{:S(2)}) collective-permute-start(bf16[8,320,128]{2,1,0:T(8,128)(2,1)S(1)} %early.4.own_ref), channel_id=1, source_target_pairs={{0,8},{2,10},{4,12},{6,14},{8,16},{10,18},{12,20},{14,22},{16,24},... | collective-permute-start | bytes 1966088 | tf_op jit(solution)/shard_map/ppermute | solution.py:571
  77.8 26.9 %collective-permute-start.22 = (bf16[8,320,128]{2,1,0:T(8,128)(2,1)S(1)}, bf16[8,320,128]{2,1,0:T(8,128)(2,1)S(1)}, u32[]{:S(2)}, u32[]{:S(2)}) collective-permute-start(bf16[8,320,128]{2,1,0:T(8,128)(2,1)S(1)} %early.5.own_ref), channel_id=1, source_target_pairs={{0,8},{2,10},{4,12},{6,14},{8,16},{10,18},{12,20},{14,22},{16,24},... | collective-permute-start | bytes 1966088 | tf_op jit(solution)/shard_map/ppermute | solution.py:571
  90.7 22.5 %collective-permute-start.26 = (bf16[8,192,128]{2,1,0:T(8,128)(2,1)S(1)}, bf16[8,192,128]{2,1,0:T(8,128)(2,1)S(1)}, u32[]{:S(2)}, u32[]{:S(2)}) collective-permute-start(bf16[8,192,128]{2,1,0:T(8,128)(2,1)S(1)} %early.6.own_ref), channel_id=1, source_target_pairs={{0,8},{2,10},{4,12},{6,14},{8,16},{10,18},{12,20},{14,22},{16,24},... | collective-permute-start | bytes 1179656 | tf_op jit(solution)/shard_map/ppermute | solution.py:571
  95.7 14.0 %collective-permute-start.14 = (bf16[2,320,128]{2,1,0:T(8,128)(2,1)S(1)}, bf16[2,320,128]{2,1,0:T(8,128)(2,1)S(1)}, u32[]{:S(2)}, u32[]{:S(2)}) collective-permute-start(bf16[2,320,128]{2,1,0:T(8,128)(2,1)S(1)} %get-tuple-element.90), channel_id=1, source_target_pairs={{0,6},{2,4},{4,2},{6,0},{8,14},{10,12},{12,10},{14,8},{16,22},{18,... | collective-permute-start | bytes 491528 | tf_op jit(solution)/shard_map/ppermute | solution.py:563
  95.8 14.0 %collective-permute-start.13 = (bf16[2,320,128]{2,1,0:T(8,128)(2,1)S(1)}, bf16[2,320,128]{2,1,0:T(8,128)(2,1)S(1)}, u32[]{:S(2)}, u32[]{:S(2)}) collective-permute-start(bf16[2,320,128]{2,1,0:T(8,128)(2,1)S(1)} %get-tuple-element.89), channel_id=1, source_target_pairs={{0,4},{2,6},{4,0},{6,2},{8,12},{10,14},{12,8},{14,10},{16,20},{18,... | collective-permute-start | bytes 491528 | tf_op jit(solution)/shard_map/ppermute | solution.py:563
  96.5 14.1 %collective-permute-start.12 = (bf16[2,320,128]{2,1,0:T(8,128)(2,1)S(1)}, bf16[2,320,128]{2,1,0:T(8,128)(2,1)S(1)}, u32[]{:S(2)}, u32[]{:S(2)}) collective-permute-start(bf16[2,320,128]{2,1,0:T(8,128)(2,1)S(1)} %get-tuple-element.88), channel_id=1, source_target_pairs={{0,2},{2,0},{4,6},{6,4},{8,10},{10,8},{12,14},{14,12},{16,18},{18,... | collective-permute-start | bytes 491528 | tf_op jit(solution)/shard_map/ppermute | solution.py:563
  104.7 15.5 %collective-permute-start.30 = (bf16[8,128,128]{2,1,0:T(8,128)(2,1)S(1)}, bf16[8,128,128]{2,1,0:T(8,128)(2,1)S(1)}, u32[]{:S(2)}, u32[]{:S(2)}) collective-permute-start(bf16[8,128,128]{2,1,0:T(8,128)(2,1)S(1)} %early.7.own_ref), channel_id=1, source_target_pairs={{0,8},{2,10},{4,12},{6,14},{8,16},{10,18},{12,20},{14,22},{16,24},... | collective-permute-start | bytes 786440 | tf_op jit(solution)/shard_map/ppermute | solution.py:571
  109.7 6.5 %collective-permute-start.25 = (bf16[2,320,128]{2,1,0:T(8,128)(2,1)S(1)}, bf16[2,320,128]{2,1,0:T(8,128)(2,1)S(1)}, u32[]{:S(2)}, u32[]{:S(2)}) collective-permute-start(bf16[2,320,128]{2,1,0:T(8,128)(2,1)S(1)} %get-tuple-element.116), channel_id=1, source_target_pairs={{0,6},{2,4},{4,2},{6,0},{8,14},{10,12},{12,10},{14,8},{16,22},{18,... | collective-permute-start | bytes 491528 | tf_op jit(solution)/shard_map/ppermute | solution.py:563
  109.8 8.6 %collective-permute-start.24 = (bf16[2,320,128]{2,1,0:T(8,128)(2,1)S(1)}, bf16[2,320,128]{2,1,0:T(8,128)(2,1)S(1)}, u32[]{:S(2)}, u32[]{:S(2)}) collective-permute-start(bf16[2,320,128]{2,1,0:T(8,128)(2,1)S(1)} %get-tuple-element.114), channel_id=1, source_target_pairs={{0,4},{2,6},{4,0},{6,2},{8,12},{10,14},{12,8},{14,10},{16,20},{18,... | collective-permute-start | bytes 491528 | tf_op jit(solution)/shard_map/ppermute | solution.py:563
  110.6 9.6 %collective-permute-start.23 = (bf16[2,320,128]{2,1,0:T(8,128)(2,1)S(1)}, bf16[2,320,128]{2,1,0:T(8,128)(2,1)S(1)}, u32[]{:S(2)}, u32[]{:S(2)}) collective-permute-start(bf16[2,320,128]{2,1,0:T(8,128)(2,1)S(1)} %get-tuple-element.112), channel_id=1, source_target_pairs={{0,2},{2,0},{4,6},{6,4},{8,10},{10,8},{12,14},{14,12},{16,18},{18,... | collective-permute-start | bytes 491528 | tf_op jit(solution)/shard_map/ppermute | solution.py:563
  116.2 4.9 %collective-permute-start.29 = (bf16[2,192,128]{2,1,0:T(8,128)(2,1)S(1)}, bf16[2,192,128]{2,1,0:T(8,128)(2,1)S(1)}, u32[]{:S(2)}, u32[]{:S(2)}) collective-permute-start(bf16[2,192,128]{2,1,0:T(8,128)(2,1)S(1)} %get-tuple-element.124), channel_id=1, source_target_pairs={{0,6},{2,4},{4,2},{6,0},{8,14},{10,12},{12,10},{14,8},{16,22},{18,... | collective-permute-start | bytes 294920 | tf_op jit(solution)/shard_map/ppermute | solution.py:563
  118.4 5.7 %collective-permute-start.28 = (bf16[2,192,128]{2,1,0:T(8,128)(2,1)S(1)}, bf16[2,192,128]{2,1,0:T(8,128)(2,1)S(1)}, u32[]{:S(2)}, u32[]{:S(2)}) collective-permute-start(bf16[2,192,128]{2,1,0:T(8,128)(2,1)S(1)} %get-tuple-element.122), channel_id=1, source_target_pairs={{0,4},{2,6},{4,0},{6,2},{8,12},{10,14},{12,8},{14,10},{16,20},{18,... | collective-permute-start | bytes 294920 | tf_op jit(solution)/shard_map/ppermute | solution.py:563
  120.2 4.8 %collective-permute-start.27 = (bf16[2,192,128]{2,1,0:T(8,128)(2,1)S(1)}, bf16[2,192,128]{2,1,0:T(8,128)(2,1)S(1)}, u32[]{:S(2)}, u32[]{:S(2)}) collective-permute-start(bf16[2,192,128]{2,1,0:T(8,128)(2,1)S(1)} %get-tuple-element.120), channel_id=1, source_target_pairs={{0,2},{2,0},{4,6},{6,4},{8,10},{10,8},{12,14},{14,12},{16,18},{18,... | collective-permute-start | bytes 294920 | tf_op jit(solution)/shard_map/ppermute | solution.py:563
  121.2 4.2 %collective-permute-start.33 = (bf16[2,128,128]{2,1,0:T(8,128)(2,1)S(1)}, bf16[2,128,128]{2,1,0:T(8,128)(2,1)S(1)}, u32[]{:S(2)}, u32[]{:S(2)}) collective-permute-start(bf16[2,128,128]{2,1,0:T(8,128)(2,1)S(1)} %get-tuple-element.132), channel_id=1, source_target_pairs={{0,6},{2,4},{4,2},{6,0},{8,14},{10,12},{12,10},{14,8},{16,22},{18,... | collective-permute-start | bytes 196616 | tf_op jit(solution)/shard_map/ppermute | solution.py:563
  124.0 4.3 %collective-permute-start.32 = (bf16[2,128,128]{2,1,0:T(8,128)(2,1)S(1)}, bf16[2,128,128]{2,1,0:T(8,128)(2,1)S(1)}, u32[]{:S(2)}, u32[]{:S(2)}) collective-permute-start(bf16[2,128,128]{2,1,0:T(8,128)(2,1)S(1)} %get-tuple-element.130), channel_id=1, source_target_pairs={{0,4},{2,6},{4,0},{6,2},{8,12},{10,14},{12,8},{14,10},{16,20},{18,... | collective-permute-start | bytes 196616 | tf_op jit(solution)/shard_map/ppermute | solution.py:563
  125.1 3.3 %collective-permute-start.31 = (bf16[2,128,128]{2,1,0:T(8,128)(2,1)S(1)}, bf16[2,128,128]{2,1,0:T(8,128)(2,1)S(1)}, u32[]{:S(2)}, u32[]{:S(2)}) collective-permute-start(bf16[2,128,128]{2,1,0:T(8,128)(2,1)S(1)} %get-tuple-element.128), channel_id=1, source_target_pairs={{0,2},{2,0},{4,6},{6,4},{8,10},{10,8},{12,14},{14,12},{16,18},{18,... | collective-permute-start | bytes 196616 | tf_op jit(solution)/shard_map/ppermute | solution.py:563

commit v4 on v3

--- a/solution.py
+++ b/solution.py
@@ -9,9 +9,8 @@
 
 GROUPS = 32
 SPAN = 8
-OWN_SIZES = (480, 480)
-GUEST_SIZES = (320, 640)
-OUT_SIZES = (320, 320, 192, 128)
+GUEST_PARTS = (26, 34)
+OUT_PARTS = (26, 16, 10, 8)
 VMEM = pltpu.VMEM
 ANY = pl.ANY
 F32 = jnp.float32
@@ -220,74 +219,75 @@
         hidden_ref[frame, row] = v.astype(BF16)
 
 
-def piece_copies(hidden_ref, frame, outs, sizes, members, sem):
+def piece_copies(hidden_ref, frame, outs, members, sem):
     frames, band, width, ch = hidden_ref.shape
     flat = hidden_ref.reshape(frames, band * width, ch)
     me = lax.axis_index("tm") % members
-    copies, offset = [], 0
-    for i, size in enumerate(sizes):
-        for k in range(members):
-            n = i * members + k
-            start = pl.multiple_of((me ^ k) * sum(sizes) + offset, 16)
+    quarter = band * width // members
+    copies = []
+    for k, blocks in enumerate(outs):
+        offset = 0
+        for block in blocks:
+            rows = pl.ds(pl.multiple_of((me ^ k) * quarter + offset, 16), block.shape[1])
             copies.append(
                 pltpu.make_async_copy(
-                    flat.at[frame, pl.ds(start, size)], outs[n].at[frame], sem.at[n, frame]
+                    flat.at[frame, rows], block.at[frame], sem.at[len(copies), frame]
                 )
             )
-        offset += size
+            offset += block.shape[1]
     return copies
 
 
-def norm_kernel(count, members, sizes, conv_ref, own_ref, other_ref, above_ref, below_ref, gain_ref, shift_ref, packet_ref, *refs):
-    outs, (hidden_ref, sem) = refs[:-2], refs[-2:]
+def norm_kernel(count, members, rows, conv_ref, own_ref, other_ref, gain_ref, shift_ref, *refs):
+    row_refs, packet_ref, (hidden_ref, sem) = refs[:rows], refs[rows], refs[-2:]
+    outs = [[ref] for ref in refs[rows + 1 : -2]]
     frames, band, width, ch = conv_ref.shape
     for frame in range(frames):
         sums = [own_ref[frame, i] + other_ref[frame, i] for i in range(2)]
-        packet_ref[frame, :width] = above_ref[frame]
-        packet_ref[frame, width : 2 * width] = below_ref[frame]
+        for i, ref in enumerate(row_refs):
+            packet_ref[frame, i * width : (i + 1) * width] = ref[frame]
         for i in range(2):
             rest = sums[i]
             for part in range(3):
                 short = rest.astype(BF16).astype(F32)
                 rest = rest - short
-                at = 2 * width + (i * 3 + part) * 16
+                at = rows * width + (i * 3 + part) * 16
                 packet_ref[frame, at : at + 16] = jnp.concatenate(
                     [short, jnp.zeros_like(short)], axis=0
                 ).astype(BF16)
         norm_frame(conv_ref, frame, sums, count, gain_ref, shift_ref, hidden_ref)
-        for copy in piece_copies(hidden_ref, frame, outs, sizes, members, sem):
+        for copy in piece_copies(hidden_ref, frame, outs, members, sem):
             copy.start()
     for frame in range(frames):
-        for copy in piece_copies(hidden_ref, frame, outs, sizes, members, sem):
+        for copy in piece_copies(hidden_ref, frame, outs, members, sem):
             copy.wait()
 
 
-def piece_shapes(frames, members, sizes, ch):
-    return [pltpu.HBM((frames, size, ch), BF16) for size in sizes for _ in range(members)]
-
-
-def norm_call(conv, own, other, above, below, gain, shift, count, members, sizes):
+def norm_call(conv, own, other, halo_rows, gain, shift, count, members):
     frames, band, width, ch = conv.shape
-    pieces = members * len(sizes)
-    return pl.pallas_call(
-        functools.partial(norm_kernel, count, members, sizes),
-        in_specs=[vspec()] * 7,
-        out_specs=[vspec()] + [hspec()] * pieces,
-        out_shape=[jax.ShapeDtypeStruct((frames, 2 * width + 96, ch), BF16)]
-        + piece_shapes(frames, members, sizes, ch),
+    rows = len(halo_rows)
+    return pl.pallas_call(
+        functools.partial(norm_kernel, count, members, rows),
+        in_specs=[vspec()] * (5 + rows),
+        out_specs=[vspec()] + [hspec()] * members,
+        out_shape=[jax.ShapeDtypeStruct((frames, rows * width + 96, ch), BF16)]
+        + [pltpu.HBM((frames, band * width // members, ch), BF16)] * members,
         scratch_shapes=[
             VMEM((frames, band, width, ch), BF16),
-            pltpu.SemaphoreType.DMA((pieces, frames)),
+            pltpu.SemaphoreType.DMA((members, frames)),
         ],
         compiler_params=params(16),
         cost_estimate=COST,
         name="norm",
-    )(conv, own, other, above, below, gain.reshape(1, ch), shift.reshape(1, ch))
-
-
-def guest_kernel(count, members, sizes, video_hbm, packet_ref, weight_ref, gain_ref, shift_ref, *refs):
-    outs, (video_ref, conv_ref, hidden_ref, wide_ref, in_sem, sem) = refs[:-6], refs[-6:]
+    )(conv, own, other, gain.reshape(1, ch), shift.reshape(1, ch), *halo_rows)
+
+
+def guest_kernel(count, members, video_hbm, packet_ref, weight_ref, gain_ref, shift_ref, *refs):
+    keep_ref, mate_ref, *away_refs = refs[:-6]
+    video_ref, conv_ref, hidden_ref, wide_ref, in_sem, sem = refs[-6:]
+    outs = [[keep_ref], [mate_ref]] + [[ref.at[k] for ref in away_refs] for k in range(2)]
     frames, band, width, ch = video_hbm.shape
+    rows = (packet_ref.shape[1] - 96) // width
     here = lax.axis_index("tm")
 
     @pl.when(jnp.logical_and(here >= members, here % 2 == 0))
@@ -309,47 +309,48 @@
                 band,
                 lambda r: video_ref[frame, r],
                 lambda: packet_ref[frame, :width],
-                lambda: packet_ref[frame, width : 2 * width],
+                lambda: packet_ref[frame, (rows - 1) * width : rows * width],
             )
             conv_rows(band, read, wide_ref, write)
             sums = []
             for i in range(2):
-                at = 2 * width + i * 48
+                at = rows * width + i * 48
                 parts = packet_ref[frame, at : at + 48].astype(F32)
                 sums.append(parts[:16] + parts[16:32] + parts[32:])
             norm_frame(conv_ref, frame, sums, count, gain_ref, shift_ref, hidden_ref)
-            for copy in piece_copies(hidden_ref, frame, outs, sizes, members, sem):
+            for copy in piece_copies(hidden_ref, frame, outs, members, sem):
                 copy.start()
         for frame in range(frames):
-            for copy in piece_copies(hidden_ref, frame, outs, sizes, members, sem):
+            for copy in piece_copies(hidden_ref, frame, outs, members, sem):
                 copy.wait()
 
     @pl.when(here < members)
     def _():
         hidden_ref[...] = jnp.zeros_like(hidden_ref)
         for frame in range(frames):
-            for copy in piece_copies(hidden_ref, frame, outs, sizes, members, sem):
+            for copy in piece_copies(hidden_ref, frame, outs, members, sem):
                 copy.start()
         for frame in range(frames):
-            for copy in piece_copies(hidden_ref, frame, outs, sizes, members, sem):
+            for copy in piece_copies(hidden_ref, frame, outs, members, sem):
                 copy.wait()
 
 
 def guest_call(video, packet, weight, gain, shift, count, members, sizes):
     frames, band, width, ch = video.shape
-    pieces = members * len(sizes)
-    return pl.pallas_call(
-        functools.partial(guest_kernel, count, members, sizes),
+    piece = (frames, band * width // members, ch)
+    shapes = [piece, piece] + [(2, frames, size, ch) for size in sizes]
+    return pl.pallas_call(
+        functools.partial(guest_kernel, count, members),
         in_specs=[hspec()] + [vspec()] * 4,
-        out_specs=[hspec()] * pieces,
-        out_shape=piece_shapes(frames, members, sizes, ch),
+        out_specs=[hspec()] * len(shapes),
+        out_shape=[pltpu.HBM(shape, BF16) for shape in shapes],
         scratch_shapes=[
             VMEM(video.shape, BF16),
             VMEM(video.shape, F32),
             VMEM(video.shape, BF16),
             VMEM((4 * ch, 6 * ch), BF16),
             pltpu.SemaphoreType.DMA((frames,)),
-            pltpu.SemaphoreType.DMA((pieces, frames)),
+            pltpu.SemaphoreType.DMA((2 + 2 * len(sizes), frames)),
         ],
         compiler_params=params(24),
         cost_estimate=LONG,
@@ -357,129 +358,160 @@
     )(video, packet, weight, gain.reshape(1, ch), shift.reshape(1, ch))
 
 
-def pair_weights(weight_ref, layer, wide_ref):
+def pack_kernel(weight_ref, out_ref):
     ch = weight_ref.shape[-1]
-    wide_ref[...] = jnp.zeros_like(wide_ref)
-    for out in range(2):
-        for tap in range(3):
-            row = out + 2 - tap
-            wide_ref[row * ch : (row + 1) * ch, out * ch : (out + 1) * ch] = weight_ref[layer, tap]
-
-
-def pair(read, write, time, dilation, wide_ref):
-    ch = wide_ref.shape[1] // 2
+    out_ref[...] = jnp.zeros_like(out_ref)
+    for layer in range(3):
+        for out in range(2):
+            for tap in range(3):
+                row = out + 2 - tap
+                out_ref[layer, row * ch : (row + 1) * ch, out * ch : (out + 1) * ch] = weight_ref[
+                    layer, tap
+                ]
+
+
+def pack_call(weight):
+    layers, _, ch, _ = weight.shape
+    return pl.pallas_call(
+        pack_kernel,
+        in_specs=[vspec()],
+        out_specs=vspec(),
+        out_shape=jax.ShapeDtypeStruct((layers, 4 * ch, 2 * ch), BF16),
+        compiler_params=params(8),
+        cost_estimate=LONG,
+        name="pack",
+    )(weight)
+
+
+def pair(read, write, time, layer, wide_ref):
+    ch = wide_ref.shape[2] // 2
+    dilation = 2**layer
     frames = [read(time + (a - 2) * dilation) for a in range(4)]
-    both = jnp.dot(jnp.concatenate(frames, axis=-1), wide_ref[...], preferred_element_type=F32)
+    both = jnp.dot(jnp.concatenate(frames, axis=-1), wide_ref[layer], preferred_element_type=F32)
     write(time, (both[:, :ch] + frames[2].astype(F32)).astype(BF16))
     write(time + dilation, (both[:, ch:] + frames[3].astype(F32)).astype(BF16))
 
 
-def early_kernel(members, spans, size, *refs):
-    own, guest = spans
-    count = [len({i for i, *_ in kind}) for kind in spans]
-    pieces, refs = refs[: count[0] * members], refs[count[0] * members :]
-    halos, refs = refs[: count[0]], refs[count[0] :]
-    guests, refs = refs[: count[1] * members], refs[count[1] * members :]
-    weight_ref, out_ref, u0_ref, u1_ref, wide_ref = refs
+def ahead_kernel(members, *refs):
+    pieces, (wide_ref, out_ref, u0_ref) = refs[:members], refs[members:]
     step = pieces[0].shape[0]
+    me = lax.axis_index("tm") % members
+    for k in range(members):
+        u0_ref[pl.ds((me ^ k) * step, step)] = pieces[k][...]
+
+    def write1(t, value):
+        out_ref[t - 2] = value
+
+    for time in range(2, SPAN, 2):
+        pair(lambda t: u0_ref[t], write1, time, 0, wide_ref)
+
+
+def ahead_call(own, wide):
+    members = len(own)
+    _, size, ch = own[0].shape
+    return pl.pallas_call(
+        functools.partial(ahead_kernel, members),
+        in_specs=[vspec()] * (members + 1),
+        out_specs=vspec(),
+        out_shape=jax.ShapeDtypeStruct((SPAN - 2, size, ch), BF16),
+        scratch_shapes=[VMEM((SPAN, size, ch), BF16)],
+        compiler_params=params(16),
+        cost_estimate=LONG,
+        name="ahead",
+    )(*own, wide)
+
+
+def early_kernel(members, plan, first, *refs):
+    arrays, (ahead_ref, wide_ref, out_ref, u0_ref, u1_ref) = refs[: len(plan)], refs[len(plan) :]
+    size = out_ref.shape[1]
     lead = SPAN - 2
     me = lax.axis_index("tm") % members
-    for i, source, target, rows in own:
-        for k in range(members):
-            u0_ref[pl.ds(lead + (me ^ k) * step, step), target : target + rows] = pieces[
-                i * members + k
-            ][:, source : source + rows]
-        u0_ref[2:4, target : target + rows] = halos[i][:, source : source + rows]
-    for i, source, target, rows in guest:
-        for k in range(members):
+    for ref, (kind, k, source, target, rows) in zip(arrays, plan):
+        value = ref.at[0] if len(ref.shape) == 4 else ref
+        step = value.shape[0]
+        here, there = slice(target, target + rows), slice(source, source + rows)
+        if kind == "own":
+
+            @pl.when(me == k)
+            def _():
+                u0_ref[lead : lead + step, here] = value[:, there]
+
+        elif kind == "middle":
+            u0_ref[2:4, here] = value[:, there]
+        else:
 
             @pl.when((me ^ k) % 2 == 0)
             def _():
-                u0_ref[pl.ds(2 * (me ^ k), step), target : target + rows] = guests[
-                    i * members + k
-                ][:, source : source + rows]
-
-    pair_weights(weight_ref, 0, wide_ref)
+                u0_ref[pl.ds(2 * (me ^ k), step), here] = value[:, there]
 
     def write1(t, value):
         u1_ref[t + 4] = value
 
+    def read1(t):
+        return u1_ref[t + 4] if t < 2 else ahead_ref[t - 2, first : first + size]
+
     def write2(t, value):
         out_ref[t] = value
 
-    for time in range(-4, SPAN, 2):
-        pair(lambda t: u0_ref[t + lead], write1, time, 1, wide_ref)
-    pair_weights(weight_ref, 1, wide_ref)
+    for time in range(-4, 2, 2):
+        pair(lambda t: u0_ref[t + lead], write1, time, 0, wide_ref)
     for time in range(0, SPAN, 4):
         for odd in range(2):
-            pair(lambda t: u1_ref[t + 4], write2, time + odd, 2, wide_ref)
-
-
-def overlaps(sizes, first, last):
-    found, at = [], 0
-    for i, size in enumerate(sizes):
-        low, high = max(first, at), min(last, at + size)
-        if low < high:
-            found.append((i, low - at, low - first, high - low))
-        at += size
-    return found
-
-
-def early_call(own, halos, guest, weight, first, size):
-    members, ch = len(own[0]), weight.shape[-1]
-    spans, arrays = [], []
-    for kind, (blocks, sizes) in enumerate(((own, OWN_SIZES), (guest, GUEST_SIZES))):
-        parts = overlaps(sizes, first, first + size)
-        base = parts[0][0]
-        spans.append([(i - base, *rest) for i, *rest in parts])
-        arrays += sum([blocks[i] for i, *_ in parts], [])
-        if kind == 0:
-            arrays += [halos[i] for i, *_ in parts]
-    return pl.pallas_call(
-        functools.partial(early_kernel, members, spans, size),
-        in_specs=[vspec()] * (len(arrays) + 1),
+            pair(read1, write2, time + odd, 1, wide_ref)
+
+
+def early_call(sources, ahead, wide, members, first, size):
+    plan, arrays = [], []
+    for kind, k, blocks in sources:
+        at = 0
+        for block in blocks:
+            rows = block.shape[-2]
+            low, high = max(first, at), min(first + size, at + rows)
+            if low < high:
+                plan.append((kind, k, low - at, low - first, high - low))
+                arrays.append(block)
+            at += rows
+    ch = wide.shape[-1] // 2
+    return pl.pallas_call(
+        functools.partial(early_kernel, members, plan, first),
+        in_specs=[vspec()] * (len(arrays) + 2),
         out_specs=vspec(),
         out_shape=jax.ShapeDtypeStruct((SPAN, size, ch), BF16),
-        scratch_shapes=[
-            VMEM((2 * SPAN - 2, size, ch), BF16),
-            VMEM((SPAN + 4, size, ch), BF16),
-            VMEM((4 * ch, 2 * ch), BF16),
-        ],
+        scratch_shapes=[VMEM((SPAN, size, ch), BF16), VMEM((6, size, ch), BF16)],
         compiler_params=params(16),
         cost_estimate=COST,
         name="early",
-    )(*arrays, weight)
-
-
-def late_kernel(members, own_ref, halo_ref, weight_ref, *refs):
-    outs, (u3_ref, wide_ref) = refs[:members], refs[members:]
+    )(*arrays, ahead, wide)
+
+
+def late_kernel(members, own_ref, halo_ref, wide_ref, *refs):
+    outs, u3_ref = refs[:-1], refs[-1]
     step = outs[0].shape[0]
-    pair_weights(weight_ref, 2, wide_ref)
+    me = lax.axis_index("tm") % members
 
     def write3(t, value):
         u3_ref[t] = value
 
     for time in range(4):
         pair(
-            lambda t: own_ref[t] if t >= 0 else halo_ref[t + SPAN], write3, time, 4, wide_ref
+            lambda t: own_ref[t] if t >= 0 else halo_ref[t + SPAN], write3, time, 2, wide_ref
         )
-    me = lax.axis_index("tm") % members
     for k in range(members):
         outs[k][...] = u3_ref[pl.ds((me ^ k) * step, step)]
 
 
-def late_call(own, halo, weight, members):
+def late_call(own, halo, wide, members):
     frames, size, ch = own.shape
     return pl.pallas_call(
         functools.partial(late_kernel, members),
         in_specs=[vspec()] * 3,
         out_specs=[vspec()] * members,
         out_shape=[jax.ShapeDtypeStruct((frames // members, size, ch), BF16)] * members,
-        scratch_shapes=[VMEM(own.shape, BF16), VMEM((4 * ch, 2 * ch), BF16)],
+        scratch_shapes=[VMEM(own.shape, BF16)],
         compiler_params=params(12),
         cost_estimate=COST,
         name="late",
-    )(own, halo, weight)
+    )(own, halo, wide)
 
 
 def place_kernel(members, sizes, *refs):
@@ -551,45 +583,50 @@
     conv, sums = conv_call(video, spatial_weight)
     conv, sums = edge_call(conv, above, below, spatial_weight, sums)
     count = band * rows * width * (ch // GROUPS)
+    quarter = band * width // members
+    guest_sizes, out_sizes = [
+        [quarter * part // 60 for part in parts] for parts in (GUEST_PARTS, OUT_PARTS)
+    ]
+    halo_list = [above] if above is below else [above, below]
     packet, *pieces = norm_call(
-        conv, sums, other_sums(sums), above, below, norm_gain, norm_shift, count, members, OWN_SIZES
+        conv, sums, other_sums(sums), halo_list, norm_gain, norm_shift, count, members
     )
-    guest_packet = lax.ppermute(packet, "tm", guest_pairs)
-
-    def swap(four, pairs, waits=None):
+
+    def swap(four, waits=None):
         got = [four[0]]
         for k in range(1, members):
             value = four[k] if waits is None else after(four[k], waits[k])
-            got.append(lax.ppermute(value, "tm", pairs[k]))
+            got.append(lax.ppermute(value, "tm", swaps[k]))
         return got
 
-    def blocks(arrays):
-        return [arrays[i : i + members] for i in range(0, len(arrays), members)]
-
-    def forward(value):
-        value = after(value, passed[-2]) if len(passed) > 1 else value
-        passed.append(lax.ppermute(value, "tm", onward))
-        return passed[-1]
-
-    guest_pieces = guest_call(
-        guest_video, guest_packet, spatial_weight, norm_gain, norm_shift, count, members, GUEST_SIZES
+    own = swap(pieces)
+    guest_packet = lax.ppermute(packet, "tm", guest_pairs)
+    keep, mate, *aways = guest_call(
+        guest_video, guest_packet, spatial_weight, norm_gain, norm_shift, count, members, guest_sizes
     )
-    passed, own, halos, guest = [], [], [], []
-    for four, guest_four in zip(blocks(pieces), blocks(guest_pieces), strict=True):
-        own.append(swap(four, swaps, guest[-1] if own else None))
-        four = after(own[-1], guest_pieces[0])
-        middle = functools.reduce(
-            lambda acc, k: jnp.where(me == (2 ^ k), four[k], acc), range(1, members), four[0]
-        )
-        halos.append(forward(middle))
-        guest.append(swap(guest_four, guest_swaps, own[-1] if guest else None))
-    results, first = [], 0
-    for size in OUT_SIZES:
-        u2 = early_call(own, halos, guest, temporal_weight, first, size)
-        late = late_call(u2, forward(u2), temporal_weight, members)
-        results.append(swap(late, swaps, results[-1] if results else None))
+    wide = pack_call(after(temporal_weight, keep))
+    crossed = [lax.ppermute(away, "tm", guest_swaps[2]) for away in aways]
+    guest = [[keep], [lax.ppermute(mate, "tm", guest_swaps[1])], crossed]
+    four = after(own, wide)
+    middle = functools.reduce(
+        lambda acc, k: jnp.where(me == (2 ^ k), four[k], acc), range(1, members), four[0]
+    )
+    halo = lax.ppermute(middle, "tm", onward)
+    ahead = ahead_call(own, after(wide, middle, crossed[0]))
+    guest.append(
+        [lax.ppermute(after(block[1], ahead), "tm", guest_swaps[1]) for block in crossed]
+    )
+    sources = [("own", k, [own[k]]) for k in range(members)]
+    sources += [("guest", k, guest[k]) for k in range(members)]
+    sources.append(("middle", 0, [halo]))
+    results, passed, first = [], [], 0
+    for i, size in enumerate(out_sizes):
+        u2 = early_call(sources, ahead, wide, members, first, size)
+        passed.append(lax.ppermute(after(u2, passed[-2]) if i > 1 else u2, "tm", onward))
+        late = late_call(u2, passed[-1], wide, members)
+        results.append(swap(late, results[-1] if results else None))
         first += size
-    out = place_call(sum(results, []), members, OUT_SIZES)
+    out = place_call(sum(results, []), members, out_sizes)
     return out.reshape(frames, band, width, ch)
 
 

time: 130 us -> 119 us (0.915)
  starting transfers between devices: 76 us -> 51 us
  waiting for transfers between devices: 33.6 us -> 46.8 us
    ppermute x30 -> x25, starting transfers between devices: 69.5 us -> 44.5 us  [the longest x4 15.6 us: body(): lax.ppermute(after(u2, passed[-2]) if i > 1 else u2, 'tm', onward)]
    ppermute x30 -> x25, waiting for transfers between devices: 31.8 us -> 45 us  [the longest x15 26.1 us: swap(): got.append(lax.ppermute(value, 'tm', swaps[k]))]
    pallas_call x6 -> x8, Pallas kernels: 8.25 us -> 8.69 us  [the longest x4 3.15 us: early_call(): pl.pallas_call(functools.partial(early_kernel, members, plan, first), in_...]
  transfers between devices with their start and end apart: 34 -> 29, of which waited for: 13 -> 13; matrix products, arithmetic and copies ran while one was open for 1% -> 1% of each run, Pallas kernels for 13% -> 15%
where the time goes in v4:
time: 119 us; the launch traced here: 118 us
  starting transfers between devices  51 us (43%)
  waiting for transfers between devices  46.8 us (39%)
  Pallas kernels  18.9 us (16%)
    ppermute x15, waiting for transfers between devices, swap(): got.append(lax.ppermute(value, 'tm', swaps[k]))  26.1 us
    ppermute x4, starting transfers between devices, body(): lax.ppermute(after(u2, passed[-2]) if i > 1 else u2, 'tm', onward)  15.6 us
    ppermute x15, starting transfers between devices, swap(): got.append(lax.ppermute(value, 'tm', swaps[k]))  14.5 us
    ppermute x4, waiting for transfers between devices, body(): lax.ppermute(after(u2, passed[-2]) if i > 1 else u2, 'tm', onward)  13 us
    ppermute x2, starting transfers between devices, body(): crossed = [lax.ppermute(away, 'tm', guest_swaps[2]) for away in aways]  6.84 us
    pallas_call x1, Pallas kernels, conv_call(): pl.pallas_call(functools.partial(conv_kernel, band), grid=(frames,), in_s...  4.86 us
    ppermute x1, waiting for transfers between devices, body(): halo = lax.ppermute(middle, 'tm', onward)  4.72 us
    ppermute x1, starting transfers between devices, body(): halo = lax.ppermute(middle, 'tm', onward)  3.51 us
  transfers between devices with their start and end apart: 29, of which 13 were waited for; matrix products, arithmetic and copies ran while one was open for 1% of the time, Pallas kernels for 15%

profile of v4, /device:TPU:0, one launch (start us, length us, event | category | flops | bytes accessed | tf_op | source)
XLA Modules:
  0.0 118.2 jit_solution(11938781707239807088)
XLA Ops:
  0.0 0.8 collective-permute-start.5
  0.8 1.0 dynamic-slice_bitcast_fusion
  1.8 3.0 %collective-permute-start = (bf16[2,480,128]{2,1,0:T(8,128)(2,1)S(1)}, bf16[2,480,128]{2,1,0:T(8,128)(2,1)S(1)}, u32[]{:S(2)}, u32[]{:S(2)}) collective-permute-start(bf16[2,480,128]{2,1,0:T(8,128)(2,1)S(1)} %dynamic-slice_bitcast_fusion), channel_id=1, source_target_pairs={{0,1},{1,0},{2,3},{3,2},{4,5},{5,4},{6,7},{7,6},{8,9},{9,8},{10,11... | collective-permute-start | bytes 737288 | tf_op jit(solution)/shard_map/ppermute | solution.py:553
  4.8 4.9 %conv.1 = (f32[2,8,480,128]{3,2,1,0:T(8,128)S(1)}, f32[2,2,8,128]{3,2,1,0:T(8,128)S(1)}) custom-call(bf16[2,8,480,128]{3,2,1,0:T(8,128)(2,1)} %video_ref.1, bf16[3,3,128,128]{3,2,1,0:T(8,128)(2,1)} %weight_ref.5), custom_call_target="tpu_custom_call" | custom-call | flops 20000000000 | tf_op jit(solution)/shard_map/conv/pallas_call | solution.py:116
  9.7 2.1 %edge.1 = (f32[2,8,480,128]{3,2,1,0:T(8,128)S(1)}, f32[2,2,8,128]{3,2,1,0:T(8,128)S(1)}) custom-call(f32[2,8,480,128]{3,2,1,0:T(8,128)S(1)} %get-tuple-element.53.conv_ref, bf16[2,480,128]{2,1,0:T(8,128)(2,1)S(1)} %collective-permute-done.above_ref.below_ref.refs_0_, ...), custom_call_target="tpu_custom_call", output_to_operand_aliasing={{0}: (0, {})} | custom-call | tf_op jit(solution)/shard_map/edge/pallas_call | solution.py:164
  11.8 2.0 %collective-permute-start.1 = (f32[2,2,8,128]{3,2,1,0:T(8,128)S(1)}, f32[2,2,8,128]{3,2,1,0:T(8,128)S(1)}, u32[]{:S(2)}, u32[]{:S(2)}) collective-permute-start(f32[2,2,8,128]{3,2,1,0:T(8,128)S(1)} %get-tuple-element.56.own_ref), channel_id=1, source_target_pairs={{0,1},{1,0},{2,3},{3,2},{4,5},{5,4},{6,7},{7,6},{8,9},{9,8},{10,11... | collective-permute-start | bytes 49160 | tf_op jit(solution)/shard_map/ppermute | solution.py:562
  13.8 1.8 %collective-permute-done.1.other_ref = f32[2,2,8,128]{3,2,1,0:T(8,128)S(1)} collective-permute-done((f32[2,2,8,128]{3,2,1,0:T(8,128)S(1)}, f32[2,2,8,128]{3,2,1,0:T(8,128)S(1)}, u32[]{:S(2)}, u32[]{:S(2)}) %collective-permute-start.1) | collective-permute-done | bytes 16416 | tf_op jit(solution)/shard_map/ppermute | solution.py:562
  15.6 2.7 %norm.1 = (bf16[2,576,128]{2,1,0:T(8,128)(2,1)S(1)}, bf16[2,960,128]{2,1,0:T(8,128)(2,1)}, bf16[2,960,128]{2,1,0:T(8,128)(2,1)}, bf16[2,960,128]{2,1,0:T(8,128)(2,1)}, bf16[2,960,128]{2,1,0:T(8,128)(2,1)}) custom-call(f32[2,8,480,128]{3,2,1,0:T(8,128)S(1)} %get-tuple-element.55.conv_ref, f32[2,2,8,128]{3,2,1,0:T(8,128)S(1)} %get-tuple-element.56.own_ref, ...), custom_call_target="tpu_custom_call" | custom-call | tf_op jit(solution)/shard_map/norm/pallas_call | solution.py:269
  18.4 0.7 collective-permute-start.6
  19.1 4.4 %collective-permute-start.2 = (bf16[2,960,128]{2,1,0:T(8,128)(2,1)}, bf16[2,960,128]{2,1,0:T(8,128)(2,1)S(1)}, u32[]{:S(2)}, u32[]{:S(2)}) collective-permute-start(bf16[2,960,128]{2,1,0:T(8,128)(2,1)} %get-tuple-element.58), channel_id=1, source_target_pairs={{0,2},{2,0},{4,6},{6,4},{8,10},{10,8},{12,14},{14,12},{16,18},{18,... | collective-permute-start | bytes 1474568 | tf_op jit(solution)/shard_map/ppermute | solution.py:599
  23.4 1.5 %collective-permute-start.3 = (bf16[2,960,128]{2,1,0:T(8,128)(2,1)}, bf16[2,960,128]{2,1,0:T(8,128)(2,1)S(1)}, u32[]{:S(2)}, u32[]{:S(2)}) collective-permute-start(bf16[2,960,128]{2,1,0:T(8,128)(2,1)} %get-tuple-element.59), channel_id=1, source_target_pairs={{0,4},{2,6},{4,0},{6,2},{8,12},{10,14},{12,8},{14,10},{16,20},{18,... | collective-permute-start | bytes 1474568 | tf_op jit(solution)/shard_map/ppermute | solution.py:599
  25.0 1.7 %guest.1 = (bf16[2,960,128]{2,1,0:T(8,128)(2,1)}, bf16[2,960,128]{2,1,0:T(8,128)(2,1)}, bf16[2,2,416,128]{3,2,1,0:T(8,128)(2,1)}, bf16[2,2,544,128]{3,2,1,0:T(8,128)(2,1)}) custom-call(bf16[2,8,480,128]{3,2,1,0:T(8,128)(2,1)S(1)} %collective-permute-done.5.video_hbm, bf16[2,576,128]{2,1,0:T(8,128)(2,1)S(1)} %collective-permute-done.6.packet_ref, ...), custom_call_target="tpu_custom_call" | custom-call | flops 20000000000 | tf_op jit(solution)/shard_map/guest/pallas_call | solution.py:342
  26.7 3.5 %collective-permute-start.8 = (bf16[2,2,416,128]{3,2,1,0:T(8,128)(2,1)}, bf16[2,2,416,128]{3,2,1,0:T(8,128)(2,1)S(1)}, u32[]{:S(2)}, u32[]{:S(2)}) collective-permute-start(bf16[2,2,416,128]{3,2,1,0:T(8,128)(2,1)} %get-tuple-element.64), channel_id=1, source_target_pairs={{0,4},{4,0},{8,12},{12,8},{16,20},{20,16},{24,28},{28,24},{1,5},{5... | collective-permute-start | bytes 1277960 | tf_op jit(solution)/shard_map/ppermute | solution.py:608
  30.3 7.5 %collective-permute-done.3.refs_2_ = bf16[2,960,128]{2,1,0:T(8,128)(2,1)S(1)} collective-permute-done((bf16[2,960,128]{2,1,0:T(8,128)(2,1)}, bf16[2,960,128]{2,1,0:T(8,128)(2,1)S(1)}, u32[]{:S(2)}, u32[]{:S(2)}) %collective-permute-start.3) | collective-permute-done | bytes 491552 | tf_op jit(solution)/shard_map/ppermute | solution.py:599
  37.7 8.8 %collective-permute-done.4.refs_3_ = bf16[2,960,128]{2,1,0:T(8,128)(2,1)S(1)} collective-permute-done((bf16[2,960,128]{2,1,0:T(8,128)(2,1)}, bf16[2,960,128]{2,1,0:T(8,128)(2,1)S(1)}, u32[]{:S(2)}, u32[]{:S(2)}) %collective-permute-start.4) | collective-permute-done | bytes 491552 | tf_op jit(solution)/shard_map/ppermute | solution.py:599
  46.5 3.4 %collective-permute-start.15 = (bf16[2,2,544,128]{3,2,1,0:T(8,128)(2,1)S(1)}, bf16[2,2,544,128]{3,2,1,0:T(8,128)(2,1)S(1)}, u32[]{:S(2)}, u32[]{:S(2)}) collective-permute-start(bf16[2,2,544,128]{3,2,1,0:T(8,128)(2,1)S(1)} %copy-done.6), channel_id=1, source_target_pairs={{0,4},{4,0},{8,12},{12,8},{16,20},{20,16},{24,28},{28,24},{1,5},{5... | collective-permute-start | bytes 1671176 | tf_op jit(solution)/shard_map/ppermute | solution.py:608
  50.0 3.5 %collective-permute-start.10 = (bf16[2,960,128]{2,1,0:T(8,128)(2,1)S(1)}, bf16[2,960,128]{2,1,0:T(8,128)(2,1)S(1)}, u32[]{:S(2)}, u32[]{:S(2)}) collective-permute-start(bf16[2,960,128]{2,1,0:T(8,128)(2,1)S(1)} %select_select_fusion), channel_id=1, source_target_pairs={{0,8},{2,10},{4,12},{6,14},{8,16},{10,18},{12,20},{14,22},{16,24},... | collective-permute-start | bytes 1474568 | tf_op jit(solution)/shard_map/ppermute | solution.py:614
  53.6 1.5 %collective-permute-start.7 = (bf16[2,960,128]{2,1,0:T(8,128)(2,1)S(1)}, bf16[2,960,128]{2,1,0:T(8,128)(2,1)S(1)}, u32[]{:S(2)}, u32[]{:S(2)}) collective-permute-start(bf16[2,960,128]{2,1,0:T(8,128)(2,1)S(1)} %copy-done.7), channel_id=1, source_target_pairs={{0,2},{4,6},{8,10},{12,14},{16,18},{20,22},{24,26},{28,30},{1,3},{... | collective-permute-start | bytes 1474568 | tf_op jit(solution)/shard_map/ppermute | solution.py:609
  55.0 1.0 ahead.1.refs_9_
  56.1 1.3 %collective-permute-start.9 = (bf16[2,416,128]{2,1,0:T(8,128)(2,1)S(1)}, bf16[2,416,128]{2,1,0:T(8,128)(2,1)S(1)}, u32[]{:S(2)}, u32[]{:S(2)}) collective-permute-start(bf16[2,416,128]{2,1,0:T(8,128)(2,1)S(1)} %slice_bitcast_fusion.1), channel_id=1, source_target_pairs={{0,2},{4,6},{8,10},{12,14},{16,18},{20,22},{24,26},{28,30},{1,3},{... | collective-permute-start | bytes 638984 | tf_op jit(solution)/shard_map/ppermute | solution.py:617
  57.4 4.7 %collective-permute-done.10.refs_8_ = bf16[2,960,128]{2,1,0:T(8,128)(2,1)S(1)} collective-permute-done((bf16[2,960,128]{2,1,0:T(8,128)(2,1)S(1)}, bf16[2,960,128]{2,1,0:T(8,128)(2,1)S(1)}, u32[]{:S(2)}, u32[]{:S(2)}) %collective-permute-start.10) | collective-permute-done | bytes 491552 | tf_op jit(solution)/shard_map/ppermute | solution.py:614
  62.1 1.1 early.4.own_ref
  63.3 4.4 %collective-permute-start.11 = (bf16[8,416,128]{2,1,0:T(8,128)(2,1)S(1)}, bf16[8,416,128]{2,1,0:T(8,128)(2,1)S(1)}, u32[]{:S(2)}, u32[]{:S(2)}) collective-permute-start(bf16[8,416,128]{2,1,0:T(8,128)(2,1)S(1)} %early.4.own_ref), channel_id=1, source_target_pairs={{0,8},{2,10},{4,12},{6,14},{8,16},{10,18},{12,20},{14,22},{16,24},... | collective-permute-start | bytes 2555912 | tf_op jit(solution)/shard_map/ppermute | solution.py:625
  67.8 1.3 %collective-permute-start.16 = (bf16[2,544,128]{2,1,0:T(8,128)(2,1)S(1)}, bf16[2,544,128]{2,1,0:T(8,128)(2,1)S(1)}, u32[]{:S(2)}, u32[]{:S(2)}) collective-permute-start(bf16[2,544,128]{2,1,0:T(8,128)(2,1)S(1)} %slice_bitcast_fusion), channel_id=1, source_target_pairs={{0,2},{4,6},{8,10},{12,14},{16,18},{20,22},{24,26},{28,30},{1,3},{... | collective-permute-start | bytes 835592 | tf_op jit(solution)/shard_map/ppermute | solution.py:617
  69.1 1.2 collective-permute-done.16.refs_7_
  70.2 0.8 early.5.own_ref
  71.0 3.4 %collective-permute-start.17 = (bf16[8,256,128]{2,1,0:T(8,128)(2,1)S(1)}, bf16[8,256,128]{2,1,0:T(8,128)(2,1)S(1)}, u32[]{:S(2)}, u32[]{:S(2)}) collective-permute-start(bf16[8,256,128]{2,1,0:T(8,128)(2,1)S(1)} %early.5.own_ref), channel_id=1, source_target_pairs={{0,8},{2,10},{4,12},{6,14},{8,16},{10,18},{12,20},{14,22},{16,24},... | collective-permute-start | bytes 1572872 | tf_op jit(solution)/shard_map/ppermute | solution.py:625
  74.4 12.6 %collective-permute-done.11.halo_ref = bf16[8,416,128]{2,1,0:T(8,128)(2,1)S(1)} collective-permute-done((bf16[8,416,128]{2,1,0:T(8,128)(2,1)S(1)}, bf16[8,416,128]{2,1,0:T(8,128)(2,1)S(1)}, u32[]{:S(2)}, u32[]{:S(2)}) %collective-permute-start.11) | collective-permute-done | bytes 852000 | tf_op jit(solution)/shard_map/ppermute | solution.py:625
  87.0 0.7 late.4
  87.8 1.6 %collective-permute-start.13 = (bf16[2,416,128]{2,1,0:T(8,128)(2,1)S(1)}, bf16[2,416,128]{2,1,0:T(8,128)(2,1)S(1)}, u32[]{:S(2)}, u32[]{:S(2)}) collective-permute-start(bf16[2,416,128]{2,1,0:T(8,128)(2,1)S(1)} %get-tuple-element.74), channel_id=1, source_target_pairs={{0,4},{2,6},{4,0},{6,2},{8,12},{10,14},{12,8},{14,10},{16,20},{18,... | collective-permute-start | bytes 638984 | tf_op jit(solution)/shard_map/ppermute | solution.py:599
  89.6 0.6 early.6.own_ref
  90.3 4.4 %collective-permute-start.21 = (bf16[8,160,128]{2,1,0:T(8,128)(2,1)S(1)}, bf16[8,160,128]{2,1,0:T(8,128)(2,1)S(1)}, u32[]{:S(2)}, u32[]{:S(2)}) collective-permute-start(bf16[8,160,128]{2,1,0:T(8,128)(2,1)S(1)} %early.6.own_ref), channel_id=1, source_target_pairs={{0,8},{2,10},{4,12},{6,14},{8,16},{10,18},{12,20},{14,22},{16,24},... | collective-permute-start | bytes 983048 | tf_op jit(solution)/shard_map/ppermute | solution.py:625
  94.7 0.6 early.7.own_ref
  95.3 3.4 %collective-permute-start.25 = (bf16[8,128,128]{2,1,0:T(8,128)(2,1)S(1)}, bf16[8,128,128]{2,1,0:T(8,128)(2,1)S(1)}, u32[]{:S(2)}, u32[]{:S(2)}) collective-permute-start(bf16[8,128,128]{2,1,0:T(8,128)(2,1)S(1)} %early.7.own_ref), channel_id=1, source_target_pairs={{0,8},{2,10},{4,12},{6,14},{8,16},{10,18},{12,20},{14,22},{16,24},... | collective-permute-start | bytes 786440 | tf_op jit(solution)/shard_map/ppermute | solution.py:625
  98.7 0.5 late.5
  99.2 0.6 collective-permute-start.20
  99.9 2.3 %collective-permute-start.19 = (bf16[2,256,128]{2,1,0:T(8,128)(2,1)S(1)}, bf16[2,256,128]{2,1,0:T(8,128)(2,1)S(1)}, u32[]{:S(2)}, u32[]{:S(2)}) collective-permute-start(bf16[2,256,128]{2,1,0:T(8,128)(2,1)S(1)} %get-tuple-element.82), channel_id=1, source_target_pairs={{0,4},{2,6},{4,0},{6,2},{8,12},{10,14},{12,8},{14,10},{16,20},{18,... | collective-permute-start | bytes 393224 | tf_op jit(solution)/shard_map/ppermute | solution.py:599
  103.1 0.6 collective-permute-done.20.refs_7_
  103.7 0.5 collective-permute-start.24
  104.2 3.9 %collective-permute-done.19.refs_6_ = bf16[2,256,128]{2,1,0:T(8,128)(2,1)S(1)} collective-permute-done((bf16[2,256,128]{2,1,0:T(8,128)(2,1)S(1)}, bf16[2,256,128]{2,1,0:T(8,128)(2,1)S(1)}, u32[]{:S(2)}, u32[]{:S(2)}) %collective-permute-start.19) | collective-permute-done | bytes 131104 | tf_op jit(solution)/shard_map/ppermute | solution.py:599
  108.1 0.4 collective-permute-start.23
  108.6 1.1 collective-permute-start.22
  110.0 0.7 collective-permute-start.28
  110.7 1.9 %collective-permute-done.23.refs_10_ = bf16[2,160,128]{2,1,0:T(8,128)(2,1)S(1)} collective-permute-done((bf16[2,160,128]{2,1,0:T(8,128)(2,1)S(1)}, bf16[2,160,128]{2,1,0:T(8,128)(2,1)S(1)}, u32[]{:S(2)}, u32[]{:S(2)}) %collective-permute-start.23) | collective-permute-done | bytes 81952 | tf_op jit(solution)/shard_map/ppermute | solution.py:599
  112.6 1.0 collective-permute-start.27
  113.5 0.7 collective-permute-done.28.refs_15_
  114.3 2.5 %collective-permute-done.27.refs_14_ = bf16[2,128,128]{2,1,0:T(8,128)(2,1)S(1)} collective-permute-done((bf16[2,128,128]{2,1,0:T(8,128)(2,1)S(1)}, bf16[2,128,128]{2,1,0:T(8,128)(2,1)S(1)}, u32[]{:S(2)}, u32[]{:S(2)}) %collective-permute-start.27) | collective-permute-done | bytes 65568 | tf_op jit(solution)/shard_map/ppermute | solution.py:599
  116.8 1.4 %place.1 = bf16[2,4,960,128]{3,2,1,0:T(8,128)(2,1)} custom-call(bf16[2,416,128]{2,1,0:T(8,128)(2,1)S(1)} %get-tuple-element.72.refs_0_, bf16[2,416,128]{2,1,0:T(8,128)(2,1)S(1)} %collective-permute-done.12.refs_1_, bf16[2,416,128]{2,1,0:T(8,128)(2,1)S(1)} %collective-permute-done.13.refs_2_, bf16[2,416,128]{2,1,0:T(8,128)(2,1)S(1)} %collective-permute-done.14.refs_3_, ...), custom_call_target="tpu_custom_call" | custom-call | tf_op jit(solution)/shard_map/place/pallas_call | solution.py:536
  (45 shorter events, 2.0 us)
Async XLA Ops:
  0.0 25.0 %collective-permute-start.5 = (bf16[2,8,480,128]{3,2,1,0:T(8,128)(2,1)}, bf16[2,8,480,128]{3,2,1,0:T(8,128)(2,1)S(1)}, u32[]{:S(2)}, u32[]{:S(2)}) collective-permute-start(bf16[2,8,480,128]{3,2,1,0:T(8,128)(2,1)} %video_ref.1), channel_id=1, source_target_pairs={{2,8},{6,12},{10,16},{14,20},{18,24},{22,28},{3,9},{7,13},{11,17},... | collective-permute-start | bytes 5898248 | tf_op jit(solution)/shard_map/ppermute | solution.py:581
  1.8 7.9 %collective-permute-start = (bf16[2,480,128]{2,1,0:T(8,128)(2,1)S(1)}, bf16[2,480,128]{2,1,0:T(8,128)(2,1)S(1)}, u32[]{:S(2)}, u32[]{:S(2)}) collective-permute-start(bf16[2,480,128]{2,1,0:T(8,128)(2,1)S(1)} %dynamic-slice_bitcast_fusion), channel_id=1, source_target_pairs={{0,1},{1,0},{2,3},{3,2},{4,5},{5,4},{6,7},{7,6},{8,9},{9,8},{10,11... | collective-permute-start | bytes 737288 | tf_op jit(solution)/shard_map/ppermute | solution.py:553
  9.7 6.0 %copy-start.3 = (f32[128]{0:T(128)S(1)}, f32[128]{0:T(128)}, u32[]{:S(2)}) copy-start(f32[128]{0:T(128)} %param.7) | copy-start | bytes 1540
  9.7 5.9 %copy-start.4 = (f32[128]{0:T(128)S(1)}, f32[128]{0:T(128)}, u32[]{:S(2)}) copy-start(f32[128]{0:T(128)} %param.8) | copy-start | bytes 1540
  11.8 3.8 %collective-permute-start.1 = (f32[2,2,8,128]{3,2,1,0:T(8,128)S(1)}, f32[2,2,8,128]{3,2,1,0:T(8,128)S(1)}, u32[]{:S(2)}, u32[]{:S(2)}) collective-permute-start(f32[2,2,8,128]{3,2,1,0:T(8,128)S(1)} %get-tuple-element.56.own_ref), channel_id=1, source_target_pairs={{0,1},{1,0},{2,3},{3,2},{4,5},{5,4},{6,7},{7,6},{8,9},{9,8},{10,11... | collective-permute-start | bytes 49160 | tf_op jit(solution)/shard_map/ppermute | solution.py:562
  15.6 9.3 %copy-start.2 = (bf16[3,3,128,128]{3,2,1,0:T(8,128)(2,1)S(1)}, bf16[3,3,128,128]{3,2,1,0:T(8,128)(2,1)}, u32[]{:S(2)}) copy-start(bf16[3,3,128,128]{3,2,1,0:T(8,128)(2,1)} %weight_ref.5) | copy-start | bytes 884740
  18.4 6.6 %collective-permute-start.6 = (bf16[2,576,128]{2,1,0:T(8,128)(2,1)S(1)}, bf16[2,576,128]{2,1,0:T(8,128)(2,1)S(1)}, u32[]{:S(2)}, u32[]{:S(2)}) collective-permute-start(bf16[2,576,128]{2,1,0:T(8,128)(2,1)S(1)} %get-tuple-element.61), channel_id=1, source_target_pairs={{2,8},{6,12},{10,16},{14,20},{18,24},{22,28},{3,9},{7,13},{11,17},... | collective-permute-start | bytes 884744 | tf_op jit(solution)/shard_map/ppermute | solution.py:603
  19.1 11.2 %collective-permute-start.2 = (bf16[2,960,128]{2,1,0:T(8,128)(2,1)}, bf16[2,960,128]{2,1,0:T(8,128)(2,1)S(1)}, u32[]{:S(2)}, u32[]{:S(2)}) collective-permute-start(bf16[2,960,128]{2,1,0:T(8,128)(2,1)} %get-tuple-element.58), channel_id=1, source_target_pairs={{0,2},{2,0},{4,6},{6,4},{8,10},{10,8},{12,14},{14,12},{16,18},{18,... | collective-permute-start | bytes 1474568 | tf_op jit(solution)/shard_map/ppermute | solution.py:599
  23.4 14.3 %collective-permute-start.3 = (bf16[2,960,128]{2,1,0:T(8,128)(2,1)}, bf16[2,960,128]{2,1,0:T(8,128)(2,1)S(1)}, u32[]{:S(2)}, u32[]{:S(2)}) collective-permute-start(bf16[2,960,128]{2,1,0:T(8,128)(2,1)} %get-tuple-element.59), channel_id=1, source_target_pairs={{0,4},{2,6},{4,0},{6,2},{8,12},{10,14},{12,8},{14,10},{16,20},{18,... | collective-permute-start | bytes 1474568 | tf_op jit(solution)/shard_map/ppermute | solution.py:599
  24.9 5.2 %copy-start.5 = (bf16[3,3,128,128]{3,2,1,0:T(8,128)(2,1)S(1)}, bf16[3,3,128,128]{3,2,1,0:T(8,128)(2,1)}, u32[]{:S(2)}) copy-start(bf16[3,3,128,128]{3,2,1,0:T(8,128)(2,1)} %weight_ref.6) | copy-start | bytes 884740
  24.9 21.6 %collective-permute-start.4 = (bf16[2,960,128]{2,1,0:T(8,128)(2,1)}, bf16[2,960,128]{2,1,0:T(8,128)(2,1)S(1)}, u32[]{:S(2)}, u32[]{:S(2)}) collective-permute-start(bf16[2,960,128]{2,1,0:T(8,128)(2,1)} %get-tuple-element.60), channel_id=1, source_target_pairs={{0,6},{2,4},{4,2},{6,0},{8,14},{10,12},{12,10},{14,8},{16,22},{18,... | collective-permute-start | bytes 1474568 | tf_op jit(solution)/shard_map/ppermute | solution.py:599
  26.6 19.9 %copy-start.6 = (bf16[2,2,544,128]{3,2,1,0:T(8,128)(2,1)S(1)}, bf16[2,2,544,128]{3,2,1,0:T(8,128)(2,1)}, u32[]{:S(2)}) copy-start(bf16[2,2,544,128]{3,2,1,0:T(8,128)(2,1)} %get-tuple-element.76) | copy-start | bytes 1671172
  26.6 23.3 %copy-start = (bf16[2,960,128]{2,1,0:T(8,128)(2,1)S(1)}, bf16[2,960,128]{2,1,0:T(8,128)(2,1)}, u32[]{:S(2)}) copy-start(bf16[2,960,128]{2,1,0:T(8,128)(2,1)} %get-tuple-element.69.refs_0_) | copy-start | bytes 1474564
  26.7 28.4 %collective-permute-start.8 = (bf16[2,2,416,128]{3,2,1,0:T(8,128)(2,1)}, bf16[2,2,416,128]{3,2,1,0:T(8,128)(2,1)S(1)}, u32[]{:S(2)}, u32[]{:S(2)}) collective-permute-start(bf16[2,2,416,128]{3,2,1,0:T(8,128)(2,1)} %get-tuple-element.64), channel_id=1, source_target_pairs={{0,4},{4,0},{8,12},{12,8},{16,20},{20,16},{24,28},{28,24},{1,5},{5... | collective-permute-start | bytes 1277960 | tf_op jit(solution)/shard_map/ppermute | solution.py:608
  30.3 23.3 %copy-start.7 = (bf16[2,960,128]{2,1,0:T(8,128)(2,1)S(1)}, bf16[2,960,128]{2,1,0:T(8,128)(2,1)}, u32[]{:S(2)}) copy-start(bf16[2,960,128]{2,1,0:T(8,128)(2,1)} %get-tuple-element.63) | copy-start | bytes 1474564
  46.5 21.2 %collective-permute-start.15 = (bf16[2,2,544,128]{3,2,1,0:T(8,128)(2,1)S(1)}, bf16[2,2,544,128]{3,2,1,0:T(8,128)(2,1)S(1)}, u32[]{:S(2)}, u32[]{:S(2)}) collective-permute-start(bf16[2,2,544,128]{3,2,1,0:T(8,128)(2,1)S(1)} %copy-done.6), channel_id=1, source_target_pairs={{0,4},{4,0},{8,12},{12,8},{16,20},{20,16},{24,28},{28,24},{1,5},{5... | collective-permute-start | bytes 1671176 | tf_op jit(solution)/shard_map/ppermute | solution.py:608
  50.0 12.1 %collective-permute-start.10 = (bf16[2,960,128]{2,1,0:T(8,128)(2,1)S(1)}, bf16[2,960,128]{2,1,0:T(8,128)(2,1)S(1)}, u32[]{:S(2)}, u32[]{:S(2)}) collective-permute-start(bf16[2,960,128]{2,1,0:T(8,128)(2,1)S(1)} %select_select_fusion), channel_id=1, source_target_pairs={{0,8},{2,10},{4,12},{6,14},{8,16},{10,18},{12,20},{14,22},{16,24},... | collective-permute-start | bytes 1474568 | tf_op jit(solution)/shard_map/ppermute | solution.py:614
  53.6 8.6 %copy-start.1 = (bf16[2,960,128]{2,1,0:T(8,128)(2,1)S(1)}, bf16[2,960,128]{2,1,0:T(8,128)(2,1)}, u32[]{:S(2)}) copy-start(bf16[2,960,128]{2,1,0:T(8,128)(2,1)} %get-tuple-element.62.refs_4_) | copy-start | bytes 1474564
  53.6 8.6 %collective-permute-start.7 = (bf16[2,960,128]{2,1,0:T(8,128)(2,1)S(1)}, bf16[2,960,128]{2,1,0:T(8,128)(2,1)S(1)}, u32[]{:S(2)}, u32[]{:S(2)}) collective-permute-start(bf16[2,960,128]{2,1,0:T(8,128)(2,1)S(1)} %copy-done.7), channel_id=1, source_target_pairs={{0,2},{4,6},{8,10},{12,14},{16,18},{20,22},{24,26},{28,30},{1,3},{... | collective-permute-start | bytes 1474568 | tf_op jit(solution)/shard_map/ppermute | solution.py:609
  56.1 6.0 %collective-permute-start.9 = (bf16[2,416,128]{2,1,0:T(8,128)(2,1)S(1)}, bf16[2,416,128]{2,1,0:T(8,128)(2,1)S(1)}, u32[]{:S(2)}, u32[]{:S(2)}) collective-permute-start(bf16[2,416,128]{2,1,0:T(8,128)(2,1)S(1)} %slice_bitcast_fusion.1), channel_id=1, source_target_pairs={{0,2},{4,6},{8,10},{12,14},{16,18},{20,22},{24,26},{28,30},{1,3},{... | collective-permute-start | bytes 638984 | tf_op jit(solution)/shard_map/ppermute | solution.py:617
  63.3 23.8 %collective-permute-start.11 = (bf16[8,416,128]{2,1,0:T(8,128)(2,1)S(1)}, bf16[8,416,128]{2,1,0:T(8,128)(2,1)S(1)}, u32[]{:S(2)}, u32[]{:S(2)}) collective-permute-start(bf16[8,416,128]{2,1,0:T(8,128)(2,1)S(1)} %early.4.own_ref), channel_id=1, source_target_pairs={{0,8},{2,10},{4,12},{6,14},{8,16},{10,18},{12,20},{14,22},{16,24},... | collective-permute-start | bytes 2555912 | tf_op jit(solution)/shard_map/ppermute | solution.py:625
  67.8 2.5 %collective-permute-start.16 = (bf16[2,544,128]{2,1,0:T(8,128)(2,1)S(1)}, bf16[2,544,128]{2,1,0:T(8,128)(2,1)S(1)}, u32[]{:S(2)}, u32[]{:S(2)}) collective-permute-start(bf16[2,544,128]{2,1,0:T(8,128)(2,1)S(1)} %slice_bitcast_fusion), channel_id=1, source_target_pairs={{0,2},{4,6},{8,10},{12,14},{16,18},{20,22},{24,26},{28,30},{1,3},{... | collective-permute-start | bytes 835592 | tf_op jit(solution)/shard_map/ppermute | solution.py:617
  71.0 24.3 %collective-permute-start.17 = (bf16[8,256,128]{2,1,0:T(8,128)(2,1)S(1)}, bf16[8,256,128]{2,1,0:T(8,128)(2,1)S(1)}, u32[]{:S(2)}, u32[]{:S(2)}) collective-permute-start(bf16[8,256,128]{2,1,0:T(8,128)(2,1)S(1)} %early.5.own_ref), channel_id=1, source_target_pairs={{0,8},{2,10},{4,12},{6,14},{8,16},{10,18},{12,20},{14,22},{16,24},... | collective-permute-start | bytes 1572872 | tf_op jit(solution)/shard_map/ppermute | solution.py:625
  87.7 11.5 %collective-permute-start.14 = (bf16[2,416,128]{2,1,0:T(8,128)(2,1)S(1)}, bf16[2,416,128]{2,1,0:T(8,128)(2,1)S(1)}, u32[]{:S(2)}, u32[]{:S(2)}) collective-permute-start(bf16[2,416,128]{2,1,0:T(8,128)(2,1)S(1)} %get-tuple-element.75), channel_id=1, source_target_pairs={{0,6},{2,4},{4,2},{6,0},{8,14},{10,12},{12,10},{14,8},{16,22},{18,... | collective-permute-start | bytes 638984 | tf_op jit(solution)/shard_map/ppermute | solution.py:599
  87.8 12.1 %collective-permute-start.13 = (bf16[2,416,128]{2,1,0:T(8,128)(2,1)S(1)}, bf16[2,416,128]{2,1,0:T(8,128)(2,1)S(1)}, u32[]{:S(2)}, u32[]{:S(2)}) collective-permute-start(bf16[2,416,128]{2,1,0:T(8,128)(2,1)S(1)} %get-tuple-element.74), channel_id=1, source_target_pairs={{0,4},{2,6},{4,0},{6,2},{8,12},{10,14},{12,8},{14,10},{16,20},{18,... | collective-permute-start | bytes 638984 | tf_op jit(solution)/shard_map/ppermute | solution.py:599
  89.3 12.9 %collective-permute-start.12 = (bf16[2,416,128]{2,1,0:T(8,128)(2,1)S(1)}, bf16[2,416,128]{2,1,0:T(8,128)(2,1)S(1)}, u32[]{:S(2)}, u32[]{:S(2)}) collective-permute-start(bf16[2,416,128]{2,1,0:T(8,128)(2,1)S(1)} %get-tuple-element.73), channel_id=1, source_target_pairs={{0,2},{2,0},{4,6},{6,4},{8,10},{10,8},{12,14},{14,12},{16,18},{18,... | collective-permute-start | bytes 638984 | tf_op jit(solution)/shard_map/ppermute | solution.py:599
  90.3 12.4 %collective-permute-start.21 = (bf16[8,160,128]{2,1,0:T(8,128)(2,1)S(1)}, bf16[8,160,128]{2,1,0:T(8,128)(2,1)S(1)}, u32[]{:S(2)}, u32[]{:S(2)}) collective-permute-start(bf16[8,160,128]{2,1,0:T(8,128)(2,1)S(1)} %early.6.own_ref), channel_id=1, source_target_pairs={{0,8},{2,10},{4,12},{6,14},{8,16},{10,18},{12,20},{14,22},{16,24},... | collective-permute-start | bytes 983048 | tf_op jit(solution)/shard_map/ppermute | solution.py:625
  95.3 14.4 %collective-permute-start.25 = (bf16[8,128,128]{2,1,0:T(8,128)(2,1)S(1)}, bf16[8,128,128]{2,1,0:T(8,128)(2,1)S(1)}, u32[]{:S(2)}, u32[]{:S(2)}) collective-permute-start(bf16[8,128,128]{2,1,0:T(8,128)(2,1)S(1)} %early.7.own_ref), channel_id=1, source_target_pairs={{0,8},{2,10},{4,12},{6,14},{8,16},{10,18},{12,20},{14,22},{16,24},... | collective-permute-start | bytes 786440 | tf_op jit(solution)/shard_map/ppermute | solution.py:625
  99.2 4.5 %collective-permute-start.20 = (bf16[2,256,128]{2,1,0:T(8,128)(2,1)S(1)}, bf16[2,256,128]{2,1,0:T(8,128)(2,1)S(1)}, u32[]{:S(2)}, u32[]{:S(2)}) collective-permute-start(bf16[2,256,128]{2,1,0:T(8,128)(2,1)S(1)} %get-tuple-element.84), channel_id=1, source_target_pairs={{0,6},{2,4},{4,2},{6,0},{8,14},{10,12},{12,10},{14,8},{16,22},{18,... | collective-permute-start | bytes 393224 | tf_op jit(solution)/shard_map/ppermute | solution.py:599
  99.9 8.2 %collective-permute-start.19 = (bf16[2,256,128]{2,1,0:T(8,128)(2,1)S(1)}, bf16[2,256,128]{2,1,0:T(8,128)(2,1)S(1)}, u32[]{:S(2)}, u32[]{:S(2)}) collective-permute-start(bf16[2,256,128]{2,1,0:T(8,128)(2,1)S(1)} %get-tuple-element.82), channel_id=1, source_target_pairs={{0,4},{2,6},{4,0},{6,2},{8,12},{10,14},{12,8},{14,10},{16,20},{18,... | collective-permute-start | bytes 393224 | tf_op jit(solution)/shard_map/ppermute | solution.py:599
  102.2 6.3 %collective-permute-start.18 = (bf16[2,256,128]{2,1,0:T(8,128)(2,1)S(1)}, bf16[2,256,128]{2,1,0:T(8,128)(2,1)S(1)}, u32[]{:S(2)}, u32[]{:S(2)}) collective-permute-start(bf16[2,256,128]{2,1,0:T(8,128)(2,1)S(1)} %get-tuple-element.80), channel_id=1, source_target_pairs={{0,2},{2,0},{4,6},{6,4},{8,10},{10,8},{12,14},{14,12},{16,18},{18,... | collective-permute-start | bytes 393224 | tf_op jit(solution)/shard_map/ppermute | solution.py:599
  103.7 6.4 %collective-permute-start.24 = (bf16[2,160,128]{2,1,0:T(8,128)(2,1)S(1)}, bf16[2,160,128]{2,1,0:T(8,128)(2,1)S(1)}, u32[]{:S(2)}, u32[]{:S(2)}) collective-permute-start(bf16[2,160,128]{2,1,0:T(8,128)(2,1)S(1)} %get-tuple-element.92), channel_id=1, source_target_pairs={{0,6},{2,4},{4,2},{6,0},{8,14},{10,12},{12,10},{14,8},{16,22},{18,... | collective-permute-start | bytes 245768 | tf_op jit(solution)/shard_map/ppermute | solution.py:599
  108.1 4.4 %collective-permute-start.23 = (bf16[2,160,128]{2,1,0:T(8,128)(2,1)S(1)}, bf16[2,160,128]{2,1,0:T(8,128)(2,1)S(1)}, u32[]{:S(2)}, u32[]{:S(2)}) collective-permute-start(bf16[2,160,128]{2,1,0:T(8,128)(2,1)S(1)} %get-tuple-element.90), channel_id=1, source_target_pairs={{0,4},{2,6},{4,0},{6,2},{8,12},{10,14},{12,8},{14,10},{16,20},{18,... | collective-permute-start | bytes 245768 | tf_op jit(solution)/shard_map/ppermute | solution.py:599
  108.6 5.0 %collective-permute-start.22 = (bf16[2,160,128]{2,1,0:T(8,128)(2,1)S(1)}, bf16[2,160,128]{2,1,0:T(8,128)(2,1)S(1)}, u32[]{:S(2)}, u32[]{:S(2)}) collective-permute-start(bf16[2,160,128]{2,1,0:T(8,128)(2,1)S(1)} %get-tuple-element.88), channel_id=1, source_target_pairs={{0,2},{2,0},{4,6},{6,4},{8,10},{10,8},{12,14},{14,12},{16,18},{18,... | collective-permute-start | bytes 245768 | tf_op jit(solution)/shard_map/ppermute | solution.py:599
  110.0 4.3 %collective-permute-start.28 = (bf16[2,128,128]{2,1,0:T(8,128)(2,1)S(1)}, bf16[2,128,128]{2,1,0:T(8,128)(2,1)S(1)}, u32[]{:S(2)}, u32[]{:S(2)}) collective-permute-start(bf16[2,128,128]{2,1,0:T(8,128)(2,1)S(1)} %get-tuple-element.100), channel_id=1, source_target_pairs={{0,6},{2,4},{4,2},{6,0},{8,14},{10,12},{12,10},{14,8},{16,22},{18,... | collective-permute-start | bytes 196616 | tf_op jit(solution)/shard_map/ppermute | solution.py:599
  112.6 4.3 %collective-permute-start.27 = (bf16[2,128,128]{2,1,0:T(8,128)(2,1)S(1)}, bf16[2,128,128]{2,1,0:T(8,128)(2,1)S(1)}, u32[]{:S(2)}, u32[]{:S(2)}) collective-permute-start(bf16[2,128,128]{2,1,0:T(8,128)(2,1)S(1)} %get-tuple-element.98), channel_id=1, source_target_pairs={{0,4},{2,6},{4,0},{6,2},{8,12},{10,14},{12,8},{14,10},{16,20},{18,... | collective-permute-start | bytes 196616 | tf_op jit(solution)/shard_map/ppermute | solution.py:599
  113.5 3.3 %collective-permute-start.26 = (bf16[2,128,128]{2,1,0:T(8,128)(2,1)S(1)}, bf16[2,128,128]{2,1,0:T(8,128)(2,1)S(1)}, u32[]{:S(2)}, u32[]{:S(2)}) collective-permute-start(bf16[2,128,128]{2,1,0:T(8,128)(2,1)S(1)} %get-tuple-element.96), channel_id=1, source_target_pairs={{0,2},{2,0},{4,6},{6,4},{8,10},{10,8},{12,14},{14,12},{16,18},{18,... | collective-permute-start | bytes 196616 | tf_op jit(solution)/shard_map/ppermute | solution.py:599

commit v5 on v4

--- a/solution.py
+++ b/solution.py
@@ -9,7 +9,8 @@
 
 GROUPS = 32
 SPAN = 8
-GUEST_PARTS = (26, 34)
+OWN_PARTS = (42, 18)
+GUEST_PARTS = (42, 18)
 OUT_PARTS = (26, 16, 10, 8)
 VMEM = pltpu.VMEM
 ANY = pl.ANY
@@ -198,8 +199,8 @@
     return value
 
 
-def norm_frame(conv_ref, frame, sums, count, gain_ref, shift_ref, hidden_ref, alive=None):
-    band, _, ch = conv_ref.shape[1:]
+def norm_of(sums, count, gain_ref, shift_ref):
+    ch = gain_ref.shape[-1]
     total = [
         over_groups(jnp.broadcast_to(jnp.sum(x, axis=0, keepdims=True), (8, ch)), ch // GROUPS)
         for x in sums
@@ -210,13 +211,11 @@
     mean = mean[:1]
     shift = shift_ref[...]
 
-    @pl.loop(0, band)
-    def _(row):
-        v = (conv_ref[frame, row] - mean) * scale + shift
-        v = 0.5 * v * (1.0 + jnp.tanh(0.5 * v))
-        if alive is not None:
-            v = jnp.where(alive, v, 0.0)
-        hidden_ref[frame, row] = v.astype(BF16)
+    def apply(value):
+        v = (value - mean) * scale + shift
+        return (0.5 * v * (1.0 + jnp.tanh(0.5 * v))).astype(BF16)
+
+    return apply
 
 
 def piece_copies(hidden_ref, frame, outs, members, sem):
@@ -240,7 +239,7 @@
 
 def norm_kernel(count, members, rows, conv_ref, own_ref, other_ref, gain_ref, shift_ref, *refs):
     row_refs, packet_ref, (hidden_ref, sem) = refs[:rows], refs[rows], refs[-2:]
-    outs = [[ref] for ref in refs[rows + 1 : -2]]
+    outs = [refs[rows + 1 + k : -2 : members] for k in range(members)]
     frames, band, width, ch = conv_ref.shape
     for frame in range(frames):
         sums = [own_ref[frame, i] + other_ref[frame, i] for i in range(2)]
@@ -255,7 +254,12 @@
                 packet_ref[frame, at : at + 16] = jnp.concatenate(
                     [short, jnp.zeros_like(short)], axis=0
                 ).astype(BF16)
-        norm_frame(conv_ref, frame, sums, count, gain_ref, shift_ref, hidden_ref)
+        apply = norm_of(sums, count, gain_ref, shift_ref)
+
+        @pl.loop(0, band)
+        def _(row):
+            hidden_ref[frame, row] = apply(conv_ref[frame, row])
+
         for copy in piece_copies(hidden_ref, frame, outs, members, sem):
             copy.start()
     for frame in range(frames):
@@ -263,18 +267,18 @@
             copy.wait()
 
 
-def norm_call(conv, own, other, halo_rows, gain, shift, count, members):
+def norm_call(conv, own, other, halo_rows, gain, shift, count, members, sizes):
     frames, band, width, ch = conv.shape
     rows = len(halo_rows)
     return pl.pallas_call(
         functools.partial(norm_kernel, count, members, rows),
         in_specs=[vspec()] * (5 + rows),
-        out_specs=[vspec()] + [hspec()] * members,
+        out_specs=[vspec()] + [hspec()] * (members * len(sizes)),
         out_shape=[jax.ShapeDtypeStruct((frames, rows * width + 96, ch), BF16)]
-        + [pltpu.HBM((frames, band * width // members, ch), BF16)] * members,
+        + [pltpu.HBM((frames, size, ch), BF16) for size in sizes for _ in range(members)],
         scratch_shapes=[
             VMEM((frames, band, width, ch), BF16),
-            pltpu.SemaphoreType.DMA((members, frames)),
+            pltpu.SemaphoreType.DMA((members * len(sizes), frames)),
         ],
         compiler_params=params(16),
         cost_estimate=COST,
@@ -283,8 +287,8 @@
 
 
 def guest_kernel(count, members, video_hbm, packet_ref, weight_ref, gain_ref, shift_ref, *refs):
-    keep_ref, mate_ref, *away_refs = refs[:-6]
-    video_ref, conv_ref, hidden_ref, wide_ref, in_sem, sem = refs[-6:]
+    keep_ref, mate_ref, *away_refs = refs[:-5]
+    video_ref, hidden_ref, wide_ref, in_sem, sem = refs[-5:]
     outs = [[keep_ref], [mate_ref]] + [[ref.at[k] for ref in away_refs] for k in range(2)]
     frames, band, width, ch = video_hbm.shape
     rows = (packet_ref.shape[1] - 96) // width
@@ -301,9 +305,15 @@
         widen(weight_ref, wide_ref)
         for frame in range(frames):
             loads[frame].wait()
+            sums = []
+            for i in range(2):
+                at = rows * width + i * 48
+                parts = packet_ref[frame, at : at + 48].astype(F32)
+                sums.append(parts[:16] + parts[16:32] + parts[32:])
+            apply = norm_of(sums, count, gain_ref, shift_ref)
 
             def write(row, value):
-                conv_ref[frame, row] = value
+                hidden_ref[frame, row] = apply(value)
 
             read = padded_read(
                 band,
@@ -312,12 +322,6 @@
                 lambda: packet_ref[frame, (rows - 1) * width : rows * width],
             )
             conv_rows(band, read, wide_ref, write)
-            sums = []
-            for i in range(2):
-                at = rows * width + i * 48
-                parts = packet_ref[frame, at : at + 48].astype(F32)
-                sums.append(parts[:16] + parts[16:32] + parts[32:])
-            norm_frame(conv_ref, frame, sums, count, gain_ref, shift_ref, hidden_ref)
             for copy in piece_copies(hidden_ref, frame, outs, members, sem):
                 copy.start()
         for frame in range(frames):
@@ -346,7 +350,6 @@
         out_shape=[pltpu.HBM(shape, BF16) for shape in shapes],
         scratch_shapes=[
             VMEM(video.shape, BF16),
-            VMEM(video.shape, F32),
             VMEM(video.shape, BF16),
             VMEM((4 * ch, 6 * ch), BF16),
             pltpu.SemaphoreType.DMA((frames,)),
@@ -406,7 +409,7 @@
         pair(lambda t: u0_ref[t], write1, time, 0, wide_ref)
 
 
-def ahead_call(own, wide):
+def ahead_call(own, wide, cost):
     members = len(own)
     _, size, ch = own[0].shape
     return pl.pallas_call(
@@ -416,7 +419,7 @@
         out_shape=jax.ShapeDtypeStruct((SPAN - 2, size, ch), BF16),
         scratch_shapes=[VMEM((SPAN, size, ch), BF16)],
         compiler_params=params(16),
-        cost_estimate=LONG,
+        cost_estimate=cost,
         name="ahead",
     )(*own, wide)
 
@@ -460,8 +463,12 @@
             pair(read1, write2, time + odd, 1, wide_ref)
 
 
-def early_call(sources, ahead, wide, members, first, size):
+def early_call(sources, aheads, wide, members, first, size):
     plan, arrays = [], []
+    start, ahead = first, aheads[0]
+    for block in aheads[1:]:
+        if start >= ahead.shape[1]:
+            start, ahead = start - ahead.shape[1], block
     for kind, k, blocks in sources:
         at = 0
         for block in blocks:
@@ -473,7 +480,7 @@
             at += rows
     ch = wide.shape[-1] // 2
     return pl.pallas_call(
-        functools.partial(early_kernel, members, plan, first),
+        functools.partial(early_kernel, members, plan, start),
         in_specs=[vspec()] * (len(arrays) + 2),
         out_specs=vspec(),
         out_shape=jax.ShapeDtypeStruct((SPAN, size, ch), BF16),
@@ -514,35 +521,40 @@
     )(own, halo, wide)
 
 
-def place_kernel(members, sizes, *refs):
-    pieces, (out_ref, sem) = refs[: members * len(sizes)], refs[members * len(sizes) :]
+def place_kernel(members, offsets, *refs):
+    count = members * len(offsets)
+    pieces, (out_ref, sem) = refs[:count], refs[-2:]
     me = lax.axis_index("tm") % members
     copies = []
-    offset = 0
-    for i, size in enumerate(sizes):
+    for i, offset in enumerate(offsets):
         for k in range(members):
             n = i * members + k
-            place = out_ref.at[:, me ^ k, pl.ds(offset, size)]
-            copies.append(pltpu.make_async_copy(pieces[n], place, sem.at[n]))
-        offset += size
+            rows = pl.ds(offset, pieces[n].shape[1])
+            copies.append(
+                pltpu.make_async_copy(pieces[n], out_ref.at[:, me ^ k, rows], sem.at[n])
+            )
     for copy in copies:
         copy.start()
     for copy in copies:
         copy.wait()
 
 
-def place_call(pieces, members, sizes):
-    frames, _, ch = pieces[0].shape
-    return pl.pallas_call(
-        functools.partial(place_kernel, members, sizes),
-        in_specs=[vspec()] * len(pieces),
-        out_specs=pl.BlockSpec(memory_space=ANY),
-        out_shape=jax.ShapeDtypeStruct((frames, members, sum(sizes), ch), BF16),
+def place_call(chunks, offsets, quarter, before=None):
+    members = len(chunks[0])
+    frames, _, ch = chunks[0][0].shape
+    pieces = sum(chunks, [])
+    shape = jax.ShapeDtypeStruct((frames, members, quarter, ch), BF16)
+    return pl.pallas_call(
+        functools.partial(place_kernel, members, offsets),
+        in_specs=[vspec()] * len(pieces) + [hspec()] * (before is not None),
+        out_specs=hspec(),
+        out_shape=pltpu.HBM(shape.shape, BF16),
+        input_output_aliases={} if before is None else {len(pieces): 0},
         scratch_shapes=[pltpu.SemaphoreType.DMA((len(pieces),))],
         compiler_params=params(8),
         cost_estimate=COST,
         name="place",
-    )(*pieces)
+    )(*pieces, *([] if before is None else [hbm(before)]))
 
 
 def halo_rows(video):
@@ -584,12 +596,12 @@
     conv, sums = edge_call(conv, above, below, spatial_weight, sums)
     count = band * rows * width * (ch // GROUPS)
     quarter = band * width // members
-    guest_sizes, out_sizes = [
-        [quarter * part // 60 for part in parts] for parts in (GUEST_PARTS, OUT_PARTS)
+    own_sizes, guest_sizes, out_sizes = [
+        [quarter * part // 60 for part in parts] for parts in (OWN_PARTS, GUEST_PARTS, OUT_PARTS)
     ]
     halo_list = [above] if above is below else [above, below]
     packet, *pieces = norm_call(
-        conv, sums, other_sums(sums), halo_list, norm_gain, norm_shift, count, members
+        conv, sums, other_sums(sums), halo_list, norm_gain, norm_shift, count, members, own_sizes
     )
 
     def swap(four, waits=None):
@@ -599,34 +611,53 @@
             got.append(lax.ppermute(value, "tm", swaps[k]))
         return got
 
-    own = swap(pieces)
     guest_packet = lax.ppermute(packet, "tm", guest_pairs)
     keep, mate, *aways = guest_call(
         guest_video, guest_packet, spatial_weight, norm_gain, norm_shift, count, members, guest_sizes
     )
     wide = pack_call(after(temporal_weight, keep))
-    crossed = [lax.ppermute(away, "tm", guest_swaps[2]) for away in aways]
-    guest = [[keep], [lax.ppermute(mate, "tm", guest_swaps[1])], crossed]
-    four = after(own, wide)
-    middle = functools.reduce(
-        lambda acc, k: jnp.where(me == (2 ^ k), four[k], acc), range(1, members), four[0]
-    )
-    halo = lax.ppermute(middle, "tm", onward)
-    ahead = ahead_call(own, after(wide, middle, crossed[0]))
-    guest.append(
-        [lax.ppermute(after(block[1], ahead), "tm", guest_swaps[1]) for block in crossed]
-    )
-    sources = [("own", k, [own[k]]) for k in range(members)]
-    sources += [("guest", k, guest[k]) for k in range(members)]
-    sources.append(("middle", 0, [halo]))
-    results, passed, first = [], [], 0
+    sources = [(kind, k, []) for kind in ("own", "guest") for k in range(members)]
+    sources.append(("middle", 0, []))
+
+    def add(start, arrays):
+        for (_, _, blocks), array in zip(sources[start:], arrays):
+            blocks.append(array)
+
+    aheads, passed, results = [], [], []
+
+    def block(i, gate):
+        four = pieces[i * members : (i + 1) * members]
+        own = swap(four, [gate] * members if i else None)
+        crossed = lax.ppermute(after(aways[i], own[2]) if i else aways[i], "tm", guest_swaps[2])
+        four = own if i else after(own, wide)
+        middle = functools.reduce(
+            lambda acc, k: jnp.where(me == (2 ^ k), four[k], acc), range(1, members), four[0]
+        )
+        add(0, own)
+        add(2 * members, [lax.ppermute(middle, "tm", onward)])
+        if i == 0:
+            add(members, [keep, lax.ppermute(after(mate, wide), "tm", guest_swaps[1])])
+        waits = [middle] if i else [middle, crossed]
+        aheads.append(ahead_call(own, after(wide, *waits), COST if i else LONG))
+        forward = crossed[1] if i else after(crossed[1], aheads[0])
+        add(members + 2, [crossed, lax.ppermute(forward, "tm", guest_swaps[1])])
+
+    block(0, None)
+    first = 0
     for i, size in enumerate(out_sizes):
-        u2 = early_call(sources, ahead, wide, members, first, size)
-        passed.append(lax.ppermute(after(u2, passed[-2]) if i > 1 else u2, "tm", onward))
-        late = late_call(u2, passed[-1], wide, members)
-        results.append(swap(late, results[-1] if results else None))
+        u2 = early_call(sources, aheads, wide, members, first, size)
+        if i == 0:
+            block(1, aheads[0])
+        if i > 1:
+            u2 = after(u2, passed[0] if i == 2 else late[0])
+        passed.append(lax.ppermute(u2, "tm", onward))
+        following = late_call(u2, passed[-1], wide, members)
+        results.append(swap(following, results[-1] if results else None))
+        late = following if i < 2 else late
         first += size
-    out = place_call(sum(results, []), members, out_sizes)
+    offsets = [sum(out_sizes[:i]) for i in range(len(out_sizes))]
+    out = place_call(results[:2], offsets[:2], quarter)
+    out = place_call(results[2:], offsets[2:], quarter, out)
     return out.reshape(frames, band, width, ch)
 
 

time: 119 us -> 115 us (0.966)
  waiting for transfers between devices: 46.8 us -> 37.7 us
  starting transfers between devices: 51 us -> 55.1 us
    ppermute x10 -> x11, waiting for transfers between devices: 18.9 us -> 9.38 us  [the longest x4 5.11 us: body(): passed.append(lax.ppermute(u2, 'tm', onward))]
    ppermute x10 -> x11, starting transfers between devices: 30 us -> 35.8 us  [the longest x4 16.8 us: body(): passed.append(lax.ppermute(u2, 'tm', onward))]
    ppermute x15 -> x18, starting transfers between devices: 14.5 us -> 12.8 us  [swap(): got.append(lax.ppermute(value, 'tm', swaps[k]))]
    pallas_call x5 -> x6, Pallas kernels: 4.55 us -> 5.39 us  [the longest x4 3.38 us: early_call(): pl.pallas_call(functools.partial(early_kernel, members, plan, start), in_...]
    ppermute x15 -> x18, waiting for transfers between devices: 26.1 us -> 26.5 us  [swap(): got.append(lax.ppermute(value, 'tm', swaps[k]))]
  transfers between devices with their start and end apart: 29 -> 33, of which waited for: 13 -> 15; matrix products, arithmetic and copies ran while one was open for 1% -> 1% of each run, Pallas kernels for 15% -> 16%
where the time goes in v5:
time: 115 us
  starting transfers between devices  55.1 us (48%)
  waiting for transfers between devices  37.7 us (33%)
  Pallas kernels  19.9 us (17%)
    ppermute x18, waiting for transfers between devices, swap(): got.append(lax.ppermute(value, 'tm', swaps[k]))  26.5 us
    ppermute x4, starting transfers between devices, body(): passed.append(lax.ppermute(u2, 'tm', onward))  16.8 us
    ppermute x18, starting transfers between devices, swap(): got.append(lax.ppermute(value, 'tm', swaps[k]))  12.8 us
    ppermute x2, starting transfers between devices, block(): add(2 * members, [lax.ppermute(middle, 'tm', onward)])  6.94 us
    ppermute x2, starting transfers between devices, block(): lax.ppermute(after(aways[i], own[2]) if i else aways[i], 'tm', guest_swap...  6.83 us
    ppermute x4, waiting for transfers between devices, body(): passed.append(lax.ppermute(u2, 'tm', onward))  5.11 us
    pallas_call x1, Pallas kernels, conv_call(): pl.pallas_call(functools.partial(conv_kernel, band), grid=(frames,), in_s...  4.86 us
    pallas_call x4, Pallas kernels, early_call(): pl.pallas_call(functools.partial(early_kernel, members, plan, start), in_...  3.38 us
  transfers between devices with their start and end apart: 33, of which 15 were waited for; matrix products, arithmetic and copies ran while one was open for 1% of the time, Pallas kernels for 16%

profile of v5, /device:TPU:0, one launch (start us, length us, event | category | flops | bytes accessed | tf_op | source)
XLA Modules:
  0.0 114.6 jit_solution(16288706634679736213)
XLA Ops:
  0.0 0.8 collective-permute-start.5
  0.8 1.0 dynamic-slice_bitcast_fusion
  1.8 3.0 %collective-permute-start = (bf16[2,480,128]{2,1,0:T(8,128)(2,1)S(1)}, bf16[2,480,128]{2,1,0:T(8,128)(2,1)S(1)}, u32[]{:S(2)}, u32[]{:S(2)}) collective-permute-start(bf16[2,480,128]{2,1,0:T(8,128)(2,1)S(1)} %dynamic-slice_bitcast_fusion), channel_id=1, source_target_pairs={{0,1},{1,0},{2,3},{3,2},{4,5},{5,4},{6,7},{7,6},{8,9},{9,8},{10,11... | collective-permute-start | bytes 737288 | tf_op jit(solution)/shard_map/ppermute | solution.py:565
  4.8 4.9 %conv.1 = (f32[2,8,480,128]{3,2,1,0:T(8,128)S(1)}, f32[2,2,8,128]{3,2,1,0:T(8,128)S(1)}) custom-call(bf16[2,8,480,128]{3,2,1,0:T(8,128)(2,1)} %video_ref.1, bf16[3,3,128,128]{3,2,1,0:T(8,128)(2,1)} %weight_ref.5), custom_call_target="tpu_custom_call" | custom-call | flops 20000000000 | tf_op jit(solution)/shard_map/conv/pallas_call | solution.py:117
  9.7 2.1 %edge.1 = (f32[2,8,480,128]{3,2,1,0:T(8,128)S(1)}, f32[2,2,8,128]{3,2,1,0:T(8,128)S(1)}) custom-call(f32[2,8,480,128]{3,2,1,0:T(8,128)S(1)} %get-tuple-element.62.conv_ref, bf16[2,480,128]{2,1,0:T(8,128)(2,1)S(1)} %collective-permute-done.above_ref.below_ref.refs_0_, ...), custom_call_target="tpu_custom_call", output_to_operand_aliasing={{0}: (0, {})} | custom-call | tf_op jit(solution)/shard_map/edge/pallas_call | solution.py:165
  11.8 2.0 %collective-permute-start.1 = (f32[2,2,8,128]{3,2,1,0:T(8,128)S(1)}, f32[2,2,8,128]{3,2,1,0:T(8,128)S(1)}, u32[]{:S(2)}, u32[]{:S(2)}) collective-permute-start(f32[2,2,8,128]{3,2,1,0:T(8,128)S(1)} %get-tuple-element.65.own_ref), channel_id=1, source_target_pairs={{0,1},{1,0},{2,3},{3,2},{4,5},{5,4},{6,7},{7,6},{8,9},{9,8},{10,11... | collective-permute-start | bytes 49160 | tf_op jit(solution)/shard_map/ppermute | solution.py:574
  13.8 1.8 %collective-permute-done.1.other_ref = f32[2,2,8,128]{3,2,1,0:T(8,128)S(1)} collective-permute-done((f32[2,2,8,128]{3,2,1,0:T(8,128)S(1)}, f32[2,2,8,128]{3,2,1,0:T(8,128)S(1)}, u32[]{:S(2)}, u32[]{:S(2)}) %collective-permute-start.1) | collective-permute-done | bytes 16416 | tf_op jit(solution)/shard_map/ppermute | solution.py:574
  15.6 2.8 %norm.1 = (bf16[2,576,128]{2,1,0:T(8,128)(2,1)S(1)}, bf16[2,672,128]{2,1,0:T(8,128)(2,1)}, bf16[2,672,128]{2,1,0:T(8,128)(2,1)}, bf16[2,672,128]{2,1,0:T(8,128)(...) custom-call(f32[2,8,480,128]{3,2,1,0:T(8,128)S(1)} %get-tuple-elemen, ...), custom_call_target="tpu_custom_call" | custom-call | tf_op jit(solution)/shard_map/norm/pallas_call | solution.py:273
  18.4 0.7 collective-permute-start.6
  19.1 4.4 %collective-permute-start.2 = (bf16[2,672,128]{2,1,0:T(8,128)(2,1)}, bf16[2,672,128]{2,1,0:T(8,128)(2,1)S(1)}, u32[]{:S(2)}, u32[]{:S(2)}) collective-permute-start(bf16[2,672,128]{2,1,0:T(8,128)(2,1)} %get-tuple-element.69), channel_id=1, source_target_pairs={{0,2},{2,0},{4,6},{6,4},{8,10},{10,8},{12,14},{14,12},{16,18},{18,... | collective-permute-start | bytes 1032200 | tf_op jit(solution)/shard_map/ppermute | solution.py:611
  23.5 1.5 %collective-permute-start.3 = (bf16[2,672,128]{2,1,0:T(8,128)(2,1)}, bf16[2,672,128]{2,1,0:T(8,128)(2,1)S(1)}, u32[]{:S(2)}, u32[]{:S(2)}) collective-permute-start(bf16[2,672,128]{2,1,0:T(8,128)(2,1)} %get-tuple-element.70), channel_id=1, source_target_pairs={{0,4},{2,6},{4,0},{6,2},{8,12},{10,14},{12,8},{14,10},{16,20},{18,... | collective-permute-start | bytes 1032200 | tf_op jit(solution)/shard_map/ppermute | solution.py:611
  25.0 1.7 %guest.1 = (bf16[2,960,128]{2,1,0:T(8,128)(2,1)}, bf16[2,960,128]{2,1,0:T(8,128)(2,1)}, bf16[2,2,672,128]{3,2,1,0:T(8,128)(2,1)}, bf16[2,2,288,128]{3,2,1,0:T(8,128)(2,1)}) custom-call(bf16[2,8,480,128]{3,2,1,0:T(8,128)(2,1)S(1)} %collective-permute-done.5.video_hbm, bf16[2,576,128]{2,1,0:T(8,128)(2,1)S(1)} %collective-permute-done.6.packet_ref, ...), custom_call_target="tpu_custom_call" | custom-call | flops 20000000000 | tf_op jit(solution)/shard_map/guest/pallas_call | solution.py:346
  26.7 3.5 %collective-permute-start.7 = (bf16[2,2,672,128]{3,2,1,0:T(8,128)(2,1)}, bf16[2,2,672,128]{3,2,1,0:T(8,128)(2,1)S(1)}, u32[]{:S(2)}, u32[]{:S(2)}) collective-permute-start(bf16[2,2,672,128]{3,2,1,0:T(8,128)(2,1)} %get-tuple-element.79), channel_id=1, source_target_pairs={{0,4},{4,0},{8,12},{12,8},{16,20},{20,16},{24,28},{28,24},{1,5},{5... | collective-permute-start | bytes 2064392 | tf_op jit(solution)/shard_map/ppermute | solution.py:631
  30.4 4.3 %collective-permute-done.3.refs_2_ = bf16[2,672,128]{2,1,0:T(8,128)(2,1)S(1)} collective-permute-done((bf16[2,672,128]{2,1,0:T(8,128)(2,1)}, bf16[2,672,128]{2,1,0:T(8,128)(2,1)S(1)}, u32[]{:S(2)}, u32[]{:S(2)}) %collective-permute-start.3) | collective-permute-done | bytes 344096 | tf_op jit(solution)/shard_map/ppermute | solution.py:611
  34.6 5.6 %collective-permute-done.4.refs_3_ = bf16[2,672,128]{2,1,0:T(8,128)(2,1)S(1)} collective-permute-done((bf16[2,672,128]{2,1,0:T(8,128)(2,1)}, bf16[2,672,128]{2,1,0:T(8,128)(2,1)S(1)}, u32[]{:S(2)}, u32[]{:S(2)}) %collective-permute-start.4) | collective-permute-done | bytes 344096 | tf_op jit(solution)/shard_map/ppermute | solution.py:611
  40.3 3.5 %collective-permute-start.16 = (bf16[2,672,128]{2,1,0:T(8,128)(2,1)S(1)}, bf16[2,672,128]{2,1,0:T(8,128)(2,1)S(1)}, u32[]{:S(2)}, u32[]{:S(2)}) collective-permute-start(bf16[2,672,128]{2,1,0:T(8,128)(2,1)S(1)} %select_select_fusion), channel_id=1, source_target_pairs={{0,8},{2,10},{4,12},{6,14},{8,16},{10,18},{12,20},{14,22},{16,24},... | collective-permute-start | bytes 1032200 | tf_op jit(solution)/shard_map/ppermute | solution.py:637
  43.9 2.5 %collective-permute-start.11 = (bf16[2,960,128]{2,1,0:T(8,128)(2,1)S(1)}, bf16[2,960,128]{2,1,0:T(8,128)(2,1)S(1)}, u32[]{:S(2)}, u32[]{:S(2)}) collective-permute-start(bf16[2,960,128]{2,1,0:T(8,128)(2,1)S(1)} %copy-done.7), channel_id=1, source_target_pairs={{0,2},{4,6},{8,10},{12,14},{16,18},{20,22},{24,26},{28,30},{1,3},{... | collective-permute-start | bytes 1474568 | tf_op jit(solution)/shard_map/ppermute | solution.py:639
  46.4 2.2 %collective-permute-done.7.refs_6_ = bf16[2,2,672,128]{3,2,1,0:T(8,128)(2,1)S(1)} collective-permute-done((bf16[2,2,672,128]{3,2,1,0:T(8,128)(2,1)}, bf16[2,2,672,128]{3,2,1,0:T(8,128)(2,1)S(1)}, u32[]{:S(2)}, u32[]{:S(2)}) %collective-permute-start.7) | collective-permute-done | bytes 688160 | tf_op jit(solution)/shard_map/ppermute | solution.py:631
  48.5 0.8 ahead.2.refs_9_
  49.4 1.4 %collective-permute-start.15 = (bf16[2,672,128]{2,1,0:T(8,128)(2,1)S(1)}, bf16[2,672,128]{2,1,0:T(8,128)(2,1)S(1)}, u32[]{:S(2)}, u32[]{:S(2)}) collective-permute-start(bf16[2,672,128]{2,1,0:T(8,128)(2,1)S(1)} %slice_bitcast_fusion), channel_id=1, source_target_pairs={{0,2},{4,6},{8,10},{12,14},{16,18},{20,22},{24,26},{28,30},{1,3},{... | collective-permute-start | bytes 1032200 | tf_op jit(solution)/shard_map/ppermute | solution.py:643
  50.8 1.2 %collective-permute-done.16.refs_8_ = bf16[2,672,128]{2,1,0:T(8,128)(2,1)S(1)} collective-permute-done((bf16[2,672,128]{2,1,0:T(8,128)(2,1)S(1)}, bf16[2,672,128]{2,1,0:T(8,128)(2,1)S(1)}, u32[]{:S(2)}, u32[]{:S(2)}) %collective-permute-start.16) | collective-permute-done | bytes 344096 | tf_op jit(solution)/shard_map/ppermute | solution.py:637
  52.1 1.1 early.5.own_ref
  53.2 4.5 %collective-permute-start.17 = (bf16[8,416,128]{2,1,0:T(8,128)(2,1)S(1)}, bf16[8,416,128]{2,1,0:T(8,128)(2,1)S(1)}, u32[]{:S(2)}, u32[]{:S(2)}) collective-permute-start(bf16[8,416,128]{2,1,0:T(8,128)(2,1)S(1)} %early.5.own_ref), channel_id=1, source_target_pairs={{0,8},{2,10},{4,12},{6,14},{8,16},{10,18},{12,20},{14,22},{16,24},... | collective-permute-start | bytes 2555912 | tf_op jit(solution)/shard_map/ppermute | solution.py:653
  57.7 1.5 %collective-permute-start.9 = (bf16[2,288,128]{2,1,0:T(8,128)(2,1)S(1)}, bf16[2,288,128]{2,1,0:T(8,128)(2,1)S(1)}, u32[]{:S(2)}, u32[]{:S(2)}) collective-permute-start(bf16[2,288,128]{2,1,0:T(8,128)(2,1)S(1)} %copy-done.11), channel_id=1, source_target_pairs={{0,4},{2,6},{4,0},{6,2},{8,12},{10,14},{12,8},{14,10},{16,20},{18,... | collective-permute-start | bytes 442376 | tf_op jit(solution)/shard_map/ppermute | solution.py:611
  59.3 0.7 collective-permute-start.8
  59.9 4.6 %collective-permute-done.9.refs_2_ = bf16[2,288,128]{2,1,0:T(8,128)(2,1)S(1)} collective-permute-done((bf16[2,288,128]{2,1,0:T(8,128)(2,1)S(1)}, bf16[2,288,128]{2,1,0:T(8,128)(2,1)S(1)}, u32[]{:S(2)}, u32[]{:S(2)}) %collective-permute-start.9) | collective-permute-done | bytes 147488 | tf_op jit(solution)/shard_map/ppermute | solution.py:611
  64.5 3.4 %collective-permute-start.12 = (bf16[2,2,288,128]{3,2,1,0:T(8,128)(2,1)S(1)}, bf16[2,2,288,128]{3,2,1,0:T(8,128)(2,1)S(1)}, u32[]{:S(2)}, u32[]{:S(2)}) collective-permute-start(bf16[2,2,288,128]{3,2,1,0:T(8,128)(2,1)S(1)} %copy-done.8), channel_id=1, source_target_pairs={{0,4},{4,0},{8,12},{12,8},{16,20},{20,16},{24,28},{28,24},{1,5},{5... | collective-permute-start | bytes 884744 | tf_op jit(solution)/shard_map/ppermute | solution.py:631
  67.9 3.4 %collective-permute-start.14 = (bf16[2,288,128]{2,1,0:T(8,128)(2,1)S(1)}, bf16[2,288,128]{2,1,0:T(8,128)(2,1)S(1)}, u32[]{:S(2)}, u32[]{:S(2)}) collective-permute-start(bf16[2,288,128]{2,1,0:T(8,128)(2,1)S(1)} %select_select_fusion.1), channel_id=1, source_target_pairs={{0,8},{2,10},{4,12},{6,14},{8,16},{10,18},{12,20},{14,22},{16,24},... | collective-permute-start | bytes 442376 | tf_op jit(solution)/shard_map/ppermute | solution.py:637
  71.4 0.8 early.6.own_ref
  72.2 3.5 %collective-permute-start.19 = (bf16[8,256,128]{2,1,0:T(8,128)(2,1)S(1)}, bf16[8,256,128]{2,1,0:T(8,128)(2,1)S(1)}, u32[]{:S(2)}, u32[]{:S(2)}) collective-permute-start(bf16[8,256,128]{2,1,0:T(8,128)(2,1)S(1)} %early.6.own_ref), channel_id=1, source_target_pairs={{0,8},{2,10},{4,12},{6,14},{8,16},{10,18},{12,20},{14,22},{16,24},... | collective-permute-start | bytes 1572872 | tf_op jit(solution)/shard_map/ppermute | solution.py:653
  75.8 1.3 %collective-permute-start.13 = (bf16[2,288,128]{2,1,0:T(8,128)(2,1)S(1)}, bf16[2,288,128]{2,1,0:T(8,128)(2,1)S(1)}, u32[]{:S(2)}, u32[]{:S(2)}) collective-permute-start(bf16[2,288,128]{2,1,0:T(8,128)(2,1)S(1)} %slice_bitcast_fusion.1), channel_id=1, source_target_pairs={{0,2},{4,6},{8,10},{12,14},{16,18},{20,22},{24,26},{28,30},{1,3},{... | collective-permute-start | bytes 442376 | tf_op jit(solution)/shard_map/ppermute | solution.py:643
  77.1 0.7 late.6
  77.8 1.4 %collective-permute-start.23 = (bf16[2,416,128]{2,1,0:T(8,128)(2,1)S(1)}, bf16[2,416,128]{2,1,0:T(8,128)(2,1)S(1)}, u32[]{:S(2)}, u32[]{:S(2)}) collective-permute-start(bf16[2,416,128]{2,1,0:T(8,128)(2,1)S(1)} %get-tuple-element.101), channel_id=1, source_target_pairs={{0,4},{2,6},{4,0},{6,2},{8,12},{10,14},{12,8},{14,10},{16,20},{18,... | collective-permute-start | bytes 638984 | tf_op jit(solution)/shard_map/ppermute | solution.py:611
  79.2 0.9 collective-permute-done.14.refs_8_
  80.5 0.8 early.4.own_ref
  81.4 4.4 %collective-permute-start.18 = (bf16[8,160,128]{2,1,0:T(8,128)(2,1)S(1)}, bf16[8,160,128]{2,1,0:T(8,128)(2,1)S(1)}, u32[]{:S(2)}, u32[]{:S(2)}) collective-permute-start(bf16[8,160,128]{2,1,0:T(8,128)(2,1)S(1)} %early.4.own_ref), channel_id=1, source_target_pairs={{0,8},{2,10},{4,12},{6,14},{8,16},{10,18},{12,20},{14,22},{16,24},... | collective-permute-start | bytes 983048 | tf_op jit(solution)/shard_map/ppermute | solution.py:653
  85.8 0.6 early.7.own_ref
  86.4 4.9 %collective-permute-done.19.halo_ref = bf16[8,256,128]{2,1,0:T(8,128)(2,1)S(1)} collective-permute-done((bf16[8,256,128]{2,1,0:T(8,128)(2,1)S(1)}, bf16[8,256,128]{2,1,0:T(8,128)(2,1)S(1)}, u32[]{:S(2)}, u32[]{:S(2)}) %collective-permute-start.19) | collective-permute-done | bytes 524320 | tf_op jit(solution)/shard_map/ppermute | solution.py:653
  91.8 4.4 %collective-permute-start.29 = (bf16[8,128,128]{2,1,0:T(8,128)(2,1)S(1)}, bf16[8,128,128]{2,1,0:T(8,128)(2,1)S(1)}, u32[]{:S(2)}, u32[]{:S(2)}) collective-permute-start(bf16[8,128,128]{2,1,0:T(8,128)(2,1)S(1)} %early.7.own_ref), channel_id=1, source_target_pairs={{0,8},{2,10},{4,12},{6,14},{8,16},{10,18},{12,20},{14,22},{16,24},... | collective-permute-start | bytes 786440 | tf_op jit(solution)/shard_map/ppermute | solution.py:653
  96.3 1.5 %collective-permute-start.24 = (bf16[2,256,128]{2,1,0:T(8,128)(2,1)S(1)}, bf16[2,256,128]{2,1,0:T(8,128)(2,1)S(1)}, u32[]{:S(2)}, u32[]{:S(2)}) collective-permute-start(bf16[2,256,128]{2,1,0:T(8,128)(2,1)S(1)} %get-tuple-element.102), channel_id=1, source_target_pairs={{0,4},{2,6},{4,0},{6,2},{8,12},{10,14},{12,8},{14,10},{16,20},{18,... | collective-permute-start | bytes 393224 | tf_op jit(solution)/shard_map/ppermute | solution.py:611
  98.7 3.3 %collective-permute-done.27.refs_7_ = bf16[2,256,128]{2,1,0:T(8,128)(2,1)S(1)} collective-permute-done((bf16[2,256,128]{2,1,0:T(8,128)(2,1)S(1)}, bf16[2,256,128]{2,1,0:T(8,128)(2,1)S(1)}, u32[]{:S(2)}, u32[]{:S(2)}) %collective-permute-start.27) | collective-permute-done | bytes 131104 | tf_op jit(solution)/shard_map/ppermute | solution.py:611
  102.0 2.8 %collective-permute-done.24.refs_6_ = bf16[2,256,128]{2,1,0:T(8,128)(2,1)S(1)} collective-permute-done((bf16[2,256,128]{2,1,0:T(8,128)(2,1)S(1)}, bf16[2,256,128]{2,1,0:T(8,128)(2,1)S(1)}, u32[]{:S(2)}, u32[]{:S(2)}) %collective-permute-start.24) | collective-permute-done | bytes 131104 | tf_op jit(solution)/shard_map/ppermute | solution.py:611
  105.3 1.1 collective-permute-done.28.refs_3_
  106.5 1.0 collective-permute-start.32
  107.4 1.9 %collective-permute-done.25.refs_2_ = bf16[2,160,128]{2,1,0:T(8,128)(2,1)S(1)} collective-permute-done((bf16[2,160,128]{2,1,0:T(8,128)(2,1)S(1)}, bf16[2,160,128]{2,1,0:T(8,128)(2,1)S(1)}, u32[]{:S(2)}, u32[]{:S(2)}) %collective-permute-start.25) | collective-permute-done | bytes 81952 | tf_op jit(solution)/shard_map/ppermute | solution.py:611
  109.6 1.1 place.2.refs_8_
  110.8 2.8 %collective-permute-done.31.refs_6_ = bf16[2,128,128]{2,1,0:T(8,128)(2,1)S(1)} collective-permute-done((bf16[2,128,128]{2,1,0:T(8,128)(2,1)S(1)}, bf16[2,128,128]{2,1,0:T(8,128)(2,1)S(1)}, u32[]{:S(2)}, u32[]{:S(2)}) %collective-permute-start.31) | collective-permute-done | bytes 65568 | tf_op jit(solution)/shard_map/ppermute | solution.py:611
  113.6 0.9 place.3
  (64 shorter events, 3.1 us)
Async XLA Ops:
  0.0 25.0 %collective-permute-start.5 = (bf16[2,8,480,128]{3,2,1,0:T(8,128)(2,1)}, bf16[2,8,480,128]{3,2,1,0:T(8,128)(2,1)S(1)}, u32[]{:S(2)}, u32[]{:S(2)}) collective-permute-start(bf16[2,8,480,128]{3,2,1,0:T(8,128)(2,1)} %video_ref.1), channel_id=1, source_target_pairs={{2,8},{6,12},{10,16},{14,20},{18,24},{22,28},{3,9},{7,13},{11,17},... | collective-permute-start | bytes 5898248 | tf_op jit(solution)/shard_map/ppermute | solution.py:593
  1.8 7.9 %collective-permute-start = (bf16[2,480,128]{2,1,0:T(8,128)(2,1)S(1)}, bf16[2,480,128]{2,1,0:T(8,128)(2,1)S(1)}, u32[]{:S(2)}, u32[]{:S(2)}) collective-permute-start(bf16[2,480,128]{2,1,0:T(8,128)(2,1)S(1)} %dynamic-slice_bitcast_fusion), channel_id=1, source_target_pairs={{0,1},{1,0},{2,3},{3,2},{4,5},{5,4},{6,7},{7,6},{8,9},{9,8},{10,11... | collective-permute-start | bytes 737288 | tf_op jit(solution)/shard_map/ppermute | solution.py:565
  9.7 6.0 %copy-start.4 = (f32[128]{0:T(128)S(1)}, f32[128]{0:T(128)}, u32[]{:S(2)}) copy-start(f32[128]{0:T(128)} %param.7) | copy-start | bytes 1540
  9.7 5.9 %copy-start.5 = (f32[128]{0:T(128)S(1)}, f32[128]{0:T(128)}, u32[]{:S(2)}) copy-start(f32[128]{0:T(128)} %param.8) | copy-start | bytes 1540
  11.8 3.8 %collective-permute-start.1 = (f32[2,2,8,128]{3,2,1,0:T(8,128)S(1)}, f32[2,2,8,128]{3,2,1,0:T(8,128)S(1)}, u32[]{:S(2)}, u32[]{:S(2)}) collective-permute-start(f32[2,2,8,128]{3,2,1,0:T(8,128)S(1)} %get-tuple-element.65.own_ref), channel_id=1, source_target_pairs={{0,1},{1,0},{2,3},{3,2},{4,5},{5,4},{6,7},{7,6},{8,9},{9,8},{10,11... | collective-permute-start | bytes 49160 | tf_op jit(solution)/shard_map/ppermute | solution.py:574
  15.6 9.4 %copy-start.3 = (bf16[3,3,128,128]{3,2,1,0:T(8,128)(2,1)S(1)}, bf16[3,3,128,128]{3,2,1,0:T(8,128)(2,1)}, u32[]{:S(2)}) copy-start(bf16[3,3,128,128]{3,2,1,0:T(8,128)(2,1)} %weight_ref.5) | copy-start | bytes 884740
  18.4 6.6 %collective-permute-start.6 = (bf16[2,576,128]{2,1,0:T(8,128)(2,1)S(1)}, bf16[2,576,128]{2,1,0:T(8,128)(2,1)S(1)}, u32[]{:S(2)}, u32[]{:S(2)}) collective-permute-start(bf16[2,576,128]{2,1,0:T(8,128)(2,1)S(1)} %get-tuple-element.72), channel_id=1, source_target_pairs={{2,8},{6,12},{10,16},{14,20},{18,24},{22,28},{3,9},{7,13},{11,17},... | collective-permute-start | bytes 884744 | tf_op jit(solution)/shard_map/ppermute | solution.py:614
  19.1 11.2 %collective-permute-start.2 = (bf16[2,672,128]{2,1,0:T(8,128)(2,1)}, bf16[2,672,128]{2,1,0:T(8,128)(2,1)S(1)}, u32[]{:S(2)}, u32[]{:S(2)}) collective-permute-start(bf16[2,672,128]{2,1,0:T(8,128)(2,1)} %get-tuple-element.69), channel_id=1, source_target_pairs={{0,2},{2,0},{4,6},{6,4},{8,10},{10,8},{12,14},{14,12},{16,18},{18,... | collective-permute-start | bytes 1032200 | tf_op jit(solution)/shard_map/ppermute | solution.py:611
  23.5 11.1 %collective-permute-start.3 = (bf16[2,672,128]{2,1,0:T(8,128)(2,1)}, bf16[2,672,128]{2,1,0:T(8,128)(2,1)S(1)}, u32[]{:S(2)}, u32[]{:S(2)}) collective-permute-start(bf16[2,672,128]{2,1,0:T(8,128)(2,1)} %get-tuple-element.70), channel_id=1, source_target_pairs={{0,4},{2,6},{4,0},{6,2},{8,12},{10,14},{12,8},{14,10},{16,20},{18,... | collective-permute-start | bytes 1032200 | tf_op jit(solution)/shard_map/ppermute | solution.py:611
  25.0 5.2 %copy-start.6 = (bf16[3,3,128,128]{3,2,1,0:T(8,128)(2,1)S(1)}, bf16[3,3,128,128]{3,2,1,0:T(8,128)(2,1)}, u32[]{:S(2)}) copy-start(bf16[3,3,128,128]{3,2,1,0:T(8,128)(2,1)} %weight_ref.6) | copy-start | bytes 884740
  25.0 15.3 %collective-permute-start.4 = (bf16[2,672,128]{2,1,0:T(8,128)(2,1)}, bf16[2,672,128]{2,1,0:T(8,128)(2,1)S(1)}, u32[]{:S(2)}, u32[]{:S(2)}) collective-permute-start(bf16[2,672,128]{2,1,0:T(8,128)(2,1)} %get-tuple-element.71), channel_id=1, source_target_pairs={{0,6},{2,4},{4,2},{6,0},{8,14},{10,12},{12,10},{14,8},{16,22},{18,... | collective-permute-start | bytes 1032200 | tf_op jit(solution)/shard_map/ppermute | solution.py:611
  26.7 13.6 %copy-start.1 = (bf16[2,672,128]{2,1,0:T(8,128)(2,1)S(1)}, bf16[2,672,128]{2,1,0:T(8,128)(2,1)}, u32[]{:S(2)}) copy-start(bf16[2,672,128]{2,1,0:T(8,128)(2,1)} %get-tuple-element.78.refs_0_) | copy-start | bytes 1032196
  26.7 17.1 %copy-start.7 = (bf16[2,960,128]{2,1,0:T(8,128)(2,1)S(1)}, bf16[2,960,128]{2,1,0:T(8,128)(2,1)}, u32[]{:S(2)}) copy-start(bf16[2,960,128]{2,1,0:T(8,128)(2,1)} %get-tuple-element.87) | copy-start | bytes 1474564
  26.7 21.8 %collective-permute-start.7 = (bf16[2,2,672,128]{3,2,1,0:T(8,128)(2,1)}, bf16[2,2,672,128]{3,2,1,0:T(8,128)(2,1)S(1)}, u32[]{:S(2)}, u32[]{:S(2)}) collective-permute-start(bf16[2,2,672,128]{3,2,1,0:T(8,128)(2,1)} %get-tuple-element.79), channel_id=1, source_target_pairs={{0,4},{4,0},{8,12},{12,8},{16,20},{20,16},{24,28},{28,24},{1,5},{5... | collective-permute-start | bytes 2064392 | tf_op jit(solution)/shard_map/ppermute | solution.py:631
  40.3 11.7 %collective-permute-start.16 = (bf16[2,672,128]{2,1,0:T(8,128)(2,1)S(1)}, bf16[2,672,128]{2,1,0:T(8,128)(2,1)S(1)}, u32[]{:S(2)}, u32[]{:S(2)}) collective-permute-start(bf16[2,672,128]{2,1,0:T(8,128)(2,1)S(1)} %select_select_fusion), channel_id=1, source_target_pairs={{0,8},{2,10},{4,12},{6,14},{8,16},{10,18},{12,20},{14,22},{16,24},... | collective-permute-start | bytes 1032200 | tf_op jit(solution)/shard_map/ppermute | solution.py:637
  43.9 8.2 %copy-start = (bf16[2,960,128]{2,1,0:T(8,128)(2,1)S(1)}, bf16[2,960,128]{2,1,0:T(8,128)(2,1)}, u32[]{:S(2)}) copy-start(bf16[2,960,128]{2,1,0:T(8,128)(2,1)} %get-tuple-element.73.refs_4_) | copy-start | bytes 1474564
  43.9 8.1 %collective-permute-start.11 = (bf16[2,960,128]{2,1,0:T(8,128)(2,1)S(1)}, bf16[2,960,128]{2,1,0:T(8,128)(2,1)S(1)}, u32[]{:S(2)}, u32[]{:S(2)}) collective-permute-start(bf16[2,960,128]{2,1,0:T(8,128)(2,1)S(1)} %copy-done.7), channel_id=1, source_target_pairs={{0,2},{4,6},{8,10},{12,14},{16,18},{20,22},{24,26},{28,30},{1,3},{... | collective-permute-start | bytes 1474568 | tf_op jit(solution)/shard_map/ppermute | solution.py:639
  49.3 8.4 %copy-start.11 = (bf16[2,288,128]{2,1,0:T(8,128)(2,1)S(1)}, bf16[2,288,128]{2,1,0:T(8,128)(2,1)}, u32[]{:S(2)}) copy-start(bf16[2,288,128]{2,1,0:T(8,128)(2,1)} %get-tuple-element.83) | copy-start | bytes 442372
  49.3 9.9 %copy-start.10 = (bf16[2,288,128]{2,1,0:T(8,128)(2,1)S(1)}, bf16[2,288,128]{2,1,0:T(8,128)(2,1)}, u32[]{:S(2)}) copy-start(bf16[2,288,128]{2,1,0:T(8,128)(2,1)} %get-tuple-element.85) | copy-start | bytes 442372
  49.3 9.9 %copy-start.9 = (bf16[2,288,128]{2,1,0:T(8,128)(2,1)S(1)}, bf16[2,288,128]{2,1,0:T(8,128)(2,1)}, u32[]{:S(2)}) copy-start(bf16[2,288,128]{2,1,0:T(8,128)(2,1)} %get-tuple-element.81) | copy-start | bytes 442372
  49.4 15.1 %copy-start.8 = (bf16[2,2,288,128]{3,2,1,0:T(8,128)(2,1)S(1)}, bf16[2,2,288,128]{3,2,1,0:T(8,128)(2,1)}, u32[]{:S(2)}) copy-start(bf16[2,2,288,128]{3,2,1,0:T(8,128)(2,1)} %get-tuple-element.89) | copy-start | bytes 884740
  49.4 18.5 %copy-start.2 = (bf16[2,288,128]{2,1,0:T(8,128)(2,1)S(1)}, bf16[2,288,128]{2,1,0:T(8,128)(2,1)}, u32[]{:S(2)}) copy-start(bf16[2,288,128]{2,1,0:T(8,128)(2,1)} %get-tuple-element.66.refs_0_) | copy-start | bytes 442372
  49.4 2.7 %collective-permute-start.15 = (bf16[2,672,128]{2,1,0:T(8,128)(2,1)S(1)}, bf16[2,672,128]{2,1,0:T(8,128)(2,1)S(1)}, u32[]{:S(2)}, u32[]{:S(2)}) collective-permute-start(bf16[2,672,128]{2,1,0:T(8,128)(2,1)S(1)} %slice_bitcast_fusion), channel_id=1, source_target_pairs={{0,2},{4,6},{8,10},{12,14},{16,18},{20,22},{24,26},{28,30},{1,3},{... | collective-permute-start | bytes 1032200 | tf_op jit(solution)/shard_map/ppermute | solution.py:643
  53.2 23.9 %collective-permute-start.17 = (bf16[8,416,128]{2,1,0:T(8,128)(2,1)S(1)}, bf16[8,416,128]{2,1,0:T(8,128)(2,1)S(1)}, u32[]{:S(2)}, u32[]{:S(2)}) collective-permute-start(bf16[8,416,128]{2,1,0:T(8,128)(2,1)S(1)} %early.5.own_ref), channel_id=1, source_target_pairs={{0,8},{2,10},{4,12},{6,14},{8,16},{10,18},{12,20},{14,22},{16,24},... | collective-permute-start | bytes 2555912 | tf_op jit(solution)/shard_map/ppermute | solution.py:653
  57.7 6.8 %collective-permute-start.9 = (bf16[2,288,128]{2,1,0:T(8,128)(2,1)S(1)}, bf16[2,288,128]{2,1,0:T(8,128)(2,1)S(1)}, u32[]{:S(2)}, u32[]{:S(2)}) collective-permute-start(bf16[2,288,128]{2,1,0:T(8,128)(2,1)S(1)} %copy-done.11), channel_id=1, source_target_pairs={{0,4},{2,6},{4,0},{6,2},{8,12},{10,14},{12,8},{14,10},{16,20},{18,... | collective-permute-start | bytes 442376 | tf_op jit(solution)/shard_map/ppermute | solution.py:611
  59.2 8.6 %collective-permute-start.10 = (bf16[2,288,128]{2,1,0:T(8,128)(2,1)S(1)}, bf16[2,288,128]{2,1,0:T(8,128)(2,1)S(1)}, u32[]{:S(2)}, u32[]{:S(2)}) collective-permute-start(bf16[2,288,128]{2,1,0:T(8,128)(2,1)S(1)} %copy-done.10), channel_id=1, source_target_pairs={{0,6},{2,4},{4,2},{6,0},{8,14},{10,12},{12,10},{14,8},{16,22},{18,... | collective-permute-start | bytes 442376 | tf_op jit(solution)/shard_map/ppermute | solution.py:611
  59.3 8.6 %collective-permute-start.8 = (bf16[2,288,128]{2,1,0:T(8,128)(2,1)S(1)}, bf16[2,288,128]{2,1,0:T(8,128)(2,1)S(1)}, u32[]{:S(2)}, u32[]{:S(2)}) collective-permute-start(bf16[2,288,128]{2,1,0:T(8,128)(2,1)S(1)} %copy-done.9), channel_id=1, source_target_pairs={{0,2},{2,0},{4,6},{6,4},{8,10},{10,8},{12,14},{14,12},{16,18},{18,... | collective-permute-start | bytes 442376 | tf_op jit(solution)/shard_map/ppermute | solution.py:611
  64.5 11.3 %collective-permute-start.12 = (bf16[2,2,288,128]{3,2,1,0:T(8,128)(2,1)S(1)}, bf16[2,2,288,128]{3,2,1,0:T(8,128)(2,1)S(1)}, u32[]{:S(2)}, u32[]{:S(2)}) collective-permute-start(bf16[2,2,288,128]{3,2,1,0:T(8,128)(2,1)S(1)} %copy-done.8), channel_id=1, source_target_pairs={{0,4},{4,0},{8,12},{12,8},{16,20},{20,16},{24,28},{28,24},{1,5},{5... | collective-permute-start | bytes 884744 | tf_op jit(solution)/shard_map/ppermute | solution.py:631
  67.9 12.1 %collective-permute-start.14 = (bf16[2,288,128]{2,1,0:T(8,128)(2,1)S(1)}, bf16[2,288,128]{2,1,0:T(8,128)(2,1)S(1)}, u32[]{:S(2)}, u32[]{:S(2)}) collective-permute-start(bf16[2,288,128]{2,1,0:T(8,128)(2,1)S(1)} %select_select_fusion.1), channel_id=1, source_target_pairs={{0,8},{2,10},{4,12},{6,14},{8,16},{10,18},{12,20},{14,22},{16,24},... | collective-permute-start | bytes 442376 | tf_op jit(solution)/shard_map/ppermute | solution.py:637
  72.2 19.1 %collective-permute-start.19 = (bf16[8,256,128]{2,1,0:T(8,128)(2,1)S(1)}, bf16[8,256,128]{2,1,0:T(8,128)(2,1)S(1)}, u32[]{:S(2)}, u32[]{:S(2)}) collective-permute-start(bf16[8,256,128]{2,1,0:T(8,128)(2,1)S(1)} %early.6.own_ref), channel_id=1, source_target_pairs={{0,8},{2,10},{4,12},{6,14},{8,16},{10,18},{12,20},{14,22},{16,24},... | collective-permute-start | bytes 1572872 | tf_op jit(solution)/shard_map/ppermute | solution.py:653
  75.8 4.7 %collective-permute-start.13 = (bf16[2,288,128]{2,1,0:T(8,128)(2,1)S(1)}, bf16[2,288,128]{2,1,0:T(8,128)(2,1)S(1)}, u32[]{:S(2)}, u32[]{:S(2)}) collective-permute-start(bf16[2,288,128]{2,1,0:T(8,128)(2,1)S(1)} %slice_bitcast_fusion.1), channel_id=1, source_target_pairs={{0,2},{4,6},{8,10},{12,14},{16,18},{20,22},{24,26},{28,30},{1,3},{... | collective-permute-start | bytes 442376 | tf_op jit(solution)/shard_map/ppermute | solution.py:643
  77.8 18.4 %collective-permute-start.26 = (bf16[2,416,128]{2,1,0:T(8,128)(2,1)S(1)}, bf16[2,416,128]{2,1,0:T(8,128)(2,1)S(1)}, u32[]{:S(2)}, u32[]{:S(2)}) collective-permute-start(bf16[2,416,128]{2,1,0:T(8,128)(2,1)S(1)} %get-tuple-element.106), channel_id=1, source_target_pairs={{0,6},{2,4},{4,2},{6,0},{8,14},{10,12},{12,10},{14,8},{16,22},{18,... | collective-permute-start | bytes 638984 | tf_op jit(solution)/shard_map/ppermute | solution.py:611
  77.8 18.4 %collective-permute-start.23 = (bf16[2,416,128]{2,1,0:T(8,128)(2,1)S(1)}, bf16[2,416,128]{2,1,0:T(8,128)(2,1)S(1)}, u32[]{:S(2)}, u32[]{:S(2)}) collective-permute-start(bf16[2,416,128]{2,1,0:T(8,128)(2,1)S(1)} %get-tuple-element.101), channel_id=1, source_target_pairs={{0,4},{2,6},{4,0},{6,2},{8,12},{10,14},{12,8},{14,10},{16,20},{18,... | collective-permute-start | bytes 638984 | tf_op jit(solution)/shard_map/ppermute | solution.py:611
  80.1 17.8 %collective-permute-start.20 = (bf16[2,416,128]{2,1,0:T(8,128)(2,1)S(1)}, bf16[2,416,128]{2,1,0:T(8,128)(2,1)S(1)}, u32[]{:S(2)}, u32[]{:S(2)}) collective-permute-start(bf16[2,416,128]{2,1,0:T(8,128)(2,1)S(1)} %get-tuple-element.96), channel_id=1, source_target_pairs={{0,2},{2,0},{4,6},{6,4},{8,10},{10,8},{12,14},{14,12},{16,18},{18,... | collective-permute-start | bytes 638984 | tf_op jit(solution)/shard_map/ppermute | solution.py:611
  81.4 17.0 %collective-permute-start.18 = (bf16[8,160,128]{2,1,0:T(8,128)(2,1)S(1)}, bf16[8,160,128]{2,1,0:T(8,128)(2,1)S(1)}, u32[]{:S(2)}, u32[]{:S(2)}) collective-permute-start(bf16[8,160,128]{2,1,0:T(8,128)(2,1)S(1)} %early.4.own_ref), channel_id=1, source_target_pairs={{0,8},{2,10},{4,12},{6,14},{8,16},{10,18},{12,20},{14,22},{16,24},... | collective-permute-start | bytes 983048 | tf_op jit(solution)/shard_map/ppermute | solution.py:653
  91.8 13.2 %collective-permute-start.29 = (bf16[8,128,128]{2,1,0:T(8,128)(2,1)S(1)}, bf16[8,128,128]{2,1,0:T(8,128)(2,1)S(1)}, u32[]{:S(2)}, u32[]{:S(2)}) collective-permute-start(bf16[8,128,128]{2,1,0:T(8,128)(2,1)S(1)} %early.7.own_ref), channel_id=1, source_target_pairs={{0,8},{2,10},{4,12},{6,14},{8,16},{10,18},{12,20},{14,22},{16,24},... | collective-permute-start | bytes 786440 | tf_op jit(solution)/shard_map/ppermute | solution.py:653
  96.2 5.8 %collective-permute-start.27 = (bf16[2,256,128]{2,1,0:T(8,128)(2,1)S(1)}, bf16[2,256,128]{2,1,0:T(8,128)(2,1)S(1)}, u32[]{:S(2)}, u32[]{:S(2)}) collective-permute-start(bf16[2,256,128]{2,1,0:T(8,128)(2,1)S(1)} %get-tuple-element.107), channel_id=1, source_target_pairs={{0,6},{2,4},{4,2},{6,0},{8,14},{10,12},{12,10},{14,8},{16,22},{18,... | collective-permute-start | bytes 393224 | tf_op jit(solution)/shard_map/ppermute | solution.py:611
  96.3 8.6 %collective-permute-start.24 = (bf16[2,256,128]{2,1,0:T(8,128)(2,1)S(1)}, bf16[2,256,128]{2,1,0:T(8,128)(2,1)S(1)}, u32[]{:S(2)}, u32[]{:S(2)}) collective-permute-start(bf16[2,256,128]{2,1,0:T(8,128)(2,1)S(1)} %get-tuple-element.102), channel_id=1, source_target_pairs={{0,4},{2,6},{4,0},{6,2},{8,12},{10,14},{12,8},{14,10},{16,20},{18,... | collective-permute-start | bytes 393224 | tf_op jit(solution)/shard_map/ppermute | solution.py:611
  97.8 7.0 %collective-permute-start.21 = (bf16[2,256,128]{2,1,0:T(8,128)(2,1)S(1)}, bf16[2,256,128]{2,1,0:T(8,128)(2,1)S(1)}, u32[]{:S(2)}, u32[]{:S(2)}) collective-permute-start(bf16[2,256,128]{2,1,0:T(8,128)(2,1)S(1)} %get-tuple-element.97), channel_id=1, source_target_pairs={{0,2},{2,0},{4,6},{6,4},{8,10},{10,8},{12,14},{14,12},{16,18},{18,... | collective-permute-start | bytes 393224 | tf_op jit(solution)/shard_map/ppermute | solution.py:611
  102.0 4.4 %collective-permute-start.28 = (bf16[2,160,128]{2,1,0:T(8,128)(2,1)S(1)}, bf16[2,160,128]{2,1,0:T(8,128)(2,1)S(1)}, u32[]{:S(2)}, u32[]{:S(2)}) collective-permute-start(bf16[2,160,128]{2,1,0:T(8,128)(2,1)S(1)} %get-tuple-element.108), channel_id=1, source_target_pairs={{0,6},{2,4},{4,2},{6,0},{8,14},{10,12},{12,10},{14,8},{16,22},{18,... | collective-permute-start | bytes 245768 | tf_op jit(solution)/shard_map/ppermute | solution.py:611
  104.9 4.4 %collective-permute-start.25 = (bf16[2,160,128]{2,1,0:T(8,128)(2,1)S(1)}, bf16[2,160,128]{2,1,0:T(8,128)(2,1)S(1)}, u32[]{:S(2)}, u32[]{:S(2)}) collective-permute-start(bf16[2,160,128]{2,1,0:T(8,128)(2,1)S(1)} %get-tuple-element.103), channel_id=1, source_target_pairs={{0,4},{2,6},{4,0},{6,2},{8,12},{10,14},{12,8},{14,10},{16,20},{18,... | collective-permute-start | bytes 245768 | tf_op jit(solution)/shard_map/ppermute | solution.py:611
  104.9 4.7 %collective-permute-start.22 = (bf16[2,160,128]{2,1,0:T(8,128)(2,1)S(1)}, bf16[2,160,128]{2,1,0:T(8,128)(2,1)S(1)}, u32[]{:S(2)}, u32[]{:S(2)}) collective-permute-start(bf16[2,160,128]{2,1,0:T(8,128)(2,1)S(1)} %get-tuple-element.98), channel_id=1, source_target_pairs={{0,2},{2,0},{4,6},{6,4},{8,10},{10,8},{12,14},{14,12},{16,18},{18,... | collective-permute-start | bytes 245768 | tf_op jit(solution)/shard_map/ppermute | solution.py:611
  106.5 4.3 %collective-permute-start.32 = (bf16[2,128,128]{2,1,0:T(8,128)(2,1)S(1)}, bf16[2,128,128]{2,1,0:T(8,128)(2,1)S(1)}, u32[]{:S(2)}, u32[]{:S(2)}) collective-permute-start(bf16[2,128,128]{2,1,0:T(8,128)(2,1)S(1)} %get-tuple-element.117), channel_id=1, source_target_pairs={{0,6},{2,4},{4,2},{6,0},{8,14},{10,12},{12,10},{14,8},{16,22},{18,... | collective-permute-start | bytes 196616 | tf_op jit(solution)/shard_map/ppermute | solution.py:611
  109.3 4.3 %collective-permute-start.31 = (bf16[2,128,128]{2,1,0:T(8,128)(2,1)S(1)}, bf16[2,128,128]{2,1,0:T(8,128)(2,1)S(1)}, u32[]{:S(2)}, u32[]{:S(2)}) collective-permute-start(bf16[2,128,128]{2,1,0:T(8,128)(2,1)S(1)} %get-tuple-element.115), channel_id=1, source_target_pairs={{0,4},{2,6},{4,0},{6,2},{8,12},{10,14},{12,8},{14,10},{16,20},{18,... | collective-permute-start | bytes 196616 | tf_op jit(solution)/shard_map/ppermute | solution.py:611
  109.6 4.0 %collective-permute-start.30 = (bf16[2,128,128]{2,1,0:T(8,128)(2,1)S(1)}, bf16[2,128,128]{2,1,0:T(8,128)(2,1)S(1)}, u32[]{:S(2)}, u32[]{:S(2)}) collective-permute-start(bf16[2,128,128]{2,1,0:T(8,128)(2,1)S(1)} %get-tuple-element.113), channel_id=1, source_target_pairs={{0,2},{2,0},{4,6},{6,4},{8,10},{10,8},{12,14},{14,12},{16,18},{18,... | collective-permute-start | bytes 196616 | tf_op jit(solution)/shard_map/ppermute | solution.py:611

commit v6 on v5

--- a/solution.py
+++ b/solution.py
@@ -11,7 +11,7 @@
 SPAN = 8
 OWN_PARTS = (42, 18)
 GUEST_PARTS = (42, 18)
-OUT_PARTS = (26, 16, 10, 8)
+OUT_PARTS = (28, 14, 10, 8)
 VMEM = pltpu.VMEM
 ANY = pl.ANY
 F32 = jnp.float32
@@ -134,45 +134,28 @@
 
 
 def edge_kernel(conv_ref, above_ref, below_ref, weight_ref, sums_ref, out_ref, out_sums_ref):
-    side = pl.program_id(1)
+    frames, band = conv_ref.shape[:2]
     row, rows = lax.axis_index("rows"), lax.axis_size("rows")
-
-    @pl.when(side == 0)
-    def _():
-        out_sums_ref[...] = sums_ref[...]
-
-    def add(halo_ref, tap, there):
-        halo = jnp.where(there, halo_ref[0], jnp.zeros_like(halo_ref[0]))
-        taps = jnp.concatenate([weight_ref[tap, col] for col in range(3)], axis=-1)
-        wide = jnp.dot(halo, taps, preferred_element_type=F32)
-        value = conv_ref[0, 0] + shifted_sum(wide)
-        out_ref[0, 0] = value
-        out_sums_ref[0, 0] += fold(value)
-        out_sums_ref[0, 1] += fold(value * value)
-
-    @pl.when(side == 0)
-    def _():
-        add(above_ref, 0, row > 0)
-
-    @pl.when(side == 1)
-    def _():
-        add(below_ref, 2, row < rows - 1)
+    sides = ((0, above_ref, 0, row > 0), (band - 1, below_ref, 2, row < rows - 1))
+    for frame in range(frames):
+        total, square = sums_ref[frame, 0], sums_ref[frame, 1]
+        for place, halo_ref, tap, there in sides:
+            halo = jnp.where(there, halo_ref[frame], jnp.zeros_like(halo_ref[frame]))
+            taps = jnp.concatenate([weight_ref[tap, col] for col in range(3)], axis=-1)
+            wide = jnp.dot(halo, taps, preferred_element_type=F32)
+            value = conv_ref[frame, place] + shifted_sum(wide)
+            out_ref[frame, place] = value
+            total = total + fold(value)
+            square = square + fold(value * value)
+        out_sums_ref[frame, 0] = total
+        out_sums_ref[frame, 1] = square
 
 
 def edge_call(conv, above, below, weight, sums):
-    frames, band, width, ch = conv.shape
-    edge = pl.BlockSpec((1, 1, width, ch), lambda f, side: (f, side * (band - 1), 0, 0))
     return pl.pallas_call(
         edge_kernel,
-        grid=(frames, 2),
-        in_specs=[
-            edge,
-            frame_spec(width, ch),
-            frame_spec(width, ch),
-            pl.BlockSpec(weight.shape, lambda f, side: (0, 0, 0, 0)),
-            frame_spec(2, 8, ch),
-        ],
-        out_specs=[edge, frame_spec(2, 8, ch)],
+        in_specs=[vspec()] * 5,
+        out_specs=[vspec()] * 2,
         out_shape=[
             jax.ShapeDtypeStruct(conv.shape, F32),
             jax.ShapeDtypeStruct(sums.shape, F32),
@@ -181,7 +164,7 @@
         compiler_params=params(12),
         cost_estimate=COST,
         name="edge",
-    )(conv, above, below, hbm(weight), sums)
+    )(conv, above, below, weight, sums)
 
 
 def over_groups(value, per_group):
@@ -286,25 +269,18 @@
     )(conv, own, other, gain.reshape(1, ch), shift.reshape(1, ch), *halo_rows)
 
 
-def guest_kernel(count, members, video_hbm, packet_ref, weight_ref, gain_ref, shift_ref, *refs):
-    keep_ref, mate_ref, *away_refs = refs[:-5]
-    video_ref, hidden_ref, wide_ref, in_sem, sem = refs[-5:]
+def guest_kernel(count, members, video_ref, packet_ref, weight_ref, gain_ref, shift_ref, *refs):
+    keep_ref, mate_ref, *away_refs = refs[:-3]
+    hidden_ref, wide_ref, sem = refs[-3:]
     outs = [[keep_ref], [mate_ref]] + [[ref.at[k] for ref in away_refs] for k in range(2)]
-    frames, band, width, ch = video_hbm.shape
+    frames, band, width, ch = video_ref.shape
     rows = (packet_ref.shape[1] - 96) // width
     here = lax.axis_index("tm")
 
     @pl.when(jnp.logical_and(here >= members, here % 2 == 0))
     def _():
-        loads = [
-            pltpu.make_async_copy(video_hbm.at[f], video_ref.at[f], in_sem.at[f])
-            for f in range(frames)
-        ]
-        for copy in loads:
-            copy.start()
         widen(weight_ref, wide_ref)
         for frame in range(frames):
-            loads[frame].wait()
             sums = []
             for i in range(2):
                 at = rows * width + i * 48
@@ -345,14 +321,12 @@
     shapes = [piece, piece] + [(2, frames, size, ch) for size in sizes]
     return pl.pallas_call(
         functools.partial(guest_kernel, count, members),
-        in_specs=[hspec()] + [vspec()] * 4,
+        in_specs=[vspec()] * 5,
         out_specs=[hspec()] * len(shapes),
         out_shape=[pltpu.HBM(shape, BF16) for shape in shapes],
         scratch_shapes=[
             VMEM(video.shape, BF16),
-            VMEM(video.shape, BF16),
             VMEM((4 * ch, 6 * ch), BF16),
-            pltpu.SemaphoreType.DMA((frames,)),
             pltpu.SemaphoreType.DMA((2 + 2 * len(sizes), frames)),
         ],
         compiler_params=params(24),

time: 115 us -> 114 us (level)
  Pallas kernels: 19.9 us -> 18.6 us
    pallas_call x1, Pallas kernels: 2.11 us -> 0.81 us  [edge_call(): pl.pallas_call(edge_kernel, in_specs=[vspec()] * 5, out_specs=[vspec()] *...]
  transfers between devices with their start and end apart: 33 -> 33, of which waited for: 15 -> 17; matrix products, arithmetic and copies ran while one was open for 1% -> 1% of each run, Pallas kernels for 16% -> 15%
where the time goes in v6:
time: 114 us; the launch traced here: 113 us
  starting transfers between devices  55.4 us (49%)
  waiting for transfers between devices  37.3 us (33%)
  Pallas kernels  18.6 us (16%)
    ppermute x18, waiting for transfers between devices, swap(): got.append(lax.ppermute(value, 'tm', swaps[k]))  26.2 us
    ppermute x4, starting transfers between devices, body(): passed.append(lax.ppermute(u2, 'tm', onward))  17.3 us
    ppermute x18, starting transfers between devices, swap(): got.append(lax.ppermute(value, 'tm', swaps[k]))  12.7 us
    ppermute x2, starting transfers between devices, block(): add(2 * members, [lax.ppermute(middle, 'tm', onward)])  7.2 us
    ppermute x2, starting transfers between devices, block(): lax.ppermute(after(aways[i], own[2]) if i else aways[i], 'tm', guest_swap...  6.81 us
    ppermute x4, waiting for transfers between devices, body(): passed.append(lax.ppermute(u2, 'tm', onward))  5.03 us
    pallas_call x1, Pallas kernels, conv_call(): pl.pallas_call(functools.partial(conv_kernel, band), grid=(frames,), in_s...  4.86 us
    pallas_call x4, Pallas kernels, early_call(): pl.pallas_call(functools.partial(early_kernel, members, plan, start), in_...  3.39 us
  transfers between devices with their start and end apart: 33, of which 17 were waited for; matrix products, arithmetic and copies ran while one was open for 1% of the time, Pallas kernels for 15%

profile of v6, /device:TPU:0, one launch (start us, length us, event | category | flops | bytes accessed | tf_op | source)
XLA Modules:
  0.0 113.1 jit_solution(3752483152172399717)
XLA Ops:
  0.0 0.8 collective-permute-start.5
  0.8 1.0 dynamic-slice_bitcast_fusion
  1.8 3.0 %collective-permute-start = (bf16[2,480,128]{2,1,0:T(8,128)(2,1)S(1)}, bf16[2,480,128]{2,1,0:T(8,128)(2,1)S(1)}, u32[]{:S(2)}, u32[]{:S(2)}) collective-permute-start(bf16[2,480,128]{2,1,0:T(8,128)(2,1)S(1)} %dynamic-slice_bitcast_fusion), channel_id=1, source_target_pairs={{0,1},{1,0},{2,3},{3,2},{4,5},{5,4},{6,7},{7,6},{8,9},{9,8},{10,11... | collective-permute-start | bytes 737288 | tf_op jit(solution)/shard_map/ppermute | solution.py:539
  4.8 4.9 %conv.1 = (f32[2,8,480,128]{3,2,1,0:T(8,128)S(1)}, f32[2,2,8,128]{3,2,1,0:T(8,128)S(1)}) custom-call(bf16[2,8,480,128]{3,2,1,0:T(8,128)(2,1)} %video_ref.1, bf16[3,3,128,128]{3,2,1,0:T(8,128)(2,1)} %weight_ref.5), custom_call_target="tpu_custom_call" | custom-call | flops 20000000000 | tf_op jit(solution)/shard_map/conv/pallas_call | solution.py:117
  9.7 0.8 edge.1
  10.5 2.0 %collective-permute-start.1 = (f32[2,2,8,128]{3,2,1,0:T(8,128)S(1)}, f32[2,2,8,128]{3,2,1,0:T(8,128)S(1)}, u32[]{:S(2)}, u32[]{:S(2)}) collective-permute-start(f32[2,2,8,128]{3,2,1,0:T(8,128)S(1)} %get-tuple-element.65.own_ref), channel_id=1, source_target_pairs={{0,1},{1,0},{2,3},{3,2},{4,5},{5,4},{6,7},{7,6},{8,9},{9,8},{10,11... | collective-permute-start | bytes 49160 | tf_op jit(solution)/shard_map/ppermute | solution.py:548
  12.5 1.8 %collective-permute-done.1.other_ref = f32[2,2,8,128]{3,2,1,0:T(8,128)S(1)} collective-permute-done((f32[2,2,8,128]{3,2,1,0:T(8,128)S(1)}, f32[2,2,8,128]{3,2,1,0:T(8,128)S(1)}, u32[]{:S(2)}, u32[]{:S(2)}) %collective-permute-start.1) | collective-permute-done | bytes 16416 | tf_op jit(solution)/shard_map/ppermute | solution.py:548
  14.3 2.8 %norm.1 = (bf16[2,576,128]{2,1,0:T(8,128)(2,1)S(1)}, bf16[2,672,128]{2,1,0:T(8,128)(2,1)}, bf16[2,672,128]{2,1,0:T(8,128)(2,1)}, bf16[2,672,128]{2,1,0:T(8,128)(...) custom-call(f32[2,8,480,128]{3,2,1,0:T(8,128)S(1)} %get-tuple-elemen, ...), custom_call_target="tpu_custom_call" | custom-call | tf_op jit(solution)/shard_map/norm/pallas_call | solution.py:256
  17.1 0.7 collective-permute-start.6
  17.8 4.4 %collective-permute-start.2 = (bf16[2,672,128]{2,1,0:T(8,128)(2,1)}, bf16[2,672,128]{2,1,0:T(8,128)(2,1)S(1)}, u32[]{:S(2)}, u32[]{:S(2)}) collective-permute-start(bf16[2,672,128]{2,1,0:T(8,128)(2,1)} %get-tuple-element.69), channel_id=1, source_target_pairs={{0,2},{2,0},{4,6},{6,4},{8,10},{10,8},{12,14},{14,12},{16,18},{18,... | collective-permute-start | bytes 1032200 | tf_op jit(solution)/shard_map/ppermute | solution.py:585
  22.2 1.5 %collective-permute-start.3 = (bf16[2,672,128]{2,1,0:T(8,128)(2,1)}, bf16[2,672,128]{2,1,0:T(8,128)(2,1)S(1)}, u32[]{:S(2)}, u32[]{:S(2)}) collective-permute-start(bf16[2,672,128]{2,1,0:T(8,128)(2,1)} %get-tuple-element.70), channel_id=1, source_target_pairs={{0,4},{2,6},{4,0},{6,2},{8,12},{10,14},{12,8},{14,10},{16,20},{18,... | collective-permute-start | bytes 1032200 | tf_op jit(solution)/shard_map/ppermute | solution.py:585
  23.7 1.6 %guest.1 = (bf16[2,960,128]{2,1,0:T(8,128)(2,1)}, bf16[2,960,128]{2,1,0:T(8,128)(2,1)}, bf16[2,2,672,128]{3,2,1,0:T(8,128)(2,1)}, bf16[2,2,288,128]{3,2,1,0:T(8,128)(2,1)}) custom-call(bf16[2,8,480,128]{3,2,1,0:T(8,128)(2,1)S(1)} %collective-permute-done.5.video_ref, bf16[2,576,128]{2,1,0:T(8,128)(2,1)S(1)} %collective-permute-done.6.packet_ref, ...), custom_call_target="tpu_custom_call" | custom-call | flops 20000000000 | tf_op jit(solution)/shard_map/guest/pallas_call | solution.py:322
  25.4 3.4 %collective-permute-start.7 = (bf16[2,2,672,128]{3,2,1,0:T(8,128)(2,1)}, bf16[2,2,672,128]{3,2,1,0:T(8,128)(2,1)S(1)}, u32[]{:S(2)}, u32[]{:S(2)}) collective-permute-start(bf16[2,2,672,128]{3,2,1,0:T(8,128)(2,1)} %get-tuple-element.79), channel_id=1, source_target_pairs={{0,4},{4,0},{8,12},{12,8},{16,20},{20,16},{24,28},{28,24},{1,5},{5... | collective-permute-start | bytes 2064392 | tf_op jit(solution)/shard_map/ppermute | solution.py:605
  29.0 4.3 %collective-permute-done.3.refs_2_ = bf16[2,672,128]{2,1,0:T(8,128)(2,1)S(1)} collective-permute-done((bf16[2,672,128]{2,1,0:T(8,128)(2,1)}, bf16[2,672,128]{2,1,0:T(8,128)(2,1)S(1)}, u32[]{:S(2)}, u32[]{:S(2)}) %collective-permute-start.3) | collective-permute-done | bytes 344096 | tf_op jit(solution)/shard_map/ppermute | solution.py:585
  33.3 5.6 %collective-permute-done.4.refs_3_ = bf16[2,672,128]{2,1,0:T(8,128)(2,1)S(1)} collective-permute-done((bf16[2,672,128]{2,1,0:T(8,128)(2,1)}, bf16[2,672,128]{2,1,0:T(8,128)(2,1)S(1)}, u32[]{:S(2)}, u32[]{:S(2)}) %collective-permute-start.4) | collective-permute-done | bytes 344096 | tf_op jit(solution)/shard_map/ppermute | solution.py:585
  39.0 3.8 %collective-permute-start.16 = (bf16[2,672,128]{2,1,0:T(8,128)(2,1)S(1)}, bf16[2,672,128]{2,1,0:T(8,128)(2,1)S(1)}, u32[]{:S(2)}, u32[]{:S(2)}) collective-permute-start(bf16[2,672,128]{2,1,0:T(8,128)(2,1)S(1)} %select_select_fusion), channel_id=1, source_target_pairs={{0,8},{2,10},{4,12},{6,14},{8,16},{10,18},{12,20},{14,22},{16,24},... | collective-permute-start | bytes 1032200 | tf_op jit(solution)/shard_map/ppermute | solution.py:611
  42.8 2.2 %collective-permute-start.11 = (bf16[2,960,128]{2,1,0:T(8,128)(2,1)S(1)}, bf16[2,960,128]{2,1,0:T(8,128)(2,1)S(1)}, u32[]{:S(2)}, u32[]{:S(2)}) collective-permute-start(bf16[2,960,128]{2,1,0:T(8,128)(2,1)S(1)} %copy-done.7), channel_id=1, source_target_pairs={{0,2},{4,6},{8,10},{12,14},{16,18},{20,22},{24,26},{28,30},{1,3},{... | collective-permute-start | bytes 1474568 | tf_op jit(solution)/shard_map/ppermute | solution.py:613
  45.1 2.2 %collective-permute-done.7.refs_6_ = bf16[2,2,672,128]{3,2,1,0:T(8,128)(2,1)S(1)} collective-permute-done((bf16[2,2,672,128]{3,2,1,0:T(8,128)(2,1)}, bf16[2,2,672,128]{3,2,1,0:T(8,128)(2,1)S(1)}, u32[]{:S(2)}, u32[]{:S(2)}) %collective-permute-start.7) | collective-permute-done | bytes 688160 | tf_op jit(solution)/shard_map/ppermute | solution.py:605
  47.2 0.8 ahead.2.refs_9_
  48.1 1.4 %collective-permute-start.15 = (bf16[2,672,128]{2,1,0:T(8,128)(2,1)S(1)}, bf16[2,672,128]{2,1,0:T(8,128)(2,1)S(1)}, u32[]{:S(2)}, u32[]{:S(2)}) collective-permute-start(bf16[2,672,128]{2,1,0:T(8,128)(2,1)S(1)} %slice_bitcast_fusion), channel_id=1, source_target_pairs={{0,2},{4,6},{8,10},{12,14},{16,18},{20,22},{24,26},{28,30},{1,3},{... | collective-permute-start | bytes 1032200 | tf_op jit(solution)/shard_map/ppermute | solution.py:617
  49.5 1.2 %collective-permute-done.16.refs_8_ = bf16[2,672,128]{2,1,0:T(8,128)(2,1)S(1)} collective-permute-done((bf16[2,672,128]{2,1,0:T(8,128)(2,1)S(1)}, bf16[2,672,128]{2,1,0:T(8,128)(2,1)S(1)}, u32[]{:S(2)}, u32[]{:S(2)}) %collective-permute-start.16) | collective-permute-done | bytes 344096 | tf_op jit(solution)/shard_map/ppermute | solution.py:611
  50.8 1.2 %early.5.own_ref = bf16[8,448,128]{2,1,0:T(8,128)(2,1)S(1)} custom-call(bf16[2,672,128]{2,1,0:T(8,128)(2,1)S(1)} %copy-done.1, bf16[2,672,128]{2,1,0:T(8,128)(2,1)S(1)} %collective-permute-done.2.refs_1_, bf16[2,672,128]{2,1,0:T(8,128)(2,1)S(1)} %collective-permute-done.3.refs_2_, bf16[2,672,128]{2,1,0:T(8,128)(2,1)S(1)} %collective-permute-done.4.refs_3_, ...), custom_call_target="tpu_custom_call" | custom-call | tf_op jit(solution)/shard_map/early/pallas_call | solution.py:456
  51.9 5.0 %collective-permute-start.17 = (bf16[8,448,128]{2,1,0:T(8,128)(2,1)S(1)}, bf16[8,448,128]{2,1,0:T(8,128)(2,1)S(1)}, u32[]{:S(2)}, u32[]{:S(2)}) collective-permute-start(bf16[8,448,128]{2,1,0:T(8,128)(2,1)S(1)} %early.5.own_ref), channel_id=1, source_target_pairs={{0,8},{2,10},{4,12},{6,14},{8,16},{10,18},{12,20},{14,22},{16,24},... | collective-permute-start | bytes 2752520 | tf_op jit(solution)/shard_map/ppermute | solution.py:627
  57.0 1.5 %collective-permute-start.9 = (bf16[2,288,128]{2,1,0:T(8,128)(2,1)S(1)}, bf16[2,288,128]{2,1,0:T(8,128)(2,1)S(1)}, u32[]{:S(2)}, u32[]{:S(2)}) collective-permute-start(bf16[2,288,128]{2,1,0:T(8,128)(2,1)S(1)} %copy-done.11), channel_id=1, source_target_pairs={{0,4},{2,6},{4,0},{6,2},{8,12},{10,14},{12,8},{14,10},{16,20},{18,... | collective-permute-start | bytes 442376 | tf_op jit(solution)/shard_map/ppermute | solution.py:585
  58.5 0.7 collective-permute-start.8
  59.2 4.6 %collective-permute-done.9.refs_2_ = bf16[2,288,128]{2,1,0:T(8,128)(2,1)S(1)} collective-permute-done((bf16[2,288,128]{2,1,0:T(8,128)(2,1)S(1)}, bf16[2,288,128]{2,1,0:T(8,128)(2,1)S(1)}, u32[]{:S(2)}, u32[]{:S(2)}) %collective-permute-start.9) | collective-permute-done | bytes 147488 | tf_op jit(solution)/shard_map/ppermute | solution.py:585
  63.7 3.4 %collective-permute-start.12 = (bf16[2,2,288,128]{3,2,1,0:T(8,128)(2,1)S(1)}, bf16[2,2,288,128]{3,2,1,0:T(8,128)(2,1)S(1)}, u32[]{:S(2)}, u32[]{:S(2)}) collective-permute-start(bf16[2,2,288,128]{3,2,1,0:T(8,128)(2,1)S(1)} %copy-done.8), channel_id=1, source_target_pairs={{0,4},{4,0},{8,12},{12,8},{16,20},{20,16},{24,28},{28,24},{1,5},{5... | collective-permute-start | bytes 884744 | tf_op jit(solution)/shard_map/ppermute | solution.py:605
  67.2 3.4 %collective-permute-start.14 = (bf16[2,288,128]{2,1,0:T(8,128)(2,1)S(1)}, bf16[2,288,128]{2,1,0:T(8,128)(2,1)S(1)}, u32[]{:S(2)}, u32[]{:S(2)}) collective-permute-start(bf16[2,288,128]{2,1,0:T(8,128)(2,1)S(1)} %select_select_fusion.1), channel_id=1, source_target_pairs={{0,8},{2,10},{4,12},{6,14},{8,16},{10,18},{12,20},{14,22},{16,24},... | collective-permute-start | bytes 442376 | tf_op jit(solution)/shard_map/ppermute | solution.py:611
  70.6 0.8 early.6.own_ref
  71.4 3.5 %collective-permute-start.19 = (bf16[8,224,128]{2,1,0:T(8,128)(2,1)S(1)}, bf16[8,224,128]{2,1,0:T(8,128)(2,1)S(1)}, u32[]{:S(2)}, u32[]{:S(2)}) collective-permute-start(bf16[8,224,128]{2,1,0:T(8,128)(2,1)S(1)} %early.6.own_ref), channel_id=1, source_target_pairs={{0,8},{2,10},{4,12},{6,14},{8,16},{10,18},{12,20},{14,22},{16,24},... | collective-permute-start | bytes 1376264 | tf_op jit(solution)/shard_map/ppermute | solution.py:627
  75.0 1.3 %collective-permute-start.13 = (bf16[2,288,128]{2,1,0:T(8,128)(2,1)S(1)}, bf16[2,288,128]{2,1,0:T(8,128)(2,1)S(1)}, u32[]{:S(2)}, u32[]{:S(2)}) collective-permute-start(bf16[2,288,128]{2,1,0:T(8,128)(2,1)S(1)} %slice_bitcast_fusion.1), channel_id=1, source_target_pairs={{0,2},{4,6},{8,10},{12,14},{16,18},{20,22},{24,26},{28,30},{1,3},{... | collective-permute-start | bytes 442376 | tf_op jit(solution)/shard_map/ppermute | solution.py:617
  76.3 1.3 %collective-permute-done.17.halo_ref = bf16[8,448,128]{2,1,0:T(8,128)(2,1)S(1)} collective-permute-done((bf16[8,448,128]{2,1,0:T(8,128)(2,1)S(1)}, bf16[8,448,128]{2,1,0:T(8,128)(2,1)S(1)}, u32[]{:S(2)}, u32[]{:S(2)}) %collective-permute-start.17) | collective-permute-done | bytes 917536 | tf_op jit(solution)/shard_map/ppermute | solution.py:627
  77.6 0.7 late.6
  78.4 1.5 %collective-permute-start.23 = (bf16[2,448,128]{2,1,0:T(8,128)(2,1)S(1)}, bf16[2,448,128]{2,1,0:T(8,128)(2,1)S(1)}, u32[]{:S(2)}, u32[]{:S(2)}) collective-permute-start(bf16[2,448,128]{2,1,0:T(8,128)(2,1)S(1)} %get-tuple-element.101), channel_id=1, source_target_pairs={{0,4},{2,6},{4,0},{6,2},{8,12},{10,14},{12,8},{14,10},{16,20},{18,... | collective-permute-start | bytes 688136 | tf_op jit(solution)/shard_map/ppermute | solution.py:585
  79.9 0.8 collective-permute-done.14.refs_8_
  81.2 0.8 early.4.own_ref
  82.0 4.4 %collective-permute-start.18 = (bf16[8,160,128]{2,1,0:T(8,128)(2,1)S(1)}, bf16[8,160,128]{2,1,0:T(8,128)(2,1)S(1)}, u32[]{:S(2)}, u32[]{:S(2)}) collective-permute-start(bf16[8,160,128]{2,1,0:T(8,128)(2,1)S(1)} %early.4.own_ref), channel_id=1, source_target_pairs={{0,8},{2,10},{4,12},{6,14},{8,16},{10,18},{12,20},{14,22},{16,24},... | collective-permute-start | bytes 983048 | tf_op jit(solution)/shard_map/ppermute | solution.py:627
  86.4 0.6 early.7.own_ref
  87.0 3.5 %collective-permute-done.19.halo_ref = bf16[8,224,128]{2,1,0:T(8,128)(2,1)S(1)} collective-permute-done((bf16[8,224,128]{2,1,0:T(8,128)(2,1)S(1)}, bf16[8,224,128]{2,1,0:T(8,128)(2,1)S(1)}, u32[]{:S(2)}, u32[]{:S(2)}) %collective-permute-start.19) | collective-permute-done | bytes 458784 | tf_op jit(solution)/shard_map/ppermute | solution.py:627
  91.0 4.4 %collective-permute-start.29 = (bf16[8,128,128]{2,1,0:T(8,128)(2,1)S(1)}, bf16[8,128,128]{2,1,0:T(8,128)(2,1)S(1)}, u32[]{:S(2)}, u32[]{:S(2)}) collective-permute-start(bf16[8,128,128]{2,1,0:T(8,128)(2,1)S(1)} %early.7.own_ref), channel_id=1, source_target_pairs={{0,8},{2,10},{4,12},{6,14},{8,16},{10,18},{12,20},{14,22},{16,24},... | collective-permute-start | bytes 786440 | tf_op jit(solution)/shard_map/ppermute | solution.py:627
  95.5 1.5 %collective-permute-start.24 = (bf16[2,224,128]{2,1,0:T(8,128)(2,1)S(1)}, bf16[2,224,128]{2,1,0:T(8,128)(2,1)S(1)}, u32[]{:S(2)}, u32[]{:S(2)}) collective-permute-start(bf16[2,224,128]{2,1,0:T(8,128)(2,1)S(1)} %get-tuple-element.102), channel_id=1, source_target_pairs={{0,4},{2,6},{4,0},{6,2},{8,12},{10,14},{12,8},{14,10},{16,20},{18,... | collective-permute-start | bytes 344072 | tf_op jit(solution)/shard_map/ppermute | solution.py:585
  97.9 2.9 %collective-permute-done.27.refs_7_ = bf16[2,224,128]{2,1,0:T(8,128)(2,1)S(1)} collective-permute-done((bf16[2,224,128]{2,1,0:T(8,128)(2,1)S(1)}, bf16[2,224,128]{2,1,0:T(8,128)(2,1)S(1)}, u32[]{:S(2)}, u32[]{:S(2)}) %collective-permute-start.27) | collective-permute-done | bytes 114720 | tf_op jit(solution)/shard_map/ppermute | solution.py:585
  100.9 2.5 %collective-permute-done.24.refs_6_ = bf16[2,224,128]{2,1,0:T(8,128)(2,1)S(1)} collective-permute-done((bf16[2,224,128]{2,1,0:T(8,128)(2,1)S(1)}, bf16[2,224,128]{2,1,0:T(8,128)(2,1)S(1)}, u32[]{:S(2)}, u32[]{:S(2)}) %collective-permute-start.24) | collective-permute-done | bytes 114720 | tf_op jit(solution)/shard_map/ppermute | solution.py:585
  103.9 1.5 %collective-permute-done.28.refs_3_ = bf16[2,160,128]{2,1,0:T(8,128)(2,1)S(1)} collective-permute-done((bf16[2,160,128]{2,1,0:T(8,128)(2,1)S(1)}, bf16[2,160,128]{2,1,0:T(8,128)(2,1)S(1)}, u32[]{:S(2)}, u32[]{:S(2)}) %collective-permute-start.28) | collective-permute-done | bytes 81952 | tf_op jit(solution)/shard_map/ppermute | solution.py:585
  105.9 1.9 %collective-permute-done.25.refs_2_ = bf16[2,160,128]{2,1,0:T(8,128)(2,1)S(1)} collective-permute-done((bf16[2,160,128]{2,1,0:T(8,128)(2,1)S(1)}, bf16[2,160,128]{2,1,0:T(8,128)(2,1)S(1)}, u32[]{:S(2)}, u32[]{:S(2)}) %collective-permute-start.25) | collective-permute-done | bytes 81952 | tf_op jit(solution)/shard_map/ppermute | solution.py:585
  108.1 1.1 place.2.refs_8_
  109.4 2.7 %collective-permute-done.31.refs_6_ = bf16[2,128,128]{2,1,0:T(8,128)(2,1)S(1)} collective-permute-done((bf16[2,128,128]{2,1,0:T(8,128)(2,1)S(1)}, bf16[2,128,128]{2,1,0:T(8,128)(2,1)S(1)}, u32[]{:S(2)}, u32[]{:S(2)}) %collective-permute-start.31) | collective-permute-done | bytes 65568 | tf_op jit(solution)/shard_map/ppermute | solution.py:585
  112.1 0.9 place.3
  (64 shorter events, 3.9 us)
Async XLA Ops:
  0.0 23.7 %collective-permute-start.5 = (bf16[2,8,480,128]{3,2,1,0:T(8,128)(2,1)}, bf16[2,8,480,128]{3,2,1,0:T(8,128)(2,1)S(1)}, u32[]{:S(2)}, u32[]{:S(2)}) collective-permute-start(bf16[2,8,480,128]{3,2,1,0:T(8,128)(2,1)} %video_ref.1), channel_id=1, source_target_pairs={{2,8},{6,12},{10,16},{14,20},{18,24},{22,28},{3,9},{7,13},{11,17},... | collective-permute-start | bytes 5898248 | tf_op jit(solution)/shard_map/ppermute | solution.py:567
  1.8 7.9 %copy-start.3 = (bf16[3,3,128,128]{3,2,1,0:T(8,128)(2,1)S(1)}, bf16[3,3,128,128]{3,2,1,0:T(8,128)(2,1)}, u32[]{:S(2)}) copy-start(bf16[3,3,128,128]{3,2,1,0:T(8,128)(2,1)} %weight_ref.5) | copy-start | bytes 884740
  1.8 7.9 %collective-permute-start = (bf16[2,480,128]{2,1,0:T(8,128)(2,1)S(1)}, bf16[2,480,128]{2,1,0:T(8,128)(2,1)S(1)}, u32[]{:S(2)}, u32[]{:S(2)}) collective-permute-start(bf16[2,480,128]{2,1,0:T(8,128)(2,1)S(1)} %dynamic-slice_bitcast_fusion), channel_id=1, source_target_pairs={{0,1},{1,0},{2,3},{3,2},{4,5},{5,4},{6,7},{7,6},{8,9},{9,8},{10,11... | collective-permute-start | bytes 737288 | tf_op jit(solution)/shard_map/ppermute | solution.py:539
  9.7 4.6 %copy-start.4 = (f32[128]{0:T(128)S(1)}, f32[128]{0:T(128)}, u32[]{:S(2)}) copy-start(f32[128]{0:T(128)} %param.7) | copy-start | bytes 1540
  9.7 4.6 %copy-start.5 = (f32[128]{0:T(128)S(1)}, f32[128]{0:T(128)}, u32[]{:S(2)}) copy-start(f32[128]{0:T(128)} %param.8) | copy-start | bytes 1540
  10.5 3.8 %collective-permute-start.1 = (f32[2,2,8,128]{3,2,1,0:T(8,128)S(1)}, f32[2,2,8,128]{3,2,1,0:T(8,128)S(1)}, u32[]{:S(2)}, u32[]{:S(2)}) collective-permute-start(f32[2,2,8,128]{3,2,1,0:T(8,128)S(1)} %get-tuple-element.65.own_ref), channel_id=1, source_target_pairs={{0,1},{1,0},{2,3},{3,2},{4,5},{5,4},{6,7},{7,6},{8,9},{9,8},{10,11... | collective-permute-start | bytes 49160 | tf_op jit(solution)/shard_map/ppermute | solution.py:548
  17.1 6.6 %collective-permute-start.6 = (bf16[2,576,128]{2,1,0:T(8,128)(2,1)S(1)}, bf16[2,576,128]{2,1,0:T(8,128)(2,1)S(1)}, u32[]{:S(2)}, u32[]{:S(2)}) collective-permute-start(bf16[2,576,128]{2,1,0:T(8,128)(2,1)S(1)} %get-tuple-element.72), channel_id=1, source_target_pairs={{2,8},{6,12},{10,16},{14,20},{18,24},{22,28},{3,9},{7,13},{11,17},... | collective-permute-start | bytes 884744 | tf_op jit(solution)/shard_map/ppermute | solution.py:588
  17.8 11.2 %collective-permute-start.2 = (bf16[2,672,128]{2,1,0:T(8,128)(2,1)}, bf16[2,672,128]{2,1,0:T(8,128)(2,1)S(1)}, u32[]{:S(2)}, u32[]{:S(2)}) collective-permute-start(bf16[2,672,128]{2,1,0:T(8,128)(2,1)} %get-tuple-element.69), channel_id=1, source_target_pairs={{0,2},{2,0},{4,6},{6,4},{8,10},{10,8},{12,14},{14,12},{16,18},{18,... | collective-permute-start | bytes 1032200 | tf_op jit(solution)/shard_map/ppermute | solution.py:585
  22.2 11.1 %collective-permute-start.3 = (bf16[2,672,128]{2,1,0:T(8,128)(2,1)}, bf16[2,672,128]{2,1,0:T(8,128)(2,1)S(1)}, u32[]{:S(2)}, u32[]{:S(2)}) collective-permute-start(bf16[2,672,128]{2,1,0:T(8,128)(2,1)} %get-tuple-element.70), channel_id=1, source_target_pairs={{0,4},{2,6},{4,0},{6,2},{8,12},{10,14},{12,8},{14,10},{16,20},{18,... | collective-permute-start | bytes 1032200 | tf_op jit(solution)/shard_map/ppermute | solution.py:585
  23.7 5.1 %copy-start.6 = (bf16[3,3,128,128]{3,2,1,0:T(8,128)(2,1)S(1)}, bf16[3,3,128,128]{3,2,1,0:T(8,128)(2,1)}, u32[]{:S(2)}) copy-start(bf16[3,3,128,128]{3,2,1,0:T(8,128)(2,1)} %weight_ref.6) | copy-start | bytes 884740
  23.7 15.3 %collective-permute-start.4 = (bf16[2,672,128]{2,1,0:T(8,128)(2,1)}, bf16[2,672,128]{2,1,0:T(8,128)(2,1)S(1)}, u32[]{:S(2)}, u32[]{:S(2)}) collective-permute-start(bf16[2,672,128]{2,1,0:T(8,128)(2,1)} %get-tuple-element.71), channel_id=1, source_target_pairs={{0,6},{2,4},{4,2},{6,0},{8,14},{10,12},{12,10},{14,8},{16,22},{18,... | collective-permute-start | bytes 1032200 | tf_op jit(solution)/shard_map/ppermute | solution.py:585
  25.4 13.6 %copy-start.1 = (bf16[2,672,128]{2,1,0:T(8,128)(2,1)S(1)}, bf16[2,672,128]{2,1,0:T(8,128)(2,1)}, u32[]{:S(2)}) copy-start(bf16[2,672,128]{2,1,0:T(8,128)(2,1)} %get-tuple-element.78.refs_0_) | copy-start | bytes 1032196
  25.4 17.4 %copy-start.7 = (bf16[2,960,128]{2,1,0:T(8,128)(2,1)S(1)}, bf16[2,960,128]{2,1,0:T(8,128)(2,1)}, u32[]{:S(2)}) copy-start(bf16[2,960,128]{2,1,0:T(8,128)(2,1)} %get-tuple-element.87) | copy-start | bytes 1474564
  25.4 21.8 %collective-permute-start.7 = (bf16[2,2,672,128]{3,2,1,0:T(8,128)(2,1)}, bf16[2,2,672,128]{3,2,1,0:T(8,128)(2,1)S(1)}, u32[]{:S(2)}, u32[]{:S(2)}) collective-permute-start(bf16[2,2,672,128]{3,2,1,0:T(8,128)(2,1)} %get-tuple-element.79), channel_id=1, source_target_pairs={{0,4},{4,0},{8,12},{12,8},{16,20},{20,16},{24,28},{28,24},{1,5},{5... | collective-permute-start | bytes 2064392 | tf_op jit(solution)/shard_map/ppermute | solution.py:605
  39.0 11.7 %collective-permute-start.16 = (bf16[2,672,128]{2,1,0:T(8,128)(2,1)S(1)}, bf16[2,672,128]{2,1,0:T(8,128)(2,1)S(1)}, u32[]{:S(2)}, u32[]{:S(2)}) collective-permute-start(bf16[2,672,128]{2,1,0:T(8,128)(2,1)S(1)} %select_select_fusion), channel_id=1, source_target_pairs={{0,8},{2,10},{4,12},{6,14},{8,16},{10,18},{12,20},{14,22},{16,24},... | collective-permute-start | bytes 1032200 | tf_op jit(solution)/shard_map/ppermute | solution.py:611
  42.8 8.0 %copy-start = (bf16[2,960,128]{2,1,0:T(8,128)(2,1)S(1)}, bf16[2,960,128]{2,1,0:T(8,128)(2,1)}, u32[]{:S(2)}) copy-start(bf16[2,960,128]{2,1,0:T(8,128)(2,1)} %get-tuple-element.73.refs_4_) | copy-start | bytes 1474564
  42.8 7.9 %collective-permute-start.11 = (bf16[2,960,128]{2,1,0:T(8,128)(2,1)S(1)}, bf16[2,960,128]{2,1,0:T(8,128)(2,1)S(1)}, u32[]{:S(2)}, u32[]{:S(2)}) collective-permute-start(bf16[2,960,128]{2,1,0:T(8,128)(2,1)S(1)} %copy-done.7), channel_id=1, source_target_pairs={{0,2},{4,6},{8,10},{12,14},{16,18},{20,22},{24,26},{28,30},{1,3},{... | collective-permute-start | bytes 1474568 | tf_op jit(solution)/shard_map/ppermute | solution.py:613
  48.0 8.9 %copy-start.11 = (bf16[2,288,128]{2,1,0:T(8,128)(2,1)S(1)}, bf16[2,288,128]{2,1,0:T(8,128)(2,1)}, u32[]{:S(2)}) copy-start(bf16[2,288,128]{2,1,0:T(8,128)(2,1)} %get-tuple-element.83) | copy-start | bytes 442372
  48.0 10.5 %copy-start.10 = (bf16[2,288,128]{2,1,0:T(8,128)(2,1)S(1)}, bf16[2,288,128]{2,1,0:T(8,128)(2,1)}, u32[]{:S(2)}) copy-start(bf16[2,288,128]{2,1,0:T(8,128)(2,1)} %get-tuple-element.85) | copy-start | bytes 442372
  48.0 10.5 %copy-start.9 = (bf16[2,288,128]{2,1,0:T(8,128)(2,1)S(1)}, bf16[2,288,128]{2,1,0:T(8,128)(2,1)}, u32[]{:S(2)}) copy-start(bf16[2,288,128]{2,1,0:T(8,128)(2,1)} %get-tuple-element.81) | copy-start | bytes 442372
  48.1 15.7 %copy-start.8 = (bf16[2,2,288,128]{3,2,1,0:T(8,128)(2,1)S(1)}, bf16[2,2,288,128]{3,2,1,0:T(8,128)(2,1)}, u32[]{:S(2)}) copy-start(bf16[2,2,288,128]{3,2,1,0:T(8,128)(2,1)} %get-tuple-element.89) | copy-start | bytes 884740
  48.1 19.1 %copy-start.2 = (bf16[2,288,128]{2,1,0:T(8,128)(2,1)S(1)}, bf16[2,288,128]{2,1,0:T(8,128)(2,1)}, u32[]{:S(2)}) copy-start(bf16[2,288,128]{2,1,0:T(8,128)(2,1)} %get-tuple-element.66.refs_0_) | copy-start | bytes 442372
  48.1 2.7 %collective-permute-start.15 = (bf16[2,672,128]{2,1,0:T(8,128)(2,1)S(1)}, bf16[2,672,128]{2,1,0:T(8,128)(2,1)S(1)}, u32[]{:S(2)}, u32[]{:S(2)}) collective-permute-start(bf16[2,672,128]{2,1,0:T(8,128)(2,1)S(1)} %slice_bitcast_fusion), channel_id=1, source_target_pairs={{0,2},{4,6},{8,10},{12,14},{16,18},{20,22},{24,26},{28,30},{1,3},{... | collective-permute-start | bytes 1032200 | tf_op jit(solution)/shard_map/ppermute | solution.py:617
  51.9 25.6 %collective-permute-start.17 = (bf16[8,448,128]{2,1,0:T(8,128)(2,1)S(1)}, bf16[8,448,128]{2,1,0:T(8,128)(2,1)S(1)}, u32[]{:S(2)}, u32[]{:S(2)}) collective-permute-start(bf16[8,448,128]{2,1,0:T(8,128)(2,1)S(1)} %early.5.own_ref), channel_id=1, source_target_pairs={{0,8},{2,10},{4,12},{6,14},{8,16},{10,18},{12,20},{14,22},{16,24},... | collective-permute-start | bytes 2752520 | tf_op jit(solution)/shard_map/ppermute | solution.py:627
  57.0 6.8 %collective-permute-start.9 = (bf16[2,288,128]{2,1,0:T(8,128)(2,1)S(1)}, bf16[2,288,128]{2,1,0:T(8,128)(2,1)S(1)}, u32[]{:S(2)}, u32[]{:S(2)}) collective-permute-start(bf16[2,288,128]{2,1,0:T(8,128)(2,1)S(1)} %copy-done.11), channel_id=1, source_target_pairs={{0,4},{2,6},{4,0},{6,2},{8,12},{10,14},{12,8},{14,10},{16,20},{18,... | collective-permute-start | bytes 442376 | tf_op jit(solution)/shard_map/ppermute | solution.py:585
  58.5 8.6 %collective-permute-start.10 = (bf16[2,288,128]{2,1,0:T(8,128)(2,1)S(1)}, bf16[2,288,128]{2,1,0:T(8,128)(2,1)S(1)}, u32[]{:S(2)}, u32[]{:S(2)}) collective-permute-start(bf16[2,288,128]{2,1,0:T(8,128)(2,1)S(1)} %copy-done.10), channel_id=1, source_target_pairs={{0,6},{2,4},{4,2},{6,0},{8,14},{10,12},{12,10},{14,8},{16,22},{18,... | collective-permute-start | bytes 442376 | tf_op jit(solution)/shard_map/ppermute | solution.py:585
  58.5 8.6 %collective-permute-start.8 = (bf16[2,288,128]{2,1,0:T(8,128)(2,1)S(1)}, bf16[2,288,128]{2,1,0:T(8,128)(2,1)S(1)}, u32[]{:S(2)}, u32[]{:S(2)}) collective-permute-start(bf16[2,288,128]{2,1,0:T(8,128)(2,1)S(1)} %copy-done.9), channel_id=1, source_target_pairs={{0,2},{2,0},{4,6},{6,4},{8,10},{10,8},{12,14},{14,12},{16,18},{18,... | collective-permute-start | bytes 442376 | tf_op jit(solution)/shard_map/ppermute | solution.py:585
  63.7 11.2 %collective-permute-start.12 = (bf16[2,2,288,128]{3,2,1,0:T(8,128)(2,1)S(1)}, bf16[2,2,288,128]{3,2,1,0:T(8,128)(2,1)S(1)}, u32[]{:S(2)}, u32[]{:S(2)}) collective-permute-start(bf16[2,2,288,128]{3,2,1,0:T(8,128)(2,1)S(1)} %copy-done.8), channel_id=1, source_target_pairs={{0,4},{4,0},{8,12},{12,8},{16,20},{20,16},{24,28},{28,24},{1,5},{5... | collective-permute-start | bytes 884744 | tf_op jit(solution)/shard_map/ppermute | solution.py:605
  67.2 13.5 %collective-permute-start.14 = (bf16[2,288,128]{2,1,0:T(8,128)(2,1)S(1)}, bf16[2,288,128]{2,1,0:T(8,128)(2,1)S(1)}, u32[]{:S(2)}, u32[]{:S(2)}) collective-permute-start(bf16[2,288,128]{2,1,0:T(8,128)(2,1)S(1)} %select_select_fusion.1), channel_id=1, source_target_pairs={{0,8},{2,10},{4,12},{6,14},{8,16},{10,18},{12,20},{14,22},{16,24},... | collective-permute-start | bytes 442376 | tf_op jit(solution)/shard_map/ppermute | solution.py:611
  71.4 19.1 %collective-permute-start.19 = (bf16[8,224,128]{2,1,0:T(8,128)(2,1)S(1)}, bf16[8,224,128]{2,1,0:T(8,128)(2,1)S(1)}, u32[]{:S(2)}, u32[]{:S(2)}) collective-permute-start(bf16[8,224,128]{2,1,0:T(8,128)(2,1)S(1)} %early.6.own_ref), channel_id=1, source_target_pairs={{0,8},{2,10},{4,12},{6,14},{8,16},{10,18},{12,20},{14,22},{16,24},... | collective-permute-start | bytes 1376264 | tf_op jit(solution)/shard_map/ppermute | solution.py:627
  75.0 6.2 %collective-permute-start.13 = (bf16[2,288,128]{2,1,0:T(8,128)(2,1)S(1)}, bf16[2,288,128]{2,1,0:T(8,128)(2,1)S(1)}, u32[]{:S(2)}, u32[]{:S(2)}) collective-permute-start(bf16[2,288,128]{2,1,0:T(8,128)(2,1)S(1)} %slice_bitcast_fusion.1), channel_id=1, source_target_pairs={{0,2},{4,6},{8,10},{12,14},{16,18},{20,22},{24,26},{28,30},{1,3},{... | collective-permute-start | bytes 442376 | tf_op jit(solution)/shard_map/ppermute | solution.py:617
  78.3 17.1 %collective-permute-start.26 = (bf16[2,448,128]{2,1,0:T(8,128)(2,1)S(1)}, bf16[2,448,128]{2,1,0:T(8,128)(2,1)S(1)}, u32[]{:S(2)}, u32[]{:S(2)}) collective-permute-start(bf16[2,448,128]{2,1,0:T(8,128)(2,1)S(1)} %get-tuple-element.106), channel_id=1, source_target_pairs={{0,6},{2,4},{4,2},{6,0},{8,14},{10,12},{12,10},{14,8},{16,22},{18,... | collective-permute-start | bytes 688136 | tf_op jit(solution)/shard_map/ppermute | solution.py:585
  78.4 17.1 %collective-permute-start.23 = (bf16[2,448,128]{2,1,0:T(8,128)(2,1)S(1)}, bf16[2,448,128]{2,1,0:T(8,128)(2,1)S(1)}, u32[]{:S(2)}, u32[]{:S(2)}) collective-permute-start(bf16[2,448,128]{2,1,0:T(8,128)(2,1)S(1)} %get-tuple-element.101), channel_id=1, source_target_pairs={{0,4},{2,6},{4,0},{6,2},{8,12},{10,14},{12,8},{14,10},{16,20},{18,... | collective-permute-start | bytes 688136 | tf_op jit(solution)/shard_map/ppermute | solution.py:585
  80.7 16.3 %collective-permute-start.20 = (bf16[2,448,128]{2,1,0:T(8,128)(2,1)S(1)}, bf16[2,448,128]{2,1,0:T(8,128)(2,1)S(1)}, u32[]{:S(2)}, u32[]{:S(2)}) collective-permute-start(bf16[2,448,128]{2,1,0:T(8,128)(2,1)S(1)} %get-tuple-element.96), channel_id=1, source_target_pairs={{0,2},{2,0},{4,6},{6,4},{8,10},{10,8},{12,14},{14,12},{16,18},{18,... | collective-permute-start | bytes 688136 | tf_op jit(solution)/shard_map/ppermute | solution.py:585
  82.0 15.6 %collective-permute-start.18 = (bf16[8,160,128]{2,1,0:T(8,128)(2,1)S(1)}, bf16[8,160,128]{2,1,0:T(8,128)(2,1)S(1)}, u32[]{:S(2)}, u32[]{:S(2)}) collective-permute-start(bf16[8,160,128]{2,1,0:T(8,128)(2,1)S(1)} %early.4.own_ref), channel_id=1, source_target_pairs={{0,8},{2,10},{4,12},{6,14},{8,16},{10,18},{12,20},{14,22},{16,24},... | collective-permute-start | bytes 983048 | tf_op jit(solution)/shard_map/ppermute | solution.py:627
  91.0 12.5 %collective-permute-start.29 = (bf16[8,128,128]{2,1,0:T(8,128)(2,1)S(1)}, bf16[8,128,128]{2,1,0:T(8,128)(2,1)S(1)}, u32[]{:S(2)}, u32[]{:S(2)}) collective-permute-start(bf16[8,128,128]{2,1,0:T(8,128)(2,1)S(1)} %early.7.own_ref), channel_id=1, source_target_pairs={{0,8},{2,10},{4,12},{6,14},{8,16},{10,18},{12,20},{14,22},{16,24},... | collective-permute-start | bytes 786440 | tf_op jit(solution)/shard_map/ppermute | solution.py:627
  95.4 5.5 %collective-permute-start.27 = (bf16[2,224,128]{2,1,0:T(8,128)(2,1)S(1)}, bf16[2,224,128]{2,1,0:T(8,128)(2,1)S(1)}, u32[]{:S(2)}, u32[]{:S(2)}) collective-permute-start(bf16[2,224,128]{2,1,0:T(8,128)(2,1)S(1)} %get-tuple-element.107), channel_id=1, source_target_pairs={{0,6},{2,4},{4,2},{6,0},{8,14},{10,12},{12,10},{14,8},{16,22},{18,... | collective-permute-start | bytes 344072 | tf_op jit(solution)/shard_map/ppermute | solution.py:585
  95.5 7.9 %collective-permute-start.24 = (bf16[2,224,128]{2,1,0:T(8,128)(2,1)S(1)}, bf16[2,224,128]{2,1,0:T(8,128)(2,1)S(1)}, u32[]{:S(2)}, u32[]{:S(2)}) collective-permute-start(bf16[2,224,128]{2,1,0:T(8,128)(2,1)S(1)} %get-tuple-element.102), channel_id=1, source_target_pairs={{0,4},{2,6},{4,0},{6,2},{8,12},{10,14},{12,8},{14,10},{16,20},{18,... | collective-permute-start | bytes 344072 | tf_op jit(solution)/shard_map/ppermute | solution.py:585
  97.1 6.3 %collective-permute-start.21 = (bf16[2,224,128]{2,1,0:T(8,128)(2,1)S(1)}, bf16[2,224,128]{2,1,0:T(8,128)(2,1)S(1)}, u32[]{:S(2)}, u32[]{:S(2)}) collective-permute-start(bf16[2,224,128]{2,1,0:T(8,128)(2,1)S(1)} %get-tuple-element.97), channel_id=1, source_target_pairs={{0,2},{2,0},{4,6},{6,4},{8,10},{10,8},{12,14},{14,12},{16,18},{18,... | collective-permute-start | bytes 344072 | tf_op jit(solution)/shard_map/ppermute | solution.py:585
  100.9 4.4 %collective-permute-start.28 = (bf16[2,160,128]{2,1,0:T(8,128)(2,1)S(1)}, bf16[2,160,128]{2,1,0:T(8,128)(2,1)S(1)}, u32[]{:S(2)}, u32[]{:S(2)}) collective-permute-start(bf16[2,160,128]{2,1,0:T(8,128)(2,1)S(1)} %get-tuple-element.108), channel_id=1, source_target_pairs={{0,6},{2,4},{4,2},{6,0},{8,14},{10,12},{12,10},{14,8},{16,22},{18,... | collective-permute-start | bytes 245768 | tf_op jit(solution)/shard_map/ppermute | solution.py:585
  103.4 4.4 %collective-permute-start.25 = (bf16[2,160,128]{2,1,0:T(8,128)(2,1)S(1)}, bf16[2,160,128]{2,1,0:T(8,128)(2,1)S(1)}, u32[]{:S(2)}, u32[]{:S(2)}) collective-permute-start(bf16[2,160,128]{2,1,0:T(8,128)(2,1)S(1)} %get-tuple-element.103), channel_id=1, source_target_pairs={{0,4},{2,6},{4,0},{6,2},{8,12},{10,14},{12,8},{14,10},{16,20},{18,... | collective-permute-start | bytes 245768 | tf_op jit(solution)/shard_map/ppermute | solution.py:585
  103.4 4.7 %collective-permute-start.22 = (bf16[2,160,128]{2,1,0:T(8,128)(2,1)S(1)}, bf16[2,160,128]{2,1,0:T(8,128)(2,1)S(1)}, u32[]{:S(2)}, u32[]{:S(2)}) collective-permute-start(bf16[2,160,128]{2,1,0:T(8,128)(2,1)S(1)} %get-tuple-element.98), channel_id=1, source_target_pairs={{0,2},{2,0},{4,6},{6,4},{8,10},{10,8},{12,14},{14,12},{16,18},{18,... | collective-permute-start | bytes 245768 | tf_op jit(solution)/shard_map/ppermute | solution.py:585
  105.3 4.1 %collective-permute-start.32 = (bf16[2,128,128]{2,1,0:T(8,128)(2,1)S(1)}, bf16[2,128,128]{2,1,0:T(8,128)(2,1)S(1)}, u32[]{:S(2)}, u32[]{:S(2)}) collective-permute-start(bf16[2,128,128]{2,1,0:T(8,128)(2,1)S(1)} %get-tuple-element.117), channel_id=1, source_target_pairs={{0,6},{2,4},{4,2},{6,0},{8,14},{10,12},{12,10},{14,8},{16,22},{18,... | collective-permute-start | bytes 196616 | tf_op jit(solution)/shard_map/ppermute | solution.py:585
  107.8 4.3 %collective-permute-start.31 = (bf16[2,128,128]{2,1,0:T(8,128)(2,1)S(1)}, bf16[2,128,128]{2,1,0:T(8,128)(2,1)S(1)}, u32[]{:S(2)}, u32[]{:S(2)}) collective-permute-start(bf16[2,128,128]{2,1,0:T(8,128)(2,1)S(1)} %get-tuple-element.115), channel_id=1, source_target_pairs={{0,4},{2,6},{4,0},{6,2},{8,12},{10,14},{12,8},{14,10},{16,20},{18,... | collective-permute-start | bytes 196616 | tf_op jit(solution)/shard_map/ppermute | solution.py:585
  108.1 4.0 %collective-permute-start.30 = (bf16[2,128,128]{2,1,0:T(8,128)(2,1)S(1)}, bf16[2,128,128]{2,1,0:T(8,128)(2,1)S(1)}, u32[]{:S(2)}, u32[]{:S(2)}) collective-permute-start(bf16[2,128,128]{2,1,0:T(8,128)(2,1)S(1)} %get-tuple-element.113), channel_id=1, source_target_pairs={{0,2},{2,0},{4,6},{6,4},{8,10},{10,8},{12,14},{14,12},{16,18},{18,... | collective-permute-start | bytes 196616 | tf_op jit(solution)/shard_map/ppermute | solution.py:585

commit v7 on v6

--- a/solution.py
+++ b/solution.py
@@ -11,7 +11,7 @@
 SPAN = 8
 OWN_PARTS = (42, 18)
 GUEST_PARTS = (42, 18)
-OUT_PARTS = (28, 14, 10, 8)
+OUT_PARTS = (32, 10, 10, 8)
 VMEM = pltpu.VMEM
 ANY = pl.ANY
 F32 = jnp.float32
@@ -228,15 +228,12 @@
         sums = [own_ref[frame, i] + other_ref[frame, i] for i in range(2)]
         for i, ref in enumerate(row_refs):
             packet_ref[frame, i * width : (i + 1) * width] = ref[frame]
-        for i in range(2):
-            rest = sums[i]
-            for part in range(3):
-                short = rest.astype(BF16).astype(F32)
-                rest = rest - short
-                at = rows * width + (i * 3 + part) * 16
-                packet_ref[frame, at : at + 16] = jnp.concatenate(
-                    [short, jnp.zeros_like(short)], axis=0
-                ).astype(BF16)
+        rest = jnp.concatenate(sums, axis=0)
+        for part in range(3):
+            at = rows * width + part * 16
+            short = rest.astype(BF16)
+            rest = rest - short.astype(F32)
+            packet_ref[frame, at : at + 16] = short
         apply = norm_of(sums, count, gain_ref, shift_ref)
 
         @pl.loop(0, band)
@@ -257,7 +254,7 @@
         functools.partial(norm_kernel, count, members, rows),
         in_specs=[vspec()] * (5 + rows),
         out_specs=[vspec()] + [hspec()] * (members * len(sizes)),
-        out_shape=[jax.ShapeDtypeStruct((frames, rows * width + 96, ch), BF16)]
+        out_shape=[jax.ShapeDtypeStruct((frames, rows * width + 48, ch), BF16)]
         + [pltpu.HBM((frames, size, ch), BF16) for size in sizes for _ in range(members)],
         scratch_shapes=[
             VMEM((frames, band, width, ch), BF16),
@@ -274,18 +271,16 @@
     hidden_ref, wide_ref, sem = refs[-3:]
     outs = [[keep_ref], [mate_ref]] + [[ref.at[k] for ref in away_refs] for k in range(2)]
     frames, band, width, ch = video_ref.shape
-    rows = (packet_ref.shape[1] - 96) // width
+    rows = (packet_ref.shape[1] - 48) // width
     here = lax.axis_index("tm")
 
     @pl.when(jnp.logical_and(here >= members, here % 2 == 0))
     def _():
         widen(weight_ref, wide_ref)
         for frame in range(frames):
-            sums = []
-            for i in range(2):
-                at = rows * width + i * 48
-                parts = packet_ref[frame, at : at + 48].astype(F32)
-                sums.append(parts[:16] + parts[16:32] + parts[32:])
+            parts = packet_ref[frame, rows * width :].astype(F32)
+            both = parts[:16] + parts[16:32] + parts[32:]
+            sums = [both[:8], both[8:]]
             apply = norm_of(sums, count, gain_ref, shift_ref)
 
             def write(row, value):

time: 114 us -> 112 us (0.982)
  waiting for transfers between devices: 37.3 us -> 36 us
    ppermute x18, waiting for transfers between devices: 26.2 us -> 24.3 us  [swap(): got.append(lax.ppermute(value, 'tm', swaps[k]))]
  transfers between devices with their start and end apart: 33 -> 33, of which waited for: 17 -> 19; matrix products, arithmetic and copies ran while one was open for 1% -> 1% of each run, Pallas kernels for 15% -> 15%
where the time goes in v7:
time: 112 us; the launch traced here: 111 us
  starting transfers between devices  54.8 us (49%)
  waiting for transfers between devices  36 us (32%)
  Pallas kernels  18.6 us (17%)
    ppermute x18, waiting for transfers between devices, swap(): got.append(lax.ppermute(value, 'tm', swaps[k]))  24.3 us
    ppermute x4, starting transfers between devices, body(): passed.append(lax.ppermute(u2, 'tm', onward))  17 us
    ppermute x18, starting transfers between devices, swap(): got.append(lax.ppermute(value, 'tm', swaps[k]))  12.4 us
    ppermute x2, starting transfers between devices, block(): add(2 * members, [lax.ppermute(middle, 'tm', onward)])  6.93 us
    ppermute x2, starting transfers between devices, block(): lax.ppermute(after(aways[i], own[2]) if i else aways[i], 'tm', guest_swap...  6.82 us
    ppermute x4, waiting for transfers between devices, body(): passed.append(lax.ppermute(u2, 'tm', onward))  5.76 us
    pallas_call x1, Pallas kernels, conv_call(): pl.pallas_call(functools.partial(conv_kernel, band), grid=(frames,), in_s...  4.86 us
    pallas_call x4, Pallas kernels, early_call(): pl.pallas_call(functools.partial(early_kernel, members, plan, start), in_...  3.34 us
  transfers between devices with their start and end apart: 33, of which 19 were waited for; matrix products, arithmetic and copies ran while one was open for 1% of the time, Pallas kernels for 15%

profile of v7, /device:TPU:0, one launch (start us, length us, event | category | flops | bytes accessed | tf_op | source)
XLA Modules:
  0.0 111.3 jit_solution(13205623066638965530)
XLA Ops:
  0.0 0.8 collective-permute-start.5
  0.8 1.0 dynamic-slice_bitcast_fusion
  1.8 3.0 %collective-permute-start = (bf16[2,480,128]{2,1,0:T(8,128)(2,1)S(1)}, bf16[2,480,128]{2,1,0:T(8,128)(2,1)S(1)}, u32[]{:S(2)}, u32[]{:S(2)}) collective-permute-start(bf16[2,480,128]{2,1,0:T(8,128)(2,1)S(1)} %dynamic-slice_bitcast_fusion), channel_id=1, source_target_pairs={{0,1},{1,0},{2,3},{3,2},{4,5},{5,4},{6,7},{7,6},{8,9},{9,8},{10,11... | collective-permute-start | bytes 737288 | tf_op jit(solution)/shard_map/ppermute | solution.py:534
  4.8 4.9 %conv.1 = (f32[2,8,480,128]{3,2,1,0:T(8,128)S(1)}, f32[2,2,8,128]{3,2,1,0:T(8,128)S(1)}) custom-call(bf16[2,8,480,128]{3,2,1,0:T(8,128)(2,1)} %video_ref.1, bf16[3,3,128,128]{3,2,1,0:T(8,128)(2,1)} %weight_ref.5), custom_call_target="tpu_custom_call" | custom-call | flops 20000000000 | tf_op jit(solution)/shard_map/conv/pallas_call | solution.py:117
  9.7 0.8 edge.1
  10.5 2.0 %collective-permute-start.1 = (f32[2,2,8,128]{3,2,1,0:T(8,128)S(1)}, f32[2,2,8,128]{3,2,1,0:T(8,128)S(1)}, u32[]{:S(2)}, u32[]{:S(2)}) collective-permute-start(f32[2,2,8,128]{3,2,1,0:T(8,128)S(1)} %get-tuple-element.65.own_ref), channel_id=1, source_target_pairs={{0,1},{1,0},{2,3},{3,2},{4,5},{5,4},{6,7},{7,6},{8,9},{9,8},{10,11... | collective-permute-start | bytes 49160 | tf_op jit(solution)/shard_map/ppermute | solution.py:543
  12.5 1.8 %collective-permute-done.1.other_ref = f32[2,2,8,128]{3,2,1,0:T(8,128)S(1)} collective-permute-done((f32[2,2,8,128]{3,2,1,0:T(8,128)S(1)}, f32[2,2,8,128]{3,2,1,0:T(8,128)S(1)}, u32[]{:S(2)}, u32[]{:S(2)}) %collective-permute-start.1) | collective-permute-done | bytes 16416 | tf_op jit(solution)/shard_map/ppermute | solution.py:543
  14.3 2.8 %norm.1 = (bf16[2,528,128]{2,1,0:T(8,128)(2,1)S(1)}, bf16[2,672,128]{2,1,0:T(8,128)(2,1)}, bf16[2,672,128]{2,1,0:T(8,128)(2,1)}, bf16[2,672,128]{2,1,0:T(8,128)(...) custom-call(f32[2,8,480,128]{3,2,1,0:T(8,128)S(1)} %get-tuple-elemen, ...), custom_call_target="tpu_custom_call" | custom-call | tf_op jit(solution)/shard_map/norm/pallas_call | solution.py:253
  17.1 0.7 collective-permute-start.6
  17.8 4.4 %collective-permute-start.2 = (bf16[2,672,128]{2,1,0:T(8,128)(2,1)}, bf16[2,672,128]{2,1,0:T(8,128)(2,1)S(1)}, u32[]{:S(2)}, u32[]{:S(2)}) collective-permute-start(bf16[2,672,128]{2,1,0:T(8,128)(2,1)} %get-tuple-element.69), channel_id=1, source_target_pairs={{0,2},{2,0},{4,6},{6,4},{8,10},{10,8},{12,14},{14,12},{16,18},{18,... | collective-permute-start | bytes 1032200 | tf_op jit(solution)/shard_map/ppermute | solution.py:580
  22.2 1.5 %collective-permute-start.3 = (bf16[2,672,128]{2,1,0:T(8,128)(2,1)}, bf16[2,672,128]{2,1,0:T(8,128)(2,1)S(1)}, u32[]{:S(2)}, u32[]{:S(2)}) collective-permute-start(bf16[2,672,128]{2,1,0:T(8,128)(2,1)} %get-tuple-element.70), channel_id=1, source_target_pairs={{0,4},{2,6},{4,0},{6,2},{8,12},{10,14},{12,8},{14,10},{16,20},{18,... | collective-permute-start | bytes 1032200 | tf_op jit(solution)/shard_map/ppermute | solution.py:580
  23.7 1.6 %guest.1 = (bf16[2,960,128]{2,1,0:T(8,128)(2,1)}, bf16[2,960,128]{2,1,0:T(8,128)(2,1)}, bf16[2,2,672,128]{3,2,1,0:T(8,128)(2,1)}, bf16[2,2,288,128]{3,2,1,0:T(8,128)(2,1)}) custom-call(bf16[2,8,480,128]{3,2,1,0:T(8,128)(2,1)S(1)} %collective-permute-done.5.video_ref, bf16[2,528,128]{2,1,0:T(8,128)(2,1)S(1)} %collective-permute-done.6.packet_ref, ...), custom_call_target="tpu_custom_call" | custom-call | flops 20000000000 | tf_op jit(solution)/shard_map/guest/pallas_call | solution.py:317
  25.4 3.4 %collective-permute-start.7 = (bf16[2,2,672,128]{3,2,1,0:T(8,128)(2,1)}, bf16[2,2,672,128]{3,2,1,0:T(8,128)(2,1)S(1)}, u32[]{:S(2)}, u32[]{:S(2)}) collective-permute-start(bf16[2,2,672,128]{3,2,1,0:T(8,128)(2,1)} %get-tuple-element.79), channel_id=1, source_target_pairs={{0,4},{4,0},{8,12},{12,8},{16,20},{20,16},{24,28},{28,24},{1,5},{5... | collective-permute-start | bytes 2064392 | tf_op jit(solution)/shard_map/ppermute | solution.py:600
  29.0 4.3 %collective-permute-done.3.refs_2_ = bf16[2,672,128]{2,1,0:T(8,128)(2,1)S(1)} collective-permute-done((bf16[2,672,128]{2,1,0:T(8,128)(2,1)}, bf16[2,672,128]{2,1,0:T(8,128)(2,1)S(1)}, u32[]{:S(2)}, u32[]{:S(2)}) %collective-permute-start.3) | collective-permute-done | bytes 344096 | tf_op jit(solution)/shard_map/ppermute | solution.py:580
  33.3 5.6 %collective-permute-done.4.refs_3_ = bf16[2,672,128]{2,1,0:T(8,128)(2,1)S(1)} collective-permute-done((bf16[2,672,128]{2,1,0:T(8,128)(2,1)}, bf16[2,672,128]{2,1,0:T(8,128)(2,1)S(1)}, u32[]{:S(2)}, u32[]{:S(2)}) %collective-permute-start.4) | collective-permute-done | bytes 344096 | tf_op jit(solution)/shard_map/ppermute | solution.py:580
  39.0 3.5 %collective-permute-start.16 = (bf16[2,672,128]{2,1,0:T(8,128)(2,1)S(1)}, bf16[2,672,128]{2,1,0:T(8,128)(2,1)S(1)}, u32[]{:S(2)}, u32[]{:S(2)}) collective-permute-start(bf16[2,672,128]{2,1,0:T(8,128)(2,1)S(1)} %select_select_fusion), channel_id=1, source_target_pairs={{0,8},{2,10},{4,12},{6,14},{8,16},{10,18},{12,20},{14,22},{16,24},... | collective-permute-start | bytes 1032200 | tf_op jit(solution)/shard_map/ppermute | solution.py:606
  42.6 2.5 %collective-permute-start.11 = (bf16[2,960,128]{2,1,0:T(8,128)(2,1)S(1)}, bf16[2,960,128]{2,1,0:T(8,128)(2,1)S(1)}, u32[]{:S(2)}, u32[]{:S(2)}) collective-permute-start(bf16[2,960,128]{2,1,0:T(8,128)(2,1)S(1)} %copy-done.7), channel_id=1, source_target_pairs={{0,2},{4,6},{8,10},{12,14},{16,18},{20,22},{24,26},{28,30},{1,3},{... | collective-permute-start | bytes 1474568 | tf_op jit(solution)/shard_map/ppermute | solution.py:608
  45.1 2.2 %collective-permute-done.7.refs_6_ = bf16[2,2,672,128]{3,2,1,0:T(8,128)(2,1)S(1)} collective-permute-done((bf16[2,2,672,128]{3,2,1,0:T(8,128)(2,1)}, bf16[2,2,672,128]{3,2,1,0:T(8,128)(2,1)S(1)}, u32[]{:S(2)}, u32[]{:S(2)}) %collective-permute-start.7) | collective-permute-done | bytes 688160 | tf_op jit(solution)/shard_map/ppermute | solution.py:600
  47.2 0.8 ahead.2.refs_9_
  48.1 1.4 %collective-permute-start.15 = (bf16[2,672,128]{2,1,0:T(8,128)(2,1)S(1)}, bf16[2,672,128]{2,1,0:T(8,128)(2,1)S(1)}, u32[]{:S(2)}, u32[]{:S(2)}) collective-permute-start(bf16[2,672,128]{2,1,0:T(8,128)(2,1)S(1)} %slice_bitcast_fusion), channel_id=1, source_target_pairs={{0,2},{4,6},{8,10},{12,14},{16,18},{20,22},{24,26},{28,30},{1,3},{... | collective-permute-start | bytes 1032200 | tf_op jit(solution)/shard_map/ppermute | solution.py:612
  49.5 1.2 %collective-permute-done.16.refs_8_ = bf16[2,672,128]{2,1,0:T(8,128)(2,1)S(1)} collective-permute-done((bf16[2,672,128]{2,1,0:T(8,128)(2,1)S(1)}, bf16[2,672,128]{2,1,0:T(8,128)(2,1)S(1)}, u32[]{:S(2)}, u32[]{:S(2)}) %collective-permute-start.16) | collective-permute-done | bytes 344096 | tf_op jit(solution)/shard_map/ppermute | solution.py:606
  50.8 1.2 %early.5.own_ref = bf16[8,512,128]{2,1,0:T(8,128)(2,1)S(1)} custom-call(bf16[2,672,128]{2,1,0:T(8,128)(2,1)S(1)} %copy-done.1, bf16[2,672,128]{2,1,0:T(8,128)(2,1)S(1)} %collective-permute-done.2.refs_1_, bf16[2,672,128]{2,1,0:T(8,128)(2,1)S(1)} %collective-permute-done.3.refs_2_, bf16[2,672,128]{2,1,0:T(8,128)(2,1)S(1)} %collective-permute-done.4.refs_3_, ...), custom_call_target="tpu_custom_call" | custom-call | tf_op jit(solution)/shard_map/early/pallas_call | solution.py:451
  52.0 4.7 %collective-permute-start.17 = (bf16[8,512,128]{2,1,0:T(8,128)(2,1)S(1)}, bf16[8,512,128]{2,1,0:T(8,128)(2,1)S(1)}, u32[]{:S(2)}, u32[]{:S(2)}) collective-permute-start(bf16[8,512,128]{2,1,0:T(8,128)(2,1)S(1)} %early.5.own_ref), channel_id=1, source_target_pairs={{0,8},{2,10},{4,12},{6,14},{8,16},{10,18},{12,20},{14,22},{16,24},... | collective-permute-start | bytes 3145736 | tf_op jit(solution)/shard_map/ppermute | solution.py:622
  56.8 1.5 %collective-permute-start.9 = (bf16[2,288,128]{2,1,0:T(8,128)(2,1)S(1)}, bf16[2,288,128]{2,1,0:T(8,128)(2,1)S(1)}, u32[]{:S(2)}, u32[]{:S(2)}) collective-permute-start(bf16[2,288,128]{2,1,0:T(8,128)(2,1)S(1)} %copy-done.11), channel_id=1, source_target_pairs={{0,4},{2,6},{4,0},{6,2},{8,12},{10,14},{12,8},{14,10},{16,20},{18,... | collective-permute-start | bytes 442376 | tf_op jit(solution)/shard_map/ppermute | solution.py:580
  58.3 0.7 collective-permute-start.8
  59.0 4.6 %collective-permute-done.9.refs_2_ = bf16[2,288,128]{2,1,0:T(8,128)(2,1)S(1)} collective-permute-done((bf16[2,288,128]{2,1,0:T(8,128)(2,1)S(1)}, bf16[2,288,128]{2,1,0:T(8,128)(2,1)S(1)}, u32[]{:S(2)}, u32[]{:S(2)}) %collective-permute-start.9) | collective-permute-done | bytes 147488 | tf_op jit(solution)/shard_map/ppermute | solution.py:580
  63.5 3.4 %collective-permute-start.12 = (bf16[2,2,288,128]{3,2,1,0:T(8,128)(2,1)S(1)}, bf16[2,2,288,128]{3,2,1,0:T(8,128)(2,1)S(1)}, u32[]{:S(2)}, u32[]{:S(2)}) collective-permute-start(bf16[2,2,288,128]{3,2,1,0:T(8,128)(2,1)S(1)} %copy-done.8), channel_id=1, source_target_pairs={{0,4},{4,0},{8,12},{12,8},{16,20},{20,16},{24,28},{28,24},{1,5},{5... | collective-permute-start | bytes 884744 | tf_op jit(solution)/shard_map/ppermute | solution.py:600
  67.0 3.4 %collective-permute-start.14 = (bf16[2,288,128]{2,1,0:T(8,128)(2,1)S(1)}, bf16[2,288,128]{2,1,0:T(8,128)(2,1)S(1)}, u32[]{:S(2)}, u32[]{:S(2)}) collective-permute-start(bf16[2,288,128]{2,1,0:T(8,128)(2,1)S(1)} %select_select_fusion.1), channel_id=1, source_target_pairs={{0,8},{2,10},{4,12},{6,14},{8,16},{10,18},{12,20},{14,22},{16,24},... | collective-permute-start | bytes 442376 | tf_op jit(solution)/shard_map/ppermute | solution.py:606
  70.4 0.7 early.6.own_ref
  71.1 3.5 %collective-permute-start.19 = (bf16[8,160,128]{2,1,0:T(8,128)(2,1)S(1)}, bf16[8,160,128]{2,1,0:T(8,128)(2,1)S(1)}, u32[]{:S(2)}, u32[]{:S(2)}) collective-permute-start(bf16[8,160,128]{2,1,0:T(8,128)(2,1)S(1)} %early.6.own_ref), channel_id=1, source_target_pairs={{0,8},{2,10},{4,12},{6,14},{8,16},{10,18},{12,20},{14,22},{16,24},... | collective-permute-start | bytes 983048 | tf_op jit(solution)/shard_map/ppermute | solution.py:622
  74.6 1.3 %collective-permute-start.13 = (bf16[2,288,128]{2,1,0:T(8,128)(2,1)S(1)}, bf16[2,288,128]{2,1,0:T(8,128)(2,1)S(1)}, u32[]{:S(2)}, u32[]{:S(2)}) collective-permute-start(bf16[2,288,128]{2,1,0:T(8,128)(2,1)S(1)} %slice_bitcast_fusion.1), channel_id=1, source_target_pairs={{0,2},{4,6},{8,10},{12,14},{16,18},{20,22},{24,26},{28,30},{1,3},{... | collective-permute-start | bytes 442376 | tf_op jit(solution)/shard_map/ppermute | solution.py:612
  75.9 4.2 %collective-permute-done.17.halo_ref = bf16[8,512,128]{2,1,0:T(8,128)(2,1)S(1)} collective-permute-done((bf16[8,512,128]{2,1,0:T(8,128)(2,1)S(1)}, bf16[8,512,128]{2,1,0:T(8,128)(2,1)S(1)}, u32[]{:S(2)}, u32[]{:S(2)}) %collective-permute-start.17) | collective-permute-done | bytes 1048608 | tf_op jit(solution)/shard_map/ppermute | solution.py:622
  80.2 0.8 late.6
  81.1 1.5 %collective-permute-start.23 = (bf16[2,512,128]{2,1,0:T(8,128)(2,1)S(1)}, bf16[2,512,128]{2,1,0:T(8,128)(2,1)S(1)}, u32[]{:S(2)}, u32[]{:S(2)}) collective-permute-start(bf16[2,512,128]{2,1,0:T(8,128)(2,1)S(1)} %get-tuple-element.101), channel_id=1, source_target_pairs={{0,4},{2,6},{4,0},{6,2},{8,12},{10,14},{12,8},{14,10},{16,20},{18,... | collective-permute-start | bytes 786440 | tf_op jit(solution)/shard_map/ppermute | solution.py:580
  82.6 0.7 collective-permute-done.14.refs_8_
  83.8 0.8 early.4.own_ref
  84.6 4.4 %collective-permute-start.18 = (bf16[8,160,128]{2,1,0:T(8,128)(2,1)S(1)}, bf16[8,160,128]{2,1,0:T(8,128)(2,1)S(1)}, u32[]{:S(2)}, u32[]{:S(2)}) collective-permute-start(bf16[8,160,128]{2,1,0:T(8,128)(2,1)S(1)} %early.4.own_ref), channel_id=1, source_target_pairs={{0,8},{2,10},{4,12},{6,14},{8,16},{10,18},{12,20},{14,22},{16,24},... | collective-permute-start | bytes 983048 | tf_op jit(solution)/shard_map/ppermute | solution.py:622
  89.0 0.6 early.7.own_ref
  90.3 4.4 %collective-permute-start.29 = (bf16[8,128,128]{2,1,0:T(8,128)(2,1)S(1)}, bf16[8,128,128]{2,1,0:T(8,128)(2,1)S(1)}, u32[]{:S(2)}, u32[]{:S(2)}) collective-permute-start(bf16[8,128,128]{2,1,0:T(8,128)(2,1)S(1)} %early.7.own_ref), channel_id=1, source_target_pairs={{0,8},{2,10},{4,12},{6,14},{8,16},{10,18},{12,20},{14,22},{16,24},... | collective-permute-start | bytes 786440 | tf_op jit(solution)/shard_map/ppermute | solution.py:622
  95.2 1.1 collective-permute-start.24
  97.5 2.0 %collective-permute-done.27.refs_7_ = bf16[2,160,128]{2,1,0:T(8,128)(2,1)S(1)} collective-permute-done((bf16[2,160,128]{2,1,0:T(8,128)(2,1)S(1)}, bf16[2,160,128]{2,1,0:T(8,128)(2,1)S(1)}, u32[]{:S(2)}, u32[]{:S(2)}) %collective-permute-start.27) | collective-permute-done | bytes 81952 | tf_op jit(solution)/shard_map/ppermute | solution.py:580
  99.5 1.8 %collective-permute-done.24.refs_6_ = bf16[2,160,128]{2,1,0:T(8,128)(2,1)S(1)} collective-permute-done((bf16[2,160,128]{2,1,0:T(8,128)(2,1)S(1)}, bf16[2,160,128]{2,1,0:T(8,128)(2,1)S(1)}, u32[]{:S(2)}, u32[]{:S(2)}) %collective-permute-start.24) | collective-permute-done | bytes 81952 | tf_op jit(solution)/shard_map/ppermute | solution.py:580
  101.6 0.8 collective-permute-done.29.halo_ref
  102.8 1.1 %collective-permute-done.28.refs_3_ = bf16[2,160,128]{2,1,0:T(8,128)(2,1)S(1)} collective-permute-done((bf16[2,160,128]{2,1,0:T(8,128)(2,1)S(1)}, bf16[2,160,128]{2,1,0:T(8,128)(2,1)S(1)}, u32[]{:S(2)}, u32[]{:S(2)}) %collective-permute-start.28) | collective-permute-done | bytes 81952 | tf_op jit(solution)/shard_map/ppermute | solution.py:580
  103.9 2.0 %collective-permute-done.25.refs_2_ = bf16[2,160,128]{2,1,0:T(8,128)(2,1)S(1)} collective-permute-done((bf16[2,160,128]{2,1,0:T(8,128)(2,1)S(1)}, bf16[2,160,128]{2,1,0:T(8,128)(2,1)S(1)}, u32[]{:S(2)}, u32[]{:S(2)}) %collective-permute-start.25) | collective-permute-done | bytes 81952 | tf_op jit(solution)/shard_map/ppermute | solution.py:580
  106.5 1.1 %place.2.refs_8_ = bf16[2,4,960,128]{3,2,1,0:T(8,128)(2,1)} custom-call(bf16[2,512,128]{2,1,0:T(8,128)(2,1)S(1)} %get-tuple-element.118.refs_0_, bf16[2,512,128]{2,1,0:T(8,128)(2,1)S(1)} %collective-permute-done.20.refs_1_, bf16[2,512,128]{2,1,0:T(8,128)(2,1)S(1)} %collective-permute-done.23.refs_2_, ...), custom_call_target="tpu_custom_call" | custom-call | tf_op jit(solution)/shard_map/place/pallas_call | solution.py:516
  107.8 2.4 %collective-permute-done.31.refs_6_ = bf16[2,128,128]{2,1,0:T(8,128)(2,1)S(1)} collective-permute-done((bf16[2,128,128]{2,1,0:T(8,128)(2,1)S(1)}, bf16[2,128,128]{2,1,0:T(8,128)(2,1)S(1)}, u32[]{:S(2)}, u32[]{:S(2)}) %collective-permute-start.31) | collective-permute-done | bytes 65568 | tf_op jit(solution)/shard_map/ppermute | solution.py:580
  110.2 0.9 place.3
  (64 shorter events, 4.7 us)
Async XLA Ops:
  0.0 23.7 %collective-permute-start.5 = (bf16[2,8,480,128]{3,2,1,0:T(8,128)(2,1)}, bf16[2,8,480,128]{3,2,1,0:T(8,128)(2,1)S(1)}, u32[]{:S(2)}, u32[]{:S(2)}) collective-permute-start(bf16[2,8,480,128]{3,2,1,0:T(8,128)(2,1)} %video_ref.1), channel_id=1, source_target_pairs={{2,8},{6,12},{10,16},{14,20},{18,24},{22,28},{3,9},{7,13},{11,17},... | collective-permute-start | bytes 5898248 | tf_op jit(solution)/shard_map/ppermute | solution.py:562
  1.8 7.9 %copy-start.3 = (bf16[3,3,128,128]{3,2,1,0:T(8,128)(2,1)S(1)}, bf16[3,3,128,128]{3,2,1,0:T(8,128)(2,1)}, u32[]{:S(2)}) copy-start(bf16[3,3,128,128]{3,2,1,0:T(8,128)(2,1)} %weight_ref.5) | copy-start | bytes 884740
  1.8 7.9 %collective-permute-start = (bf16[2,480,128]{2,1,0:T(8,128)(2,1)S(1)}, bf16[2,480,128]{2,1,0:T(8,128)(2,1)S(1)}, u32[]{:S(2)}, u32[]{:S(2)}) collective-permute-start(bf16[2,480,128]{2,1,0:T(8,128)(2,1)S(1)} %dynamic-slice_bitcast_fusion), channel_id=1, source_target_pairs={{0,1},{1,0},{2,3},{3,2},{4,5},{5,4},{6,7},{7,6},{8,9},{9,8},{10,11... | collective-permute-start | bytes 737288 | tf_op jit(solution)/shard_map/ppermute | solution.py:534
  9.7 4.6 %copy-start.4 = (f32[128]{0:T(128)S(1)}, f32[128]{0:T(128)}, u32[]{:S(2)}) copy-start(f32[128]{0:T(128)} %param.7) | copy-start | bytes 1540
  9.7 4.6 %copy-start.5 = (f32[128]{0:T(128)S(1)}, f32[128]{0:T(128)}, u32[]{:S(2)}) copy-start(f32[128]{0:T(128)} %param.8) | copy-start | bytes 1540
  10.5 3.8 %collective-permute-start.1 = (f32[2,2,8,128]{3,2,1,0:T(8,128)S(1)}, f32[2,2,8,128]{3,2,1,0:T(8,128)S(1)}, u32[]{:S(2)}, u32[]{:S(2)}) collective-permute-start(f32[2,2,8,128]{3,2,1,0:T(8,128)S(1)} %get-tuple-element.65.own_ref), channel_id=1, source_target_pairs={{0,1},{1,0},{2,3},{3,2},{4,5},{5,4},{6,7},{7,6},{8,9},{9,8},{10,11... | collective-permute-start | bytes 49160 | tf_op jit(solution)/shard_map/ppermute | solution.py:543
  17.1 6.6 %collective-permute-start.6 = (bf16[2,528,128]{2,1,0:T(8,128)(2,1)S(1)}, bf16[2,528,128]{2,1,0:T(8,128)(2,1)S(1)}, u32[]{:S(2)}, u32[]{:S(2)}) collective-permute-start(bf16[2,528,128]{2,1,0:T(8,128)(2,1)S(1)} %get-tuple-element.72), channel_id=1, source_target_pairs={{2,8},{6,12},{10,16},{14,20},{18,24},{22,28},{3,9},{7,13},{11,17},... | collective-permute-start | bytes 811016 | tf_op jit(solution)/shard_map/ppermute | solution.py:583
  17.8 11.2 %collective-permute-start.2 = (bf16[2,672,128]{2,1,0:T(8,128)(2,1)}, bf16[2,672,128]{2,1,0:T(8,128)(2,1)S(1)}, u32[]{:S(2)}, u32[]{:S(2)}) collective-permute-start(bf16[2,672,128]{2,1,0:T(8,128)(2,1)} %get-tuple-element.69), channel_id=1, source_target_pairs={{0,2},{2,0},{4,6},{6,4},{8,10},{10,8},{12,14},{14,12},{16,18},{18,... | collective-permute-start | bytes 1032200 | tf_op jit(solution)/shard_map/ppermute | solution.py:580
  22.2 11.1 %collective-permute-start.3 = (bf16[2,672,128]{2,1,0:T(8,128)(2,1)}, bf16[2,672,128]{2,1,0:T(8,128)(2,1)S(1)}, u32[]{:S(2)}, u32[]{:S(2)}) collective-permute-start(bf16[2,672,128]{2,1,0:T(8,128)(2,1)} %get-tuple-element.70), channel_id=1, source_target_pairs={{0,4},{2,6},{4,0},{6,2},{8,12},{10,14},{12,8},{14,10},{16,20},{18,... | collective-permute-start | bytes 1032200 | tf_op jit(solution)/shard_map/ppermute | solution.py:580
  23.7 5.1 %copy-start.6 = (bf16[3,3,128,128]{3,2,1,0:T(8,128)(2,1)S(1)}, bf16[3,3,128,128]{3,2,1,0:T(8,128)(2,1)}, u32[]{:S(2)}) copy-start(bf16[3,3,128,128]{3,2,1,0:T(8,128)(2,1)} %weight_ref.6) | copy-start | bytes 884740
  23.7 15.3 %collective-permute-start.4 = (bf16[2,672,128]{2,1,0:T(8,128)(2,1)}, bf16[2,672,128]{2,1,0:T(8,128)(2,1)S(1)}, u32[]{:S(2)}, u32[]{:S(2)}) collective-permute-start(bf16[2,672,128]{2,1,0:T(8,128)(2,1)} %get-tuple-element.71), channel_id=1, source_target_pairs={{0,6},{2,4},{4,2},{6,0},{8,14},{10,12},{12,10},{14,8},{16,22},{18,... | collective-permute-start | bytes 1032200 | tf_op jit(solution)/shard_map/ppermute | solution.py:580
  25.4 13.6 %copy-start.1 = (bf16[2,672,128]{2,1,0:T(8,128)(2,1)S(1)}, bf16[2,672,128]{2,1,0:T(8,128)(2,1)}, u32[]{:S(2)}) copy-start(bf16[2,672,128]{2,1,0:T(8,128)(2,1)} %get-tuple-element.78.refs_0_) | copy-start | bytes 1032196
  25.4 17.2 %copy-start.7 = (bf16[2,960,128]{2,1,0:T(8,128)(2,1)S(1)}, bf16[2,960,128]{2,1,0:T(8,128)(2,1)}, u32[]{:S(2)}) copy-start(bf16[2,960,128]{2,1,0:T(8,128)(2,1)} %get-tuple-element.87) | copy-start | bytes 1474564
  25.4 21.8 %collective-permute-start.7 = (bf16[2,2,672,128]{3,2,1,0:T(8,128)(2,1)}, bf16[2,2,672,128]{3,2,1,0:T(8,128)(2,1)S(1)}, u32[]{:S(2)}, u32[]{:S(2)}) collective-permute-start(bf16[2,2,672,128]{3,2,1,0:T(8,128)(2,1)} %get-tuple-element.79), channel_id=1, source_target_pairs={{0,4},{4,0},{8,12},{12,8},{16,20},{20,16},{24,28},{28,24},{1,5},{5... | collective-permute-start | bytes 2064392 | tf_op jit(solution)/shard_map/ppermute | solution.py:600
  39.0 11.7 %collective-permute-start.16 = (bf16[2,672,128]{2,1,0:T(8,128)(2,1)S(1)}, bf16[2,672,128]{2,1,0:T(8,128)(2,1)S(1)}, u32[]{:S(2)}, u32[]{:S(2)}) collective-permute-start(bf16[2,672,128]{2,1,0:T(8,128)(2,1)S(1)} %select_select_fusion), channel_id=1, source_target_pairs={{0,8},{2,10},{4,12},{6,14},{8,16},{10,18},{12,20},{14,22},{16,24},... | collective-permute-start | bytes 1032200 | tf_op jit(solution)/shard_map/ppermute | solution.py:606
  42.6 8.2 %copy-start = (bf16[2,960,128]{2,1,0:T(8,128)(2,1)S(1)}, bf16[2,960,128]{2,1,0:T(8,128)(2,1)}, u32[]{:S(2)}) copy-start(bf16[2,960,128]{2,1,0:T(8,128)(2,1)} %get-tuple-element.73.refs_4_) | copy-start | bytes 1474564
  42.6 8.1 %collective-permute-start.11 = (bf16[2,960,128]{2,1,0:T(8,128)(2,1)S(1)}, bf16[2,960,128]{2,1,0:T(8,128)(2,1)S(1)}, u32[]{:S(2)}, u32[]{:S(2)}) collective-permute-start(bf16[2,960,128]{2,1,0:T(8,128)(2,1)S(1)} %copy-done.7), channel_id=1, source_target_pairs={{0,2},{4,6},{8,10},{12,14},{16,18},{20,22},{24,26},{28,30},{1,3},{... | collective-permute-start | bytes 1474568 | tf_op jit(solution)/shard_map/ppermute | solution.py:608
  48.0 8.7 %copy-start.11 = (bf16[2,288,128]{2,1,0:T(8,128)(2,1)S(1)}, bf16[2,288,128]{2,1,0:T(8,128)(2,1)}, u32[]{:S(2)}) copy-start(bf16[2,288,128]{2,1,0:T(8,128)(2,1)} %get-tuple-element.83) | copy-start | bytes 442372
  48.0 10.3 %copy-start.10 = (bf16[2,288,128]{2,1,0:T(8,128)(2,1)S(1)}, bf16[2,288,128]{2,1,0:T(8,128)(2,1)}, u32[]{:S(2)}) copy-start(bf16[2,288,128]{2,1,0:T(8,128)(2,1)} %get-tuple-element.85) | copy-start | bytes 442372
  48.0 10.3 %copy-start.9 = (bf16[2,288,128]{2,1,0:T(8,128)(2,1)S(1)}, bf16[2,288,128]{2,1,0:T(8,128)(2,1)}, u32[]{:S(2)}) copy-start(bf16[2,288,128]{2,1,0:T(8,128)(2,1)} %get-tuple-element.81) | copy-start | bytes 442372
  48.1 15.5 %copy-start.8 = (bf16[2,2,288,128]{3,2,1,0:T(8,128)(2,1)S(1)}, bf16[2,2,288,128]{3,2,1,0:T(8,128)(2,1)}, u32[]{:S(2)}) copy-start(bf16[2,2,288,128]{3,2,1,0:T(8,128)(2,1)} %get-tuple-element.89) | copy-start | bytes 884740
  48.1 18.9 %copy-start.2 = (bf16[2,288,128]{2,1,0:T(8,128)(2,1)S(1)}, bf16[2,288,128]{2,1,0:T(8,128)(2,1)}, u32[]{:S(2)}) copy-start(bf16[2,288,128]{2,1,0:T(8,128)(2,1)} %get-tuple-element.66.refs_0_) | copy-start | bytes 442372
  48.1 2.7 %collective-permute-start.15 = (bf16[2,672,128]{2,1,0:T(8,128)(2,1)S(1)}, bf16[2,672,128]{2,1,0:T(8,128)(2,1)S(1)}, u32[]{:S(2)}, u32[]{:S(2)}) collective-permute-start(bf16[2,672,128]{2,1,0:T(8,128)(2,1)S(1)} %slice_bitcast_fusion), channel_id=1, source_target_pairs={{0,2},{4,6},{8,10},{12,14},{16,18},{20,22},{24,26},{28,30},{1,3},{... | collective-permute-start | bytes 1032200 | tf_op jit(solution)/shard_map/ppermute | solution.py:612
  52.0 28.2 %collective-permute-start.17 = (bf16[8,512,128]{2,1,0:T(8,128)(2,1)S(1)}, bf16[8,512,128]{2,1,0:T(8,128)(2,1)S(1)}, u32[]{:S(2)}, u32[]{:S(2)}) collective-permute-start(bf16[8,512,128]{2,1,0:T(8,128)(2,1)S(1)} %early.5.own_ref), channel_id=1, source_target_pairs={{0,8},{2,10},{4,12},{6,14},{8,16},{10,18},{12,20},{14,22},{16,24},... | collective-permute-start | bytes 3145736 | tf_op jit(solution)/shard_map/ppermute | solution.py:622
  56.8 6.8 %collective-permute-start.9 = (bf16[2,288,128]{2,1,0:T(8,128)(2,1)S(1)}, bf16[2,288,128]{2,1,0:T(8,128)(2,1)S(1)}, u32[]{:S(2)}, u32[]{:S(2)}) collective-permute-start(bf16[2,288,128]{2,1,0:T(8,128)(2,1)S(1)} %copy-done.11), channel_id=1, source_target_pairs={{0,4},{2,6},{4,0},{6,2},{8,12},{10,14},{12,8},{14,10},{16,20},{18,... | collective-permute-start | bytes 442376 | tf_op jit(solution)/shard_map/ppermute | solution.py:580
  58.3 8.6 %collective-permute-start.10 = (bf16[2,288,128]{2,1,0:T(8,128)(2,1)S(1)}, bf16[2,288,128]{2,1,0:T(8,128)(2,1)S(1)}, u32[]{:S(2)}, u32[]{:S(2)}) collective-permute-start(bf16[2,288,128]{2,1,0:T(8,128)(2,1)S(1)} %copy-done.10), channel_id=1, source_target_pairs={{0,6},{2,4},{4,2},{6,0},{8,14},{10,12},{12,10},{14,8},{16,22},{18,... | collective-permute-start | bytes 442376 | tf_op jit(solution)/shard_map/ppermute | solution.py:580
  58.3 8.6 %collective-permute-start.8 = (bf16[2,288,128]{2,1,0:T(8,128)(2,1)S(1)}, bf16[2,288,128]{2,1,0:T(8,128)(2,1)S(1)}, u32[]{:S(2)}, u32[]{:S(2)}) collective-permute-start(bf16[2,288,128]{2,1,0:T(8,128)(2,1)S(1)} %copy-done.9), channel_id=1, source_target_pairs={{0,2},{2,0},{4,6},{6,4},{8,10},{10,8},{12,14},{14,12},{16,18},{18,... | collective-permute-start | bytes 442376 | tf_op jit(solution)/shard_map/ppermute | solution.py:580
  63.5 11.1 %collective-permute-start.12 = (bf16[2,2,288,128]{3,2,1,0:T(8,128)(2,1)S(1)}, bf16[2,2,288,128]{3,2,1,0:T(8,128)(2,1)S(1)}, u32[]{:S(2)}, u32[]{:S(2)}) collective-permute-start(bf16[2,2,288,128]{3,2,1,0:T(8,128)(2,1)S(1)} %copy-done.8), channel_id=1, source_target_pairs={{0,4},{4,0},{8,12},{12,8},{16,20},{20,16},{24,28},{28,24},{1,5},{5... | collective-permute-start | bytes 884744 | tf_op jit(solution)/shard_map/ppermute | solution.py:600
  67.0 16.3 %collective-permute-start.14 = (bf16[2,288,128]{2,1,0:T(8,128)(2,1)S(1)}, bf16[2,288,128]{2,1,0:T(8,128)(2,1)S(1)}, u32[]{:S(2)}, u32[]{:S(2)}) collective-permute-start(bf16[2,288,128]{2,1,0:T(8,128)(2,1)S(1)} %select_select_fusion.1), channel_id=1, source_target_pairs={{0,8},{2,10},{4,12},{6,14},{8,16},{10,18},{12,20},{14,22},{16,24},... | collective-permute-start | bytes 442376 | tf_op jit(solution)/shard_map/ppermute | solution.py:606
  71.1 18.8 %collective-permute-start.19 = (bf16[8,160,128]{2,1,0:T(8,128)(2,1)S(1)}, bf16[8,160,128]{2,1,0:T(8,128)(2,1)S(1)}, u32[]{:S(2)}, u32[]{:S(2)}) collective-permute-start(bf16[8,160,128]{2,1,0:T(8,128)(2,1)S(1)} %early.6.own_ref), channel_id=1, source_target_pairs={{0,8},{2,10},{4,12},{6,14},{8,16},{10,18},{12,20},{14,22},{16,24},... | collective-permute-start | bytes 983048 | tf_op jit(solution)/shard_map/ppermute | solution.py:622
  74.6 9.1 %collective-permute-start.13 = (bf16[2,288,128]{2,1,0:T(8,128)(2,1)S(1)}, bf16[2,288,128]{2,1,0:T(8,128)(2,1)S(1)}, u32[]{:S(2)}, u32[]{:S(2)}) collective-permute-start(bf16[2,288,128]{2,1,0:T(8,128)(2,1)S(1)} %slice_bitcast_fusion.1), channel_id=1, source_target_pairs={{0,2},{4,6},{8,10},{12,14},{16,18},{20,22},{24,26},{28,30},{1,3},{... | collective-permute-start | bytes 442376 | tf_op jit(solution)/shard_map/ppermute | solution.py:612
  80.9 13.7 %collective-permute-start.26 = (bf16[2,512,128]{2,1,0:T(8,128)(2,1)S(1)}, bf16[2,512,128]{2,1,0:T(8,128)(2,1)S(1)}, u32[]{:S(2)}, u32[]{:S(2)}) collective-permute-start(bf16[2,512,128]{2,1,0:T(8,128)(2,1)S(1)} %get-tuple-element.106), channel_id=1, source_target_pairs={{0,6},{2,4},{4,2},{6,0},{8,14},{10,12},{12,10},{14,8},{16,22},{18,... | collective-permute-start | bytes 786440 | tf_op jit(solution)/shard_map/ppermute | solution.py:580
  81.1 14.1 %collective-permute-start.23 = (bf16[2,512,128]{2,1,0:T(8,128)(2,1)S(1)}, bf16[2,512,128]{2,1,0:T(8,128)(2,1)S(1)}, u32[]{:S(2)}, u32[]{:S(2)}) collective-permute-start(bf16[2,512,128]{2,1,0:T(8,128)(2,1)S(1)} %get-tuple-element.101), channel_id=1, source_target_pairs={{0,4},{2,6},{4,0},{6,2},{8,12},{10,14},{12,8},{14,10},{16,20},{18,... | collective-permute-start | bytes 786440 | tf_op jit(solution)/shard_map/ppermute | solution.py:580
  83.3 13.0 %collective-permute-start.20 = (bf16[2,512,128]{2,1,0:T(8,128)(2,1)S(1)}, bf16[2,512,128]{2,1,0:T(8,128)(2,1)S(1)}, u32[]{:S(2)}, u32[]{:S(2)}) collective-permute-start(bf16[2,512,128]{2,1,0:T(8,128)(2,1)S(1)} %get-tuple-element.96), channel_id=1, source_target_pairs={{0,2},{2,0},{4,6},{6,4},{8,10},{10,8},{12,14},{14,12},{16,18},{18,... | collective-permute-start | bytes 786440 | tf_op jit(solution)/shard_map/ppermute | solution.py:580
  84.6 12.5 %collective-permute-start.18 = (bf16[8,160,128]{2,1,0:T(8,128)(2,1)S(1)}, bf16[8,160,128]{2,1,0:T(8,128)(2,1)S(1)}, u32[]{:S(2)}, u32[]{:S(2)}) collective-permute-start(bf16[8,160,128]{2,1,0:T(8,128)(2,1)S(1)} %early.4.own_ref), channel_id=1, source_target_pairs={{0,8},{2,10},{4,12},{6,14},{8,16},{10,18},{12,20},{14,22},{16,24},... | collective-permute-start | bytes 983048 | tf_op jit(solution)/shard_map/ppermute | solution.py:622
  90.3 12.2 %collective-permute-start.29 = (bf16[8,128,128]{2,1,0:T(8,128)(2,1)S(1)}, bf16[8,128,128]{2,1,0:T(8,128)(2,1)S(1)}, u32[]{:S(2)}, u32[]{:S(2)}) collective-permute-start(bf16[8,128,128]{2,1,0:T(8,128)(2,1)S(1)} %early.7.own_ref), channel_id=1, source_target_pairs={{0,8},{2,10},{4,12},{6,14},{8,16},{10,18},{12,20},{14,22},{16,24},... | collective-permute-start | bytes 786440 | tf_op jit(solution)/shard_map/ppermute | solution.py:622
  94.7 4.8 %collective-permute-start.27 = (bf16[2,160,128]{2,1,0:T(8,128)(2,1)S(1)}, bf16[2,160,128]{2,1,0:T(8,128)(2,1)S(1)}, u32[]{:S(2)}, u32[]{:S(2)}) collective-permute-start(bf16[2,160,128]{2,1,0:T(8,128)(2,1)S(1)} %get-tuple-element.107), channel_id=1, source_target_pairs={{0,6},{2,4},{4,2},{6,0},{8,14},{10,12},{12,10},{14,8},{16,22},{18,... | collective-permute-start | bytes 245768 | tf_op jit(solution)/shard_map/ppermute | solution.py:580
  95.2 6.0 %collective-permute-start.24 = (bf16[2,160,128]{2,1,0:T(8,128)(2,1)S(1)}, bf16[2,160,128]{2,1,0:T(8,128)(2,1)S(1)}, u32[]{:S(2)}, u32[]{:S(2)}) collective-permute-start(bf16[2,160,128]{2,1,0:T(8,128)(2,1)S(1)} %get-tuple-element.102), channel_id=1, source_target_pairs={{0,4},{2,6},{4,0},{6,2},{8,12},{10,14},{12,8},{14,10},{16,20},{18,... | collective-permute-start | bytes 245768 | tf_op jit(solution)/shard_map/ppermute | solution.py:580
  96.3 5.3 %collective-permute-start.21 = (bf16[2,160,128]{2,1,0:T(8,128)(2,1)S(1)}, bf16[2,160,128]{2,1,0:T(8,128)(2,1)S(1)}, u32[]{:S(2)}, u32[]{:S(2)}) collective-permute-start(bf16[2,160,128]{2,1,0:T(8,128)(2,1)S(1)} %get-tuple-element.97), channel_id=1, source_target_pairs={{0,2},{2,0},{4,6},{6,4},{8,10},{10,8},{12,14},{14,12},{16,18},{18,... | collective-permute-start | bytes 245768 | tf_op jit(solution)/shard_map/ppermute | solution.py:580
  99.4 4.4 %collective-permute-start.28 = (bf16[2,160,128]{2,1,0:T(8,128)(2,1)S(1)}, bf16[2,160,128]{2,1,0:T(8,128)(2,1)S(1)}, u32[]{:S(2)}, u32[]{:S(2)}) collective-permute-start(bf16[2,160,128]{2,1,0:T(8,128)(2,1)S(1)} %get-tuple-element.108), channel_id=1, source_target_pairs={{0,6},{2,4},{4,2},{6,0},{8,14},{10,12},{12,10},{14,8},{16,22},{18,... | collective-permute-start | bytes 245768 | tf_op jit(solution)/shard_map/ppermute | solution.py:580
  101.2 4.7 %collective-permute-start.25 = (bf16[2,160,128]{2,1,0:T(8,128)(2,1)S(1)}, bf16[2,160,128]{2,1,0:T(8,128)(2,1)S(1)}, u32[]{:S(2)}, u32[]{:S(2)}) collective-permute-start(bf16[2,160,128]{2,1,0:T(8,128)(2,1)S(1)} %get-tuple-element.103), channel_id=1, source_target_pairs={{0,4},{2,6},{4,0},{6,2},{8,12},{10,14},{12,8},{14,10},{16,20},{18,... | collective-permute-start | bytes 245768 | tf_op jit(solution)/shard_map/ppermute | solution.py:580
  101.6 4.9 %collective-permute-start.22 = (bf16[2,160,128]{2,1,0:T(8,128)(2,1)S(1)}, bf16[2,160,128]{2,1,0:T(8,128)(2,1)S(1)}, u32[]{:S(2)}, u32[]{:S(2)}) collective-permute-start(bf16[2,160,128]{2,1,0:T(8,128)(2,1)S(1)} %get-tuple-element.98), channel_id=1, source_target_pairs={{0,2},{2,0},{4,6},{6,4},{8,10},{10,8},{12,14},{14,12},{16,18},{18,... | collective-permute-start | bytes 245768 | tf_op jit(solution)/shard_map/ppermute | solution.py:580
  103.9 3.9 %collective-permute-start.32 = (bf16[2,128,128]{2,1,0:T(8,128)(2,1)S(1)}, bf16[2,128,128]{2,1,0:T(8,128)(2,1)S(1)}, u32[]{:S(2)}, u32[]{:S(2)}) collective-permute-start(bf16[2,128,128]{2,1,0:T(8,128)(2,1)S(1)} %get-tuple-element.117), channel_id=1, source_target_pairs={{0,6},{2,4},{4,2},{6,0},{8,14},{10,12},{12,10},{14,8},{16,22},{18,... | collective-permute-start | bytes 196616 | tf_op jit(solution)/shard_map/ppermute | solution.py:580
  106.0 4.3 %collective-permute-start.31 = (bf16[2,128,128]{2,1,0:T(8,128)(2,1)S(1)}, bf16[2,128,128]{2,1,0:T(8,128)(2,1)S(1)}, u32[]{:S(2)}, u32[]{:S(2)}) collective-permute-start(bf16[2,128,128]{2,1,0:T(8,128)(2,1)S(1)} %get-tuple-element.115), channel_id=1, source_target_pairs={{0,4},{2,6},{4,0},{6,2},{8,12},{10,14},{12,8},{14,10},{16,20},{18,... | collective-permute-start | bytes 196616 | tf_op jit(solution)/shard_map/ppermute | solution.py:580
  106.5 3.7 %collective-permute-start.30 = (bf16[2,128,128]{2,1,0:T(8,128)(2,1)S(1)}, bf16[2,128,128]{2,1,0:T(8,128)(2,1)S(1)}, u32[]{:S(2)}, u32[]{:S(2)}) collective-permute-start(bf16[2,128,128]{2,1,0:T(8,128)(2,1)S(1)} %get-tuple-element.113), channel_id=1, source_target_pairs={{0,2},{2,0},{4,6},{6,4},{8,10},{10,8},{12,14},{14,12},{16,18},{18,... | collective-permute-start | bytes 196616 | tf_op jit(solution)/shard_map/ppermute | solution.py:580

commit v8 on v7

--- a/solution.py
+++ b/solution.py
@@ -618,7 +618,7 @@
         if i == 0:
             block(1, aheads[0])
         if i > 1:
-            u2 = after(u2, passed[0] if i == 2 else late[0])
+            u2 = after(u2, passed[i - 2])
         passed.append(lax.ppermute(u2, "tm", onward))
         following = late_call(u2, passed[-1], wide, members)
         results.append(swap(following, results[-1] if results else None))

time: 112 us -> 112 us (level)
  no operation moved by 1% of the time
where the time goes in v8:
time: 112 us; the launch traced here: 111 us
  starting transfers between devices  54.8 us (49%)
  waiting for transfers between devices  36.1 us (32%)
  Pallas kernels  18.6 us (17%)
    ppermute x18, waiting for transfers between devices, swap(): got.append(lax.ppermute(value, 'tm', swaps[k]))  24.3 us
    ppermute x4, starting transfers between devices, body(): passed.append(lax.ppermute(u2, 'tm', onward))  17 us
    ppermute x18, starting transfers between devices, swap(): got.append(lax.ppermute(value, 'tm', swaps[k]))  12.3 us
    ppermute x2, starting transfers between devices, block(): add(2 * members, [lax.ppermute(middle, 'tm', onward)])  6.93 us
    ppermute x2, starting transfers between devices, block(): lax.ppermute(after(aways[i], own[2]) if i else aways[i], 'tm', guest_swap...  6.82 us
    ppermute x4, waiting for transfers between devices, body(): passed.append(lax.ppermute(u2, 'tm', onward))  5.77 us
    pallas_call x1, Pallas kernels, conv_call(): pl.pallas_call(functools.partial(conv_kernel, band), grid=(frames,), in_s...  4.86 us
    pallas_call x4, Pallas kernels, early_call(): pl.pallas_call(functools.partial(early_kernel, members, plan, start), in_...  3.34 us
  transfers between devices with their start and end apart: 33, of which 19 were waited for; matrix products, arithmetic and copies ran while one was open for 1% of the time, Pallas kernels for 15%

profile of v8, /device:TPU:0, one launch (start us, length us, event | category | flops | bytes accessed | tf_op | source)
XLA Modules:
  0.0 111.2 jit_solution(9154635553772511264)
XLA Ops:
  0.0 0.8 collective-permute-start.5
  0.8 1.0 dynamic-slice_bitcast_fusion
  1.8 3.0 %collective-permute-start = (bf16[2,480,128]{2,1,0:T(8,128)(2,1)S(1)}, bf16[2,480,128]{2,1,0:T(8,128)(2,1)S(1)}, u32[]{:S(2)}, u32[]{:S(2)}) collective-permute-start(bf16[2,480,128]{2,1,0:T(8,128)(2,1)S(1)} %dynamic-slice_bitcast_fusion), channel_id=1, source_target_pairs={{0,1},{1,0},{2,3},{3,2},{4,5},{5,4},{6,7},{7,6},{8,9},{9,8},{10,11... | collective-permute-start | bytes 737288 | tf_op jit(solution)/shard_map/ppermute | solution.py:534
  4.8 4.9 %conv.1 = (f32[2,8,480,128]{3,2,1,0:T(8,128)S(1)}, f32[2,2,8,128]{3,2,1,0:T(8,128)S(1)}) custom-call(bf16[2,8,480,128]{3,2,1,0:T(8,128)(2,1)} %video_ref.1, bf16[3,3,128,128]{3,2,1,0:T(8,128)(2,1)} %weight_ref.5), custom_call_target="tpu_custom_call" | custom-call | flops 20000000000 | tf_op jit(solution)/shard_map/conv/pallas_call | solution.py:117
  9.7 0.8 edge.1
  10.5 2.0 %collective-permute-start.1 = (f32[2,2,8,128]{3,2,1,0:T(8,128)S(1)}, f32[2,2,8,128]{3,2,1,0:T(8,128)S(1)}, u32[]{:S(2)}, u32[]{:S(2)}) collective-permute-start(f32[2,2,8,128]{3,2,1,0:T(8,128)S(1)} %get-tuple-element.65.own_ref), channel_id=1, source_target_pairs={{0,1},{1,0},{2,3},{3,2},{4,5},{5,4},{6,7},{7,6},{8,9},{9,8},{10,11... | collective-permute-start | bytes 49160 | tf_op jit(solution)/shard_map/ppermute | solution.py:543
  12.5 1.8 %collective-permute-done.1.other_ref = f32[2,2,8,128]{3,2,1,0:T(8,128)S(1)} collective-permute-done((f32[2,2,8,128]{3,2,1,0:T(8,128)S(1)}, f32[2,2,8,128]{3,2,1,0:T(8,128)S(1)}, u32[]{:S(2)}, u32[]{:S(2)}) %collective-permute-start.1) | collective-permute-done | bytes 16416 | tf_op jit(solution)/shard_map/ppermute | solution.py:543
  14.3 2.8 %norm.1 = (bf16[2,528,128]{2,1,0:T(8,128)(2,1)S(1)}, bf16[2,672,128]{2,1,0:T(8,128)(2,1)}, bf16[2,672,128]{2,1,0:T(8,128)(2,1)}, bf16[2,672,128]{2,1,0:T(8,128)(...) custom-call(f32[2,8,480,128]{3,2,1,0:T(8,128)S(1)} %get-tuple-elemen, ...), custom_call_target="tpu_custom_call" | custom-call | tf_op jit(solution)/shard_map/norm/pallas_call | solution.py:253
  17.1 0.7 collective-permute-start.6
  17.8 4.4 %collective-permute-start.2 = (bf16[2,672,128]{2,1,0:T(8,128)(2,1)}, bf16[2,672,128]{2,1,0:T(8,128)(2,1)S(1)}, u32[]{:S(2)}, u32[]{:S(2)}) collective-permute-start(bf16[2,672,128]{2,1,0:T(8,128)(2,1)} %get-tuple-element.69), channel_id=1, source_target_pairs={{0,2},{2,0},{4,6},{6,4},{8,10},{10,8},{12,14},{14,12},{16,18},{18,... | collective-permute-start | bytes 1032200 | tf_op jit(solution)/shard_map/ppermute | solution.py:580
  22.2 1.5 %collective-permute-start.3 = (bf16[2,672,128]{2,1,0:T(8,128)(2,1)}, bf16[2,672,128]{2,1,0:T(8,128)(2,1)S(1)}, u32[]{:S(2)}, u32[]{:S(2)}) collective-permute-start(bf16[2,672,128]{2,1,0:T(8,128)(2,1)} %get-tuple-element.70), channel_id=1, source_target_pairs={{0,4},{2,6},{4,0},{6,2},{8,12},{10,14},{12,8},{14,10},{16,20},{18,... | collective-permute-start | bytes 1032200 | tf_op jit(solution)/shard_map/ppermute | solution.py:580
  23.7 1.6 %guest.1 = (bf16[2,960,128]{2,1,0:T(8,128)(2,1)}, bf16[2,960,128]{2,1,0:T(8,128)(2,1)}, bf16[2,2,672,128]{3,2,1,0:T(8,128)(2,1)}, bf16[2,2,288,128]{3,2,1,0:T(8,128)(2,1)}) custom-call(bf16[2,8,480,128]{3,2,1,0:T(8,128)(2,1)S(1)} %collective-permute-done.5.video_ref, bf16[2,528,128]{2,1,0:T(8,128)(2,1)S(1)} %collective-permute-done.6.packet_ref, ...), custom_call_target="tpu_custom_call" | custom-call | flops 20000000000 | tf_op jit(solution)/shard_map/guest/pallas_call | solution.py:317
  25.4 3.4 %collective-permute-start.7 = (bf16[2,2,672,128]{3,2,1,0:T(8,128)(2,1)}, bf16[2,2,672,128]{3,2,1,0:T(8,128)(2,1)S(1)}, u32[]{:S(2)}, u32[]{:S(2)}) collective-permute-start(bf16[2,2,672,128]{3,2,1,0:T(8,128)(2,1)} %get-tuple-element.79), channel_id=1, source_target_pairs={{0,4},{4,0},{8,12},{12,8},{16,20},{20,16},{24,28},{28,24},{1,5},{5... | collective-permute-start | bytes 2064392 | tf_op jit(solution)/shard_map/ppermute | solution.py:600
  29.0 4.3 %collective-permute-done.3.refs_2_ = bf16[2,672,128]{2,1,0:T(8,128)(2,1)S(1)} collective-permute-done((bf16[2,672,128]{2,1,0:T(8,128)(2,1)}, bf16[2,672,128]{2,1,0:T(8,128)(2,1)S(1)}, u32[]{:S(2)}, u32[]{:S(2)}) %collective-permute-start.3) | collective-permute-done | bytes 344096 | tf_op jit(solution)/shard_map/ppermute | solution.py:580
  33.3 5.6 %collective-permute-done.4.refs_3_ = bf16[2,672,128]{2,1,0:T(8,128)(2,1)S(1)} collective-permute-done((bf16[2,672,128]{2,1,0:T(8,128)(2,1)}, bf16[2,672,128]{2,1,0:T(8,128)(2,1)S(1)}, u32[]{:S(2)}, u32[]{:S(2)}) %collective-permute-start.4) | collective-permute-done | bytes 344096 | tf_op jit(solution)/shard_map/ppermute | solution.py:580
  39.0 3.5 %collective-permute-start.16 = (bf16[2,672,128]{2,1,0:T(8,128)(2,1)S(1)}, bf16[2,672,128]{2,1,0:T(8,128)(2,1)S(1)}, u32[]{:S(2)}, u32[]{:S(2)}) collective-permute-start(bf16[2,672,128]{2,1,0:T(8,128)(2,1)S(1)} %select_select_fusion), channel_id=1, source_target_pairs={{0,8},{2,10},{4,12},{6,14},{8,16},{10,18},{12,20},{14,22},{16,24},... | collective-permute-start | bytes 1032200 | tf_op jit(solution)/shard_map/ppermute | solution.py:606
  42.6 2.5 %collective-permute-start.11 = (bf16[2,960,128]{2,1,0:T(8,128)(2,1)S(1)}, bf16[2,960,128]{2,1,0:T(8,128)(2,1)S(1)}, u32[]{:S(2)}, u32[]{:S(2)}) collective-permute-start(bf16[2,960,128]{2,1,0:T(8,128)(2,1)S(1)} %copy-done.7), channel_id=1, source_target_pairs={{0,2},{4,6},{8,10},{12,14},{16,18},{20,22},{24,26},{28,30},{1,3},{... | collective-permute-start | bytes 1474568 | tf_op jit(solution)/shard_map/ppermute | solution.py:608
  45.1 2.2 %collective-permute-done.7.refs_6_ = bf16[2,2,672,128]{3,2,1,0:T(8,128)(2,1)S(1)} collective-permute-done((bf16[2,2,672,128]{3,2,1,0:T(8,128)(2,1)}, bf16[2,2,672,128]{3,2,1,0:T(8,128)(2,1)S(1)}, u32[]{:S(2)}, u32[]{:S(2)}) %collective-permute-start.7) | collective-permute-done | bytes 688160 | tf_op jit(solution)/shard_map/ppermute | solution.py:600
  47.2 0.8 ahead.2.refs_9_
  48.1 1.4 %collective-permute-start.15 = (bf16[2,672,128]{2,1,0:T(8,128)(2,1)S(1)}, bf16[2,672,128]{2,1,0:T(8,128)(2,1)S(1)}, u32[]{:S(2)}, u32[]{:S(2)}) collective-permute-start(bf16[2,672,128]{2,1,0:T(8,128)(2,1)S(1)} %slice_bitcast_fusion), channel_id=1, source_target_pairs={{0,2},{4,6},{8,10},{12,14},{16,18},{20,22},{24,26},{28,30},{1,3},{... | collective-permute-start | bytes 1032200 | tf_op jit(solution)/shard_map/ppermute | solution.py:612
  49.5 1.2 %collective-permute-done.16.refs_8_ = bf16[2,672,128]{2,1,0:T(8,128)(2,1)S(1)} collective-permute-done((bf16[2,672,128]{2,1,0:T(8,128)(2,1)S(1)}, bf16[2,672,128]{2,1,0:T(8,128)(2,1)S(1)}, u32[]{:S(2)}, u32[]{:S(2)}) %collective-permute-start.16) | collective-permute-done | bytes 344096 | tf_op jit(solution)/shard_map/ppermute | solution.py:606
  50.8 1.2 %early.5.own_ref = bf16[8,512,128]{2,1,0:T(8,128)(2,1)S(1)} custom-call(bf16[2,672,128]{2,1,0:T(8,128)(2,1)S(1)} %copy-done.1, bf16[2,672,128]{2,1,0:T(8,128)(2,1)S(1)} %collective-permute-done.2.refs_1_, bf16[2,672,128]{2,1,0:T(8,128)(2,1)S(1)} %collective-permute-done.3.refs_2_, bf16[2,672,128]{2,1,0:T(8,128)(2,1)S(1)} %collective-permute-done.4.refs_3_, ...), custom_call_target="tpu_custom_call" | custom-call | tf_op jit(solution)/shard_map/early/pallas_call | solution.py:451
  52.0 4.7 %collective-permute-start.17 = (bf16[8,512,128]{2,1,0:T(8,128)(2,1)S(1)}, bf16[8,512,128]{2,1,0:T(8,128)(2,1)S(1)}, u32[]{:S(2)}, u32[]{:S(2)}) collective-permute-start(bf16[8,512,128]{2,1,0:T(8,128)(2,1)S(1)} %early.5.own_ref), channel_id=1, source_target_pairs={{0,8},{2,10},{4,12},{6,14},{8,16},{10,18},{12,20},{14,22},{16,24},... | collective-permute-start | bytes 3145736 | tf_op jit(solution)/shard_map/ppermute | solution.py:622
  56.8 1.5 %collective-permute-start.9 = (bf16[2,288,128]{2,1,0:T(8,128)(2,1)S(1)}, bf16[2,288,128]{2,1,0:T(8,128)(2,1)S(1)}, u32[]{:S(2)}, u32[]{:S(2)}) collective-permute-start(bf16[2,288,128]{2,1,0:T(8,128)(2,1)S(1)} %copy-done.11), channel_id=1, source_target_pairs={{0,4},{2,6},{4,0},{6,2},{8,12},{10,14},{12,8},{14,10},{16,20},{18,... | collective-permute-start | bytes 442376 | tf_op jit(solution)/shard_map/ppermute | solution.py:580
  58.3 0.7 collective-permute-start.8
  59.0 4.6 %collective-permute-done.9.refs_2_ = bf16[2,288,128]{2,1,0:T(8,128)(2,1)S(1)} collective-permute-done((bf16[2,288,128]{2,1,0:T(8,128)(2,1)S(1)}, bf16[2,288,128]{2,1,0:T(8,128)(2,1)S(1)}, u32[]{:S(2)}, u32[]{:S(2)}) %collective-permute-start.9) | collective-permute-done | bytes 147488 | tf_op jit(solution)/shard_map/ppermute | solution.py:580
  63.5 3.4 %collective-permute-start.12 = (bf16[2,2,288,128]{3,2,1,0:T(8,128)(2,1)S(1)}, bf16[2,2,288,128]{3,2,1,0:T(8,128)(2,1)S(1)}, u32[]{:S(2)}, u32[]{:S(2)}) collective-permute-start(bf16[2,2,288,128]{3,2,1,0:T(8,128)(2,1)S(1)} %copy-done.8), channel_id=1, source_target_pairs={{0,4},{4,0},{8,12},{12,8},{16,20},{20,16},{24,28},{28,24},{1,5},{5... | collective-permute-start | bytes 884744 | tf_op jit(solution)/shard_map/ppermute | solution.py:600
  67.0 3.4 %collective-permute-start.14 = (bf16[2,288,128]{2,1,0:T(8,128)(2,1)S(1)}, bf16[2,288,128]{2,1,0:T(8,128)(2,1)S(1)}, u32[]{:S(2)}, u32[]{:S(2)}) collective-permute-start(bf16[2,288,128]{2,1,0:T(8,128)(2,1)S(1)} %select_select_fusion.1), channel_id=1, source_target_pairs={{0,8},{2,10},{4,12},{6,14},{8,16},{10,18},{12,20},{14,22},{16,24},... | collective-permute-start | bytes 442376 | tf_op jit(solution)/shard_map/ppermute | solution.py:606
  70.4 0.7 early.6.own_ref
  71.1 3.5 %collective-permute-start.19 = (bf16[8,160,128]{2,1,0:T(8,128)(2,1)S(1)}, bf16[8,160,128]{2,1,0:T(8,128)(2,1)S(1)}, u32[]{:S(2)}, u32[]{:S(2)}) collective-permute-start(bf16[8,160,128]{2,1,0:T(8,128)(2,1)S(1)} %early.6.own_ref), channel_id=1, source_target_pairs={{0,8},{2,10},{4,12},{6,14},{8,16},{10,18},{12,20},{14,22},{16,24},... | collective-permute-start | bytes 983048 | tf_op jit(solution)/shard_map/ppermute | solution.py:622
  74.6 1.3 %collective-permute-start.13 = (bf16[2,288,128]{2,1,0:T(8,128)(2,1)S(1)}, bf16[2,288,128]{2,1,0:T(8,128)(2,1)S(1)}, u32[]{:S(2)}, u32[]{:S(2)}) collective-permute-start(bf16[2,288,128]{2,1,0:T(8,128)(2,1)S(1)} %slice_bitcast_fusion.1), channel_id=1, source_target_pairs={{0,2},{4,6},{8,10},{12,14},{16,18},{20,22},{24,26},{28,30},{1,3},{... | collective-permute-start | bytes 442376 | tf_op jit(solution)/shard_map/ppermute | solution.py:612
  75.9 4.2 %collective-permute-done.17.halo_ref = bf16[8,512,128]{2,1,0:T(8,128)(2,1)S(1)} collective-permute-done((bf16[8,512,128]{2,1,0:T(8,128)(2,1)S(1)}, bf16[8,512,128]{2,1,0:T(8,128)(2,1)S(1)}, u32[]{:S(2)}, u32[]{:S(2)}) %collective-permute-start.17) | collective-permute-done | bytes 1048608 | tf_op jit(solution)/shard_map/ppermute | solution.py:622
  80.2 0.8 late.6
  81.1 1.5 %collective-permute-start.23 = (bf16[2,512,128]{2,1,0:T(8,128)(2,1)S(1)}, bf16[2,512,128]{2,1,0:T(8,128)(2,1)S(1)}, u32[]{:S(2)}, u32[]{:S(2)}) collective-permute-start(bf16[2,512,128]{2,1,0:T(8,128)(2,1)S(1)} %get-tuple-element.101), channel_id=1, source_target_pairs={{0,4},{2,6},{4,0},{6,2},{8,12},{10,14},{12,8},{14,10},{16,20},{18,... | collective-permute-start | bytes 786440 | tf_op jit(solution)/shard_map/ppermute | solution.py:580
  82.6 0.7 collective-permute-done.14.refs_8_
  83.8 0.8 early.4.own_ref
  84.6 4.4 %collective-permute-start.18 = (bf16[8,160,128]{2,1,0:T(8,128)(2,1)S(1)}, bf16[8,160,128]{2,1,0:T(8,128)(2,1)S(1)}, u32[]{:S(2)}, u32[]{:S(2)}) collective-permute-start(bf16[8,160,128]{2,1,0:T(8,128)(2,1)S(1)} %early.4.own_ref), channel_id=1, source_target_pairs={{0,8},{2,10},{4,12},{6,14},{8,16},{10,18},{12,20},{14,22},{16,24},... | collective-permute-start | bytes 983048 | tf_op jit(solution)/shard_map/ppermute | solution.py:622
  89.0 0.6 early.7.own_ref
  89.9 4.4 %collective-permute-start.29 = (bf16[8,128,128]{2,1,0:T(8,128)(2,1)S(1)}, bf16[8,128,128]{2,1,0:T(8,128)(2,1)S(1)}, u32[]{:S(2)}, u32[]{:S(2)}) collective-permute-start(bf16[8,128,128]{2,1,0:T(8,128)(2,1)S(1)} %early.7.own_ref), channel_id=1, source_target_pairs={{0,8},{2,10},{4,12},{6,14},{8,16},{10,18},{12,20},{14,22},{16,24},... | collective-permute-start | bytes 786440 | tf_op jit(solution)/shard_map/ppermute | solution.py:622
  95.2 1.1 collective-permute-start.24
  97.5 2.0 %collective-permute-done.27.refs_7_ = bf16[2,160,128]{2,1,0:T(8,128)(2,1)S(1)} collective-permute-done((bf16[2,160,128]{2,1,0:T(8,128)(2,1)S(1)}, bf16[2,160,128]{2,1,0:T(8,128)(2,1)S(1)}, u32[]{:S(2)}, u32[]{:S(2)}) %collective-permute-start.27) | collective-permute-done | bytes 81952 | tf_op jit(solution)/shard_map/ppermute | solution.py:580
  99.4 1.8 %collective-permute-done.24.refs_6_ = bf16[2,160,128]{2,1,0:T(8,128)(2,1)S(1)} collective-permute-done((bf16[2,160,128]{2,1,0:T(8,128)(2,1)S(1)}, bf16[2,160,128]{2,1,0:T(8,128)(2,1)S(1)}, u32[]{:S(2)}, u32[]{:S(2)}) %collective-permute-start.24) | collective-permute-done | bytes 81952 | tf_op jit(solution)/shard_map/ppermute | solution.py:580
  101.6 0.8 collective-permute-done.29.halo_ref
  102.8 1.1 %collective-permute-done.28.refs_3_ = bf16[2,160,128]{2,1,0:T(8,128)(2,1)S(1)} collective-permute-done((bf16[2,160,128]{2,1,0:T(8,128)(2,1)S(1)}, bf16[2,160,128]{2,1,0:T(8,128)(2,1)S(1)}, u32[]{:S(2)}, u32[]{:S(2)}) %collective-permute-start.28) | collective-permute-done | bytes 81952 | tf_op jit(solution)/shard_map/ppermute | solution.py:580
  103.9 2.0 %collective-permute-done.25.refs_2_ = bf16[2,160,128]{2,1,0:T(8,128)(2,1)S(1)} collective-permute-done((bf16[2,160,128]{2,1,0:T(8,128)(2,1)S(1)}, bf16[2,160,128]{2,1,0:T(8,128)(2,1)S(1)}, u32[]{:S(2)}, u32[]{:S(2)}) %collective-permute-start.25) | collective-permute-done | bytes 81952 | tf_op jit(solution)/shard_map/ppermute | solution.py:580
  106.5 1.1 %place.2.refs_8_ = bf16[2,4,960,128]{3,2,1,0:T(8,128)(2,1)} custom-call(bf16[2,512,128]{2,1,0:T(8,128)(2,1)S(1)} %get-tuple-element.117.refs_0_, bf16[2,512,128]{2,1,0:T(8,128)(2,1)S(1)} %collective-permute-done.20.refs_1_, bf16[2,512,128]{2,1,0:T(8,128)(2,1)S(1)} %collective-permute-done.23.refs_2_, ...), custom_call_target="tpu_custom_call" | custom-call | tf_op jit(solution)/shard_map/place/pallas_call | solution.py:516
  107.8 2.4 %collective-permute-done.31.refs_6_ = bf16[2,128,128]{2,1,0:T(8,128)(2,1)S(1)} collective-permute-done((bf16[2,128,128]{2,1,0:T(8,128)(2,1)S(1)}, bf16[2,128,128]{2,1,0:T(8,128)(2,1)S(1)}, u32[]{:S(2)}, u32[]{:S(2)}) %collective-permute-start.31) | collective-permute-done | bytes 65568 | tf_op jit(solution)/shard_map/ppermute | solution.py:580
  110.2 0.9 place.3
  (64 shorter events, 4.7 us)
Async XLA Ops:
  0.0 23.7 %collective-permute-start.5 = (bf16[2,8,480,128]{3,2,1,0:T(8,128)(2,1)}, bf16[2,8,480,128]{3,2,1,0:T(8,128)(2,1)S(1)}, u32[]{:S(2)}, u32[]{:S(2)}) collective-permute-start(bf16[2,8,480,128]{3,2,1,0:T(8,128)(2,1)} %video_ref.1), channel_id=1, source_target_pairs={{2,8},{6,12},{10,16},{14,20},{18,24},{22,28},{3,9},{7,13},{11,17},... | collective-permute-start | bytes 5898248 | tf_op jit(solution)/shard_map/ppermute | solution.py:562
  1.8 7.9 %copy-start.3 = (bf16[3,3,128,128]{3,2,1,0:T(8,128)(2,1)S(1)}, bf16[3,3,128,128]{3,2,1,0:T(8,128)(2,1)}, u32[]{:S(2)}) copy-start(bf16[3,3,128,128]{3,2,1,0:T(8,128)(2,1)} %weight_ref.5) | copy-start | bytes 884740
  1.8 7.9 %collective-permute-start = (bf16[2,480,128]{2,1,0:T(8,128)(2,1)S(1)}, bf16[2,480,128]{2,1,0:T(8,128)(2,1)S(1)}, u32[]{:S(2)}, u32[]{:S(2)}) collective-permute-start(bf16[2,480,128]{2,1,0:T(8,128)(2,1)S(1)} %dynamic-slice_bitcast_fusion), channel_id=1, source_target_pairs={{0,1},{1,0},{2,3},{3,2},{4,5},{5,4},{6,7},{7,6},{8,9},{9,8},{10,11... | collective-permute-start | bytes 737288 | tf_op jit(solution)/shard_map/ppermute | solution.py:534
  9.7 4.6 %copy-start.4 = (f32[128]{0:T(128)S(1)}, f32[128]{0:T(128)}, u32[]{:S(2)}) copy-start(f32[128]{0:T(128)} %param.7) | copy-start | bytes 1540
  9.7 4.6 %copy-start.5 = (f32[128]{0:T(128)S(1)}, f32[128]{0:T(128)}, u32[]{:S(2)}) copy-start(f32[128]{0:T(128)} %param.8) | copy-start | bytes 1540
  10.5 3.8 %collective-permute-start.1 = (f32[2,2,8,128]{3,2,1,0:T(8,128)S(1)}, f32[2,2,8,128]{3,2,1,0:T(8,128)S(1)}, u32[]{:S(2)}, u32[]{:S(2)}) collective-permute-start(f32[2,2,8,128]{3,2,1,0:T(8,128)S(1)} %get-tuple-element.65.own_ref), channel_id=1, source_target_pairs={{0,1},{1,0},{2,3},{3,2},{4,5},{5,4},{6,7},{7,6},{8,9},{9,8},{10,11... | collective-permute-start | bytes 49160 | tf_op jit(solution)/shard_map/ppermute | solution.py:543
  17.1 6.6 %collective-permute-start.6 = (bf16[2,528,128]{2,1,0:T(8,128)(2,1)S(1)}, bf16[2,528,128]{2,1,0:T(8,128)(2,1)S(1)}, u32[]{:S(2)}, u32[]{:S(2)}) collective-permute-start(bf16[2,528,128]{2,1,0:T(8,128)(2,1)S(1)} %get-tuple-element.72), channel_id=1, source_target_pairs={{2,8},{6,12},{10,16},{14,20},{18,24},{22,28},{3,9},{7,13},{11,17},... | collective-permute-start | bytes 811016 | tf_op jit(solution)/shard_map/ppermute | solution.py:583
  17.8 11.2 %collective-permute-start.2 = (bf16[2,672,128]{2,1,0:T(8,128)(2,1)}, bf16[2,672,128]{2,1,0:T(8,128)(2,1)S(1)}, u32[]{:S(2)}, u32[]{:S(2)}) collective-permute-start(bf16[2,672,128]{2,1,0:T(8,128)(2,1)} %get-tuple-element.69), channel_id=1, source_target_pairs={{0,2},{2,0},{4,6},{6,4},{8,10},{10,8},{12,14},{14,12},{16,18},{18,... | collective-permute-start | bytes 1032200 | tf_op jit(solution)/shard_map/ppermute | solution.py:580
  22.2 11.1 %collective-permute-start.3 = (bf16[2,672,128]{2,1,0:T(8,128)(2,1)}, bf16[2,672,128]{2,1,0:T(8,128)(2,1)S(1)}, u32[]{:S(2)}, u32[]{:S(2)}) collective-permute-start(bf16[2,672,128]{2,1,0:T(8,128)(2,1)} %get-tuple-element.70), channel_id=1, source_target_pairs={{0,4},{2,6},{4,0},{6,2},{8,12},{10,14},{12,8},{14,10},{16,20},{18,... | collective-permute-start | bytes 1032200 | tf_op jit(solution)/shard_map/ppermute | solution.py:580
  23.7 5.1 %copy-start.6 = (bf16[3,3,128,128]{3,2,1,0:T(8,128)(2,1)S(1)}, bf16[3,3,128,128]{3,2,1,0:T(8,128)(2,1)}, u32[]{:S(2)}) copy-start(bf16[3,3,128,128]{3,2,1,0:T(8,128)(2,1)} %weight_ref.6) | copy-start | bytes 884740
  23.7 15.3 %collective-permute-start.4 = (bf16[2,672,128]{2,1,0:T(8,128)(2,1)}, bf16[2,672,128]{2,1,0:T(8,128)(2,1)S(1)}, u32[]{:S(2)}, u32[]{:S(2)}) collective-permute-start(bf16[2,672,128]{2,1,0:T(8,128)(2,1)} %get-tuple-element.71), channel_id=1, source_target_pairs={{0,6},{2,4},{4,2},{6,0},{8,14},{10,12},{12,10},{14,8},{16,22},{18,... | collective-permute-start | bytes 1032200 | tf_op jit(solution)/shard_map/ppermute | solution.py:580
  25.4 13.6 %copy-start.1 = (bf16[2,672,128]{2,1,0:T(8,128)(2,1)S(1)}, bf16[2,672,128]{2,1,0:T(8,128)(2,1)}, u32[]{:S(2)}) copy-start(bf16[2,672,128]{2,1,0:T(8,128)(2,1)} %get-tuple-element.78.refs_0_) | copy-start | bytes 1032196
  25.4 17.2 %copy-start.7 = (bf16[2,960,128]{2,1,0:T(8,128)(2,1)S(1)}, bf16[2,960,128]{2,1,0:T(8,128)(2,1)}, u32[]{:S(2)}) copy-start(bf16[2,960,128]{2,1,0:T(8,128)(2,1)} %get-tuple-element.87) | copy-start | bytes 1474564
  25.4 21.8 %collective-permute-start.7 = (bf16[2,2,672,128]{3,2,1,0:T(8,128)(2,1)}, bf16[2,2,672,128]{3,2,1,0:T(8,128)(2,1)S(1)}, u32[]{:S(2)}, u32[]{:S(2)}) collective-permute-start(bf16[2,2,672,128]{3,2,1,0:T(8,128)(2,1)} %get-tuple-element.79), channel_id=1, source_target_pairs={{0,4},{4,0},{8,12},{12,8},{16,20},{20,16},{24,28},{28,24},{1,5},{5... | collective-permute-start | bytes 2064392 | tf_op jit(solution)/shard_map/ppermute | solution.py:600
  39.0 11.7 %collective-permute-start.16 = (bf16[2,672,128]{2,1,0:T(8,128)(2,1)S(1)}, bf16[2,672,128]{2,1,0:T(8,128)(2,1)S(1)}, u32[]{:S(2)}, u32[]{:S(2)}) collective-permute-start(bf16[2,672,128]{2,1,0:T(8,128)(2,1)S(1)} %select_select_fusion), channel_id=1, source_target_pairs={{0,8},{2,10},{4,12},{6,14},{8,16},{10,18},{12,20},{14,22},{16,24},... | collective-permute-start | bytes 1032200 | tf_op jit(solution)/shard_map/ppermute | solution.py:606
  42.6 8.2 %copy-start = (bf16[2,960,128]{2,1,0:T(8,128)(2,1)S(1)}, bf16[2,960,128]{2,1,0:T(8,128)(2,1)}, u32[]{:S(2)}) copy-start(bf16[2,960,128]{2,1,0:T(8,128)(2,1)} %get-tuple-element.73.refs_4_) | copy-start | bytes 1474564
  42.6 8.1 %collective-permute-start.11 = (bf16[2,960,128]{2,1,0:T(8,128)(2,1)S(1)}, bf16[2,960,128]{2,1,0:T(8,128)(2,1)S(1)}, u32[]{:S(2)}, u32[]{:S(2)}) collective-permute-start(bf16[2,960,128]{2,1,0:T(8,128)(2,1)S(1)} %copy-done.7), channel_id=1, source_target_pairs={{0,2},{4,6},{8,10},{12,14},{16,18},{20,22},{24,26},{28,30},{1,3},{... | collective-permute-start | bytes 1474568 | tf_op jit(solution)/shard_map/ppermute | solution.py:608
  48.0 8.7 %copy-start.11 = (bf16[2,288,128]{2,1,0:T(8,128)(2,1)S(1)}, bf16[2,288,128]{2,1,0:T(8,128)(2,1)}, u32[]{:S(2)}) copy-start(bf16[2,288,128]{2,1,0:T(8,128)(2,1)} %get-tuple-element.83) | copy-start | bytes 442372
  48.0 10.3 %copy-start.10 = (bf16[2,288,128]{2,1,0:T(8,128)(2,1)S(1)}, bf16[2,288,128]{2,1,0:T(8,128)(2,1)}, u32[]{:S(2)}) copy-start(bf16[2,288,128]{2,1,0:T(8,128)(2,1)} %get-tuple-element.85) | copy-start | bytes 442372
  48.0 10.3 %copy-start.9 = (bf16[2,288,128]{2,1,0:T(8,128)(2,1)S(1)}, bf16[2,288,128]{2,1,0:T(8,128)(2,1)}, u32[]{:S(2)}) copy-start(bf16[2,288,128]{2,1,0:T(8,128)(2,1)} %get-tuple-element.81) | copy-start | bytes 442372
  48.1 15.5 %copy-start.8 = (bf16[2,2,288,128]{3,2,1,0:T(8,128)(2,1)S(1)}, bf16[2,2,288,128]{3,2,1,0:T(8,128)(2,1)}, u32[]{:S(2)}) copy-start(bf16[2,2,288,128]{3,2,1,0:T(8,128)(2,1)} %get-tuple-element.89) | copy-start | bytes 884740
  48.1 18.9 %copy-start.2 = (bf16[2,288,128]{2,1,0:T(8,128)(2,1)S(1)}, bf16[2,288,128]{2,1,0:T(8,128)(2,1)}, u32[]{:S(2)}) copy-start(bf16[2,288,128]{2,1,0:T(8,128)(2,1)} %get-tuple-element.66.refs_0_) | copy-start | bytes 442372
  48.1 2.7 %collective-permute-start.15 = (bf16[2,672,128]{2,1,0:T(8,128)(2,1)S(1)}, bf16[2,672,128]{2,1,0:T(8,128)(2,1)S(1)}, u32[]{:S(2)}, u32[]{:S(2)}) collective-permute-start(bf16[2,672,128]{2,1,0:T(8,128)(2,1)S(1)} %slice_bitcast_fusion), channel_id=1, source_target_pairs={{0,2},{4,6},{8,10},{12,14},{16,18},{20,22},{24,26},{28,30},{1,3},{... | collective-permute-start | bytes 1032200 | tf_op jit(solution)/shard_map/ppermute | solution.py:612
  52.0 28.2 %collective-permute-start.17 = (bf16[8,512,128]{2,1,0:T(8,128)(2,1)S(1)}, bf16[8,512,128]{2,1,0:T(8,128)(2,1)S(1)}, u32[]{:S(2)}, u32[]{:S(2)}) collective-permute-start(bf16[8,512,128]{2,1,0:T(8,128)(2,1)S(1)} %early.5.own_ref), channel_id=1, source_target_pairs={{0,8},{2,10},{4,12},{6,14},{8,16},{10,18},{12,20},{14,22},{16,24},... | collective-permute-start | bytes 3145736 | tf_op jit(solution)/shard_map/ppermute | solution.py:622
  56.8 6.8 %collective-permute-start.9 = (bf16[2,288,128]{2,1,0:T(8,128)(2,1)S(1)}, bf16[2,288,128]{2,1,0:T(8,128)(2,1)S(1)}, u32[]{:S(2)}, u32[]{:S(2)}) collective-permute-start(bf16[2,288,128]{2,1,0:T(8,128)(2,1)S(1)} %copy-done.11), channel_id=1, source_target_pairs={{0,4},{2,6},{4,0},{6,2},{8,12},{10,14},{12,8},{14,10},{16,20},{18,... | collective-permute-start | bytes 442376 | tf_op jit(solution)/shard_map/ppermute | solution.py:580
  58.3 8.6 %collective-permute-start.10 = (bf16[2,288,128]{2,1,0:T(8,128)(2,1)S(1)}, bf16[2,288,128]{2,1,0:T(8,128)(2,1)S(1)}, u32[]{:S(2)}, u32[]{:S(2)}) collective-permute-start(bf16[2,288,128]{2,1,0:T(8,128)(2,1)S(1)} %copy-done.10), channel_id=1, source_target_pairs={{0,6},{2,4},{4,2},{6,0},{8,14},{10,12},{12,10},{14,8},{16,22},{18,... | collective-permute-start | bytes 442376 | tf_op jit(solution)/shard_map/ppermute | solution.py:580
  58.3 8.6 %collective-permute-start.8 = (bf16[2,288,128]{2,1,0:T(8,128)(2,1)S(1)}, bf16[2,288,128]{2,1,0:T(8,128)(2,1)S(1)}, u32[]{:S(2)}, u32[]{:S(2)}) collective-permute-start(bf16[2,288,128]{2,1,0:T(8,128)(2,1)S(1)} %copy-done.9), channel_id=1, source_target_pairs={{0,2},{2,0},{4,6},{6,4},{8,10},{10,8},{12,14},{14,12},{16,18},{18,... | collective-permute-start | bytes 442376 | tf_op jit(solution)/shard_map/ppermute | solution.py:580
  63.5 11.1 %collective-permute-start.12 = (bf16[2,2,288,128]{3,2,1,0:T(8,128)(2,1)S(1)}, bf16[2,2,288,128]{3,2,1,0:T(8,128)(2,1)S(1)}, u32[]{:S(2)}, u32[]{:S(2)}) collective-permute-start(bf16[2,2,288,128]{3,2,1,0:T(8,128)(2,1)S(1)} %copy-done.8), channel_id=1, source_target_pairs={{0,4},{4,0},{8,12},{12,8},{16,20},{20,16},{24,28},{28,24},{1,5},{5... | collective-permute-start | bytes 884744 | tf_op jit(solution)/shard_map/ppermute | solution.py:600
  67.0 16.3 %collective-permute-start.14 = (bf16[2,288,128]{2,1,0:T(8,128)(2,1)S(1)}, bf16[2,288,128]{2,1,0:T(8,128)(2,1)S(1)}, u32[]{:S(2)}, u32[]{:S(2)}) collective-permute-start(bf16[2,288,128]{2,1,0:T(8,128)(2,1)S(1)} %select_select_fusion.1), channel_id=1, source_target_pairs={{0,8},{2,10},{4,12},{6,14},{8,16},{10,18},{12,20},{14,22},{16,24},... | collective-permute-start | bytes 442376 | tf_op jit(solution)/shard_map/ppermute | solution.py:606
  71.1 18.8 %collective-permute-start.19 = (bf16[8,160,128]{2,1,0:T(8,128)(2,1)S(1)}, bf16[8,160,128]{2,1,0:T(8,128)(2,1)S(1)}, u32[]{:S(2)}, u32[]{:S(2)}) collective-permute-start(bf16[8,160,128]{2,1,0:T(8,128)(2,1)S(1)} %early.6.own_ref), channel_id=1, source_target_pairs={{0,8},{2,10},{4,12},{6,14},{8,16},{10,18},{12,20},{14,22},{16,24},... | collective-permute-start | bytes 983048 | tf_op jit(solution)/shard_map/ppermute | solution.py:622
  74.6 9.1 %collective-permute-start.13 = (bf16[2,288,128]{2,1,0:T(8,128)(2,1)S(1)}, bf16[2,288,128]{2,1,0:T(8,128)(2,1)S(1)}, u32[]{:S(2)}, u32[]{:S(2)}) collective-permute-start(bf16[2,288,128]{2,1,0:T(8,128)(2,1)S(1)} %slice_bitcast_fusion.1), channel_id=1, source_target_pairs={{0,2},{4,6},{8,10},{12,14},{16,18},{20,22},{24,26},{28,30},{1,3},{... | collective-permute-start | bytes 442376 | tf_op jit(solution)/shard_map/ppermute | solution.py:612
  80.9 13.7 %collective-permute-start.26 = (bf16[2,512,128]{2,1,0:T(8,128)(2,1)S(1)}, bf16[2,512,128]{2,1,0:T(8,128)(2,1)S(1)}, u32[]{:S(2)}, u32[]{:S(2)}) collective-permute-start(bf16[2,512,128]{2,1,0:T(8,128)(2,1)S(1)} %get-tuple-element.106), channel_id=1, source_target_pairs={{0,6},{2,4},{4,2},{6,0},{8,14},{10,12},{12,10},{14,8},{16,22},{18,... | collective-permute-start | bytes 786440 | tf_op jit(solution)/shard_map/ppermute | solution.py:580
  81.1 14.1 %collective-permute-start.23 = (bf16[2,512,128]{2,1,0:T(8,128)(2,1)S(1)}, bf16[2,512,128]{2,1,0:T(8,128)(2,1)S(1)}, u32[]{:S(2)}, u32[]{:S(2)}) collective-permute-start(bf16[2,512,128]{2,1,0:T(8,128)(2,1)S(1)} %get-tuple-element.101), channel_id=1, source_target_pairs={{0,4},{2,6},{4,0},{6,2},{8,12},{10,14},{12,8},{14,10},{16,20},{18,... | collective-permute-start | bytes 786440 | tf_op jit(solution)/shard_map/ppermute | solution.py:580
  83.3 13.0 %collective-permute-start.20 = (bf16[2,512,128]{2,1,0:T(8,128)(2,1)S(1)}, bf16[2,512,128]{2,1,0:T(8,128)(2,1)S(1)}, u32[]{:S(2)}, u32[]{:S(2)}) collective-permute-start(bf16[2,512,128]{2,1,0:T(8,128)(2,1)S(1)} %get-tuple-element.96), channel_id=1, source_target_pairs={{0,2},{2,0},{4,6},{6,4},{8,10},{10,8},{12,14},{14,12},{16,18},{18,... | collective-permute-start | bytes 786440 | tf_op jit(solution)/shard_map/ppermute | solution.py:580
  84.6 12.5 %collective-permute-start.18 = (bf16[8,160,128]{2,1,0:T(8,128)(2,1)S(1)}, bf16[8,160,128]{2,1,0:T(8,128)(2,1)S(1)}, u32[]{:S(2)}, u32[]{:S(2)}) collective-permute-start(bf16[8,160,128]{2,1,0:T(8,128)(2,1)S(1)} %early.4.own_ref), channel_id=1, source_target_pairs={{0,8},{2,10},{4,12},{6,14},{8,16},{10,18},{12,20},{14,22},{16,24},... | collective-permute-start | bytes 983048 | tf_op jit(solution)/shard_map/ppermute | solution.py:622
  89.9 12.5 %collective-permute-start.29 = (bf16[8,128,128]{2,1,0:T(8,128)(2,1)S(1)}, bf16[8,128,128]{2,1,0:T(8,128)(2,1)S(1)}, u32[]{:S(2)}, u32[]{:S(2)}) collective-permute-start(bf16[8,128,128]{2,1,0:T(8,128)(2,1)S(1)} %early.7.own_ref), channel_id=1, source_target_pairs={{0,8},{2,10},{4,12},{6,14},{8,16},{10,18},{12,20},{14,22},{16,24},... | collective-permute-start | bytes 786440 | tf_op jit(solution)/shard_map/ppermute | solution.py:622
  94.7 4.8 %collective-permute-start.27 = (bf16[2,160,128]{2,1,0:T(8,128)(2,1)S(1)}, bf16[2,160,128]{2,1,0:T(8,128)(2,1)S(1)}, u32[]{:S(2)}, u32[]{:S(2)}) collective-permute-start(bf16[2,160,128]{2,1,0:T(8,128)(2,1)S(1)} %get-tuple-element.107), channel_id=1, source_target_pairs={{0,6},{2,4},{4,2},{6,0},{8,14},{10,12},{12,10},{14,8},{16,22},{18,... | collective-permute-start | bytes 245768 | tf_op jit(solution)/shard_map/ppermute | solution.py:580
  95.2 6.0 %collective-permute-start.24 = (bf16[2,160,128]{2,1,0:T(8,128)(2,1)S(1)}, bf16[2,160,128]{2,1,0:T(8,128)(2,1)S(1)}, u32[]{:S(2)}, u32[]{:S(2)}) collective-permute-start(bf16[2,160,128]{2,1,0:T(8,128)(2,1)S(1)} %get-tuple-element.102), channel_id=1, source_target_pairs={{0,4},{2,6},{4,0},{6,2},{8,12},{10,14},{12,8},{14,10},{16,20},{18,... | collective-permute-start | bytes 245768 | tf_op jit(solution)/shard_map/ppermute | solution.py:580
  96.3 5.3 %collective-permute-start.21 = (bf16[2,160,128]{2,1,0:T(8,128)(2,1)S(1)}, bf16[2,160,128]{2,1,0:T(8,128)(2,1)S(1)}, u32[]{:S(2)}, u32[]{:S(2)}) collective-permute-start(bf16[2,160,128]{2,1,0:T(8,128)(2,1)S(1)} %get-tuple-element.97), channel_id=1, source_target_pairs={{0,2},{2,0},{4,6},{6,4},{8,10},{10,8},{12,14},{14,12},{16,18},{18,... | collective-permute-start | bytes 245768 | tf_op jit(solution)/shard_map/ppermute | solution.py:580
  99.4 4.4 %collective-permute-start.28 = (bf16[2,160,128]{2,1,0:T(8,128)(2,1)S(1)}, bf16[2,160,128]{2,1,0:T(8,128)(2,1)S(1)}, u32[]{:S(2)}, u32[]{:S(2)}) collective-permute-start(bf16[2,160,128]{2,1,0:T(8,128)(2,1)S(1)} %get-tuple-element.108), channel_id=1, source_target_pairs={{0,6},{2,4},{4,2},{6,0},{8,14},{10,12},{12,10},{14,8},{16,22},{18,... | collective-permute-start | bytes 245768 | tf_op jit(solution)/shard_map/ppermute | solution.py:580
  101.2 4.7 %collective-permute-start.25 = (bf16[2,160,128]{2,1,0:T(8,128)(2,1)S(1)}, bf16[2,160,128]{2,1,0:T(8,128)(2,1)S(1)}, u32[]{:S(2)}, u32[]{:S(2)}) collective-permute-start(bf16[2,160,128]{2,1,0:T(8,128)(2,1)S(1)} %get-tuple-element.103), channel_id=1, source_target_pairs={{0,4},{2,6},{4,0},{6,2},{8,12},{10,14},{12,8},{14,10},{16,20},{18,... | collective-permute-start | bytes 245768 | tf_op jit(solution)/shard_map/ppermute | solution.py:580
  101.6 4.9 %collective-permute-start.22 = (bf16[2,160,128]{2,1,0:T(8,128)(2,1)S(1)}, bf16[2,160,128]{2,1,0:T(8,128)(2,1)S(1)}, u32[]{:S(2)}, u32[]{:S(2)}) collective-permute-start(bf16[2,160,128]{2,1,0:T(8,128)(2,1)S(1)} %get-tuple-element.98), channel_id=1, source_target_pairs={{0,2},{2,0},{4,6},{6,4},{8,10},{10,8},{12,14},{14,12},{16,18},{18,... | collective-permute-start | bytes 245768 | tf_op jit(solution)/shard_map/ppermute | solution.py:580
  103.9 3.9 %collective-permute-start.32 = (bf16[2,128,128]{2,1,0:T(8,128)(2,1)S(1)}, bf16[2,128,128]{2,1,0:T(8,128)(2,1)S(1)}, u32[]{:S(2)}, u32[]{:S(2)}) collective-permute-start(bf16[2,128,128]{2,1,0:T(8,128)(2,1)S(1)} %get-tuple-element.116), channel_id=1, source_target_pairs={{0,6},{2,4},{4,2},{6,0},{8,14},{10,12},{12,10},{14,8},{16,22},{18,... | collective-permute-start | bytes 196616 | tf_op jit(solution)/shard_map/ppermute | solution.py:580
  105.9 4.3 %collective-permute-start.31 = (bf16[2,128,128]{2,1,0:T(8,128)(2,1)S(1)}, bf16[2,128,128]{2,1,0:T(8,128)(2,1)S(1)}, u32[]{:S(2)}, u32[]{:S(2)}) collective-permute-start(bf16[2,128,128]{2,1,0:T(8,128)(2,1)S(1)} %get-tuple-element.114), channel_id=1, source_target_pairs={{0,4},{2,6},{4,0},{6,2},{8,12},{10,14},{12,8},{14,10},{16,20},{18,... | collective-permute-start | bytes 196616 | tf_op jit(solution)/shard_map/ppermute | solution.py:580
  106.5 3.7 %collective-permute-start.30 = (bf16[2,128,128]{2,1,0:T(8,128)(2,1)S(1)}, bf16[2,128,128]{2,1,0:T(8,128)(2,1)S(1)}, u32[]{:S(2)}, u32[]{:S(2)}) collective-permute-start(bf16[2,128,128]{2,1,0:T(8,128)(2,1)S(1)} %get-tuple-element.112), channel_id=1, source_target_pairs={{0,2},{2,0},{4,6},{6,4},{8,10},{10,8},{12,14},{14,12},{16,18},{18,... | collective-permute-start | bytes 196616 | tf_op jit(solution)/shard_map/ppermute | solution.py:580

commit v9 on v7

--- a/solution.py
+++ b/solution.py
@@ -11,7 +11,7 @@
 SPAN = 8
 OWN_PARTS = (42, 18)
 GUEST_PARTS = (42, 18)
-OUT_PARTS = (32, 10, 10, 8)
+OUT_PARTS = (32, 10, 9, 9)
 VMEM = pltpu.VMEM
 ANY = pl.ANY
 F32 = jnp.float32

time: 112 us -> 111 us (level)
  transfers between devices with their start and end apart: 33 -> 33, of which waited for: 19 -> 18; matrix products, arithmetic and copies ran while one was open for 1% -> 1% of each run, Pallas kernels for 15% -> 15%
where the time goes in v9:
time: 111 us
  starting transfers between devices  54.9 us (49%)
  waiting for transfers between devices  35.7 us (32%)
  Pallas kernels  18.6 us (17%)
    ppermute x18, waiting for transfers between devices, swap(): got.append(lax.ppermute(value, 'tm', swaps[k]))  24.4 us
    ppermute x4, starting transfers between devices, body(): passed.append(lax.ppermute(u2, 'tm', onward))  17 us
    ppermute x18, starting transfers between devices, swap(): got.append(lax.ppermute(value, 'tm', swaps[k]))  12.4 us
    ppermute x2, starting transfers between devices, block(): add(2 * members, [lax.ppermute(middle, 'tm', onward)])  6.93 us
    ppermute x2, starting transfers between devices, block(): lax.ppermute(after(aways[i], own[2]) if i else aways[i], 'tm', guest_swap...  6.82 us
    ppermute x4, waiting for transfers between devices, body(): passed.append(lax.ppermute(u2, 'tm', onward))  5.31 us
    pallas_call x1, Pallas kernels, conv_call(): pl.pallas_call(functools.partial(conv_kernel, band), grid=(frames,), in_s...  4.86 us
    pallas_call x4, Pallas kernels, early_call(): pl.pallas_call(functools.partial(early_kernel, members, plan, start), in_...  3.33 us
  transfers between devices with their start and end apart: 33, of which 18 were waited for; matrix products, arithmetic and copies ran while one was open for 1% of the time, Pallas kernels for 15%

profile of v9, /device:TPU:0, one launch (start us, length us, event | category | flops | bytes accessed | tf_op | source)
XLA Modules:
  0.0 111.0 jit_solution(4504728946443026896)
XLA Ops:
  0.0 0.8 collective-permute-start.5
  0.8 1.0 dynamic-slice_bitcast_fusion
  1.8 3.0 %collective-permute-start = (bf16[2,480,128]{2,1,0:T(8,128)(2,1)S(1)}, bf16[2,480,128]{2,1,0:T(8,128)(2,1)S(1)}, u32[]{:S(2)}, u32[]{:S(2)}) collective-permute-start(bf16[2,480,128]{2,1,0:T(8,128)(2,1)S(1)} %dynamic-slice_bitcast_fusion), channel_id=1, source_target_pairs={{0,1},{1,0},{2,3},{3,2},{4,5},{5,4},{6,7},{7,6},{8,9},{9,8},{10,11... | collective-permute-start | bytes 737288 | tf_op jit(solution)/shard_map/ppermute | solution.py:534
  4.8 4.9 %conv.1 = (f32[2,8,480,128]{3,2,1,0:T(8,128)S(1)}, f32[2,2,8,128]{3,2,1,0:T(8,128)S(1)}) custom-call(bf16[2,8,480,128]{3,2,1,0:T(8,128)(2,1)} %video_ref.1, bf16[3,3,128,128]{3,2,1,0:T(8,128)(2,1)} %weight_ref.5), custom_call_target="tpu_custom_call" | custom-call | flops 20000000000 | tf_op jit(solution)/shard_map/conv/pallas_call | solution.py:117
  9.7 0.8 edge.1
  10.5 2.0 %collective-permute-start.1 = (f32[2,2,8,128]{3,2,1,0:T(8,128)S(1)}, f32[2,2,8,128]{3,2,1,0:T(8,128)S(1)}, u32[]{:S(2)}, u32[]{:S(2)}) collective-permute-start(f32[2,2,8,128]{3,2,1,0:T(8,128)S(1)} %get-tuple-element.65.own_ref), channel_id=1, source_target_pairs={{0,1},{1,0},{2,3},{3,2},{4,5},{5,4},{6,7},{7,6},{8,9},{9,8},{10,11... | collective-permute-start | bytes 49160 | tf_op jit(solution)/shard_map/ppermute | solution.py:543
  12.5 1.8 %collective-permute-done.1.other_ref = f32[2,2,8,128]{3,2,1,0:T(8,128)S(1)} collective-permute-done((f32[2,2,8,128]{3,2,1,0:T(8,128)S(1)}, f32[2,2,8,128]{3,2,1,0:T(8,128)S(1)}, u32[]{:S(2)}, u32[]{:S(2)}) %collective-permute-start.1) | collective-permute-done | bytes 16416 | tf_op jit(solution)/shard_map/ppermute | solution.py:543
  14.3 2.8 %norm.1 = (bf16[2,528,128]{2,1,0:T(8,128)(2,1)S(1)}, bf16[2,672,128]{2,1,0:T(8,128)(2,1)}, bf16[2,672,128]{2,1,0:T(8,128)(2,1)}, bf16[2,672,128]{2,1,0:T(8,128)(...) custom-call(f32[2,8,480,128]{3,2,1,0:T(8,128)S(1)} %get-tuple-elemen, ...), custom_call_target="tpu_custom_call" | custom-call | tf_op jit(solution)/shard_map/norm/pallas_call | solution.py:253
  17.1 0.7 collective-permute-start.6
  17.8 4.4 %collective-permute-start.2 = (bf16[2,672,128]{2,1,0:T(8,128)(2,1)}, bf16[2,672,128]{2,1,0:T(8,128)(2,1)S(1)}, u32[]{:S(2)}, u32[]{:S(2)}) collective-permute-start(bf16[2,672,128]{2,1,0:T(8,128)(2,1)} %get-tuple-element.69), channel_id=1, source_target_pairs={{0,2},{2,0},{4,6},{6,4},{8,10},{10,8},{12,14},{14,12},{16,18},{18,... | collective-permute-start | bytes 1032200 | tf_op jit(solution)/shard_map/ppermute | solution.py:580
  22.2 1.5 %collective-permute-start.3 = (bf16[2,672,128]{2,1,0:T(8,128)(2,1)}, bf16[2,672,128]{2,1,0:T(8,128)(2,1)S(1)}, u32[]{:S(2)}, u32[]{:S(2)}) collective-permute-start(bf16[2,672,128]{2,1,0:T(8,128)(2,1)} %get-tuple-element.70), channel_id=1, source_target_pairs={{0,4},{2,6},{4,0},{6,2},{8,12},{10,14},{12,8},{14,10},{16,20},{18,... | collective-permute-start | bytes 1032200 | tf_op jit(solution)/shard_map/ppermute | solution.py:580
  23.7 1.6 %guest.1 = (bf16[2,960,128]{2,1,0:T(8,128)(2,1)}, bf16[2,960,128]{2,1,0:T(8,128)(2,1)}, bf16[2,2,672,128]{3,2,1,0:T(8,128)(2,1)}, bf16[2,2,288,128]{3,2,1,0:T(8,128)(2,1)}) custom-call(bf16[2,8,480,128]{3,2,1,0:T(8,128)(2,1)S(1)} %collective-permute-done.5.video_ref, bf16[2,528,128]{2,1,0:T(8,128)(2,1)S(1)} %collective-permute-done.6.packet_ref, ...), custom_call_target="tpu_custom_call" | custom-call | flops 20000000000 | tf_op jit(solution)/shard_map/guest/pallas_call | solution.py:317
  25.4 3.4 %collective-permute-start.7 = (bf16[2,2,672,128]{3,2,1,0:T(8,128)(2,1)}, bf16[2,2,672,128]{3,2,1,0:T(8,128)(2,1)S(1)}, u32[]{:S(2)}, u32[]{:S(2)}) collective-permute-start(bf16[2,2,672,128]{3,2,1,0:T(8,128)(2,1)} %get-tuple-element.79), channel_id=1, source_target_pairs={{0,4},{4,0},{8,12},{12,8},{16,20},{20,16},{24,28},{28,24},{1,5},{5... | collective-permute-start | bytes 2064392 | tf_op jit(solution)/shard_map/ppermute | solution.py:600
  29.0 4.3 %collective-permute-done.3.refs_2_ = bf16[2,672,128]{2,1,0:T(8,128)(2,1)S(1)} collective-permute-done((bf16[2,672,128]{2,1,0:T(8,128)(2,1)}, bf16[2,672,128]{2,1,0:T(8,128)(2,1)S(1)}, u32[]{:S(2)}, u32[]{:S(2)}) %collective-permute-start.3) | collective-permute-done | bytes 344096 | tf_op jit(solution)/shard_map/ppermute | solution.py:580
  33.3 5.6 %collective-permute-done.4.refs_3_ = bf16[2,672,128]{2,1,0:T(8,128)(2,1)S(1)} collective-permute-done((bf16[2,672,128]{2,1,0:T(8,128)(2,1)}, bf16[2,672,128]{2,1,0:T(8,128)(2,1)S(1)}, u32[]{:S(2)}, u32[]{:S(2)}) %collective-permute-start.4) | collective-permute-done | bytes 344096 | tf_op jit(solution)/shard_map/ppermute | solution.py:580
  39.0 3.5 %collective-permute-start.16 = (bf16[2,672,128]{2,1,0:T(8,128)(2,1)S(1)}, bf16[2,672,128]{2,1,0:T(8,128)(2,1)S(1)}, u32[]{:S(2)}, u32[]{:S(2)}) collective-permute-start(bf16[2,672,128]{2,1,0:T(8,128)(2,1)S(1)} %select_select_fusion), channel_id=1, source_target_pairs={{0,8},{2,10},{4,12},{6,14},{8,16},{10,18},{12,20},{14,22},{16,24},... | collective-permute-start | bytes 1032200 | tf_op jit(solution)/shard_map/ppermute | solution.py:606
  42.6 2.5 %collective-permute-start.11 = (bf16[2,960,128]{2,1,0:T(8,128)(2,1)S(1)}, bf16[2,960,128]{2,1,0:T(8,128)(2,1)S(1)}, u32[]{:S(2)}, u32[]{:S(2)}) collective-permute-start(bf16[2,960,128]{2,1,0:T(8,128)(2,1)S(1)} %copy-done.7), channel_id=1, source_target_pairs={{0,2},{4,6},{8,10},{12,14},{16,18},{20,22},{24,26},{28,30},{1,3},{... | collective-permute-start | bytes 1474568 | tf_op jit(solution)/shard_map/ppermute | solution.py:608
  45.1 2.2 %collective-permute-done.7.refs_6_ = bf16[2,2,672,128]{3,2,1,0:T(8,128)(2,1)S(1)} collective-permute-done((bf16[2,2,672,128]{3,2,1,0:T(8,128)(2,1)}, bf16[2,2,672,128]{3,2,1,0:T(8,128)(2,1)S(1)}, u32[]{:S(2)}, u32[]{:S(2)}) %collective-permute-start.7) | collective-permute-done | bytes 688160 | tf_op jit(solution)/shard_map/ppermute | solution.py:600
  47.2 0.8 ahead.2.refs_9_
  48.1 1.4 %collective-permute-start.15 = (bf16[2,672,128]{2,1,0:T(8,128)(2,1)S(1)}, bf16[2,672,128]{2,1,0:T(8,128)(2,1)S(1)}, u32[]{:S(2)}, u32[]{:S(2)}) collective-permute-start(bf16[2,672,128]{2,1,0:T(8,128)(2,1)S(1)} %slice_bitcast_fusion), channel_id=1, source_target_pairs={{0,2},{4,6},{8,10},{12,14},{16,18},{20,22},{24,26},{28,30},{1,3},{... | collective-permute-start | bytes 1032200 | tf_op jit(solution)/shard_map/ppermute | solution.py:612
  49.5 1.2 %collective-permute-done.16.refs_8_ = bf16[2,672,128]{2,1,0:T(8,128)(2,1)S(1)} collective-permute-done((bf16[2,672,128]{2,1,0:T(8,128)(2,1)S(1)}, bf16[2,672,128]{2,1,0:T(8,128)(2,1)S(1)}, u32[]{:S(2)}, u32[]{:S(2)}) %collective-permute-start.16) | collective-permute-done | bytes 344096 | tf_op jit(solution)/shard_map/ppermute | solution.py:606
  50.8 1.2 %early.5.own_ref = bf16[8,512,128]{2,1,0:T(8,128)(2,1)S(1)} custom-call(bf16[2,672,128]{2,1,0:T(8,128)(2,1)S(1)} %copy-done.1, bf16[2,672,128]{2,1,0:T(8,128)(2,1)S(1)} %collective-permute-done.2.refs_1_, bf16[2,672,128]{2,1,0:T(8,128)(2,1)S(1)} %collective-permute-done.3.refs_2_, bf16[2,672,128]{2,1,0:T(8,128)(2,1)S(1)} %collective-permute-done.4.refs_3_, ...), custom_call_target="tpu_custom_call" | custom-call | tf_op jit(solution)/shard_map/early/pallas_call | solution.py:451
  52.0 4.7 %collective-permute-start.17 = (bf16[8,512,128]{2,1,0:T(8,128)(2,1)S(1)}, bf16[8,512,128]{2,1,0:T(8,128)(2,1)S(1)}, u32[]{:S(2)}, u32[]{:S(2)}) collective-permute-start(bf16[8,512,128]{2,1,0:T(8,128)(2,1)S(1)} %early.5.own_ref), channel_id=1, source_target_pairs={{0,8},{2,10},{4,12},{6,14},{8,16},{10,18},{12,20},{14,22},{16,24},... | collective-permute-start | bytes 3145736 | tf_op jit(solution)/shard_map/ppermute | solution.py:622
  56.8 1.5 %collective-permute-start.9 = (bf16[2,288,128]{2,1,0:T(8,128)(2,1)S(1)}, bf16[2,288,128]{2,1,0:T(8,128)(2,1)S(1)}, u32[]{:S(2)}, u32[]{:S(2)}) collective-permute-start(bf16[2,288,128]{2,1,0:T(8,128)(2,1)S(1)} %copy-done.11), channel_id=1, source_target_pairs={{0,4},{2,6},{4,0},{6,2},{8,12},{10,14},{12,8},{14,10},{16,20},{18,... | collective-permute-start | bytes 442376 | tf_op jit(solution)/shard_map/ppermute | solution.py:580
  58.3 0.7 collective-permute-start.8
  59.0 4.6 %collective-permute-done.9.refs_2_ = bf16[2,288,128]{2,1,0:T(8,128)(2,1)S(1)} collective-permute-done((bf16[2,288,128]{2,1,0:T(8,128)(2,1)S(1)}, bf16[2,288,128]{2,1,0:T(8,128)(2,1)S(1)}, u32[]{:S(2)}, u32[]{:S(2)}) %collective-permute-start.9) | collective-permute-done | bytes 147488 | tf_op jit(solution)/shard_map/ppermute | solution.py:580
  63.5 3.4 %collective-permute-start.12 = (bf16[2,2,288,128]{3,2,1,0:T(8,128)(2,1)S(1)}, bf16[2,2,288,128]{3,2,1,0:T(8,128)(2,1)S(1)}, u32[]{:S(2)}, u32[]{:S(2)}) collective-permute-start(bf16[2,2,288,128]{3,2,1,0:T(8,128)(2,1)S(1)} %copy-done.8), channel_id=1, source_target_pairs={{0,4},{4,0},{8,12},{12,8},{16,20},{20,16},{24,28},{28,24},{1,5},{5... | collective-permute-start | bytes 884744 | tf_op jit(solution)/shard_map/ppermute | solution.py:600
  67.0 3.4 %collective-permute-start.14 = (bf16[2,288,128]{2,1,0:T(8,128)(2,1)S(1)}, bf16[2,288,128]{2,1,0:T(8,128)(2,1)S(1)}, u32[]{:S(2)}, u32[]{:S(2)}) collective-permute-start(bf16[2,288,128]{2,1,0:T(8,128)(2,1)S(1)} %select_select_fusion.1), channel_id=1, source_target_pairs={{0,8},{2,10},{4,12},{6,14},{8,16},{10,18},{12,20},{14,22},{16,24},... | collective-permute-start | bytes 442376 | tf_op jit(solution)/shard_map/ppermute | solution.py:606
  70.4 0.7 early.6.own_ref
  71.1 3.5 %collective-permute-start.19 = (bf16[8,160,128]{2,1,0:T(8,128)(2,1)S(1)}, bf16[8,160,128]{2,1,0:T(8,128)(2,1)S(1)}, u32[]{:S(2)}, u32[]{:S(2)}) collective-permute-start(bf16[8,160,128]{2,1,0:T(8,128)(2,1)S(1)} %early.6.own_ref), channel_id=1, source_target_pairs={{0,8},{2,10},{4,12},{6,14},{8,16},{10,18},{12,20},{14,22},{16,24},... | collective-permute-start | bytes 983048 | tf_op jit(solution)/shard_map/ppermute | solution.py:622
  74.6 1.3 %collective-permute-start.13 = (bf16[2,288,128]{2,1,0:T(8,128)(2,1)S(1)}, bf16[2,288,128]{2,1,0:T(8,128)(2,1)S(1)}, u32[]{:S(2)}, u32[]{:S(2)}) collective-permute-start(bf16[2,288,128]{2,1,0:T(8,128)(2,1)S(1)} %slice_bitcast_fusion.1), channel_id=1, source_target_pairs={{0,2},{4,6},{8,10},{12,14},{16,18},{20,22},{24,26},{28,30},{1,3},{... | collective-permute-start | bytes 442376 | tf_op jit(solution)/shard_map/ppermute | solution.py:612
  75.9 4.2 %collective-permute-done.17.halo_ref = bf16[8,512,128]{2,1,0:T(8,128)(2,1)S(1)} collective-permute-done((bf16[8,512,128]{2,1,0:T(8,128)(2,1)S(1)}, bf16[8,512,128]{2,1,0:T(8,128)(2,1)S(1)}, u32[]{:S(2)}, u32[]{:S(2)}) %collective-permute-start.17) | collective-permute-done | bytes 1048608 | tf_op jit(solution)/shard_map/ppermute | solution.py:622
  80.2 0.8 late.6
  81.1 1.5 %collective-permute-start.23 = (bf16[2,512,128]{2,1,0:T(8,128)(2,1)S(1)}, bf16[2,512,128]{2,1,0:T(8,128)(2,1)S(1)}, u32[]{:S(2)}, u32[]{:S(2)}) collective-permute-start(bf16[2,512,128]{2,1,0:T(8,128)(2,1)S(1)} %get-tuple-element.101), channel_id=1, source_target_pairs={{0,4},{2,6},{4,0},{6,2},{8,12},{10,14},{12,8},{14,10},{16,20},{18,... | collective-permute-start | bytes 786440 | tf_op jit(solution)/shard_map/ppermute | solution.py:580
  82.6 0.7 collective-permute-done.14.refs_8_
  83.8 0.8 early.4.own_ref
  84.6 4.4 %collective-permute-start.18 = (bf16[8,144,128]{2,1,0:T(8,128)(2,1)S(1)}, bf16[8,144,128]{2,1,0:T(8,128)(2,1)S(1)}, u32[]{:S(2)}, u32[]{:S(2)}) collective-permute-start(bf16[8,144,128]{2,1,0:T(8,128)(2,1)S(1)} %early.4.own_ref), channel_id=1, source_target_pairs={{0,8},{2,10},{4,12},{6,14},{8,16},{10,18},{12,20},{14,22},{16,24},... | collective-permute-start | bytes 884744 | tf_op jit(solution)/shard_map/ppermute | solution.py:622
  90.3 4.4 %collective-permute-start.29 = (bf16[8,144,128]{2,1,0:T(8,128)(2,1)S(1)}, bf16[8,144,128]{2,1,0:T(8,128)(2,1)S(1)}, u32[]{:S(2)}, u32[]{:S(2)}) collective-permute-start(bf16[8,144,128]{2,1,0:T(8,128)(2,1)S(1)} %early.7.own_ref), channel_id=1, source_target_pairs={{0,8},{2,10},{4,12},{6,14},{8,16},{10,18},{12,20},{14,22},{16,24},... | collective-permute-start | bytes 884744 | tf_op jit(solution)/shard_map/ppermute | solution.py:622
  95.2 1.1 %collective-permute-start.24 = (bf16[2,160,128]{2,1,0:T(8,128)(2,1)S(1)}, bf16[2,160,128]{2,1,0:T(8,128)(2,1)S(1)}, u32[]{:S(2)}, u32[]{:S(2)}) collective-permute-start(bf16[2,160,128]{2,1,0:T(8,128)(2,1)S(1)} %get-tuple-element.102), channel_id=1, source_target_pairs={{0,4},{2,6},{4,0},{6,2},{8,12},{10,14},{12,8},{14,10},{16,20},{18,... | collective-permute-start | bytes 245768 | tf_op jit(solution)/shard_map/ppermute | solution.py:580
  97.0 2.5 %collective-permute-done.27.refs_7_ = bf16[2,160,128]{2,1,0:T(8,128)(2,1)S(1)} collective-permute-done((bf16[2,160,128]{2,1,0:T(8,128)(2,1)S(1)}, bf16[2,160,128]{2,1,0:T(8,128)(2,1)S(1)}, u32[]{:S(2)}, u32[]{:S(2)}) %collective-permute-start.27) | collective-permute-done | bytes 81952 | tf_op jit(solution)/shard_map/ppermute | solution.py:580
  99.5 1.8 %collective-permute-done.24.refs_6_ = bf16[2,160,128]{2,1,0:T(8,128)(2,1)S(1)} collective-permute-done((bf16[2,160,128]{2,1,0:T(8,128)(2,1)S(1)}, bf16[2,160,128]{2,1,0:T(8,128)(2,1)S(1)}, u32[]{:S(2)}, u32[]{:S(2)}) %collective-permute-start.24) | collective-permute-done | bytes 81952 | tf_op jit(solution)/shard_map/ppermute | solution.py:580
  101.6 0.8 collective-permute-done.29.halo_ref
  102.8 1.0 collective-permute-done.28.refs_3_
  103.9 1.8 %collective-permute-done.25.refs_2_ = bf16[2,144,128]{2,1,0:T(8,128)(2,1)S(1)} collective-permute-done((bf16[2,144,128]{2,1,0:T(8,128)(2,1)S(1)}, bf16[2,144,128]{2,1,0:T(8,128)(2,1)S(1)}, u32[]{:S(2)}, u32[]{:S(2)}) %collective-permute-start.25) | collective-permute-done | bytes 73760 | tf_op jit(solution)/shard_map/ppermute | solution.py:580
  106.2 1.1 %place.2.refs_8_ = bf16[2,4,960,128]{3,2,1,0:T(8,128)(2,1)} custom-call(bf16[2,512,128]{2,1,0:T(8,128)(2,1)S(1)} %get-tuple-element.118.refs_0_, bf16[2,512,128]{2,1,0:T(8,128)(2,1)S(1)} %collective-permute-done.20.refs_1_, bf16[2,512,128]{2,1,0:T(8,128)(2,1)S(1)} %collective-permute-done.23.refs_2_, ...), custom_call_target="tpu_custom_call" | custom-call | tf_op jit(solution)/shard_map/place/pallas_call | solution.py:516
  107.4 0.7 collective-permute-done.32.refs_7_
  108.0 2.0 %collective-permute-done.31.refs_6_ = bf16[2,144,128]{2,1,0:T(8,128)(2,1)S(1)} collective-permute-done((bf16[2,144,128]{2,1,0:T(8,128)(2,1)S(1)}, bf16[2,144,128]{2,1,0:T(8,128)(2,1)S(1)}, u32[]{:S(2)}, u32[]{:S(2)}) %collective-permute-start.31) | collective-permute-done | bytes 73760 | tf_op jit(solution)/shard_map/ppermute | solution.py:580
  110.0 0.9 place.3
  (64 shorter events, 4.8 us)
Async XLA Ops:
  0.0 23.7 %collective-permute-start.5 = (bf16[2,8,480,128]{3,2,1,0:T(8,128)(2,1)}, bf16[2,8,480,128]{3,2,1,0:T(8,128)(2,1)S(1)}, u32[]{:S(2)}, u32[]{:S(2)}) collective-permute-start(bf16[2,8,480,128]{3,2,1,0:T(8,128)(2,1)} %video_ref.1), channel_id=1, source_target_pairs={{2,8},{6,12},{10,16},{14,20},{18,24},{22,28},{3,9},{7,13},{11,17},... | collective-permute-start | bytes 5898248 | tf_op jit(solution)/shard_map/ppermute | solution.py:562
  1.8 7.9 %copy-start.3 = (bf16[3,3,128,128]{3,2,1,0:T(8,128)(2,1)S(1)}, bf16[3,3,128,128]{3,2,1,0:T(8,128)(2,1)}, u32[]{:S(2)}) copy-start(bf16[3,3,128,128]{3,2,1,0:T(8,128)(2,1)} %weight_ref.5) | copy-start | bytes 884740
  1.8 7.9 %collective-permute-start = (bf16[2,480,128]{2,1,0:T(8,128)(2,1)S(1)}, bf16[2,480,128]{2,1,0:T(8,128)(2,1)S(1)}, u32[]{:S(2)}, u32[]{:S(2)}) collective-permute-start(bf16[2,480,128]{2,1,0:T(8,128)(2,1)S(1)} %dynamic-slice_bitcast_fusion), channel_id=1, source_target_pairs={{0,1},{1,0},{2,3},{3,2},{4,5},{5,4},{6,7},{7,6},{8,9},{9,8},{10,11... | collective-permute-start | bytes 737288 | tf_op jit(solution)/shard_map/ppermute | solution.py:534
  9.7 4.6 %copy-start.4 = (f32[128]{0:T(128)S(1)}, f32[128]{0:T(128)}, u32[]{:S(2)}) copy-start(f32[128]{0:T(128)} %param.7) | copy-start | bytes 1540
  9.7 4.6 %copy-start.5 = (f32[128]{0:T(128)S(1)}, f32[128]{0:T(128)}, u32[]{:S(2)}) copy-start(f32[128]{0:T(128)} %param.8) | copy-start | bytes 1540
  10.5 3.8 %collective-permute-start.1 = (f32[2,2,8,128]{3,2,1,0:T(8,128)S(1)}, f32[2,2,8,128]{3,2,1,0:T(8,128)S(1)}, u32[]{:S(2)}, u32[]{:S(2)}) collective-permute-start(f32[2,2,8,128]{3,2,1,0:T(8,128)S(1)} %get-tuple-element.65.own_ref), channel_id=1, source_target_pairs={{0,1},{1,0},{2,3},{3,2},{4,5},{5,4},{6,7},{7,6},{8,9},{9,8},{10,11... | collective-permute-start | bytes 49160 | tf_op jit(solution)/shard_map/ppermute | solution.py:543
  17.1 6.6 %collective-permute-start.6 = (bf16[2,528,128]{2,1,0:T(8,128)(2,1)S(1)}, bf16[2,528,128]{2,1,0:T(8,128)(2,1)S(1)}, u32[]{:S(2)}, u32[]{:S(2)}) collective-permute-start(bf16[2,528,128]{2,1,0:T(8,128)(2,1)S(1)} %get-tuple-element.72), channel_id=1, source_target_pairs={{2,8},{6,12},{10,16},{14,20},{18,24},{22,28},{3,9},{7,13},{11,17},... | collective-permute-start | bytes 811016 | tf_op jit(solution)/shard_map/ppermute | solution.py:583
  17.8 11.2 %collective-permute-start.2 = (bf16[2,672,128]{2,1,0:T(8,128)(2,1)}, bf16[2,672,128]{2,1,0:T(8,128)(2,1)S(1)}, u32[]{:S(2)}, u32[]{:S(2)}) collective-permute-start(bf16[2,672,128]{2,1,0:T(8,128)(2,1)} %get-tuple-element.69), channel_id=1, source_target_pairs={{0,2},{2,0},{4,6},{6,4},{8,10},{10,8},{12,14},{14,12},{16,18},{18,... | collective-permute-start | bytes 1032200 | tf_op jit(solution)/shard_map/ppermute | solution.py:580
  22.2 11.1 %collective-permute-start.3 = (bf16[2,672,128]{2,1,0:T(8,128)(2,1)}, bf16[2,672,128]{2,1,0:T(8,128)(2,1)S(1)}, u32[]{:S(2)}, u32[]{:S(2)}) collective-permute-start(bf16[2,672,128]{2,1,0:T(8,128)(2,1)} %get-tuple-element.70), channel_id=1, source_target_pairs={{0,4},{2,6},{4,0},{6,2},{8,12},{10,14},{12,8},{14,10},{16,20},{18,... | collective-permute-start | bytes 1032200 | tf_op jit(solution)/shard_map/ppermute | solution.py:580
  23.7 5.1 %copy-start.6 = (bf16[3,3,128,128]{3,2,1,0:T(8,128)(2,1)S(1)}, bf16[3,3,128,128]{3,2,1,0:T(8,128)(2,1)}, u32[]{:S(2)}) copy-start(bf16[3,3,128,128]{3,2,1,0:T(8,128)(2,1)} %weight_ref.6) | copy-start | bytes 884740
  23.7 15.3 %collective-permute-start.4 = (bf16[2,672,128]{2,1,0:T(8,128)(2,1)}, bf16[2,672,128]{2,1,0:T(8,128)(2,1)S(1)}, u32[]{:S(2)}, u32[]{:S(2)}) collective-permute-start(bf16[2,672,128]{2,1,0:T(8,128)(2,1)} %get-tuple-element.71), channel_id=1, source_target_pairs={{0,6},{2,4},{4,2},{6,0},{8,14},{10,12},{12,10},{14,8},{16,22},{18,... | collective-permute-start | bytes 1032200 | tf_op jit(solution)/shard_map/ppermute | solution.py:580
  25.4 13.6 %copy-start.1 = (bf16[2,672,128]{2,1,0:T(8,128)(2,1)S(1)}, bf16[2,672,128]{2,1,0:T(8,128)(2,1)}, u32[]{:S(2)}) copy-start(bf16[2,672,128]{2,1,0:T(8,128)(2,1)} %get-tuple-element.78.refs_0_) | copy-start | bytes 1032196
  25.4 17.2 %copy-start.7 = (bf16[2,960,128]{2,1,0:T(8,128)(2,1)S(1)}, bf16[2,960,128]{2,1,0:T(8,128)(2,1)}, u32[]{:S(2)}) copy-start(bf16[2,960,128]{2,1,0:T(8,128)(2,1)} %get-tuple-element.87) | copy-start | bytes 1474564
  25.4 21.8 %collective-permute-start.7 = (bf16[2,2,672,128]{3,2,1,0:T(8,128)(2,1)}, bf16[2,2,672,128]{3,2,1,0:T(8,128)(2,1)S(1)}, u32[]{:S(2)}, u32[]{:S(2)}) collective-permute-start(bf16[2,2,672,128]{3,2,1,0:T(8,128)(2,1)} %get-tuple-element.79), channel_id=1, source_target_pairs={{0,4},{4,0},{8,12},{12,8},{16,20},{20,16},{24,28},{28,24},{1,5},{5... | collective-permute-start | bytes 2064392 | tf_op jit(solution)/shard_map/ppermute | solution.py:600
  39.0 11.7 %collective-permute-start.16 = (bf16[2,672,128]{2,1,0:T(8,128)(2,1)S(1)}, bf16[2,672,128]{2,1,0:T(8,128)(2,1)S(1)}, u32[]{:S(2)}, u32[]{:S(2)}) collective-permute-start(bf16[2,672,128]{2,1,0:T(8,128)(2,1)S(1)} %select_select_fusion), channel_id=1, source_target_pairs={{0,8},{2,10},{4,12},{6,14},{8,16},{10,18},{12,20},{14,22},{16,24},... | collective-permute-start | bytes 1032200 | tf_op jit(solution)/shard_map/ppermute | solution.py:606
  42.6 8.2 %copy-start = (bf16[2,960,128]{2,1,0:T(8,128)(2,1)S(1)}, bf16[2,960,128]{2,1,0:T(8,128)(2,1)}, u32[]{:S(2)}) copy-start(bf16[2,960,128]{2,1,0:T(8,128)(2,1)} %get-tuple-element.73.refs_4_) | copy-start | bytes 1474564
  42.6 8.1 %collective-permute-start.11 = (bf16[2,960,128]{2,1,0:T(8,128)(2,1)S(1)}, bf16[2,960,128]{2,1,0:T(8,128)(2,1)S(1)}, u32[]{:S(2)}, u32[]{:S(2)}) collective-permute-start(bf16[2,960,128]{2,1,0:T(8,128)(2,1)S(1)} %copy-done.7), channel_id=1, source_target_pairs={{0,2},{4,6},{8,10},{12,14},{16,18},{20,22},{24,26},{28,30},{1,3},{... | collective-permute-start | bytes 1474568 | tf_op jit(solution)/shard_map/ppermute | solution.py:608
  48.0 8.7 %copy-start.11 = (bf16[2,288,128]{2,1,0:T(8,128)(2,1)S(1)}, bf16[2,288,128]{2,1,0:T(8,128)(2,1)}, u32[]{:S(2)}) copy-start(bf16[2,288,128]{2,1,0:T(8,128)(2,1)} %get-tuple-element.83) | copy-start | bytes 442372
  48.0 10.3 %copy-start.10 = (bf16[2,288,128]{2,1,0:T(8,128)(2,1)S(1)}, bf16[2,288,128]{2,1,0:T(8,128)(2,1)}, u32[]{:S(2)}) copy-start(bf16[2,288,128]{2,1,0:T(8,128)(2,1)} %get-tuple-element.85) | copy-start | bytes 442372
  48.0 10.3 %copy-start.9 = (bf16[2,288,128]{2,1,0:T(8,128)(2,1)S(1)}, bf16[2,288,128]{2,1,0:T(8,128)(2,1)}, u32[]{:S(2)}) copy-start(bf16[2,288,128]{2,1,0:T(8,128)(2,1)} %get-tuple-element.81) | copy-start | bytes 442372
  48.1 15.5 %copy-start.8 = (bf16[2,2,288,128]{3,2,1,0:T(8,128)(2,1)S(1)}, bf16[2,2,288,128]{3,2,1,0:T(8,128)(2,1)}, u32[]{:S(2)}) copy-start(bf16[2,2,288,128]{3,2,1,0:T(8,128)(2,1)} %get-tuple-element.89) | copy-start | bytes 884740
  48.1 18.9 %copy-start.2 = (bf16[2,288,128]{2,1,0:T(8,128)(2,1)S(1)}, bf16[2,288,128]{2,1,0:T(8,128)(2,1)}, u32[]{:S(2)}) copy-start(bf16[2,288,128]{2,1,0:T(8,128)(2,1)} %get-tuple-element.66.refs_0_) | copy-start | bytes 442372
  48.1 2.7 %collective-permute-start.15 = (bf16[2,672,128]{2,1,0:T(8,128)(2,1)S(1)}, bf16[2,672,128]{2,1,0:T(8,128)(2,1)S(1)}, u32[]{:S(2)}, u32[]{:S(2)}) collective-permute-start(bf16[2,672,128]{2,1,0:T(8,128)(2,1)S(1)} %slice_bitcast_fusion), channel_id=1, source_target_pairs={{0,2},{4,6},{8,10},{12,14},{16,18},{20,22},{24,26},{28,30},{1,3},{... | collective-permute-start | bytes 1032200 | tf_op jit(solution)/shard_map/ppermute | solution.py:612
  52.0 28.2 %collective-permute-start.17 = (bf16[8,512,128]{2,1,0:T(8,128)(2,1)S(1)}, bf16[8,512,128]{2,1,0:T(8,128)(2,1)S(1)}, u32[]{:S(2)}, u32[]{:S(2)}) collective-permute-start(bf16[8,512,128]{2,1,0:T(8,128)(2,1)S(1)} %early.5.own_ref), channel_id=1, source_target_pairs={{0,8},{2,10},{4,12},{6,14},{8,16},{10,18},{12,20},{14,22},{16,24},... | collective-permute-start | bytes 3145736 | tf_op jit(solution)/shard_map/ppermute | solution.py:622
  56.8 6.8 %collective-permute-start.9 = (bf16[2,288,128]{2,1,0:T(8,128)(2,1)S(1)}, bf16[2,288,128]{2,1,0:T(8,128)(2,1)S(1)}, u32[]{:S(2)}, u32[]{:S(2)}) collective-permute-start(bf16[2,288,128]{2,1,0:T(8,128)(2,1)S(1)} %copy-done.11), channel_id=1, source_target_pairs={{0,4},{2,6},{4,0},{6,2},{8,12},{10,14},{12,8},{14,10},{16,20},{18,... | collective-permute-start | bytes 442376 | tf_op jit(solution)/shard_map/ppermute | solution.py:580
  58.3 8.6 %collective-permute-start.10 = (bf16[2,288,128]{2,1,0:T(8,128)(2,1)S(1)}, bf16[2,288,128]{2,1,0:T(8,128)(2,1)S(1)}, u32[]{:S(2)}, u32[]{:S(2)}) collective-permute-start(bf16[2,288,128]{2,1,0:T(8,128)(2,1)S(1)} %copy-done.10), channel_id=1, source_target_pairs={{0,6},{2,4},{4,2},{6,0},{8,14},{10,12},{12,10},{14,8},{16,22},{18,... | collective-permute-start | bytes 442376 | tf_op jit(solution)/shard_map/ppermute | solution.py:580
  58.3 8.6 %collective-permute-start.8 = (bf16[2,288,128]{2,1,0:T(8,128)(2,1)S(1)}, bf16[2,288,128]{2,1,0:T(8,128)(2,1)S(1)}, u32[]{:S(2)}, u32[]{:S(2)}) collective-permute-start(bf16[2,288,128]{2,1,0:T(8,128)(2,1)S(1)} %copy-done.9), channel_id=1, source_target_pairs={{0,2},{2,0},{4,6},{6,4},{8,10},{10,8},{12,14},{14,12},{16,18},{18,... | collective-permute-start | bytes 442376 | tf_op jit(solution)/shard_map/ppermute | solution.py:580
  63.5 11.1 %collective-permute-start.12 = (bf16[2,2,288,128]{3,2,1,0:T(8,128)(2,1)S(1)}, bf16[2,2,288,128]{3,2,1,0:T(8,128)(2,1)S(1)}, u32[]{:S(2)}, u32[]{:S(2)}) collective-permute-start(bf16[2,2,288,128]{3,2,1,0:T(8,128)(2,1)S(1)} %copy-done.8), channel_id=1, source_target_pairs={{0,4},{4,0},{8,12},{12,8},{16,20},{20,16},{24,28},{28,24},{1,5},{5... | collective-permute-start | bytes 884744 | tf_op jit(solution)/shard_map/ppermute | solution.py:600
  67.0 16.3 %collective-permute-start.14 = (bf16[2,288,128]{2,1,0:T(8,128)(2,1)S(1)}, bf16[2,288,128]{2,1,0:T(8,128)(2,1)S(1)}, u32[]{:S(2)}, u32[]{:S(2)}) collective-permute-start(bf16[2,288,128]{2,1,0:T(8,128)(2,1)S(1)} %select_select_fusion.1), channel_id=1, source_target_pairs={{0,8},{2,10},{4,12},{6,14},{8,16},{10,18},{12,20},{14,22},{16,24},... | collective-permute-start | bytes 442376 | tf_op jit(solution)/shard_map/ppermute | solution.py:606
  71.1 18.8 %collective-permute-start.19 = (bf16[8,160,128]{2,1,0:T(8,128)(2,1)S(1)}, bf16[8,160,128]{2,1,0:T(8,128)(2,1)S(1)}, u32[]{:S(2)}, u32[]{:S(2)}) collective-permute-start(bf16[8,160,128]{2,1,0:T(8,128)(2,1)S(1)} %early.6.own_ref), channel_id=1, source_target_pairs={{0,8},{2,10},{4,12},{6,14},{8,16},{10,18},{12,20},{14,22},{16,24},... | collective-permute-start | bytes 983048 | tf_op jit(solution)/shard_map/ppermute | solution.py:622
  74.6 9.1 %collective-permute-start.13 = (bf16[2,288,128]{2,1,0:T(8,128)(2,1)S(1)}, bf16[2,288,128]{2,1,0:T(8,128)(2,1)S(1)}, u32[]{:S(2)}, u32[]{:S(2)}) collective-permute-start(bf16[2,288,128]{2,1,0:T(8,128)(2,1)S(1)} %slice_bitcast_fusion.1), channel_id=1, source_target_pairs={{0,2},{4,6},{8,10},{12,14},{16,18},{20,22},{24,26},{28,30},{1,3},{... | collective-permute-start | bytes 442376 | tf_op jit(solution)/shard_map/ppermute | solution.py:612
  80.9 13.8 %collective-permute-start.26 = (bf16[2,512,128]{2,1,0:T(8,128)(2,1)S(1)}, bf16[2,512,128]{2,1,0:T(8,128)(2,1)S(1)}, u32[]{:S(2)}, u32[]{:S(2)}) collective-permute-start(bf16[2,512,128]{2,1,0:T(8,128)(2,1)S(1)} %get-tuple-element.106), channel_id=1, source_target_pairs={{0,6},{2,4},{4,2},{6,0},{8,14},{10,12},{12,10},{14,8},{16,22},{18,... | collective-permute-start | bytes 786440 | tf_op jit(solution)/shard_map/ppermute | solution.py:580
  81.1 14.1 %collective-permute-start.23 = (bf16[2,512,128]{2,1,0:T(8,128)(2,1)S(1)}, bf16[2,512,128]{2,1,0:T(8,128)(2,1)S(1)}, u32[]{:S(2)}, u32[]{:S(2)}) collective-permute-start(bf16[2,512,128]{2,1,0:T(8,128)(2,1)S(1)} %get-tuple-element.101), channel_id=1, source_target_pairs={{0,4},{2,6},{4,0},{6,2},{8,12},{10,14},{12,8},{14,10},{16,20},{18,... | collective-permute-start | bytes 786440 | tf_op jit(solution)/shard_map/ppermute | solution.py:580
  83.3 13.0 %collective-permute-start.20 = (bf16[2,512,128]{2,1,0:T(8,128)(2,1)S(1)}, bf16[2,512,128]{2,1,0:T(8,128)(2,1)S(1)}, u32[]{:S(2)}, u32[]{:S(2)}) collective-permute-start(bf16[2,512,128]{2,1,0:T(8,128)(2,1)S(1)} %get-tuple-element.96), channel_id=1, source_target_pairs={{0,2},{2,0},{4,6},{6,4},{8,10},{10,8},{12,14},{14,12},{16,18},{18,... | collective-permute-start | bytes 786440 | tf_op jit(solution)/shard_map/ppermute | solution.py:580
  84.6 12.1 %collective-permute-start.18 = (bf16[8,144,128]{2,1,0:T(8,128)(2,1)S(1)}, bf16[8,144,128]{2,1,0:T(8,128)(2,1)S(1)}, u32[]{:S(2)}, u32[]{:S(2)}) collective-permute-start(bf16[8,144,128]{2,1,0:T(8,128)(2,1)S(1)} %early.4.own_ref), channel_id=1, source_target_pairs={{0,8},{2,10},{4,12},{6,14},{8,16},{10,18},{12,20},{14,22},{16,24},... | collective-permute-start | bytes 884744 | tf_op jit(solution)/shard_map/ppermute | solution.py:622
  90.3 12.1 %collective-permute-start.29 = (bf16[8,144,128]{2,1,0:T(8,128)(2,1)S(1)}, bf16[8,144,128]{2,1,0:T(8,128)(2,1)S(1)}, u32[]{:S(2)}, u32[]{:S(2)}) collective-permute-start(bf16[8,144,128]{2,1,0:T(8,128)(2,1)S(1)} %early.7.own_ref), channel_id=1, source_target_pairs={{0,8},{2,10},{4,12},{6,14},{8,16},{10,18},{12,20},{14,22},{16,24},... | collective-permute-start | bytes 884744 | tf_op jit(solution)/shard_map/ppermute | solution.py:622
  94.7 4.8 %collective-permute-start.27 = (bf16[2,160,128]{2,1,0:T(8,128)(2,1)S(1)}, bf16[2,160,128]{2,1,0:T(8,128)(2,1)S(1)}, u32[]{:S(2)}, u32[]{:S(2)}) collective-permute-start(bf16[2,160,128]{2,1,0:T(8,128)(2,1)S(1)} %get-tuple-element.107), channel_id=1, source_target_pairs={{0,6},{2,4},{4,2},{6,0},{8,14},{10,12},{12,10},{14,8},{16,22},{18,... | collective-permute-start | bytes 245768 | tf_op jit(solution)/shard_map/ppermute | solution.py:580
  95.2 6.0 %collective-permute-start.24 = (bf16[2,160,128]{2,1,0:T(8,128)(2,1)S(1)}, bf16[2,160,128]{2,1,0:T(8,128)(2,1)S(1)}, u32[]{:S(2)}, u32[]{:S(2)}) collective-permute-start(bf16[2,160,128]{2,1,0:T(8,128)(2,1)S(1)} %get-tuple-element.102), channel_id=1, source_target_pairs={{0,4},{2,6},{4,0},{6,2},{8,12},{10,14},{12,8},{14,10},{16,20},{18,... | collective-permute-start | bytes 245768 | tf_op jit(solution)/shard_map/ppermute | solution.py:580
  96.4 5.3 %collective-permute-start.21 = (bf16[2,160,128]{2,1,0:T(8,128)(2,1)S(1)}, bf16[2,160,128]{2,1,0:T(8,128)(2,1)S(1)}, u32[]{:S(2)}, u32[]{:S(2)}) collective-permute-start(bf16[2,160,128]{2,1,0:T(8,128)(2,1)S(1)} %get-tuple-element.97), channel_id=1, source_target_pairs={{0,2},{2,0},{4,6},{6,4},{8,10},{10,8},{12,14},{14,12},{16,18},{18,... | collective-permute-start | bytes 245768 | tf_op jit(solution)/shard_map/ppermute | solution.py:580
  99.5 4.3 %collective-permute-start.28 = (bf16[2,144,128]{2,1,0:T(8,128)(2,1)S(1)}, bf16[2,144,128]{2,1,0:T(8,128)(2,1)S(1)}, u32[]{:S(2)}, u32[]{:S(2)}) collective-permute-start(bf16[2,144,128]{2,1,0:T(8,128)(2,1)S(1)} %get-tuple-element.108), channel_id=1, source_target_pairs={{0,6},{2,4},{4,2},{6,0},{8,14},{10,12},{12,10},{14,8},{16,22},{18,... | collective-permute-start | bytes 221192 | tf_op jit(solution)/shard_map/ppermute | solution.py:580
  101.3 4.4 %collective-permute-start.25 = (bf16[2,144,128]{2,1,0:T(8,128)(2,1)S(1)}, bf16[2,144,128]{2,1,0:T(8,128)(2,1)S(1)}, u32[]{:S(2)}, u32[]{:S(2)}) collective-permute-start(bf16[2,144,128]{2,1,0:T(8,128)(2,1)S(1)} %get-tuple-element.103), channel_id=1, source_target_pairs={{0,4},{2,6},{4,0},{6,2},{8,12},{10,14},{12,8},{14,10},{16,20},{18,... | collective-permute-start | bytes 221192 | tf_op jit(solution)/shard_map/ppermute | solution.py:580
  101.6 4.6 %collective-permute-start.22 = (bf16[2,144,128]{2,1,0:T(8,128)(2,1)S(1)}, bf16[2,144,128]{2,1,0:T(8,128)(2,1)S(1)}, u32[]{:S(2)}, u32[]{:S(2)}) collective-permute-start(bf16[2,144,128]{2,1,0:T(8,128)(2,1)S(1)} %get-tuple-element.98), channel_id=1, source_target_pairs={{0,2},{2,0},{4,6},{6,4},{8,10},{10,8},{12,14},{14,12},{16,18},{18,... | collective-permute-start | bytes 221192 | tf_op jit(solution)/shard_map/ppermute | solution.py:580
  103.8 4.3 %collective-permute-start.32 = (bf16[2,144,128]{2,1,0:T(8,128)(2,1)S(1)}, bf16[2,144,128]{2,1,0:T(8,128)(2,1)S(1)}, u32[]{:S(2)}, u32[]{:S(2)}) collective-permute-start(bf16[2,144,128]{2,1,0:T(8,128)(2,1)S(1)} %get-tuple-element.117), channel_id=1, source_target_pairs={{0,6},{2,4},{4,2},{6,0},{8,14},{10,12},{12,10},{14,8},{16,22},{18,... | collective-permute-start | bytes 221192 | tf_op jit(solution)/shard_map/ppermute | solution.py:580
  105.6 4.4 %collective-permute-start.31 = (bf16[2,144,128]{2,1,0:T(8,128)(2,1)S(1)}, bf16[2,144,128]{2,1,0:T(8,128)(2,1)S(1)}, u32[]{:S(2)}, u32[]{:S(2)}) collective-permute-start(bf16[2,144,128]{2,1,0:T(8,128)(2,1)S(1)} %get-tuple-element.115), channel_id=1, source_target_pairs={{0,4},{2,6},{4,0},{6,2},{8,12},{10,14},{12,8},{14,10},{16,20},{18,... | collective-permute-start | bytes 221192 | tf_op jit(solution)/shard_map/ppermute | solution.py:580
  106.2 3.8 %collective-permute-start.30 = (bf16[2,144,128]{2,1,0:T(8,128)(2,1)S(1)}, bf16[2,144,128]{2,1,0:T(8,128)(2,1)S(1)}, u32[]{:S(2)}, u32[]{:S(2)}) collective-permute-start(bf16[2,144,128]{2,1,0:T(8,128)(2,1)S(1)} %get-tuple-element.113), channel_id=1, source_target_pairs={{0,2},{2,0},{4,6},{6,4},{8,10},{10,8},{12,14},{14,12},{16,18},{18,... | collective-permute-start | bytes 221192 | tf_op jit(solution)/shard_map/ppermute | solution.py:580

commit v10 on v9

--- a/solution.py
+++ b/solution.py
@@ -236,7 +236,7 @@
             packet_ref[frame, at : at + 16] = short
         apply = norm_of(sums, count, gain_ref, shift_ref)
 
-        @pl.loop(0, band)
+        @pl.loop(0, band, unroll=4)
         def _(row):
             hidden_ref[frame, row] = apply(conv_ref[frame, row])
 
@@ -618,7 +618,7 @@
         if i == 0:
             block(1, aheads[0])
         if i > 1:
-            u2 = after(u2, passed[0] if i == 2 else late[0])
+            u2 = after(u2, passed[i - 2])
         passed.append(lax.ppermute(u2, "tm", onward))
         following = late_call(u2, passed[-1], wide, members)
         results.append(swap(following, results[-1] if results else None))

time: 111 us -> 112 us (level)
  no operation moved by 1% of the time
where the time goes in v10:
time: 112 us; the launch traced here: 111 us
  starting transfers between devices  55.4 us (49%)
  waiting for transfers between devices  35.7 us (32%)
  Pallas kernels  18.3 us (16%)
    ppermute x18, waiting for transfers between devices, swap(): got.append(lax.ppermute(value, 'tm', swaps[k]))  24.4 us
    ppermute x4, starting transfers between devices, body(): passed.append(lax.ppermute(u2, 'tm', onward))  17.1 us
    ppermute x18, starting transfers between devices, swap(): got.append(lax.ppermute(value, 'tm', swaps[k]))  12.7 us
    ppermute x2, starting transfers between devices, block(): add(2 * members, [lax.ppermute(middle, 'tm', onward)])  7.03 us
    ppermute x2, starting transfers between devices, block(): lax.ppermute(after(aways[i], own[2]) if i else aways[i], 'tm', guest_swap...  6.82 us
    ppermute x4, waiting for transfers between devices, body(): passed.append(lax.ppermute(u2, 'tm', onward))  5.34 us
    pallas_call x1, Pallas kernels, conv_call(): pl.pallas_call(functools.partial(conv_kernel, band), grid=(frames,), in_s...  4.86 us
    pallas_call x4, Pallas kernels, early_call(): pl.pallas_call(functools.partial(early_kernel, members, plan, start), in_...  3.15 us
  transfers between devices with their start and end apart: 33, of which 18 were waited for; matrix products, arithmetic and copies ran while one was open for 1% of the time, Pallas kernels for 15%

profile of v10, /device:TPU:0, one launch (start us, length us, event | category | flops | bytes accessed | tf_op | source)
XLA Modules:
  0.0 111.2 jit_solution(4165641692256515064)
XLA Ops:
  0.0 0.8 collective-permute-start.5
  0.8 1.0 dynamic-slice_bitcast_fusion
  1.8 3.0 %collective-permute-start = (bf16[2,480,128]{2,1,0:T(8,128)(2,1)S(1)}, bf16[2,480,128]{2,1,0:T(8,128)(2,1)S(1)}, u32[]{:S(2)}, u32[]{:S(2)}) collective-permute-start(bf16[2,480,128]{2,1,0:T(8,128)(2,1)S(1)} %dynamic-slice_bitcast_fusion), channel_id=1, source_target_pairs={{0,1},{1,0},{2,3},{3,2},{4,5},{5,4},{6,7},{7,6},{8,9},{9,8},{10,11... | collective-permute-start | bytes 737288 | tf_op jit(solution)/shard_map/ppermute | solution.py:534
  4.8 4.9 %conv.1 = (f32[2,8,480,128]{3,2,1,0:T(8,128)S(1)}, f32[2,2,8,128]{3,2,1,0:T(8,128)S(1)}) custom-call(bf16[2,8,480,128]{3,2,1,0:T(8,128)(2,1)} %video_ref.1, bf16[3,3,128,128]{3,2,1,0:T(8,128)(2,1)} %weight_ref.5), custom_call_target="tpu_custom_call" | custom-call | flops 20000000000 | tf_op jit(solution)/shard_map/conv/pallas_call | solution.py:117
  9.7 0.8 edge.1
  10.5 2.0 %collective-permute-start.1 = (f32[2,2,8,128]{3,2,1,0:T(8,128)S(1)}, f32[2,2,8,128]{3,2,1,0:T(8,128)S(1)}, u32[]{:S(2)}, u32[]{:S(2)}) collective-permute-start(f32[2,2,8,128]{3,2,1,0:T(8,128)S(1)} %get-tuple-element.65.own_ref), channel_id=1, source_target_pairs={{0,1},{1,0},{2,3},{3,2},{4,5},{5,4},{6,7},{7,6},{8,9},{9,8},{10,11... | collective-permute-start | bytes 49160 | tf_op jit(solution)/shard_map/ppermute | solution.py:543
  12.5 1.8 %collective-permute-done.1.other_ref = f32[2,2,8,128]{3,2,1,0:T(8,128)S(1)} collective-permute-done((f32[2,2,8,128]{3,2,1,0:T(8,128)S(1)}, f32[2,2,8,128]{3,2,1,0:T(8,128)S(1)}, u32[]{:S(2)}, u32[]{:S(2)}) %collective-permute-start.1) | collective-permute-done | bytes 16416 | tf_op jit(solution)/shard_map/ppermute | solution.py:543
  14.3 2.7 %norm.1 = (bf16[2,528,128]{2,1,0:T(8,128)(2,1)S(1)}, bf16[2,672,128]{2,1,0:T(8,128)(2,1)}, bf16[2,672,128]{2,1,0:T(8,128)(2,1)}, bf16[2,672,128]{2,1,0:T(8,128)(...) custom-call(f32[2,8,480,128]{3,2,1,0:T(8,128)S(1)} %get-tuple-elemen, ...), custom_call_target="tpu_custom_call" | custom-call | tf_op jit(solution)/shard_map/norm/pallas_call | solution.py:253
  17.0 0.7 collective-permute-start.6
  17.7 4.4 %collective-permute-start.2 = (bf16[2,672,128]{2,1,0:T(8,128)(2,1)}, bf16[2,672,128]{2,1,0:T(8,128)(2,1)S(1)}, u32[]{:S(2)}, u32[]{:S(2)}) collective-permute-start(bf16[2,672,128]{2,1,0:T(8,128)(2,1)} %get-tuple-element.69), channel_id=1, source_target_pairs={{0,2},{2,0},{4,6},{6,4},{8,10},{10,8},{12,14},{14,12},{16,18},{18,... | collective-permute-start | bytes 1032200 | tf_op jit(solution)/shard_map/ppermute | solution.py:580
  22.1 1.5 %collective-permute-start.3 = (bf16[2,672,128]{2,1,0:T(8,128)(2,1)}, bf16[2,672,128]{2,1,0:T(8,128)(2,1)S(1)}, u32[]{:S(2)}, u32[]{:S(2)}) collective-permute-start(bf16[2,672,128]{2,1,0:T(8,128)(2,1)} %get-tuple-element.70), channel_id=1, source_target_pairs={{0,4},{2,6},{4,0},{6,2},{8,12},{10,14},{12,8},{14,10},{16,20},{18,... | collective-permute-start | bytes 1032200 | tf_op jit(solution)/shard_map/ppermute | solution.py:580
  23.6 1.6 %guest.1 = (bf16[2,960,128]{2,1,0:T(8,128)(2,1)}, bf16[2,960,128]{2,1,0:T(8,128)(2,1)}, bf16[2,2,672,128]{3,2,1,0:T(8,128)(2,1)}, bf16[2,2,288,128]{3,2,1,0:T(8,128)(2,1)}) custom-call(bf16[2,8,480,128]{3,2,1,0:T(8,128)(2,1)S(1)} %collective-permute-done.5.video_ref, bf16[2,528,128]{2,1,0:T(8,128)(2,1)S(1)} %collective-permute-done.6.packet_ref, ...), custom_call_target="tpu_custom_call" | custom-call | flops 20000000000 | tf_op jit(solution)/shard_map/guest/pallas_call | solution.py:317
  25.3 3.4 %collective-permute-start.7 = (bf16[2,2,672,128]{3,2,1,0:T(8,128)(2,1)}, bf16[2,2,672,128]{3,2,1,0:T(8,128)(2,1)S(1)}, u32[]{:S(2)}, u32[]{:S(2)}) collective-permute-start(bf16[2,2,672,128]{3,2,1,0:T(8,128)(2,1)} %get-tuple-element.79), channel_id=1, source_target_pairs={{0,4},{4,0},{8,12},{12,8},{16,20},{20,16},{24,28},{28,24},{1,5},{5... | collective-permute-start | bytes 2064392 | tf_op jit(solution)/shard_map/ppermute | solution.py:600
  28.9 4.3 %collective-permute-done.3.refs_2_ = bf16[2,672,128]{2,1,0:T(8,128)(2,1)S(1)} collective-permute-done((bf16[2,672,128]{2,1,0:T(8,128)(2,1)}, bf16[2,672,128]{2,1,0:T(8,128)(2,1)S(1)}, u32[]{:S(2)}, u32[]{:S(2)}) %collective-permute-start.3) | collective-permute-done | bytes 344096 | tf_op jit(solution)/shard_map/ppermute | solution.py:580
  33.2 5.6 %collective-permute-done.4.refs_3_ = bf16[2,672,128]{2,1,0:T(8,128)(2,1)S(1)} collective-permute-done((bf16[2,672,128]{2,1,0:T(8,128)(2,1)}, bf16[2,672,128]{2,1,0:T(8,128)(2,1)S(1)}, u32[]{:S(2)}, u32[]{:S(2)}) %collective-permute-start.4) | collective-permute-done | bytes 344096 | tf_op jit(solution)/shard_map/ppermute | solution.py:580
  38.9 3.6 %collective-permute-start.16 = (bf16[2,672,128]{2,1,0:T(8,128)(2,1)S(1)}, bf16[2,672,128]{2,1,0:T(8,128)(2,1)S(1)}, u32[]{:S(2)}, u32[]{:S(2)}) collective-permute-start(bf16[2,672,128]{2,1,0:T(8,128)(2,1)S(1)} %select_select_fusion), channel_id=1, source_target_pairs={{0,8},{2,10},{4,12},{6,14},{8,16},{10,18},{12,20},{14,22},{16,24},... | collective-permute-start | bytes 1032200 | tf_op jit(solution)/shard_map/ppermute | solution.py:606
  42.5 2.4 %collective-permute-start.11 = (bf16[2,960,128]{2,1,0:T(8,128)(2,1)S(1)}, bf16[2,960,128]{2,1,0:T(8,128)(2,1)S(1)}, u32[]{:S(2)}, u32[]{:S(2)}) collective-permute-start(bf16[2,960,128]{2,1,0:T(8,128)(2,1)S(1)} %copy-done.7), channel_id=1, source_target_pairs={{0,2},{4,6},{8,10},{12,14},{16,18},{20,22},{24,26},{28,30},{1,3},{... | collective-permute-start | bytes 1474568 | tf_op jit(solution)/shard_map/ppermute | solution.py:608
  44.9 2.2 %collective-permute-done.7.refs_6_ = bf16[2,2,672,128]{3,2,1,0:T(8,128)(2,1)S(1)} collective-permute-done((bf16[2,2,672,128]{3,2,1,0:T(8,128)(2,1)}, bf16[2,2,672,128]{3,2,1,0:T(8,128)(2,1)S(1)}, u32[]{:S(2)}, u32[]{:S(2)}) %collective-permute-start.7) | collective-permute-done | bytes 688160 | tf_op jit(solution)/shard_map/ppermute | solution.py:600
  47.1 0.8 ahead.2.refs_9_
  48.0 1.4 %collective-permute-start.15 = (bf16[2,672,128]{2,1,0:T(8,128)(2,1)S(1)}, bf16[2,672,128]{2,1,0:T(8,128)(2,1)S(1)}, u32[]{:S(2)}, u32[]{:S(2)}) collective-permute-start(bf16[2,672,128]{2,1,0:T(8,128)(2,1)S(1)} %slice_bitcast_fusion), channel_id=1, source_target_pairs={{0,2},{4,6},{8,10},{12,14},{16,18},{20,22},{24,26},{28,30},{1,3},{... | collective-permute-start | bytes 1032200 | tf_op jit(solution)/shard_map/ppermute | solution.py:612
  49.4 1.2 %collective-permute-done.16.refs_8_ = bf16[2,672,128]{2,1,0:T(8,128)(2,1)S(1)} collective-permute-done((bf16[2,672,128]{2,1,0:T(8,128)(2,1)S(1)}, bf16[2,672,128]{2,1,0:T(8,128)(2,1)S(1)}, u32[]{:S(2)}, u32[]{:S(2)}) %collective-permute-start.16) | collective-permute-done | bytes 344096 | tf_op jit(solution)/shard_map/ppermute | solution.py:606
  50.6 1.2 %early.5.own_ref = bf16[8,512,128]{2,1,0:T(8,128)(2,1)S(1)} custom-call(bf16[2,672,128]{2,1,0:T(8,128)(2,1)S(1)} %copy-done.1, bf16[2,672,128]{2,1,0:T(8,128)(2,1)S(1)} %collective-permute-done.2.refs_1_, bf16[2,672,128]{2,1,0:T(8,128)(2,1)S(1)} %collective-permute-done.3.refs_2_, bf16[2,672,128]{2,1,0:T(8,128)(2,1)S(1)} %collective-permute-done.4.refs_3_, ...), custom_call_target="tpu_custom_call" | custom-call | tf_op jit(solution)/shard_map/early/pallas_call | solution.py:451
  51.9 4.9 %collective-permute-start.17 = (bf16[8,512,128]{2,1,0:T(8,128)(2,1)S(1)}, bf16[8,512,128]{2,1,0:T(8,128)(2,1)S(1)}, u32[]{:S(2)}, u32[]{:S(2)}) collective-permute-start(bf16[8,512,128]{2,1,0:T(8,128)(2,1)S(1)} %early.5.own_ref), channel_id=1, source_target_pairs={{0,8},{2,10},{4,12},{6,14},{8,16},{10,18},{12,20},{14,22},{16,24},... | collective-permute-start | bytes 3145736 | tf_op jit(solution)/shard_map/ppermute | solution.py:622
  56.8 1.5 %collective-permute-start.9 = (bf16[2,288,128]{2,1,0:T(8,128)(2,1)S(1)}, bf16[2,288,128]{2,1,0:T(8,128)(2,1)S(1)}, u32[]{:S(2)}, u32[]{:S(2)}) collective-permute-start(bf16[2,288,128]{2,1,0:T(8,128)(2,1)S(1)} %copy-done.11), channel_id=1, source_target_pairs={{0,4},{2,6},{4,0},{6,2},{8,12},{10,14},{12,8},{14,10},{16,20},{18,... | collective-permute-start | bytes 442376 | tf_op jit(solution)/shard_map/ppermute | solution.py:580
  58.3 0.7 collective-permute-start.8
  59.0 4.6 %collective-permute-done.9.refs_2_ = bf16[2,288,128]{2,1,0:T(8,128)(2,1)S(1)} collective-permute-done((bf16[2,288,128]{2,1,0:T(8,128)(2,1)S(1)}, bf16[2,288,128]{2,1,0:T(8,128)(2,1)S(1)}, u32[]{:S(2)}, u32[]{:S(2)}) %collective-permute-start.9) | collective-permute-done | bytes 147488 | tf_op jit(solution)/shard_map/ppermute | solution.py:580
  63.5 3.4 %collective-permute-start.12 = (bf16[2,2,288,128]{3,2,1,0:T(8,128)(2,1)S(1)}, bf16[2,2,288,128]{3,2,1,0:T(8,128)(2,1)S(1)}, u32[]{:S(2)}, u32[]{:S(2)}) collective-permute-start(bf16[2,2,288,128]{3,2,1,0:T(8,128)(2,1)S(1)} %copy-done.8), channel_id=1, source_target_pairs={{0,4},{4,0},{8,12},{12,8},{16,20},{20,16},{24,28},{28,24},{1,5},{5... | collective-permute-start | bytes 884744 | tf_op jit(solution)/shard_map/ppermute | solution.py:600
  67.0 3.4 %collective-permute-start.14 = (bf16[2,288,128]{2,1,0:T(8,128)(2,1)S(1)}, bf16[2,288,128]{2,1,0:T(8,128)(2,1)S(1)}, u32[]{:S(2)}, u32[]{:S(2)}) collective-permute-start(bf16[2,288,128]{2,1,0:T(8,128)(2,1)S(1)} %select_select_fusion.1), channel_id=1, source_target_pairs={{0,8},{2,10},{4,12},{6,14},{8,16},{10,18},{12,20},{14,22},{16,24},... | collective-permute-start | bytes 442376 | tf_op jit(solution)/shard_map/ppermute | solution.py:606
  70.4 0.7 early.6.own_ref
  71.1 3.5 %collective-permute-start.19 = (bf16[8,160,128]{2,1,0:T(8,128)(2,1)S(1)}, bf16[8,160,128]{2,1,0:T(8,128)(2,1)S(1)}, u32[]{:S(2)}, u32[]{:S(2)}) collective-permute-start(bf16[8,160,128]{2,1,0:T(8,128)(2,1)S(1)} %early.6.own_ref), channel_id=1, source_target_pairs={{0,8},{2,10},{4,12},{6,14},{8,16},{10,18},{12,20},{14,22},{16,24},... | collective-permute-start | bytes 983048 | tf_op jit(solution)/shard_map/ppermute | solution.py:622
  74.6 1.5 %collective-permute-start.13 = (bf16[2,288,128]{2,1,0:T(8,128)(2,1)S(1)}, bf16[2,288,128]{2,1,0:T(8,128)(2,1)S(1)}, u32[]{:S(2)}, u32[]{:S(2)}) collective-permute-start(bf16[2,288,128]{2,1,0:T(8,128)(2,1)S(1)} %slice_bitcast_fusion.1), channel_id=1, source_target_pairs={{0,2},{4,6},{8,10},{12,14},{16,18},{20,22},{24,26},{28,30},{1,3},{... | collective-permute-start | bytes 442376 | tf_op jit(solution)/shard_map/ppermute | solution.py:612
  76.1 4.1 %collective-permute-done.17.halo_ref = bf16[8,512,128]{2,1,0:T(8,128)(2,1)S(1)} collective-permute-done((bf16[8,512,128]{2,1,0:T(8,128)(2,1)S(1)}, bf16[8,512,128]{2,1,0:T(8,128)(2,1)S(1)}, u32[]{:S(2)}, u32[]{:S(2)}) %collective-permute-start.17) | collective-permute-done | bytes 1048608 | tf_op jit(solution)/shard_map/ppermute | solution.py:622
  80.2 0.8 late.6
  81.1 1.5 %collective-permute-start.23 = (bf16[2,512,128]{2,1,0:T(8,128)(2,1)S(1)}, bf16[2,512,128]{2,1,0:T(8,128)(2,1)S(1)}, u32[]{:S(2)}, u32[]{:S(2)}) collective-permute-start(bf16[2,512,128]{2,1,0:T(8,128)(2,1)S(1)} %get-tuple-element.101), channel_id=1, source_target_pairs={{0,4},{2,6},{4,0},{6,2},{8,12},{10,14},{12,8},{14,10},{16,20},{18,... | collective-permute-start | bytes 786440 | tf_op jit(solution)/shard_map/ppermute | solution.py:580
  82.6 0.7 collective-permute-done.14.refs_8_
  83.8 0.6 early.4.own_ref
  84.4 4.4 %collective-permute-start.18 = (bf16[8,144,128]{2,1,0:T(8,128)(2,1)S(1)}, bf16[8,144,128]{2,1,0:T(8,128)(2,1)S(1)}, u32[]{:S(2)}, u32[]{:S(2)}) collective-permute-start(bf16[8,144,128]{2,1,0:T(8,128)(2,1)S(1)} %early.4.own_ref), channel_id=1, source_target_pairs={{0,8},{2,10},{4,12},{6,14},{8,16},{10,18},{12,20},{14,22},{16,24},... | collective-permute-start | bytes 884744 | tf_op jit(solution)/shard_map/ppermute | solution.py:622
  89.5 0.7 collective-permute-done.19.halo_ref
  90.1 4.4 %collective-permute-start.29 = (bf16[8,144,128]{2,1,0:T(8,128)(2,1)S(1)}, bf16[8,144,128]{2,1,0:T(8,128)(2,1)S(1)}, u32[]{:S(2)}, u32[]{:S(2)}) collective-permute-start(bf16[8,144,128]{2,1,0:T(8,128)(2,1)S(1)} %early.7.own_ref), channel_id=1, source_target_pairs={{0,8},{2,10},{4,12},{6,14},{8,16},{10,18},{12,20},{14,22},{16,24},... | collective-permute-start | bytes 884744 | tf_op jit(solution)/shard_map/ppermute | solution.py:622
  95.2 1.3 %collective-permute-start.24 = (bf16[2,160,128]{2,1,0:T(8,128)(2,1)S(1)}, bf16[2,160,128]{2,1,0:T(8,128)(2,1)S(1)}, u32[]{:S(2)}, u32[]{:S(2)}) collective-permute-start(bf16[2,160,128]{2,1,0:T(8,128)(2,1)S(1)} %get-tuple-element.102), channel_id=1, source_target_pairs={{0,4},{2,6},{4,0},{6,2},{8,12},{10,14},{12,8},{14,10},{16,20},{18,... | collective-permute-start | bytes 245768 | tf_op jit(solution)/shard_map/ppermute | solution.py:580
  97.2 2.5 %collective-permute-done.27.refs_7_ = bf16[2,160,128]{2,1,0:T(8,128)(2,1)S(1)} collective-permute-done((bf16[2,160,128]{2,1,0:T(8,128)(2,1)S(1)}, bf16[2,160,128]{2,1,0:T(8,128)(2,1)S(1)}, u32[]{:S(2)}, u32[]{:S(2)}) %collective-permute-start.27) | collective-permute-done | bytes 81952 | tf_op jit(solution)/shard_map/ppermute | solution.py:580
  99.7 1.8 %collective-permute-done.24.refs_6_ = bf16[2,160,128]{2,1,0:T(8,128)(2,1)S(1)} collective-permute-done((bf16[2,160,128]{2,1,0:T(8,128)(2,1)S(1)}, bf16[2,160,128]{2,1,0:T(8,128)(2,1)S(1)}, u32[]{:S(2)}, u32[]{:S(2)}) %collective-permute-start.24) | collective-permute-done | bytes 81952 | tf_op jit(solution)/shard_map/ppermute | solution.py:580
  102.8 1.2 %collective-permute-done.28.refs_3_ = bf16[2,144,128]{2,1,0:T(8,128)(2,1)S(1)} collective-permute-done((bf16[2,144,128]{2,1,0:T(8,128)(2,1)S(1)}, bf16[2,144,128]{2,1,0:T(8,128)(2,1)S(1)}, u32[]{:S(2)}, u32[]{:S(2)}) %collective-permute-start.28) | collective-permute-done | bytes 73760 | tf_op jit(solution)/shard_map/ppermute | solution.py:580
  104.3 1.5 %collective-permute-done.25.refs_2_ = bf16[2,144,128]{2,1,0:T(8,128)(2,1)S(1)} collective-permute-done((bf16[2,144,128]{2,1,0:T(8,128)(2,1)S(1)}, bf16[2,144,128]{2,1,0:T(8,128)(2,1)S(1)}, u32[]{:S(2)}, u32[]{:S(2)}) %collective-permute-start.25) | collective-permute-done | bytes 73760 | tf_op jit(solution)/shard_map/ppermute | solution.py:580
  106.4 1.1 %place.2.refs_8_ = bf16[2,4,960,128]{3,2,1,0:T(8,128)(2,1)} custom-call(bf16[2,512,128]{2,1,0:T(8,128)(2,1)S(1)} %get-tuple-element.117.refs_0_, bf16[2,512,128]{2,1,0:T(8,128)(2,1)S(1)} %collective-permute-done.20.refs_1_, bf16[2,512,128]{2,1,0:T(8,128)(2,1)S(1)} %collective-permute-done.23.refs_2_, ...), custom_call_target="tpu_custom_call" | custom-call | tf_op jit(solution)/shard_map/place/pallas_call | solution.py:516
  107.5 0.7 collective-permute-done.32.refs_7_
  108.2 1.9 %collective-permute-done.31.refs_6_ = bf16[2,144,128]{2,1,0:T(8,128)(2,1)S(1)} collective-permute-done((bf16[2,144,128]{2,1,0:T(8,128)(2,1)S(1)}, bf16[2,144,128]{2,1,0:T(8,128)(2,1)S(1)}, u32[]{:S(2)}, u32[]{:S(2)}) %collective-permute-start.31) | collective-permute-done | bytes 73760 | tf_op jit(solution)/shard_map/ppermute | solution.py:580
  110.2 0.9 place.3
  (64 shorter events, 5.2 us)
Async XLA Ops:
  0.0 23.6 %collective-permute-start.5 = (bf16[2,8,480,128]{3,2,1,0:T(8,128)(2,1)}, bf16[2,8,480,128]{3,2,1,0:T(8,128)(2,1)S(1)}, u32[]{:S(2)}, u32[]{:S(2)}) collective-permute-start(bf16[2,8,480,128]{3,2,1,0:T(8,128)(2,1)} %video_ref.1), channel_id=1, source_target_pairs={{2,8},{6,12},{10,16},{14,20},{18,24},{22,28},{3,9},{7,13},{11,17},... | collective-permute-start | bytes 5898248 | tf_op jit(solution)/shard_map/ppermute | solution.py:562
  1.8 7.9 %copy-start.3 = (bf16[3,3,128,128]{3,2,1,0:T(8,128)(2,1)S(1)}, bf16[3,3,128,128]{3,2,1,0:T(8,128)(2,1)}, u32[]{:S(2)}) copy-start(bf16[3,3,128,128]{3,2,1,0:T(8,128)(2,1)} %weight_ref.5) | copy-start | bytes 884740
  1.8 7.9 %collective-permute-start = (bf16[2,480,128]{2,1,0:T(8,128)(2,1)S(1)}, bf16[2,480,128]{2,1,0:T(8,128)(2,1)S(1)}, u32[]{:S(2)}, u32[]{:S(2)}) collective-permute-start(bf16[2,480,128]{2,1,0:T(8,128)(2,1)S(1)} %dynamic-slice_bitcast_fusion), channel_id=1, source_target_pairs={{0,1},{1,0},{2,3},{3,2},{4,5},{5,4},{6,7},{7,6},{8,9},{9,8},{10,11... | collective-permute-start | bytes 737288 | tf_op jit(solution)/shard_map/ppermute | solution.py:534
  9.7 4.6 %copy-start.4 = (f32[128]{0:T(128)S(1)}, f32[128]{0:T(128)}, u32[]{:S(2)}) copy-start(f32[128]{0:T(128)} %param.7) | copy-start | bytes 1540
  9.7 4.6 %copy-start.5 = (f32[128]{0:T(128)S(1)}, f32[128]{0:T(128)}, u32[]{:S(2)}) copy-start(f32[128]{0:T(128)} %param.8) | copy-start | bytes 1540
  10.5 3.8 %collective-permute-start.1 = (f32[2,2,8,128]{3,2,1,0:T(8,128)S(1)}, f32[2,2,8,128]{3,2,1,0:T(8,128)S(1)}, u32[]{:S(2)}, u32[]{:S(2)}) collective-permute-start(f32[2,2,8,128]{3,2,1,0:T(8,128)S(1)} %get-tuple-element.65.own_ref), channel_id=1, source_target_pairs={{0,1},{1,0},{2,3},{3,2},{4,5},{5,4},{6,7},{7,6},{8,9},{9,8},{10,11... | collective-permute-start | bytes 49160 | tf_op jit(solution)/shard_map/ppermute | solution.py:543
  17.0 6.6 %collective-permute-start.6 = (bf16[2,528,128]{2,1,0:T(8,128)(2,1)S(1)}, bf16[2,528,128]{2,1,0:T(8,128)(2,1)S(1)}, u32[]{:S(2)}, u32[]{:S(2)}) collective-permute-start(bf16[2,528,128]{2,1,0:T(8,128)(2,1)S(1)} %get-tuple-element.72), channel_id=1, source_target_pairs={{2,8},{6,12},{10,16},{14,20},{18,24},{22,28},{3,9},{7,13},{11,17},... | collective-permute-start | bytes 811016 | tf_op jit(solution)/shard_map/ppermute | solution.py:583
  17.7 11.2 %collective-permute-start.2 = (bf16[2,672,128]{2,1,0:T(8,128)(2,1)}, bf16[2,672,128]{2,1,0:T(8,128)(2,1)S(1)}, u32[]{:S(2)}, u32[]{:S(2)}) collective-permute-start(bf16[2,672,128]{2,1,0:T(8,128)(2,1)} %get-tuple-element.69), channel_id=1, source_target_pairs={{0,2},{2,0},{4,6},{6,4},{8,10},{10,8},{12,14},{14,12},{16,18},{18,... | collective-permute-start | bytes 1032200 | tf_op jit(solution)/shard_map/ppermute | solution.py:580
  22.1 11.1 %collective-permute-start.3 = (bf16[2,672,128]{2,1,0:T(8,128)(2,1)}, bf16[2,672,128]{2,1,0:T(8,128)(2,1)S(1)}, u32[]{:S(2)}, u32[]{:S(2)}) collective-permute-start(bf16[2,672,128]{2,1,0:T(8,128)(2,1)} %get-tuple-element.70), channel_id=1, source_target_pairs={{0,4},{2,6},{4,0},{6,2},{8,12},{10,14},{12,8},{14,10},{16,20},{18,... | collective-permute-start | bytes 1032200 | tf_op jit(solution)/shard_map/ppermute | solution.py:580
  23.6 5.1 %copy-start.6 = (bf16[3,3,128,128]{3,2,1,0:T(8,128)(2,1)S(1)}, bf16[3,3,128,128]{3,2,1,0:T(8,128)(2,1)}, u32[]{:S(2)}) copy-start(bf16[3,3,128,128]{3,2,1,0:T(8,128)(2,1)} %weight_ref.6) | copy-start | bytes 884740
  23.6 15.3 %collective-permute-start.4 = (bf16[2,672,128]{2,1,0:T(8,128)(2,1)}, bf16[2,672,128]{2,1,0:T(8,128)(2,1)S(1)}, u32[]{:S(2)}, u32[]{:S(2)}) collective-permute-start(bf16[2,672,128]{2,1,0:T(8,128)(2,1)} %get-tuple-element.71), channel_id=1, source_target_pairs={{0,6},{2,4},{4,2},{6,0},{8,14},{10,12},{12,10},{14,8},{16,22},{18,... | collective-permute-start | bytes 1032200 | tf_op jit(solution)/shard_map/ppermute | solution.py:580
  25.3 13.6 %copy-start.1 = (bf16[2,672,128]{2,1,0:T(8,128)(2,1)S(1)}, bf16[2,672,128]{2,1,0:T(8,128)(2,1)}, u32[]{:S(2)}) copy-start(bf16[2,672,128]{2,1,0:T(8,128)(2,1)} %get-tuple-element.78.refs_0_) | copy-start | bytes 1032196
  25.3 17.3 %copy-start.7 = (bf16[2,960,128]{2,1,0:T(8,128)(2,1)S(1)}, bf16[2,960,128]{2,1,0:T(8,128)(2,1)}, u32[]{:S(2)}) copy-start(bf16[2,960,128]{2,1,0:T(8,128)(2,1)} %get-tuple-element.87) | copy-start | bytes 1474564
  25.3 21.8 %collective-permute-start.7 = (bf16[2,2,672,128]{3,2,1,0:T(8,128)(2,1)}, bf16[2,2,672,128]{3,2,1,0:T(8,128)(2,1)S(1)}, u32[]{:S(2)}, u32[]{:S(2)}) collective-permute-start(bf16[2,2,672,128]{3,2,1,0:T(8,128)(2,1)} %get-tuple-element.79), channel_id=1, source_target_pairs={{0,4},{4,0},{8,12},{12,8},{16,20},{20,16},{24,28},{28,24},{1,5},{5... | collective-permute-start | bytes 2064392 | tf_op jit(solution)/shard_map/ppermute | solution.py:600
  38.9 11.7 %collective-permute-start.16 = (bf16[2,672,128]{2,1,0:T(8,128)(2,1)S(1)}, bf16[2,672,128]{2,1,0:T(8,128)(2,1)S(1)}, u32[]{:S(2)}, u32[]{:S(2)}) collective-permute-start(bf16[2,672,128]{2,1,0:T(8,128)(2,1)S(1)} %select_select_fusion), channel_id=1, source_target_pairs={{0,8},{2,10},{4,12},{6,14},{8,16},{10,18},{12,20},{14,22},{16,24},... | collective-permute-start | bytes 1032200 | tf_op jit(solution)/shard_map/ppermute | solution.py:606
  42.5 8.1 %copy-start = (bf16[2,960,128]{2,1,0:T(8,128)(2,1)S(1)}, bf16[2,960,128]{2,1,0:T(8,128)(2,1)}, u32[]{:S(2)}) copy-start(bf16[2,960,128]{2,1,0:T(8,128)(2,1)} %get-tuple-element.73.refs_4_) | copy-start | bytes 1474564
  42.5 8.0 %collective-permute-start.11 = (bf16[2,960,128]{2,1,0:T(8,128)(2,1)S(1)}, bf16[2,960,128]{2,1,0:T(8,128)(2,1)S(1)}, u32[]{:S(2)}, u32[]{:S(2)}) collective-permute-start(bf16[2,960,128]{2,1,0:T(8,128)(2,1)S(1)} %copy-done.7), channel_id=1, source_target_pairs={{0,2},{4,6},{8,10},{12,14},{16,18},{20,22},{24,26},{28,30},{1,3},{... | collective-permute-start | bytes 1474568 | tf_op jit(solution)/shard_map/ppermute | solution.py:608
  47.9 8.8 %copy-start.11 = (bf16[2,288,128]{2,1,0:T(8,128)(2,1)S(1)}, bf16[2,288,128]{2,1,0:T(8,128)(2,1)}, u32[]{:S(2)}) copy-start(bf16[2,288,128]{2,1,0:T(8,128)(2,1)} %get-tuple-element.83) | copy-start | bytes 442372
  47.9 10.4 %copy-start.10 = (bf16[2,288,128]{2,1,0:T(8,128)(2,1)S(1)}, bf16[2,288,128]{2,1,0:T(8,128)(2,1)}, u32[]{:S(2)}) copy-start(bf16[2,288,128]{2,1,0:T(8,128)(2,1)} %get-tuple-element.85) | copy-start | bytes 442372
  47.9 10.4 %copy-start.9 = (bf16[2,288,128]{2,1,0:T(8,128)(2,1)S(1)}, bf16[2,288,128]{2,1,0:T(8,128)(2,1)}, u32[]{:S(2)}) copy-start(bf16[2,288,128]{2,1,0:T(8,128)(2,1)} %get-tuple-element.81) | copy-start | bytes 442372
  47.9 15.6 %copy-start.8 = (bf16[2,2,288,128]{3,2,1,0:T(8,128)(2,1)S(1)}, bf16[2,2,288,128]{3,2,1,0:T(8,128)(2,1)}, u32[]{:S(2)}) copy-start(bf16[2,2,288,128]{3,2,1,0:T(8,128)(2,1)} %get-tuple-element.89) | copy-start | bytes 884740
  47.9 19.0 %copy-start.2 = (bf16[2,288,128]{2,1,0:T(8,128)(2,1)S(1)}, bf16[2,288,128]{2,1,0:T(8,128)(2,1)}, u32[]{:S(2)}) copy-start(bf16[2,288,128]{2,1,0:T(8,128)(2,1)} %get-tuple-element.66.refs_0_) | copy-start | bytes 442372
  48.0 2.7 %collective-permute-start.15 = (bf16[2,672,128]{2,1,0:T(8,128)(2,1)S(1)}, bf16[2,672,128]{2,1,0:T(8,128)(2,1)S(1)}, u32[]{:S(2)}, u32[]{:S(2)}) collective-permute-start(bf16[2,672,128]{2,1,0:T(8,128)(2,1)S(1)} %slice_bitcast_fusion), channel_id=1, source_target_pairs={{0,2},{4,6},{8,10},{12,14},{16,18},{20,22},{24,26},{28,30},{1,3},{... | collective-permute-start | bytes 1032200 | tf_op jit(solution)/shard_map/ppermute | solution.py:612
  51.9 28.3 %collective-permute-start.17 = (bf16[8,512,128]{2,1,0:T(8,128)(2,1)S(1)}, bf16[8,512,128]{2,1,0:T(8,128)(2,1)S(1)}, u32[]{:S(2)}, u32[]{:S(2)}) collective-permute-start(bf16[8,512,128]{2,1,0:T(8,128)(2,1)S(1)} %early.5.own_ref), channel_id=1, source_target_pairs={{0,8},{2,10},{4,12},{6,14},{8,16},{10,18},{12,20},{14,22},{16,24},... | collective-permute-start | bytes 3145736 | tf_op jit(solution)/shard_map/ppermute | solution.py:622
  56.8 6.8 %collective-permute-start.9 = (bf16[2,288,128]{2,1,0:T(8,128)(2,1)S(1)}, bf16[2,288,128]{2,1,0:T(8,128)(2,1)S(1)}, u32[]{:S(2)}, u32[]{:S(2)}) collective-permute-start(bf16[2,288,128]{2,1,0:T(8,128)(2,1)S(1)} %copy-done.11), channel_id=1, source_target_pairs={{0,4},{2,6},{4,0},{6,2},{8,12},{10,14},{12,8},{14,10},{16,20},{18,... | collective-permute-start | bytes 442376 | tf_op jit(solution)/shard_map/ppermute | solution.py:580
  58.3 8.6 %collective-permute-start.10 = (bf16[2,288,128]{2,1,0:T(8,128)(2,1)S(1)}, bf16[2,288,128]{2,1,0:T(8,128)(2,1)S(1)}, u32[]{:S(2)}, u32[]{:S(2)}) collective-permute-start(bf16[2,288,128]{2,1,0:T(8,128)(2,1)S(1)} %copy-done.10), channel_id=1, source_target_pairs={{0,6},{2,4},{4,2},{6,0},{8,14},{10,12},{12,10},{14,8},{16,22},{18,... | collective-permute-start | bytes 442376 | tf_op jit(solution)/shard_map/ppermute | solution.py:580
  58.3 8.6 %collective-permute-start.8 = (bf16[2,288,128]{2,1,0:T(8,128)(2,1)S(1)}, bf16[2,288,128]{2,1,0:T(8,128)(2,1)S(1)}, u32[]{:S(2)}, u32[]{:S(2)}) collective-permute-start(bf16[2,288,128]{2,1,0:T(8,128)(2,1)S(1)} %copy-done.9), channel_id=1, source_target_pairs={{0,2},{2,0},{4,6},{6,4},{8,10},{10,8},{12,14},{14,12},{16,18},{18,... | collective-permute-start | bytes 442376 | tf_op jit(solution)/shard_map/ppermute | solution.py:580
  63.5 11.1 %collective-permute-start.12 = (bf16[2,2,288,128]{3,2,1,0:T(8,128)(2,1)S(1)}, bf16[2,2,288,128]{3,2,1,0:T(8,128)(2,1)S(1)}, u32[]{:S(2)}, u32[]{:S(2)}) collective-permute-start(bf16[2,2,288,128]{3,2,1,0:T(8,128)(2,1)S(1)} %copy-done.8), channel_id=1, source_target_pairs={{0,4},{4,0},{8,12},{12,8},{16,20},{20,16},{24,28},{28,24},{1,5},{5... | collective-permute-start | bytes 884744 | tf_op jit(solution)/shard_map/ppermute | solution.py:600
  67.0 16.3 %collective-permute-start.14 = (bf16[2,288,128]{2,1,0:T(8,128)(2,1)S(1)}, bf16[2,288,128]{2,1,0:T(8,128)(2,1)S(1)}, u32[]{:S(2)}, u32[]{:S(2)}) collective-permute-start(bf16[2,288,128]{2,1,0:T(8,128)(2,1)S(1)} %select_select_fusion.1), channel_id=1, source_target_pairs={{0,8},{2,10},{4,12},{6,14},{8,16},{10,18},{12,20},{14,22},{16,24},... | collective-permute-start | bytes 442376 | tf_op jit(solution)/shard_map/ppermute | solution.py:606
  71.1 19.0 %collective-permute-start.19 = (bf16[8,160,128]{2,1,0:T(8,128)(2,1)S(1)}, bf16[8,160,128]{2,1,0:T(8,128)(2,1)S(1)}, u32[]{:S(2)}, u32[]{:S(2)}) collective-permute-start(bf16[8,160,128]{2,1,0:T(8,128)(2,1)S(1)} %early.6.own_ref), channel_id=1, source_target_pairs={{0,8},{2,10},{4,12},{6,14},{8,16},{10,18},{12,20},{14,22},{16,24},... | collective-permute-start | bytes 983048 | tf_op jit(solution)/shard_map/ppermute | solution.py:622
  74.6 9.1 %collective-permute-start.13 = (bf16[2,288,128]{2,1,0:T(8,128)(2,1)S(1)}, bf16[2,288,128]{2,1,0:T(8,128)(2,1)S(1)}, u32[]{:S(2)}, u32[]{:S(2)}) collective-permute-start(bf16[2,288,128]{2,1,0:T(8,128)(2,1)S(1)} %slice_bitcast_fusion.1), channel_id=1, source_target_pairs={{0,2},{4,6},{8,10},{12,14},{16,18},{20,22},{24,26},{28,30},{1,3},{... | collective-permute-start | bytes 442376 | tf_op jit(solution)/shard_map/ppermute | solution.py:612
  80.9 13.9 %collective-permute-start.26 = (bf16[2,512,128]{2,1,0:T(8,128)(2,1)S(1)}, bf16[2,512,128]{2,1,0:T(8,128)(2,1)S(1)}, u32[]{:S(2)}, u32[]{:S(2)}) collective-permute-start(bf16[2,512,128]{2,1,0:T(8,128)(2,1)S(1)} %get-tuple-element.106), channel_id=1, source_target_pairs={{0,6},{2,4},{4,2},{6,0},{8,14},{10,12},{12,10},{14,8},{16,22},{18,... | collective-permute-start | bytes 786440 | tf_op jit(solution)/shard_map/ppermute | solution.py:580
  81.1 14.1 %collective-permute-start.23 = (bf16[2,512,128]{2,1,0:T(8,128)(2,1)S(1)}, bf16[2,512,128]{2,1,0:T(8,128)(2,1)S(1)}, u32[]{:S(2)}, u32[]{:S(2)}) collective-permute-start(bf16[2,512,128]{2,1,0:T(8,128)(2,1)S(1)} %get-tuple-element.101), channel_id=1, source_target_pairs={{0,4},{2,6},{4,0},{6,2},{8,12},{10,14},{12,8},{14,10},{16,20},{18,... | collective-permute-start | bytes 786440 | tf_op jit(solution)/shard_map/ppermute | solution.py:580
  83.3 13.2 %collective-permute-start.20 = (bf16[2,512,128]{2,1,0:T(8,128)(2,1)S(1)}, bf16[2,512,128]{2,1,0:T(8,128)(2,1)S(1)}, u32[]{:S(2)}, u32[]{:S(2)}) collective-permute-start(bf16[2,512,128]{2,1,0:T(8,128)(2,1)S(1)} %get-tuple-element.96), channel_id=1, source_target_pairs={{0,2},{2,0},{4,6},{6,4},{8,10},{10,8},{12,14},{14,12},{16,18},{18,... | collective-permute-start | bytes 786440 | tf_op jit(solution)/shard_map/ppermute | solution.py:580
  84.4 12.4 %collective-permute-start.18 = (bf16[8,144,128]{2,1,0:T(8,128)(2,1)S(1)}, bf16[8,144,128]{2,1,0:T(8,128)(2,1)S(1)}, u32[]{:S(2)}, u32[]{:S(2)}) collective-permute-start(bf16[8,144,128]{2,1,0:T(8,128)(2,1)S(1)} %early.4.own_ref), channel_id=1, source_target_pairs={{0,8},{2,10},{4,12},{6,14},{8,16},{10,18},{12,20},{14,22},{16,24},... | collective-permute-start | bytes 884744 | tf_op jit(solution)/shard_map/ppermute | solution.py:622
  90.1 12.3 %collective-permute-start.29 = (bf16[8,144,128]{2,1,0:T(8,128)(2,1)S(1)}, bf16[8,144,128]{2,1,0:T(8,128)(2,1)S(1)}, u32[]{:S(2)}, u32[]{:S(2)}) collective-permute-start(bf16[8,144,128]{2,1,0:T(8,128)(2,1)S(1)} %early.7.own_ref), channel_id=1, source_target_pairs={{0,8},{2,10},{4,12},{6,14},{8,16},{10,18},{12,20},{14,22},{16,24},... | collective-permute-start | bytes 884744 | tf_op jit(solution)/shard_map/ppermute | solution.py:622
  94.9 4.8 %collective-permute-start.27 = (bf16[2,160,128]{2,1,0:T(8,128)(2,1)S(1)}, bf16[2,160,128]{2,1,0:T(8,128)(2,1)S(1)}, u32[]{:S(2)}, u32[]{:S(2)}) collective-permute-start(bf16[2,160,128]{2,1,0:T(8,128)(2,1)S(1)} %get-tuple-element.107), channel_id=1, source_target_pairs={{0,6},{2,4},{4,2},{6,0},{8,14},{10,12},{12,10},{14,8},{16,22},{18,... | collective-permute-start | bytes 245768 | tf_op jit(solution)/shard_map/ppermute | solution.py:580
  95.2 6.2 %collective-permute-start.24 = (bf16[2,160,128]{2,1,0:T(8,128)(2,1)S(1)}, bf16[2,160,128]{2,1,0:T(8,128)(2,1)S(1)}, u32[]{:S(2)}, u32[]{:S(2)}) collective-permute-start(bf16[2,160,128]{2,1,0:T(8,128)(2,1)S(1)} %get-tuple-element.102), channel_id=1, source_target_pairs={{0,4},{2,6},{4,0},{6,2},{8,12},{10,14},{12,8},{14,10},{16,20},{18,... | collective-permute-start | bytes 245768 | tf_op jit(solution)/shard_map/ppermute | solution.py:580
  96.5 5.3 %collective-permute-start.21 = (bf16[2,160,128]{2,1,0:T(8,128)(2,1)S(1)}, bf16[2,160,128]{2,1,0:T(8,128)(2,1)S(1)}, u32[]{:S(2)}, u32[]{:S(2)}) collective-permute-start(bf16[2,160,128]{2,1,0:T(8,128)(2,1)S(1)} %get-tuple-element.97), channel_id=1, source_target_pairs={{0,2},{2,0},{4,6},{6,4},{8,10},{10,8},{12,14},{14,12},{16,18},{18,... | collective-permute-start | bytes 245768 | tf_op jit(solution)/shard_map/ppermute | solution.py:580
  99.7 4.3 %collective-permute-start.28 = (bf16[2,144,128]{2,1,0:T(8,128)(2,1)S(1)}, bf16[2,144,128]{2,1,0:T(8,128)(2,1)S(1)}, u32[]{:S(2)}, u32[]{:S(2)}) collective-permute-start(bf16[2,144,128]{2,1,0:T(8,128)(2,1)S(1)} %get-tuple-element.108), channel_id=1, source_target_pairs={{0,6},{2,4},{4,2},{6,0},{8,14},{10,12},{12,10},{14,8},{16,22},{18,... | collective-permute-start | bytes 221192 | tf_op jit(solution)/shard_map/ppermute | solution.py:580
  101.5 4.4 %collective-permute-start.25 = (bf16[2,144,128]{2,1,0:T(8,128)(2,1)S(1)}, bf16[2,144,128]{2,1,0:T(8,128)(2,1)S(1)}, u32[]{:S(2)}, u32[]{:S(2)}) collective-permute-start(bf16[2,144,128]{2,1,0:T(8,128)(2,1)S(1)} %get-tuple-element.103), channel_id=1, source_target_pairs={{0,4},{2,6},{4,0},{6,2},{8,12},{10,14},{12,8},{14,10},{16,20},{18,... | collective-permute-start | bytes 221192 | tf_op jit(solution)/shard_map/ppermute | solution.py:580
  101.8 4.6 %collective-permute-start.22 = (bf16[2,144,128]{2,1,0:T(8,128)(2,1)S(1)}, bf16[2,144,128]{2,1,0:T(8,128)(2,1)S(1)}, u32[]{:S(2)}, u32[]{:S(2)}) collective-permute-start(bf16[2,144,128]{2,1,0:T(8,128)(2,1)S(1)} %get-tuple-element.98), channel_id=1, source_target_pairs={{0,2},{2,0},{4,6},{6,4},{8,10},{10,8},{12,14},{14,12},{16,18},{18,... | collective-permute-start | bytes 221192 | tf_op jit(solution)/shard_map/ppermute | solution.py:580
  103.9 4.3 %collective-permute-start.32 = (bf16[2,144,128]{2,1,0:T(8,128)(2,1)S(1)}, bf16[2,144,128]{2,1,0:T(8,128)(2,1)S(1)}, u32[]{:S(2)}, u32[]{:S(2)}) collective-permute-start(bf16[2,144,128]{2,1,0:T(8,128)(2,1)S(1)} %get-tuple-element.116), channel_id=1, source_target_pairs={{0,6},{2,4},{4,2},{6,0},{8,14},{10,12},{12,10},{14,8},{16,22},{18,... | collective-permute-start | bytes 221192 | tf_op jit(solution)/shard_map/ppermute | solution.py:580
  105.8 4.4 %collective-permute-start.31 = (bf16[2,144,128]{2,1,0:T(8,128)(2,1)S(1)}, bf16[2,144,128]{2,1,0:T(8,128)(2,1)S(1)}, u32[]{:S(2)}, u32[]{:S(2)}) collective-permute-start(bf16[2,144,128]{2,1,0:T(8,128)(2,1)S(1)} %get-tuple-element.114), channel_id=1, source_target_pairs={{0,4},{2,6},{4,0},{6,2},{8,12},{10,14},{12,8},{14,10},{16,20},{18,... | collective-permute-start | bytes 221192 | tf_op jit(solution)/shard_map/ppermute | solution.py:580
  106.4 3.8 %collective-permute-start.30 = (bf16[2,144,128]{2,1,0:T(8,128)(2,1)S(1)}, bf16[2,144,128]{2,1,0:T(8,128)(2,1)S(1)}, u32[]{:S(2)}, u32[]{:S(2)}) collective-permute-start(bf16[2,144,128]{2,1,0:T(8,128)(2,1)S(1)} %get-tuple-element.112), channel_id=1, source_target_pairs={{0,2},{2,0},{4,6},{6,4},{8,10},{10,8},{12,14},{14,12},{16,18},{18,... | collective-permute-start | bytes 221192 | tf_op jit(solution)/shard_map/ppermute | solution.py:580
